TPU v7x, 32 devices: a whole 2x2x4 slice. The times are simulated.
32 devices in a mesh: grp: 4 (over y, x), ctx: 8 (over z, core).
Axes of the slice: x: 2, y: 2, z: 4, core: 2. Of those that a mesh axis runs over, the one named last changes fastest.
Arguments:
- hidden_in: bfloat16 [8, 1024, 1024], P('grp', 'ctx'), may hold values from -6 to 6
- grad_out: bfloat16 [8, 1024, 1024], P('grp', 'ctx'), may hold values from -6 to 6
- segments: int32 [8, 1024], P('grp'), may hold values from 0 to 4, as said below
- routes: int32 [8, 1024, 8], P('grp', 'ctx'), may hold values from 0 to 31, all different within a row; in each aligned block of 128 rows (0 to 127, 128 to 255, ..., all dimensions but the last counted through in order) at most 42 rows name the same one
- attn_gain: bfloat16 [2, 1024], P(None, ('grp', 'ctx')), may hold values from 0.5 to 1.5
- w_query: bfloat16 [2, 1024, 1024], P(None, ('grp', 'ctx')), may hold values from -0.1875 to 0.1875
- key_weight: bfloat16 [2, 1024, 512], P(None, ('grp', 'ctx')), may hold values from -0.1875 to 0.1875
- value_weight: bfloat16 [2, 1024, 512], P(None, ('grp', 'ctx')), may hold values from -0.1875 to 0.1875
- w_output: bfloat16 [2, 1024, 1024], P(None, ('grp', 'ctx')), may hold values from -1.5 to 1.5
- ffn_gain: bfloat16 [2, 1024], P(None, ('grp', 'ctx')), may hold values from 0.5 to 1.5
- w_router: bfloat16 [2, 1024, 32], P(None, ('grp', 'ctx')), may hold values from -0.09375 to 0.09375
- w_gate: bfloat16 [2, 32, 1024, 512], P(None, 'grp', 'ctx'), may hold values from -0.1875 to 0.1875
- w_up: bfloat16 [2, 32, 1024, 512], P(None, 'grp', 'ctx'), may hold values from -0.1875 to 0.1875
- w_down: bfloat16 [2, 32, 512, 1024], P(None, 'grp', 'ctx'), may hold values from -0.75 to 0.75
Outputs:
- hidden_out: bfloat16 [8, 1024, 1024], P('grp', 'ctx')
- grad_in: float32 [8, 1024, 1024], P('grp', 'ctx')
- grad_attn_gain: float32 [2, 1024], P(None, ('grp', 'ctx'))
- grad_query: float32 [2, 1024, 1024], P(None, ('grp', 'ctx'))
- grad_key: float32 [2, 1024, 512], P(None, ('grp', 'ctx'))
- grad_value: float32 [2, 1024, 512], P(None, ('grp', 'ctx'))
- grad_output: float32 [2, 1024, 1024], P(None, ('grp', 'ctx'))
- grad_ffn_gain: float32 [2, 1024], P(None, ('grp', 'ctx'))
- grad_router: float32 [2, 1024, 32], P(None, ('grp', 'ctx'))
- grad_gate: float32 [2, 32, 1024, 512], P(None, 'grp', 'ctx')
- grad_up: float32 [2, 32, 1024, 512], P(None, 'grp', 'ctx')
- grad_down: float32 [2, 32, 512, 1024], P(None, 'grp', 'ctx')
Inputs may be any that keep to these rules, and one draw needn't show every extreme that they name: `segments`: within each group the ids never fall; the prompt (0) comes first and holds at least half of the group; every id 1 to 4 occurs. `routes`: each token names 8 different experts; among the 128 tokens of one device (aligned blocks) no expert is named more than 42 times.
All inputs are finite; a program needn't handle non-finite values.
Results may differ from a plain program's by a relative error of at most 0.025.
Values may be sent and summed in bfloat16 or wider, within the bound.
A program may use at most 320 MiB of HBM per device.

v0:
```python
import math

import jax
import jax.numpy as jnp
from jax import lax
from jax.sharding import PartitionSpec as P

MODEL_WIDTH = 1024
QUERY_HEADS = 16
KEY_VALUE_HEADS = 8
HEAD_SIZE = 64
E = 32
TOP = 8
LAYER_COUNT = 2
MICRO = 2
NCONT = 4
TOK_MB = 128
CAP = 42


EPSILON = 1e-06


def positions_of(seg_row):
    length_total = seg_row.shape[0]
    seg_ids = jnp.arange(NCONT + 1, dtype=jnp.int32)
    member = seg_row[:, None] == seg_ids[None, :]
    counts = jnp.sum(member.astype(jnp.int32), axis=0, dtype=jnp.int32)
    starts = jnp.cumsum(counts, dtype=jnp.int32) - counts
    own_start = jnp.sum(jnp.where(member, starts[None, :], 0), axis=1, dtype=jnp.int32)
    places = jnp.arange(length_total, dtype=jnp.int32)
    return jnp.where(seg_row == 0, places, counts[0] + places - own_start)


def rope_tables(places):
    half_dim = HEAD_SIZE // 2
    freqs = jnp.exp(
        jnp.arange(half_dim, dtype=jnp.float32) * (-2.0 * math.log(10000.0) / HEAD_SIZE)
    )
    angles = places.astype(jnp.float32)[:, None] * freqs[None, :]
    return (jnp.cos(angles), jnp.sin(angles))


def apply_rotation(value_matrix, cosine_table, sines_lookup):
    half_dim = value_matrix.shape[-1] // 2
    first_half = value_matrix[..., :half_dim]
    second_half = value_matrix[..., half_dim:]
    cos_rows = cosine_table[:, None, :]
    sin_rows = sines_lookup[:, None, :]
    return jnp.concatenate(
        [
            first_half * cos_rows - second_half * sin_rows,
            second_half * cos_rows + first_half * sin_rows,
        ],
        axis=-1,
    )


def reverse_rotation(value_matrix, cosine_table, sines_lookup):
    half_dim = value_matrix.shape[-1] // 2
    first_half = value_matrix[..., :half_dim]
    second_half = value_matrix[..., half_dim:]
    cos_rows = cosine_table[:, None, :]
    sin_rows = sines_lookup[:, None, :]
    return jnp.concatenate(
        [
            first_half * cos_rows + second_half * sin_rows,
            second_half * cos_rows - first_half * sin_rows,
        ],
        axis=-1,
    )


def norm_back(stream, inv_rms, gain_row, d_normed):
    gain_f = gain_row.astype(jnp.float32)
    grad_gain = jnp.sum(d_normed * stream * inv_rms, axis=0)
    scaled = d_normed * gain_f
    d_stream = inv_rms * scaled - stream * inv_rms * inv_rms * inv_rms * jnp.mean(
        stream * scaled, axis=-1, keepdims=True
    )
    return (d_stream, grad_gain)


def split_query(query_matrix):
    row_values = query_matrix.shape[0]
    return query_matrix.reshape(row_values, KEY_VALUE_HEADS // 2, 2, 2, HEAD_SIZE).transpose(
        1, 2, 3, 0, 4
    )


def split_keys(key_matrix):
    row_values = key_matrix.shape[0]
    return key_matrix.reshape(row_values, KEY_VALUE_HEADS // 2, 2, HEAD_SIZE).transpose(1, 2, 0, 3)


def merge_query(block_list):
    row_values = block_list.shape[3]
    return block_list.transpose(3, 0, 1, 2, 4).reshape(row_values, QUERY_HEADS * HEAD_SIZE)


def merge_keys(block_list):
    row_values = block_list.shape[2]
    return block_list.transpose(2, 0, 1, 3).reshape(row_values, KEY_VALUE_HEADS * HEAD_SIZE)


def attend(query_matrix, keys_all, values_all, key_mask):
    scale_factor = float(HEAD_SIZE) ** (-0.5)

    def block_fwd(pieces):
        query_blk, keys_blk, values_blk = pieces
        raw_scores = jnp.einsum(
            "citd,csd->cits", query_blk, keys_blk, preferred_element_type=jnp.float32
        )
        scores = jnp.where(key_mask[None, None], raw_scores * scale_factor, -1e30)
        highest = jnp.max(scores, axis=-1, keepdims=True)
        expo = jnp.exp(scores - highest)
        totals = jnp.sum(expo, axis=-1, keepdims=True)
        probs = (expo / totals).astype(jnp.bfloat16)
        mixed = jnp.einsum("cits,csd->citd", probs, values_blk, preferred_element_type=jnp.float32)
        return (mixed, highest + jnp.log(totals))

    mixed, log_sums = lax.map(
        block_fwd, (split_query(query_matrix), split_keys(keys_all), split_keys(values_all))
    )
    return (merge_query(mixed), log_sums)


def attend_back(query_matrix, keys_all, values_all, d_mixed, log_sums, key_mask):
    scale_factor = float(HEAD_SIZE) ** (-0.5)

    def block_back(pieces):
        query_blk, keys_blk, values_blk, dmix_blk, lse_blk = pieces
        raw_scores = jnp.einsum(
            "citd,csd->cits", query_blk, keys_blk, preferred_element_type=jnp.float32
        )
        scores = jnp.where(key_mask[None, None], raw_scores * scale_factor, -1e30)
        probs = jnp.exp(scores - lse_blk)
        d_probs = jnp.einsum(
            "citd,csd->cits", dmix_blk, values_blk, preferred_element_type=jnp.float32
        )
        delta = jnp.sum(probs * d_probs, axis=-1, keepdims=True)
        d_scores = (probs * (d_probs - delta) * scale_factor).astype(jnp.bfloat16)
        d_query = jnp.einsum(
            "cits,csd->citd", d_scores, keys_blk, preferred_element_type=jnp.float32
        )
        key_gradient = jnp.einsum(
            "cits,citd->csd", d_scores, query_blk, preferred_element_type=jnp.float32
        )
        d_values = jnp.einsum(
            "cits,citd->csd",
            probs.astype(jnp.bfloat16),
            dmix_blk,
            preferred_element_type=jnp.float32,
        )
        return (d_query, key_gradient, d_values)

    d_query, key_gradient, d_values = lax.map(
        block_back,
        (
            split_query(query_matrix),
            split_keys(keys_all),
            split_keys(values_all),
            split_query(d_mixed),
            log_sums,
        ),
    )
    return (merge_query(d_query), merge_keys(key_gradient), merge_keys(d_values))


def slot_table(route_rows):
    flat_routes = route_rows.reshape(-1)
    per_block = flat_routes.shape[0]
    one_hot = (flat_routes[:, None] == jnp.arange(E, dtype=jnp.int32)[None, :]).astype(jnp.int32)
    before = jnp.cumsum(one_hot, axis=0, dtype=jnp.int32) - one_hot
    ranks = jnp.sum(one_hot * before, axis=-1, dtype=jnp.int32)
    local_slot = flat_routes * CAP + ranks
    table = (
        jnp.full((E * CAP,), per_block, jnp.int32)
        .at[local_slot]
        .set(jnp.arange(per_block, dtype=jnp.int32))
    )
    return (local_slot, table)


def attn_forward(stream, attn_w, cosine_table, sines_lookup, key_mask):
    gain_row, wq_mat, key_weight_matrix, value_weight_matrix, wo_mat = (
        attn_w[0],
        attn_w[1],
        attn_w[2],
        attn_w[3],
        attn_w[4],
    )
    row_values = stream.shape[0]
    inv_rms = lax.rsqrt(jnp.mean(stream * stream, axis=-1, keepdims=True) + EPSILON)
    normalized_input = (stream * inv_rms * gain_row.astype(jnp.float32)).astype(jnp.bfloat16)
    query_matrix = apply_rotation(
        jnp.dot(normalized_input, wq_mat, preferred_element_type=jnp.float32).reshape(
            row_values, QUERY_HEADS, HEAD_SIZE
        ),
        cosine_table,
        sines_lookup,
    )
    query_matrix = query_matrix.astype(jnp.bfloat16).reshape(row_values, QUERY_HEADS * HEAD_SIZE)
    key_matrix = apply_rotation(
        jnp.dot(normalized_input, key_weight_matrix, preferred_element_type=jnp.float32).reshape(
            row_values, KEY_VALUE_HEADS, HEAD_SIZE
        ),
        cosine_table,
        sines_lookup,
    )
    key_matrix = key_matrix.astype(jnp.bfloat16).reshape(row_values, KEY_VALUE_HEADS * HEAD_SIZE)
    value_matrix = jnp.dot(
        normalized_input, value_weight_matrix, preferred_element_type=jnp.float32
    ).astype(jnp.bfloat16)
    keys_all, values_all = (
        lax.all_gather(key_matrix, "ctx", axis=0, tiled=True),
        lax.all_gather(value_matrix, "ctx", axis=0, tiled=True),
    )
    mixed, log_sums = attend(query_matrix, keys_all, values_all, key_mask)
    mixed_low = mixed.astype(jnp.bfloat16)
    stream_new = stream + jnp.dot(mixed_low, wo_mat, preferred_element_type=jnp.float32)
    return (
        stream_new,
        (
            stream,
            inv_rms,
            normalized_input,
            query_matrix,
            keys_all,
            values_all,
            mixed_low,
            log_sums,
        ),
    )


def attn_backward(grad_stream, saved, attn_w, cosine_table, sines_lookup, key_mask):
    stream, inv_rms, normalized_input, query_matrix, keys_all, values_all, mixed_low, log_sums = (
        saved
    )
    gain_row, wq_mat, key_weight_matrix, value_weight_matrix, wo_mat = (
        attn_w[0],
        attn_w[1],
        attn_w[2],
        attn_w[3],
        attn_w[4],
    )
    row_values = stream.shape[0]
    grad_low = grad_stream.astype(jnp.bfloat16)
    d_mixed = jnp.einsum("td,hd->th", grad_low, wo_mat, preferred_element_type=jnp.float32).astype(
        jnp.bfloat16
    )
    grad_wo = jnp.einsum("th,td->hd", mixed_low, grad_low, preferred_element_type=jnp.float32)
    d_query, d_keys_all, d_values_all = attend_back(
        query_matrix, keys_all, values_all, d_mixed, log_sums, key_mask
    )
    key_gradient, d_values = (
        lax.psum_scatter(
            d_keys_all.astype(jnp.bfloat16), "ctx", scatter_dimension=0, tiled=True
        ).astype(jnp.float32),
        lax.psum_scatter(
            d_values_all.astype(jnp.bfloat16), "ctx", scatter_dimension=0, tiled=True
        ).astype(jnp.float32),
    )
    dq_lin = (
        reverse_rotation(
            d_query.reshape(row_values, QUERY_HEADS, HEAD_SIZE), cosine_table, sines_lookup
        )
        .reshape(row_values, QUERY_HEADS * HEAD_SIZE)
        .astype(jnp.bfloat16)
    )
    dk_lin = (
        reverse_rotation(
            key_gradient.reshape(row_values, KEY_VALUE_HEADS, HEAD_SIZE), cosine_table, sines_lookup
        )
        .reshape(row_values, KEY_VALUE_HEADS * HEAD_SIZE)
        .astype(jnp.bfloat16)
    )
    dv_lin = d_values.astype(jnp.bfloat16)
    d_normed = jnp.einsum("th,dh->td", dq_lin, wq_mat, preferred_element_type=jnp.float32)
    d_normed = d_normed + jnp.einsum(
        "th,dh->td", dk_lin, key_weight_matrix, preferred_element_type=jnp.float32
    )
    d_normed = d_normed + jnp.einsum(
        "th,dh->td", dv_lin, value_weight_matrix, preferred_element_type=jnp.float32
    )
    grad_wq = jnp.einsum("td,th->dh", normalized_input, dq_lin, preferred_element_type=jnp.float32)
    grad_wk = jnp.einsum("td,th->dh", normalized_input, dk_lin, preferred_element_type=jnp.float32)
    grad_wv = jnp.einsum("td,th->dh", normalized_input, dv_lin, preferred_element_type=jnp.float32)
    d_stream, grad_gain = norm_back(stream, inv_rms, gain_row, d_normed)
    return (grad_stream + d_stream, (grad_gain, grad_wq, grad_wk, grad_wv, grad_wo))


def ffn_forward(stream, attn_w, expert_w, route_rows, grp_size):
    gain_row, router_mat = (attn_w[5], attn_w[6])
    gate_mat, up_mat, down_mat = expert_w
    row_values = stream.shape[0]
    experts_here = gate_mat.shape[0]
    inv_rms = lax.rsqrt(jnp.mean(stream * stream, axis=-1, keepdims=True) + EPSILON)
    normalized_input = (stream * inv_rms * gain_row.astype(jnp.float32)).astype(jnp.bfloat16)
    logits = jnp.dot(normalized_input, router_mat, preferred_element_type=jnp.float32)
    chosen = route_rows[:, :, None] == jnp.arange(E, dtype=jnp.int32)[None, None, :]
    picked = jnp.sum(jnp.where(chosen, logits[:, None, :], 0.0), axis=-1)
    gates = jax.nn.softmax(picked, axis=-1)
    local_slot, table = slot_table(route_rows)
    per_block = row_values * TOP
    token_of = jnp.where(table < per_block, table // TOP, row_values)
    padded = jnp.concatenate([normalized_input, jnp.zeros((1, MODEL_WIDTH), jnp.bfloat16)], axis=0)
    send_rows = padded[token_of].reshape(grp_size, experts_here, CAP, MODEL_WIDTH)
    received = lax.all_to_all(send_rows, "grp", split_axis=0, concat_axis=0, tiled=True)
    gate_pre = jnp.einsum("secd,edf->secf", received, gate_mat, preferred_element_type=jnp.float32)
    up_pre = jnp.einsum("secd,edf->secf", received, up_mat, preferred_element_type=jnp.float32)
    hidden = (gate_pre * jax.nn.sigmoid(gate_pre) * up_pre).astype(jnp.bfloat16)
    result = jnp.einsum(
        "secf,efd->secd", hidden, down_mat, preferred_element_type=jnp.float32
    ).astype(jnp.bfloat16)
    returned = lax.all_to_all(result, "grp", split_axis=0, concat_axis=0, tiled=True).reshape(
        E * CAP, MODEL_WIDTH
    )
    picked_out = returned[local_slot].reshape(row_values, TOP, MODEL_WIDTH)
    branch = jnp.einsum("tj,tjd->td", gates, picked_out.astype(jnp.float32))
    saved = (
        stream,
        inv_rms,
        normalized_input,
        chosen,
        gates,
        local_slot,
        table,
        received,
        gate_pre,
        up_pre,
        picked_out,
    )
    return (stream + branch, saved)


def ffn_backward(grad_stream, saved, attn_w, expert_w, grp_size):
    (
        stream,
        inv_rms,
        normalized_input,
        chosen,
        gates,
        local_slot,
        table,
        received,
        gate_pre,
        up_pre,
        picked_out,
    ) = saved
    gain_row, router_mat = (attn_w[5], attn_w[6])
    gate_mat, up_mat, down_mat = expert_w
    row_values = stream.shape[0]
    experts_here = gate_mat.shape[0]
    d_gates = jnp.einsum("td,tjd->tj", grad_stream, picked_out.astype(jnp.float32))
    d_picked = gates * (d_gates - jnp.sum(gates * d_gates, axis=-1, keepdims=True))
    d_logits = jnp.sum(jnp.where(chosen, d_picked[:, :, None], 0.0), axis=1).astype(jnp.bfloat16)
    d_routes = (
        (gates[:, :, None] * grad_stream[:, None, :])
        .astype(jnp.bfloat16)
        .reshape(row_values * TOP, MODEL_WIDTH)
    )
    padded = jnp.concatenate([d_routes, jnp.zeros((1, MODEL_WIDTH), jnp.bfloat16)], axis=0)
    d_send = padded[table].reshape(grp_size, experts_here, CAP, MODEL_WIDTH)
    d_received = lax.all_to_all(d_send, "grp", split_axis=0, concat_axis=0, tiled=True)
    d_hidden = jnp.einsum(
        "secd,efd->secf", d_received, down_mat, preferred_element_type=jnp.float32
    )
    sigma = jax.nn.sigmoid(gate_pre)
    active = gate_pre * sigma
    hidden = (active * up_pre).astype(jnp.bfloat16)
    d_gate_pre = (d_hidden * up_pre * (sigma * (1.0 + gate_pre * (1.0 - sigma)))).astype(
        jnp.bfloat16
    )
    d_up_pre = (d_hidden * active).astype(jnp.bfloat16)
    d_rows = jnp.einsum("secf,edf->secd", d_gate_pre, gate_mat, preferred_element_type=jnp.float32)
    d_rows = (
        d_rows + jnp.einsum("secf,edf->secd", d_up_pre, up_mat, preferred_element_type=jnp.float32)
    ).astype(jnp.bfloat16)
    d_back = lax.all_to_all(d_rows, "grp", split_axis=0, concat_axis=0, tiled=True).reshape(
        E * CAP, MODEL_WIDTH
    )
    d_normed = jnp.sum(
        d_back[local_slot].reshape(row_values, TOP, MODEL_WIDTH).astype(jnp.float32), axis=1
    )
    d_normed = d_normed + jnp.einsum(
        "te,de->td", d_logits, router_mat, preferred_element_type=jnp.float32
    )
    grad_router = jnp.einsum(
        "td,te->de", normalized_input, d_logits, preferred_element_type=jnp.float32
    )
    d_stream, grad_gain = norm_back(stream, inv_rms, gain_row, d_normed)
    return (
        grad_stream + d_stream,
        (grad_gain, grad_router),
        (hidden, d_received, received, d_gate_pre, d_up_pre),
    )


def expert_gradients(stored):
    hidden = jnp.concatenate([item[0] for item in stored], axis=0)
    d_received = jnp.concatenate([item[1] for item in stored], axis=0)
    received = jnp.concatenate([item[2] for item in stored], axis=0)
    d_gate_pre = jnp.concatenate([item[3] for item in stored], axis=0)
    d_up_pre = jnp.concatenate([item[4] for item in stored], axis=0)
    grad_down = jnp.einsum("secf,secd->efd", hidden, d_received, preferred_element_type=jnp.float32)
    grad_gate = jnp.einsum(
        "secd,secf->edf", received, d_gate_pre, preferred_element_type=jnp.float32
    )
    grad_up = jnp.einsum("secd,secf->edf", received, d_up_pre, preferred_element_type=jnp.float32)
    return [grad_gate, grad_up, grad_down]


def per_device(
    hidden_in,
    grad_out,
    segments,
    routes,
    attn_gain,
    w_query,
    key_weight,
    value_weight,
    w_output,
    ffn_gain,
    w_router,
    w_gate,
    w_up,
    w_down,
):
    grp_size = lax.axis_size("grp")
    ctx_index = lax.axis_index("ctx")
    group_len = segments.shape[1]

    def fetch_attn(layer_index):
        return (
            lax.all_gather(attn_gain[layer_index], ("grp", "ctx"), axis=0, tiled=True),
            lax.all_gather(w_query[layer_index], ("grp", "ctx"), axis=0, tiled=True),
            lax.all_gather(key_weight[layer_index], ("grp", "ctx"), axis=0, tiled=True),
            lax.all_gather(value_weight[layer_index], ("grp", "ctx"), axis=0, tiled=True),
            lax.all_gather(w_output[layer_index], ("grp", "ctx"), axis=0, tiled=True),
            lax.all_gather(ffn_gain[layer_index], ("grp", "ctx"), axis=0, tiled=True),
            lax.all_gather(w_router[layer_index], ("grp", "ctx"), axis=0, tiled=True),
        )

    def fetch_expert(layer_index):
        return (
            lax.all_gather(w_gate[layer_index], "ctx", axis=1, tiled=True),
            lax.all_gather(w_up[layer_index], "ctx", axis=1, tiled=True),
            lax.all_gather(w_down[layer_index], "ctx", axis=1, tiled=True),
        )

    def attn_for(layer_index):
        return fetch_attn(layer_index)

    def expert_for(layer_index):
        return fetch_expert(layer_index)

    attn_acc = [None] * LAYER_COUNT
    expert_acc = [None] * LAYER_COUNT
    expert_store = [[] for layer_index in range(LAYER_COUNT)]
    outputs = []
    input_grads = []
    for micro_step in range(MICRO):
        seg_row = segments[micro_step]
        places_all = positions_of(seg_row)
        start_row = ctx_index * TOK_MB
        places_here = lax.dynamic_slice_in_dim(places_all, start_row, TOK_MB)
        seg_here = lax.dynamic_slice_in_dim(seg_row, start_row, TOK_MB)
        cosine_table, sines_lookup = rope_tables(places_here)
        query_rows = start_row + jnp.arange(TOK_MB, dtype=jnp.int32)
        key_rows = jnp.arange(group_len, dtype=jnp.int32)
        key_mask = (key_rows[None, :] <= query_rows[:, None]) & (
            (seg_row[None, :] == 0) | (seg_row[None, :] == seg_here[:, None])
        )
        route_rows = routes[micro_step]
        stream = hidden_in[micro_step].astype(jnp.float32)
        saved_attn = []
        saved_ffn = []
        for layer_index in range(LAYER_COUNT):
            attn_w = attn_for(layer_index)
            stream, kept_attn = attn_forward(stream, attn_w, cosine_table, sines_lookup, key_mask)
            expert_w = expert_for(layer_index)
            stream, kept_ffn = ffn_forward(stream, attn_w, expert_w, route_rows, grp_size)
            saved_attn.append(kept_attn)
            saved_ffn.append(kept_ffn)
        outputs.append(stream.astype(jnp.bfloat16))
        grad_stream = grad_out[micro_step].astype(jnp.float32)
        for layer_index in reversed(range(LAYER_COUNT)):
            attn_w = attn_for(layer_index)
            expert_w = expert_for(layer_index)
            grad_stream, ffn_small, expert_parts = ffn_backward(
                grad_stream, saved_ffn[layer_index], attn_w, expert_w, grp_size
            )
            grad_stream, attn_grads = attn_backward(
                grad_stream, saved_attn[layer_index], attn_w, cosine_table, sines_lookup, key_mask
            )
            updates = [
                attn_grads[0],
                attn_grads[1],
                attn_grads[2],
                attn_grads[3],
                attn_grads[4],
                ffn_small[0],
                ffn_small[1],
            ]
            if attn_acc[layer_index] is None:
                attn_acc[layer_index] = updates
            else:
                attn_acc[layer_index] = [
                    total + extra for total, extra in zip(attn_acc[layer_index], updates)
                ]
            expert_store[layer_index].append(expert_parts)
            if micro_step == MICRO - 1:
                expert_acc[layer_index] = expert_gradients(expert_store[layer_index])
        input_grads.append(grad_stream)
    stacked_attn = [
        jnp.stack([attn_acc[layer_index][member] for layer_index in range(LAYER_COUNT)])
        for member in range(7)
    ]
    stacked_expert = [
        jnp.stack([expert_acc[layer_index][member] for layer_index in range(LAYER_COUNT)])
        for member in range(3)
    ]
    owned_attn = (
        lax.psum_scatter(stacked_attn[0], ("grp", "ctx"), scatter_dimension=1, tiled=True),
        lax.psum_scatter(stacked_attn[1], ("grp", "ctx"), scatter_dimension=1, tiled=True),
        lax.psum_scatter(stacked_attn[2], ("grp", "ctx"), scatter_dimension=1, tiled=True),
        lax.psum_scatter(stacked_attn[3], ("grp", "ctx"), scatter_dimension=1, tiled=True),
        lax.psum_scatter(stacked_attn[4], ("grp", "ctx"), scatter_dimension=1, tiled=True),
        lax.psum_scatter(stacked_attn[5], ("grp", "ctx"), scatter_dimension=1, tiled=True),
        lax.psum_scatter(stacked_attn[6], ("grp", "ctx"), scatter_dimension=1, tiled=True),
    )
    owned_expert = (
        lax.psum_scatter(
            stacked_expert[0].astype(jnp.bfloat16), "ctx", scatter_dimension=2, tiled=True
        ).astype(jnp.float32),
        lax.psum_scatter(
            stacked_expert[1].astype(jnp.bfloat16), "ctx", scatter_dimension=2, tiled=True
        ).astype(jnp.float32),
        lax.psum_scatter(
            stacked_expert[2].astype(jnp.bfloat16), "ctx", scatter_dimension=2, tiled=True
        ).astype(jnp.float32),
    )
    return (
        jnp.stack(outputs),
        jnp.stack(input_grads),
        owned_attn[0],
        owned_attn[1],
        owned_attn[2],
        owned_attn[3],
        owned_attn[4],
        owned_attn[5],
        owned_attn[6],
        owned_expert[0],
        owned_expert[1],
        owned_expert[2],
    )


def solution(mesh):
    placed = (
        P("grp", "ctx", None),
        P("grp", "ctx", None),
        P("grp", None),
        P("grp", "ctx", None),
        P(None, ("grp", "ctx")),
        P(None, ("grp", "ctx"), None),
        P(None, ("grp", "ctx"), None),
        P(None, ("grp", "ctx"), None),
        P(None, ("grp", "ctx"), None),
        P(None, ("grp", "ctx")),
        P(None, ("grp", "ctx"), None),
        P(None, "grp", "ctx", None),
        P(None, "grp", "ctx", None),
        P(None, "grp", "ctx", None),
    )
    return jax.shard_map(
        per_device,
        mesh=mesh,
        in_specs=placed,
        out_specs=(
            P("grp", "ctx", None),
            P("grp", "ctx", None),
            P(None, ("grp", "ctx")),
            P(None, ("grp", "ctx"), None),
            P(None, ("grp", "ctx"), None),
            P(None, ("grp", "ctx"), None),
            P(None, ("grp", "ctx"), None),
            P(None, ("grp", "ctx")),
            P(None, ("grp", "ctx"), None),
            P(None, "grp", "ctx", None),
            P(None, "grp", "ctx", None),
            P(None, "grp", "ctx", None),
        ),
        check_vma=False,
    )
```

profile of v0, /device:TPU:0, one launch (start us, length us, event | category | flops | bytes accessed | tf_op | source)
XLA Modules:
  0.0 3674.1 jit_solution(7634926529367198615)
XLA Ops:
  12.5 42.1 %all-reduce.12 = (bf16[1024]{0:T(1024)(128)(2,1)S(1)}, bf16[1024]{0:T(1024)(128)(2,1)S(1)}, bf16[1024]{0:T(1024)(128)(2,1)}, bf16[1024]{0:T(1024)(128)(2,1)}) all-reduce(bf16[1024]{0:T(1024)(128)(2,1)S(1)} %dynamic-update-slice, bf16[1024]{0:T(1024)(128)(2,1)S(1)} %dynamic-update-slice.1, ...), channel_id=2, replica_groups=mesh['grp'=4,'ctx'=8] {'grp','ctx'}, use_global_device_ids=true, to_apply=%add.8 | all-reduce | flops 4096 | bytes 16384
  75.0 49.5 %all-gather.61.cloned.1.call-done = bf16[1,1024,512]{2,1,0:T(8,128)(2,1)} async-done(((bf16[1,32,512]{2,1,0:T(8,128)(2,1)}), bf16[1,1024,512]{2,1,0:T(8,128)(2,1)}) %all-gather.61.cloned.1.call-update) | async-done | bytes 1048592 | tf_op jit(solution)/shard_map/all_gather | solution.py:439
  158.1 13.5 all-gather.45.cloned.1.call-done
  173.9 57.3 %all-gather.59.cloned.1.call-done = bf16[1,1024,1024]{2,1,0:T(8,128)(2,1)} async-done(((bf16[1,32,1024]{2,1,0:T(8,128)(2,1)}), bf16[1,1024,1024]{2,1,0:T(8,128)(2,1)}) %all-gather.59.cloned.1.call-update) | async-done | bytes 2097168 | tf_op jit(solution)/shard_map/all_gather | solution.py:438
  235.8 20.2 all-gather.51.cloned.1.call-done
  256.1 16.8 while.114
  280.9 16.8 while.112
  297.8 42.4 %all-gather.65.cloned.1.call-done = bf16[1,1024,1024]{2,1,0:T(8,128)(2,1)} async-done(((bf16[1,32,1024]{2,1,0:T(8,128)(2,1)}), bf16[1,1024,1024]{2,1,0:T(8,128)(2,1)}) %all-gather.65.cloned.1.call-update) | async-done | bytes 2097168 | tf_op jit(solution)/shard_map/all_gather | solution.py:441
  404.4 18.4 all-gather.67.cloned.1.call-done
  431.5 73.3 %all-gather.69.cloned.1.call-done = bf16[1,8,1024,512]{3,2,1,0:T(8,128)(2,1)} async-done(((bf16[1,8,128,512]{3,2,1,0:T(8,128)(2,1)}), bf16[1,8,1024,512]{3,2,1,0:T(8,128)(2,1)}) %all-gather.69.cloned.1.call-update) | async-done | bytes 8388624 | tf_op jit(solution)/shard_map/all_gather | solution.py:449
  515.5 71.6 %all-gather.71.cloned.1.call-done = bf16[1,8,512,1024]{3,2,1,0:T(8,128)(2,1)} async-done(((bf16[1,8,64,1024]{3,2,1,0:T(8,128)(2,1)}), bf16[1,8,512,1024]{3,2,1,0:T(8,128)(2,1)}) %all-gather.71.cloned.1.call-update) | async-done | bytes 8388624 | tf_op jit(solution)/shard_map/all_gather | solution.py:450
  640.4 39.5 %all-gather.6 = bf16[1,1024,32]{2,1,0:T(8,128)(2,1)S(1)} all-gather(bf16[1,32,32]{2,1,0:T(8,128)(2,1)S(1)} %get-tuple-element.975), channel_id=8, replica_groups=mesh['grp'=4,'ctx'=8] {'grp','ctx'}, dimensions={1}, use_global_device_ids=true | all-gather | bytes 67584 | tf_op jit(solution)/shard_map/all_gather | solution.py:443
  730.6 37.2 %all-gather.73.cloned.1.call-done = bf16[1,1024,1024]{2,1,0:T(8,128)(2,1)} async-done(((bf16[1,32,1024]{2,1,0:T(8,128)(2,1)}), bf16[1,1024,1024]{2,1,0:T(8,128)(2,1)}) %all-gather.73.cloned.1.call-update) | async-done | bytes 2097168 | tf_op jit(solution)/shard_map/all_gather | solution.py:438
  770.5 20.4 all-gather.49.cloned.1.call-done
  792.3 24.2 all-gather.47.cloned.1.call-done
  817.1 15.3 while.113
  832.4 42.0 %all-gather.79.cloned.1.call-done = bf16[1,1024,1024]{2,1,0:T(8,128)(2,1)} async-done(((bf16[1,32,1024]{2,1,0:T(8,128)(2,1)}), bf16[1,1024,1024]{2,1,0:T(8,128)(2,1)}) %all-gather.79.cloned.1.call-update) | async-done | bytes 2097168 | tf_op jit(solution)/shard_map/all_gather | solution.py:441
  893.1 63.7 %all-gather.81.cloned.1.call-done = bf16[1,8,1024,512]{3,2,1,0:T(8,128)(2,1)} async-done(((bf16[1,8,128,512]{3,2,1,0:T(8,128)(2,1)}), bf16[1,8,1024,512]{3,2,1,0:T(8,128)(2,1)}) %all-gather.81.cloned.1.call-update) | async-done | bytes 8388624 | tf_op jit(solution)/shard_map/all_gather | solution.py:448
  966.6 72.5 %all-gather.83.cloned.1.call-done = bf16[1,8,1024,512]{3,2,1,0:T(8,128)(2,1)} async-done(((bf16[1,8,128,512]{3,2,1,0:T(8,128)(2,1)}), bf16[1,8,1024,512]{3,2,1,0:T(8,128)(2,1)}) %all-gather.83.cloned.1.call-update) | async-done | bytes 8388624 | tf_op jit(solution)/shard_map/all_gather | solution.py:449
  1049.7 71.5 %all-gather.85.cloned.1.call-done = bf16[1,8,512,1024]{3,2,1,0:T(8,128)(2,1)} async-done(((bf16[1,8,64,1024]{3,2,1,0:T(8,128)(2,1)}), bf16[1,8,512,1024]{3,2,1,0:T(8,128)(2,1)}) %all-gather.85.cloned.1.call-update) | async-done | bytes 8388624 | tf_op jit(solution)/shard_map/all_gather | solution.py:450
  1134.7 41.4 %all-gather.16 = bf16[1,1024,32]{2,1,0:T(8,128)(2,1)S(1)} all-gather(bf16[1,32,32]{2,1,0:T(8,128)(2,1)S(1)} %copy-done.222), channel_id=18, replica_groups=mesh['grp'=4,'ctx'=8] {'grp','ctx'}, dimensions={1}, use_global_device_ids=true | all-gather | bytes 67584 | tf_op jit(solution)/shard_map/all_gather | solution.py:443
  1218.1 27.3 all-to-all-done.8
  1278.0 16.9 while.115
  1338.6 34.9 all_to_all.80
  1396.9 29.5 all-to-all-done.7
  1452.2 35.6 all_to_all.81
  1530.0 23.1 all-to-all-done.13
  1574.3 51.1 %while.116 = (s32[]{:T(128)}, f32[4,2,2,128,64]{3,4,2,1,0:T(8,128)S(1)}, bf16[4,2,1024,64]{2,3,1,0:T(8,128)(2,1)}, bf16[4,2,1024,64]{2,3,1,0:T(8,128)(2,1)}, bf1...) while((s32[]{:T(128)}, ...), condition=%wide.region_56.57_spmd.clone, body=%wide.region_54.56_spmd.clone.sunk | while | flops 343411712 | bytes 25576584 | solution.py:157
  1631.5 48.2 %while.118 = (s32[]{:T(128)}, f32[4,2,2,128,64]{3,4,2,1,0:T(8,128)}, bf16[4,2,1024,64]{2,3,1,0:T(8,128)(2,1)S(1)}, bf16[4,2,1024,64]{2,3,1,0:T(8,128)(2,1)}, bf1...) while((s32[]{:T(128)}, f32[4,2,2,128,64]{3,4,2,1,0:T(8,128)}, ...), condition=%wide.region_76.77_spmd.clone, body=%wide.region_74.76_spmd.clone.sunk | while | flops 343411712 | bytes 25576584 | solution.py:157
  1693.0 19.9 reduce-scatter.63.cloned.1.call-done
  1716.8 29.5 reduce-scatter.65.cloned.1.call-done
  1748.6 30.4 reduce-scatter.57.cloned.1.call-done
  1813.4 16.6 all-to-all-done.10
  1959.6 51.0 %while.117 = (s32[]{:T(128)}, f32[4,2,2,128,64]{3,4,2,1,0:T(8,128)S(1)}, bf16[4,2,1024,64]{2,3,1,0:T(8,128)(2,1)}, bf16[4,2,1024,64]{2,3,1,0:T(8,128)(2,1)}, bf1...) while((s32[]{:T(128)}, ...), condition=%wide.region_66.67_spmd.clone, body=%wide.region_64.66_spmd.clone.sunk | while | flops 343411712 | bytes 25576584 | solution.py:157
  2017.5 51.1 %while.119 = (s32[]{:T(128)}, f32[4,2,2,128,64]{3,4,2,1,0:T(8,128)}, bf16[4,2,1024,64]{2,3,1,0:T(8,128)(2,1)S(1)}, bf16[4,2,1024,64]{2,3,1,0:T(8,128)(2,1)}, bf1...) while((s32[]{:T(128)}, f32[4,2,2,128,64]{3,4,2,1,0:T(8,128)}, ...), condition=%wide.region_86.87_spmd.clone, body=%wide.region_84.86_spmd.clone.sunk | while | flops 343411712 | bytes 25576584 | solution.py:157
  2139.2 31.3 reduce-scatter.61.cloned.1.call-done
  2174.7 13.8 pad_maximum_fusion.2
  2227.5 13.8 pad_maximum_fusion.1
  2266.1 13.8 pad_maximum_fusion
  2311.8 125.8 %reduce-scatter.73.cloned.1.call-done = f32[32,2]{1,0:T(8,128)} async-done(((f32[1024,2]{1,0:T(8,128)}), f32[32,2]{1,0:T(8,128)}) %reduce-scatter.73.cloned.1.call-update) | async-done | bytes 272
  2440.4 129.9 %reduce-scatter.71.cloned.1.call-done = f32[32,2]{1,0:T(8,128)} async-done(((f32[1024,2]{1,0:T(8,128)}), f32[32,2]{1,0:T(8,128)}) %reduce-scatter.71.cloned.1.call-update) | async-done | bytes 272
  2571.6 166.0 %reduce-scatter.53.cloned.1.call-done = bf16[2,8,64,1024]{3,2,1,0:T(8,128)(2,1)} async-done(((bf16[2,8,512,1024]{3,2,1,0:T(8,128)(2,1)}), bf16[2,8,64,1024]{3,2,1,0:T(8,128)(2,1)}) %reduce-scatter.53.cloned.1.call-update) | async-done | bytes 2097168 | tf_op jit(solution)/shard_map/reduce_scatter | solution.py:541
  2741.8 165.0 %reduce-scatter.51.cloned.1.call-done = bf16[2,8,128,512]{3,2,1,0:T(8,128)(2,1)} async-done(((bf16[2,8,1024,512]{3,2,1,0:T(8,128)(2,1)}), bf16[2,8,128,512]{3,2,1,0:T(8,128)(2,1)}) %reduce-scatter.51.cloned.1.call-update) | async-done | bytes 2097168 | tf_op jit(solution)/shard_map/reduce_scatter | solution.py:538
  2911.0 164.8 %reduce-scatter.49.cloned.1.call-done = bf16[2,8,128,512]{3,2,1,0:T(8,128)(2,1)} async-done(((bf16[2,8,1024,512]{3,2,1,0:T(8,128)(2,1)}), bf16[2,8,128,512]{3,2,1,0:T(8,128)(2,1)}) %reduce-scatter.49.cloned.1.call-update) | async-done | bytes 2097168 | tf_op jit(solution)/shard_map/reduce_scatter | solution.py:535
  3079.9 139.6 %reduce-scatter.45.cloned.1.call-done = f32[2,32,512]{2,1,0:T(8,128)} async-done(((f32[2,1024,512]{2,1,0:T(8,128)}), f32[2,32,512]{2,1,0:T(8,128)}) %reduce-scatter.45.cloned.1.call-update) | async-done | bytes 131088 | tf_op jit(solution)/shard_map/reduce_scatter | solution.py:529
  3219.5 142.4 %reduce-scatter.43.cloned.1.call-done = f32[2,32,512]{2,1,0:T(8,128)} async-done(((f32[2,1024,512]{2,1,0:T(8,128)}), f32[2,32,512]{2,1,0:T(8,128)}) %reduce-scatter.43.cloned.1.call-update) | async-done | bytes 131088 | tf_op jit(solution)/shard_map/reduce_scatter | solution.py:528
  3361.9 152.3 %reduce-scatter.47.cloned.1.call-done = f32[2,32,1024]{2,1,0:T(8,128)} async-done(((f32[2,1024,1024]{2,1,0:T(8,128)}), f32[2,32,1024]{2,1,0:T(8,128)}) %reduce-scatter.47.cloned.1.call-update) | async-done | bytes 262160 | tf_op jit(solution)/shard_map/reduce_scatter | solution.py:530
  3514.2 152.8 %reduce-scatter.41.cloned.1.call-done = f32[2,32,1024]{2,1,0:T(8,128)} async-done(((f32[2,1024,1024]{2,1,0:T(8,128)}), f32[2,32,1024]{2,1,0:T(8,128)}) %reduce-scatter.41.cloned.1.call-update) | async-done | bytes 262160 | tf_op jit(solution)/shard_map/reduce_scatter | solution.py:527
  (1267 shorter events, 1195.3 us)
Async XLA Ops:
  7.2 61.0 %all-gather.63.cloned.1.call-start = ((), (), s32[]{:S(2)}) async-start(), calls=%async_computation.51 | async-start | bytes 1081344 | tf_op jit(solution)/shard_map/all_gather | solution.py:440
  8.7 115.9 %all-gather.61.cloned.1.call-start = ((), (), s32[]{:S(2)}) async-start(), calls=%async_computation.50 | async-start | bytes 1081344 | tf_op jit(solution)/shard_map/all_gather | solution.py:439
  10.2 145.7 %all-gather.53.cloned.1.call-start = ((), (), s32[]{:S(2)}) async-start(), calls=%async_computation.39 | async-start | bytes 1179648 | tf_op jit(solution)/shard_map/all_gather | solution.py:217
  70.5 101.1 %all-gather.45.cloned.1.call-start = ((), (), s32[]{:S(2)}) async-start(), calls=%async_computation.35 | async-start | bytes 1179648 | tf_op jit(solution)/shard_map/all_gather | solution.py:217
  73.0 158.3 %all-gather.59.cloned.1.call-start = ((), (), s32[]{:S(2)}) async-start(), calls=%async_computation.49 | async-start | bytes 2162688 | tf_op jit(solution)/shard_map/all_gather | solution.py:438
  73.7 182.4 %all-gather.51.cloned.1.call-start = ((), (), s32[]{:S(2)}) async-start(), calls=%async_computation.38 | async-start | bytes 1179648 | tf_op jit(solution)/shard_map/all_gather | solution.py:216
  127.3 153.5 %all-gather.43.cloned.1.call-start = ((), (), s32[]{:S(2)}) async-start(), calls=%async_computation.34 | async-start | bytes 1179648 | tf_op jit(solution)/shard_map/all_gather | solution.py:216
  128.7 211.6 %all-gather.65.cloned.1.call-start = ((), (), s32[]{:S(2)}) async-start(), calls=%async_computation.52 | async-start | bytes 2162688 | tf_op jit(solution)/shard_map/all_gather | solution.py:441
  129.4 293.4 %all-gather.67.cloned.1.call-start = ((), (), s32[]{:S(2)}) async-start(), calls=%async_computation.53 | async-start | bytes 9437184 | tf_op jit(solution)/shard_map/all_gather | solution.py:448
  132.6 372.3 %all-gather.69.cloned.1.call-start = ((), (), s32[]{:S(2)}) async-start(), calls=%async_computation.54 | async-start | bytes 9437184 | tf_op jit(solution)/shard_map/all_gather | solution.py:449
  134.2 452.9 %all-gather.71.cloned.1.call-start = ((), (), s32[]{:S(2)}) async-start(), calls=%async_computation.55 | async-start | bytes 9437184 | tf_op jit(solution)/shard_map/all_gather | solution.py:450
  137.4 585.7 %all-gather.77.cloned.1.call-start = ((), (), s32[]{:S(2)}) async-start(), calls=%async_computation.58 | async-start | bytes 1081344 | tf_op jit(solution)/shard_map/all_gather | solution.py:440
  138.0 587.6 %all-gather.75.cloned.1.call-start = ((), (), s32[]{:S(2)}) async-start(), calls=%async_computation.57 | async-start | bytes 1081344 | tf_op jit(solution)/shard_map/all_gather | solution.py:439
  359.3 40.5 %all-to-all-start.4 = ((bf16[4,8,42,1024]{3,1,2,0:T(8,128)(2,1)}), bf16[4,8,42,1024]{3,1,2,0:T(8,128)(2,1)S(1)}, u32[]{:S(2)}, u32[]{:S(2)}) async-start(bf16[4,8,42,1024]{3,1,2,0:T(8,128)(2,1)} %copy.196), calls=%async_computation.4 | async-start | bytes 5505024 | tf_op jit(solution)/shard_map/all_to_all | solution.py:310
  363.1 404.7 %all-gather.73.cloned.1.call-start = ((), (), s32[]{:S(2)}) async-start(), calls=%async_computation.56 | async-start | bytes 2162688 | tf_op jit(solution)/shard_map/all_gather | solution.py:438
  399.8 196.1 %all-to-all-start = ((bf16[4,8,42,1024]{3,1,2,0:T(8,128)(2,1)}), bf16[4,8,42,1024]{3,1,2,0:T(8,128)(2,1)}, u32[]{:S(2)}, u32[]{:S(2)}) async-start(bf16[4,8,42,1024]{3,1,2,0:T(8,128)(2,1)} %copy.177), calls=%async_computation | async-start | bytes 5505024 | tf_op jit(solution)/shard_map/all_to_all | solution.py:310
  595.9 39.2 %all-to-all-start.5 = ((bf16[4,8,42,1024]{3,1,2,0:T(8,128)(2,1)}), bf16[4,8,42,1024]{3,1,2,0:T(8,128)(2,1)S(1)}, u32[]{:S(2)}, u32[]{:S(2)}) async-start(bf16[4,8,42,1024]{3,1,2,0:T(8,128)(2,1)} %copy.199), calls=%async_computation.5 | async-start | bytes 5505024 | tf_op jit(solution)/shard_map/all_to_all | solution.py:317
  635.1 62.0 %all-to-all-start.1 = ((bf16[4,8,42,1024]{3,1,2,0:T(8,128)(2,1)}), bf16[4,8,42,1024]{3,1,2,0:T(8,128)(2,1)}, u32[]{:S(2)}, u32[]{:S(2)}) async-start(bf16[4,8,42,1024]{3,1,2,0:T(8,128)(2,1)} %copy.180), calls=%async_computation.1 | async-start | bytes 5505024 | tf_op jit(solution)/shard_map/all_to_all | solution.py:317
  639.7 151.1 %all-gather.49.cloned.1.call-start = ((), (), s32[]{:S(2)}) async-start(), calls=%async_computation.37 | async-start | bytes 1179648 | tf_op jit(solution)/shard_map/all_gather | solution.py:217
  725.4 91.0 %all-gather.47.cloned.1.call-start = ((), (), s32[]{:S(2)}) async-start(), calls=%async_computation.36 | async-start | bytes 1179648 | tf_op jit(solution)/shard_map/all_gather | solution.py:216
  728.0 146.4 %all-gather.79.cloned.1.call-start = ((), (), s32[]{:S(2)}) async-start(), calls=%async_computation.59 | async-start | bytes 2162688 | tf_op jit(solution)/shard_map/all_gather | solution.py:441
  728.6 228.2 %all-gather.81.cloned.1.call-start = ((), (), s32[]{:S(2)}) async-start(), calls=%async_computation.60 | async-start | bytes 9437184 | tf_op jit(solution)/shard_map/all_gather | solution.py:448
  729.2 309.9 %all-gather.83.cloned.1.call-start = ((), (), s32[]{:S(2)}) async-start(), calls=%async_computation.61 | async-start | bytes 9437184 | tf_op jit(solution)/shard_map/all_gather | solution.py:449
  730.0 391.2 %all-gather.85.cloned.1.call-start = ((), (), s32[]{:S(2)}) async-start(), calls=%async_computation.62 | async-start | bytes 9437184 | tf_op jit(solution)/shard_map/all_gather | solution.py:450
  889.3 67.6 %all-to-all-start.2 = ((bf16[4,8,42,1024]{3,1,2,0:T(8,128)(2,1)}), bf16[4,8,42,1024]{3,1,2,0:T(8,128)(2,1)S(1)}, u32[]{:S(2)}, u32[]{:S(2)}) async-start(bf16[4,8,42,1024]{3,1,2,0:T(8,128)(2,1)} %copy.185), calls=%async_computation.2 | async-start | bytes 5505024 | tf_op jit(solution)/shard_map/all_to_all | solution.py:310
  1129.9 48.7 %all-to-all-start.3 = ((bf16[4,8,42,1024]{3,1,2,0:T(8,128)(2,1)}), bf16[4,8,42,1024]{3,1,2,0:T(8,128)(2,1)}, u32[]{:S(2)}, u32[]{:S(2)}) async-start(bf16[4,8,42,1024]{3,1,2,0:T(8,128)(2,1)} %copy.188), calls=%async_computation.3 | async-start | bytes 5505024 | tf_op jit(solution)/shard_map/all_to_all | solution.py:317
  1134.7 80.4 %all-gather.57.cloned.1.call-start = ((), (), s32[]{:S(2)}) async-start(), calls=%async_computation.41 | async-start | bytes 1179648 | tf_op jit(solution)/shard_map/all_gather | solution.py:217
  1207.8 37.6 %all-to-all-start.8 = ((bf16[4,8,42,1024]{3,1,2,0:T(8,128)(2,1)}), bf16[4,8,42,1024]{3,1,2,0:T(8,128)(2,1)}, u32[]{:S(2)}, u32[]{:S(2)}) async-start(bf16[4,8,42,1024]{3,1,2,0:T(8,128)(2,1)} %copy.210), calls=%async_computation.8 | async-start | bytes 5505024 | tf_op jit(solution)/shard_map/all_to_all | solution.py:366
  1212.7 65.2 %all-gather.55.cloned.1.call-start = ((), (), s32[]{:S(2)}) async-start(), calls=%async_computation.40 | async-start | bytes 1179648 | tf_op jit(solution)/shard_map/all_gather | solution.py:216
  1273.0 36.8 %all-to-all-start.9 = ((bf16[4,8,42,1024]{3,1,2,0:T(8,128)(2,1)}), bf16[4,8,42,1024]{3,1,2,0:T(8,128)(2,1)}, u32[]{:S(2)}, u32[]{:S(2)}) async-start(bf16[4,8,42,1024]{3,1,2,0:T(8,128)(2,1)} %copy.212), calls=%async_computation.9 | async-start | bytes 5505024 | tf_op jit(solution)/shard_map/all_to_all | solution.py:381
  1523.2 168.7 %reduce-scatter.55.cloned.1.call-start = ((), (), s32[]{:S(2)}) async-start(), calls=%async_computation.63 | async-start | bytes 1179648
  1627.9 85.0 %reduce-scatter.63.cloned.1.call-start = ((), (), s32[]{:S(2)}) async-start(), calls=%async_computation.67 | async-start | bytes 1179648
  1683.1 63.2 %reduce-scatter.65.cloned.1.call-start = ((), (), s32[]{:S(2)}) async-start(), calls=%async_computation.68 | async-start | bytes 1179648
  1684.5 94.6 %reduce-scatter.57.cloned.1.call-start = ((), (), s32[]{:S(2)}) async-start(), calls=%async_computation.64 | async-start | bytes 1179648
  1906.0 214.5 %reduce-scatter.59.cloned.1.call-start = ((), (), s32[]{:S(2)}) async-start(), calls=%async_computation.65 | async-start | bytes 1179648
  2015.4 106.3 %reduce-scatter.67.cloned.1.call-start = ((), (), s32[]{:S(2)}) async-start(), calls=%async_computation.69 | async-start | bytes 1179648
  2069.9 67.7 %reduce-scatter.69.cloned.1.call-start = ((), (), s32[]{:S(2)}) async-start(), calls=%async_computation.70 | async-start | bytes 1179648
  2071.4 99.1 %reduce-scatter.61.cloned.1.call-start = ((), (), s32[]{:S(2)}) async-start(), calls=%async_computation.66 | async-start | bytes 1179648
  2072.8 237.6 %reduce-scatter.75.cloned.1.call-start = ((), (), s32[]{:S(2)}) async-start(), calls=%async_computation.73 | async-start | bytes 540672
  2095.5 342.1 %reduce-scatter.73.cloned.1.call-start = ((), (), s32[]{:S(2)}) async-start(), calls=%async_computation.72 | async-start | bytes 540672
  2117.1 453.2 %reduce-scatter.71.cloned.1.call-start = ((), (), s32[]{:S(2)}) async-start(), calls=%async_computation.71 | async-start | bytes 540672
  2174.7 563.0 %reduce-scatter.53.cloned.1.call-start = ((), (), s32[]{:S(2)}) async-start(), calls=%async_computation.48 | async-start | bytes 18874368 | tf_op jit(solution)/shard_map/reduce_scatter | solution.py:541
  2188.6 718.2 %reduce-scatter.51.cloned.1.call-start = ((), (), s32[]{:S(2)}) async-start(), calls=%async_computation.47 | async-start | bytes 18874368 | tf_op jit(solution)/shard_map/reduce_scatter | solution.py:538
  2241.3 834.5 %reduce-scatter.49.cloned.1.call-start = ((), (), s32[]{:S(2)}) async-start(), calls=%async_computation.46 | async-start | bytes 18874368 | tf_op jit(solution)/shard_map/reduce_scatter | solution.py:535
  2279.9 939.7 %reduce-scatter.45.cloned.1.call-start = ((), (), s32[]{:S(2)}) async-start(), calls=%async_computation.44 | async-start | bytes 4325376 | tf_op jit(solution)/shard_map/reduce_scatter | solution.py:529
  2285.8 1076.2 %reduce-scatter.43.cloned.1.call-start = ((), (), s32[]{:S(2)}) async-start(), calls=%async_computation.43 | async-start | bytes 4325376 | tf_op jit(solution)/shard_map/reduce_scatter | solution.py:528
  2291.1 1223.1 %reduce-scatter.47.cloned.1.call-start = ((), (), s32[]{:S(2)}) async-start(), calls=%async_computation.45 | async-start | bytes 8650752 | tf_op jit(solution)/shard_map/reduce_scatter | solution.py:530
  2300.0 1367.1 %reduce-scatter.41.cloned.1.call-start = ((), (), s32[]{:S(2)}) async-start(), calls=%async_computation.42 | async-start | bytes 8650752 | tf_op jit(solution)/shard_map/reduce_scatter | solution.py:527
  (269 other events, 6878.1 us)
Sparse Core Ops, SparseCore 0:
  11.6 56.5 all-gather.62
  71.8 52.7 all-gather.60
  126.7 21.0 all-gather.52
  149.9 21.7 all-gather.44
  175.1 56.0 all-gather.58
  233.2 22.8 all-gather.50
  258.3 22.5 all-gather.42
  284.4 55.7 all-gather.64
  341.8 80.8 all-gather.66
  424.2 80.5 all-gather.68
  506.5 80.5 all-gather.70
  589.9 53.0 all-gather.76
  646.6 62.8 all-gather.74
  712.3 55.4 all-gather.72
  769.8 20.9 all-gather.48
  792.8 23.5 all-gather.46
  819.3 55.0 all-gather.78
  875.9 80.8 all-gather.80
  958.4 80.5 all-gather.82
  1040.5 80.5 all-gather.84
  1178.4 18.3 all-gather.56
  1215.7 22.5 all-gather.54
  1628.0 29.5 reduce-scatter.54
  1683.2 29.6 reduce-scatter.62
  1715.8 30.4 reduce-scatter.64
  1748.4 30.6 reduce-scatter.56
  2015.5 34.1 reduce-scatter.58
  2070.1 34.1 reduce-scatter.66
  2107.1 30.4 reduce-scatter.68
  2139.8 30.7 reduce-scatter.60
  2172.7 132.4 reduce-scatter.74
  2307.6 129.9 reduce-scatter.72
  2440.2 130.0 reduce-scatter.70
  2572.8 164.8 reduce-scatter.52
  2740.2 166.6 reduce-scatter.50
  2909.1 166.5 reduce-scatter.48
  3078.5 140.9 reduce-scatter.44
  3222.5 139.3 reduce-scatter.42
  3364.7 149.4 reduce-scatter.46
  3517.2 149.8 reduce-scatter.40
where the time goes:
time: 3690 us; the launch traced here: 3670 us
  waiting for transfers between devices  2300 us (62%)
  matrix products  582 us (16%)
  local copies, waits for them, and re-layouts  366 us (10%)
  blocking collectives  194 us (5%)
  other arithmetic  148 us (4%)
  starting transfers between devices  64.1 us (2%)
    unnamed x51, waiting for transfers between devices  383 us
    reduce_scatter x1, waiting for transfers between devices, per_device(): lax.psum_scatter(stacked_expert[2].astype(jnp.bfloat16), 'ctx', scatter_d...  166 us
    reduce_scatter x1, waiting for transfers between devices, per_device(): lax.psum_scatter(stacked_expert[1].astype(jnp.bfloat16), 'ctx', scatter_d...  165 us
    reduce_scatter x1, waiting for transfers between devices, per_device(): lax.psum_scatter(stacked_expert[0].astype(jnp.bfloat16), 'ctx', scatter_d...  165 us
    reduce_scatter x1, waiting for transfers between devices, per_device(): lax.psum_scatter(stacked_attn[1], ('grp', 'ctx'), scatter_dimension=1, ti...  153 us
    reduce_scatter x1, waiting for transfers between devices, per_device(): lax.psum_scatter(stacked_attn[4], ('grp', 'ctx'), scatter_dimension=1, ti...  152 us
    all_gather x2, waiting for transfers between devices, fetch_expert(): lax.all_gather(w_up[layer_index], 'ctx', axis=1, tiled=True)  146 us
    all_gather x2, waiting for transfers between devices, fetch_expert(): lax.all_gather(w_down[layer_index], 'ctx', axis=1, tiled=True)  143 us
  transfers between devices with their start and end apart: 54, of which 40 were waited for; matrix products, arithmetic and copies ran while one was open for 22% of the time, Pallas kernels for 0%

commit v1 on v0

v1 whole, which is shorter than its diff:
```python
import functools
import math

import jax
import jax.numpy as jnp
from jax import lax
from jax.experimental import pallas as pl
from jax.experimental.pallas import tpu as pltpu
from jax.sharding import Mesh, PartitionSpec as P

D = 1024
QUERY_HEADS = 16
KEY_VALUE_HEADS = 8
HS = 64
E = 32
F = 512
TOP = 8
LAYERS = 2
CAP = 42
SLOTS = 48
EPSILON = 1e-06
SCALE = float(HS) ** (-0.5)
QB = 256
BF = jnp.bfloat16
F32 = jnp.float32
MESH = pl.DeviceIdType.MESH
VMEM_BYTES = 60 * 1024 * 1024


def dot(a, b, ca=1, cb=0):
    return lax.dot_general(a, b, (((ca,), (cb,)), ((), ())), preferred_element_type=F32)


def call(kernel, outs, args, flops, in_specs=None, out_specs=None, grid=None, scratch=()):
    nbytes = sum(a.size * a.dtype.itemsize for a in args)
    nbytes += sum(math.prod(o.shape) * jnp.dtype(o.dtype).itemsize for o in outs)
    kw = {} if grid is None else {"grid": grid}
    if in_specs is not None:
        kw["in_specs"] = in_specs
    if out_specs is not None:
        kw["out_specs"] = out_specs
    return pl.pallas_call(
        kernel,
        out_shape=tuple(outs),
        scratch_shapes=list(scratch),
        compiler_params=pltpu.CompilerParams(vmem_limit_bytes=VMEM_BYTES),
        cost_estimate=pl.CostEstimate(
            flops=int(flops), bytes_accessed=int(nbytes), transcendentals=0
        ),
        **kw,
    )(*args)


def sds(shape, dtype):
    return jax.ShapeDtypeStruct(tuple(shape), dtype)


def full(shape):
    n = len(shape)
    return pl.BlockSpec(tuple(shape), lambda *_: (0,) * n)


def exchange(ops, cid, grp_size):
    n = grp_size * 2
    count = len(ops)
    modes = [mode for _, mode in ops]

    def kernel(*refs):
        ins = refs[:count]
        outs = refs[count : 2 * count]
        send, recv, local = refs[2 * count :]
        me = lax.axis_index("grp") * 2 + lax.axis_index("zp")
        barrier = pltpu.get_barrier_semaphore()

        def where(k):
            peer = lax.rem(me + k, n)
            return peer, {"grp": peer // 2, "zp": lax.rem(peer, 2)}

        for k in range(1, n):
            _, place = where(k)
            pl.semaphore_signal(barrier, inc=1, device_id=place, device_id_type=MESH)
        pl.semaphore_wait(barrier, n - 1)
        copies = []
        for k in range(1, n):
            peer, place = where(k)
            for i in range(count):
                src = ins[i] if modes[i] == "gather" else ins[i].at[peer]
                copy = pltpu.make_async_remote_copy(
                    src_ref=src,
                    dst_ref=outs[i].at[me],
                    send_sem=send.at[i, k],
                    recv_sem=recv.at[i, k],
                    device_id=place,
                    device_id_type=MESH,
                )
                copy.start()
                copies.append(copy)
        own = []
        for i in range(count):
            src = ins[i] if modes[i] == "gather" else ins[i].at[me]
            copy = pltpu.make_async_copy(src, outs[i].at[me], local.at[i])
            copy.start()
            own.append(copy)
        for copy in own:
            copy.wait()
        for copy in copies:
            copy.wait()

    shapes = []
    total = 0
    for x, mode in ops:
        shape = (n,) + x.shape if mode == "gather" else x.shape
        shapes.append(sds(shape, x.dtype))
        total += math.prod(shape) * x.dtype.itemsize
    any_spec = pl.BlockSpec(memory_space=pl.ANY)
    return pl.pallas_call(
        kernel,
        out_shape=tuple(shapes),
        in_specs=[any_spec] * count,
        out_specs=tuple([any_spec] * count),
        scratch_shapes=[
            pltpu.SemaphoreType.DMA((count, n)),
            pltpu.SemaphoreType.DMA((count, n)),
            pltpu.SemaphoreType.DMA((count,)),
        ],
        compiler_params=pltpu.CompilerParams(collective_id=cid, has_side_effects=True),
        cost_estimate=pl.CostEstimate(
            flops=0, bytes_accessed=40 * int(total), transcendentals=0
        ),
    )(*[x for x, _ in ops])


def swap_halves(x):
    lane = lax.broadcasted_iota(jnp.int32, x.shape, 1)
    width = x.shape[1]
    up = pltpu.roll(x, width - HS // 2, 1)
    down = pltpu.roll(x, HS // 2, 1)
    return jnp.where((lane & (HS - 1)) < HS // 2, up, down)


def inv_rms_of(x):
    return lax.rsqrt(jnp.mean(x * x, axis=-1, keepdims=True) + EPSILON)


def qkv_forward(stream_parts, packed, cos_t, sin_t, ctx):
    first = len(stream_parts) == 1
    rows = stream_parts[0].shape[0]
    width = 256 * ctx
    tail = (width + D) // 128

    def kernel(*refs):
        if first:
            h_ref, w_ref, t_ref, c_ref, s_ref, out_ref, gains_ref = refs
            x = h_ref[...].astype(F32)
        else:
            h_ref, p_ref, w_ref, t_ref, c_ref, s_ref, out_ref, gains_ref, x_ref = refs
            x = h_ref[...]
            for j in range(p_ref.shape[0]):
                x = x + p_ref[j].astype(F32)
            x_ref[...] = x
        gains = jnp.transpose(t_ref[...].astype(F32))[32:40]
        gains_ref[...] = gains
        normed = (x * inv_rms_of(x) * gains[0:1]).astype(BF)
        cos_v = c_ref[...]
        sin_v = s_ref[...]
        for i in range(ctx):
            y = dot(normed, w_ref[:, 256 * i : 256 * (i + 1)])
            out_ref[i] = (y * cos_v + swap_halves(y) * sin_v).astype(BF)

    args = list(stream_parts) + [packed, packed, cos_t, sin_t]
    in_specs = [full(a.shape) for a in stream_parts] + [
        pl.BlockSpec((D, width), lambda i: (0, 0)),
        pl.BlockSpec((D, 128), lambda i: (0, tail)),
        full(cos_t.shape),
        full(sin_t.shape),
    ]
    outs = [sds((ctx, rows, 256), BF), sds((8, D), F32)]
    if not first:
        outs.append(sds((rows, D), F32))
    return call(
        kernel,
        outs,
        args,
        2 * rows * D * width,
        in_specs=in_specs,
        out_specs=tuple(full(o.shape) for o in outs),
        grid=(1,),
    )


def block_mask(seg_row, seg_col, qb, length):
    keys = (qb + 1) * QB
    qi = lax.broadcasted_iota(jnp.int32, (QB, keys), 0) + qb * QB
    ki = lax.broadcasted_iota(jnp.int32, (QB, keys), 1)
    sr = seg_row[:, :keys]
    return (ki <= qi) & ((sr == 0) | (sr == seg_col))


def attention_forward(x, seg_row, seg_col, ctx, hq, tok):
    micro = x.shape[1] // tok
    length = ctx * tok
    per = QB // tok

    def kernel(x_ref, sr_ref, sc_ref, o_ref, l_ref):
        xs = x_ref[...].reshape(length, 256)
        ks = xs[:, 128:192]
        vs = xs[:, 192:256]
        for qb in range(length // QB):
            keys = (qb + 1) * QB
            rows = slice(qb * QB, (qb + 1) * QB)
            mask = block_mask(sr_ref[0], sc_ref[0, rows, :], qb, length)
            outs = []
            lses = []
            for h in range(hq):
                q = xs[rows, HS * h : HS * (h + 1)]
                s = jnp.where(mask, dot(q, ks[:keys], 1, 1) * SCALE, -1e30)
                top = jnp.max(s, axis=-1, keepdims=True)
                p = jnp.exp(s - top)
                total = jnp.sum(p, axis=-1, keepdims=True)
                o = dot(p.astype(BF), vs[:keys]) / total
                outs.append(o)
                lses.append(jnp.broadcast_to(top + jnp.log(total), (QB, HS)))
            for _ in range(hq, 2):
                outs.append(jnp.zeros((QB, HS), F32))
                lses.append(jnp.zeros((QB, HS), F32))
            o_ref[qb * per : (qb + 1) * per] = (
                jnp.concatenate(outs, axis=1).astype(BF).reshape(per, tok, 128)
            )
            l_ref[0, rows, :] = jnp.concatenate(lses, axis=1)

    return call(
        kernel,
        [sds((ctx, micro * tok, 128), BF), sds((micro, length, 128), F32)],
        [x, seg_row, seg_col],
        2 * micro * hq * length * length * HS,
        in_specs=[
            pl.BlockSpec((ctx, tok, 256), lambda m: (0, m, 0)),
            pl.BlockSpec((1, 1, length), lambda m: (m, 0, 0)),
            pl.BlockSpec((1, length, 1), lambda m: (m, 0, 0)),
        ],
        out_specs=(
            pl.BlockSpec((ctx, tok, 128), lambda m: (0, m, 0)),
            pl.BlockSpec((1, length, 128), lambda m: (m, 0, 0)),
        ),
        grid=(micro,),
    )


def attention_backward(x, d_out, out, lse, seg_row, seg_col, ctx, hq, tok):
    micro = x.shape[1] // tok
    length = ctx * tok
    per = QB // tok

    def kernel(x_ref, d_ref, o_ref, l_ref, sr_ref, sc_ref, dx_ref, dk_ref, dv_ref):
        xs = x_ref[...].reshape(length, 256)
        ks = xs[:, 128:192]
        vs = xs[:, 192:256]
        ds_all = d_ref[...].reshape(length, 128)
        os_all = o_ref[...].reshape(length, 128)
        dk_ref[...] = jnp.zeros((length, HS), F32)
        dv_ref[...] = jnp.zeros((length, HS), F32)
        for qb in range(length // QB):
            keys = (qb + 1) * QB
            rows = slice(qb * QB, (qb + 1) * QB)
            mask = block_mask(sr_ref[0], sc_ref[0, rows, :], qb, length)
            dqs = []
            for h in range(hq):
                cols = slice(HS * h, HS * (h + 1))
                q = xs[rows, cols]
                do = ds_all[rows, cols]
                delta = jnp.sum(
                    do.astype(F32) * os_all[rows, cols].astype(F32), axis=-1, keepdims=True
                )
                s = dot(q, ks[:keys], 1, 1) * SCALE - l_ref[0, rows, HS * h : HS * h + 1]
                p = jnp.exp(jnp.where(mask, s, -1e30))
                dp = dot(do, vs[:keys], 1, 1)
                ds = (p * (dp - delta) * SCALE).astype(BF)
                dqs.append(dot(ds, ks[:keys]))
                dk_ref[:keys] += dot(ds, q, 0, 0)
                dv_ref[:keys] += dot(p.astype(BF), do, 0, 0)
            for _ in range(hq, 2):
                dqs.append(jnp.zeros((QB, HS), F32))
            dx_ref[qb * per : (qb + 1) * per, :, 0:128] = (
                jnp.concatenate(dqs, axis=1).astype(BF).reshape(per, tok, 128)
            )
        dx_ref[:, :, 128:256] = (
            jnp.concatenate([dk_ref[...], dv_ref[...]], axis=1)
            .astype(BF)
            .reshape(ctx, tok, 128)
        )

    return call(
        kernel,
        [sds((ctx, micro * tok, 256), BF)],
        [x, d_out, out, lse, seg_row, seg_col],
        5 * micro * hq * length * length * HS,
        in_specs=[
            pl.BlockSpec((ctx, tok, 256), lambda m: (0, m, 0)),
            pl.BlockSpec((ctx, tok, 128), lambda m: (0, m, 0)),
            pl.BlockSpec((ctx, tok, 128), lambda m: (0, m, 0)),
            pl.BlockSpec((1, length, 128), lambda m: (m, 0, 0)),
            pl.BlockSpec((1, 1, length), lambda m: (m, 0, 0)),
            pl.BlockSpec((1, length, 1), lambda m: (m, 0, 0)),
        ],
        out_specs=(pl.BlockSpec((ctx, tok, 256), lambda m: (0, m, 0)),),
        grid=(micro,),
        scratch=[pltpu.VMEM((length, HS), F32), pltpu.VMEM((length, HS), F32)],
    )[0]


def side_by_side(m_ref, ctx, hq):
    return jnp.concatenate([m_ref[i][:, : HS * hq] for i in range(ctx)], axis=1)


def output_forward(mixed, stream, packed, gains, chosen, ctx, hq, n, held):
    rows = stream.shape[0]
    at = 256 * ctx // D
    tail = (256 * ctx + D) // 128

    def kernel(m_ref, x_ref, w_ref, t_ref, g_ref, c_ref, s_ref, n_ref, gate_ref):
        x = x_ref[...].astype(F32) + dot(side_by_side(m_ref, ctx, hq), w_ref[...])
        s_ref[...] = x
        normed = (x * inv_rms_of(x) * g_ref[1:2]).astype(BF)
        n_ref[...] = normed
        logits = dot(t_ref[...], normed, 0, 1)[:E]
        named = c_ref[...] > 0.0
        logits = jnp.where(named, logits, -1e30)
        top = jnp.max(logits, axis=0, keepdims=True)
        p = jnp.where(named, jnp.exp(logits - top), 0.0)
        gates = p / jnp.sum(p, axis=0, keepdims=True)
        gate_ref[...] = jnp.zeros(gate_ref.shape, F32)
        for j in range(n):
            gate_ref[j, 0:held, :] = gates[held * j : held * (j + 1)]

    outs = [sds((rows, D), F32), sds((rows, D), BF), sds((n, 8, rows), F32)]
    return call(
        kernel,
        outs,
        [mixed, stream, packed, packed, gains, chosen],
        2 * rows * D * D,
        in_specs=[
            full(mixed.shape),
            full(stream.shape),
            pl.BlockSpec((D, D), lambda i: (0, at)),
            pl.BlockSpec((D, 128), lambda i: (0, tail)),
            full(gains.shape),
            full(chosen.shape),
        ],
        out_specs=tuple(full(o.shape) for o in outs),
        grid=(1,),
    )


def norm_back(x, gain, d_normed):
    r = inv_rms_of(x)
    grad_gain = jnp.sum(d_normed * x * r, axis=0, keepdims=True)
    q = d_normed * gain
    dx = r * q - x * (r * r * r) * jnp.mean(x * q, axis=-1, keepdims=True)
    return dx, grad_gain


def output_backward(parts, d_gates, gates, g, stream, normed, mixed, packed, gains, extra, ctx, hq, n, held):
    rows = stream.shape[0]
    at = 256 * ctx // D
    tail = (256 * ctx + D) // 128

    def kernel(p_ref, dg_ref, gt_ref, g_ref, x_ref, nm_ref, m_ref, w_ref, t_ref, gain_ref, ex_ref, g1_ref, dm_ref, gw_ref):
        gates_v = jnp.concatenate([gt_ref[j, 0:held, :] for j in range(n)], axis=0)
        dgate_v = jnp.concatenate([dg_ref[j, 0:held, :] for j in range(n)], axis=0)
        mean = jnp.sum(gates_v * dgate_v, axis=0, keepdims=True)
        d_logits = (gates_v * (dgate_v - mean)).astype(BF)
        d_logits = jnp.concatenate([d_logits, jnp.zeros((128 - E, rows), BF)], axis=0)
        router = t_ref[...]
        d_normed = dot(d_logits, router, 0, 1)
        for j in range(n):
            d_normed = d_normed + p_ref[j].astype(F32)
        x = x_ref[...]
        dx, grad_gain = norm_back(x, gain_ref[1:2], d_normed)
        g1 = g_ref[...].astype(F32) + dx
        g1_ref[...] = g1
        low = g1.astype(BF)
        dm = dot(low, w_ref[...], 1, 1).astype(BF)
        for i in range(ctx):
            part = dm[:, HS * hq * i : HS * hq * (i + 1)]
            if hq < 2:
                part = jnp.concatenate([part, jnp.zeros((rows, 128 - HS * hq), BF)], axis=1)
            dm_ref[i] = part
        gw_ref[:, 0:D] = dot(side_by_side(m_ref, ctx, hq), low, 0, 0).astype(BF)
        grad_router = dot(nm_ref[...], d_logits, 0, 1)
        row = lax.broadcasted_iota(jnp.int32, (128, D), 0)
        cols = jnp.where(row == 33, jnp.broadcast_to(grad_gain, (128, D)), 0.0)
        cols = jnp.where(row == 32, jnp.broadcast_to(ex_ref[0:1, :], (128, D)), cols)
        gw_ref[:, D : D + 128] = (grad_router + jnp.transpose(cols)).astype(BF)

    outs = [sds((rows, D), F32), sds((ctx, rows, 128), BF), sds((D, D + 128), BF)]
    args = [parts, d_gates, gates, g, stream, normed, mixed, packed, packed, gains, extra]
    in_specs = [full(a.shape) for a in args]
    in_specs[7] = pl.BlockSpec((D, D), lambda i: (0, at))
    in_specs[8] = pl.BlockSpec((D, 128), lambda i: (0, tail))
    return call(
        kernel,
        outs,
        args,
        4 * rows * D * D,
        in_specs=in_specs,
        out_specs=tuple(full(o.shape) for o in outs),
        grid=(1,),
    )


def qkv_backward(dx, g1, stream, packed, gains, cos_t, sin_t, ctx):
    rows = g1.shape[0]
    width = 256 * ctx

    def kernel(d_ref, g_ref, x_ref, w_ref, gain_ref, c_ref, s_ref, out_ref, gain_out, gw_ref):
        x = x_ref[...].astype(F32)
        gain = gain_ref[0:1]
        normed = (x * inv_rms_of(x) * gain).astype(BF)
        cos_v = c_ref[...]
        sin_v = s_ref[...]
        d_normed = jnp.zeros((rows, D), F32)
        for i in range(ctx):
            y = d_ref[i].astype(F32)
            lin = (y * cos_v - swap_halves(y) * sin_v).astype(BF)
            cols = slice(256 * i, 256 * (i + 1))
            d_normed = d_normed + dot(lin, w_ref[:, cols], 1, 1)
            gw_ref[:, cols] = dot(normed, lin, 0, 0).astype(BF)
        back, grad_gain = norm_back(x, gain, d_normed)
        out_ref[...] = g_ref[...] + back
        gain_out[...] = jnp.broadcast_to(grad_gain, (8, D))

    outs = [sds((rows, D), F32), sds((8, D), F32), sds((D, width), BF)]
    args = [dx, g1, stream, packed, gains, cos_t, sin_t]
    in_specs = [full(a.shape) for a in args]
    in_specs[3] = pl.BlockSpec((D, width), lambda i: (0, 0))
    return call(
        kernel,
        outs,
        args,
        4 * rows * D * width,
        in_specs=in_specs,
        out_specs=tuple(full(o.shape) for o in outs),
        grid=(1,),
    )


def pick_matrix(slot_row, rows):
    at = lax.broadcasted_iota(jnp.int32, (2 * SLOTS, rows), 0)
    return at == slot_row


def weight_specs(half, ctx, buffers=2):
    def own(e):
        return (0, jnp.minimum(e, half - 1), 0, 0)

    def other(e):
        return (0, jnp.maximum(e - half, 0), 0, 0)

    wide = (ctx, 1, D // ctx, F)
    tall = (ctx, 1, F // ctx, D)
    kinds = [(wide, own), (wide, other)] * 2 + [(tall, own), (tall, other)]
    return [
        pl.BlockSpec(shape, index, pipeline_mode=pl.Buffered(buffers))
        for shape, index in kinds
    ]


def pick_weights(e, half, refs, shape):
    own, other = refs
    return jnp.where(e < half, own[...], other[...]).reshape(shape)


def experts_forward(x, gates, slots, core, weights, ctx, held):
    n, rows, _ = x.shape
    half = held // 2
    lanes = 2 * SLOTS

    def kernel(core_ref, x_ref, g_ref, s_ref, w0, w1, w2, w3, w4, w5, out_ref, acc_ref, row_ref, eo_ref):
        e = pl.program_id(0)
        at = lax.rem(e + core_ref[0] * half, held)
        w_gate = pick_weights(e, half, (w0, w1), (D, F))
        w_up = pick_weights(e, half, (w2, w3), (D, F))
        w_down = pick_weights(e, half, (w4, w5), (F, D))
        for s in range(n):
            pick = pick_matrix(s_ref[s, pl.ds(at, 1), :], rows).astype(BF)
            row_ref[lanes * s : lanes * (s + 1), :] = dot(pick, x_ref[s]).astype(BF)
        rws = row_ref[...]
        ga = dot(rws, w_gate)
        up = dot(rws, w_up)
        hidden = (ga * jax.nn.sigmoid(ga) * up).astype(BF)
        eo_ref[...] = dot(hidden, w_down).astype(BF)
        for s in range(n):
            pick = pick_matrix(s_ref[s, pl.ds(at, 1), :], rows)
            gated = jnp.where(pick, g_ref[s, pl.ds(at, 1), :], 0.0).astype(BF)
            add = dot(gated, eo_ref[lanes * s : lanes * (s + 1), :], 0, 0)

            @pl.when(e == 0)
            def _():
                acc_ref[s] = add.astype(F32)

            @pl.when((e > 0) & (e < held - 1))
            def _():
                acc_ref[s] = (acc_ref[s].astype(F32) + add).astype(F32)

            @pl.when(e == held - 1)
            def _():
                out_ref[s] = (acc_ref[s].astype(F32) + add).astype(BF)

    flops = 2 * held * n * (lanes * D * F * 3 + 2 * lanes * rows * D)
    spec = pl.BlockSpec(memory_space=pltpu.SMEM)
    return call(
        kernel,
        [sds(x.shape, BF)],
        [core, x, gates, slots] + list(weights),
        flops,
        in_specs=[spec, full(x.shape), full(gates.shape), full(slots.shape)]
        + weight_specs(half, ctx),
        out_specs=(full(x.shape),),
        grid=(held,),
        scratch=[
            pltpu.VMEM(x.shape, F32),
            pltpu.VMEM((n * lanes, D), BF),
            pltpu.VMEM((n * lanes, D), BF),
        ],
    )[0]


def experts_backward(x, g, gates, slots, core, weights, ctx, held, with_out):
    n, rows, _ = x.shape
    half = held // 2
    lanes = 2 * SLOTS

    def kernel(core_ref, x_ref, gr_ref, g_ref, s_ref, w0, w1, w2, w3, w4, w5, *rest):
        dx_ref, dg_ref, o0, o1, o2, o3, o4, o5 = rest[:8]
        if with_out:
            out_ref, acc_ref, row_ref, grow_ref = rest[8:]
        else:
            acc_ref, row_ref, grow_ref = rest[8:]
        e = pl.program_id(0)
        at = lax.rem(e + core_ref[0] * half, held)
        w_gate = pick_weights(e, half, (w0, w1), (D, F))
        w_up = pick_weights(e, half, (w2, w3), (D, F))
        w_down = pick_weights(e, half, (w4, w5), (F, D))
        slot_gates = []
        for s in range(n):
            mine = slice(lanes * s, lanes * (s + 1))
            pick = pick_matrix(s_ref[s, pl.ds(at, 1), :], rows)
            low = pick.astype(BF)
            row_ref[mine, :] = dot(low, x_ref[s]).astype(BF)
            grow_ref[mine, :] = dot(low, gr_ref[s]).astype(BF)
            gated = jnp.where(pick, g_ref[s, pl.ds(at, 1), :], 0.0)
            slot_gates.append(jnp.sum(gated, axis=1, keepdims=True))
        gate = jnp.concatenate(slot_gates, axis=0)
        rws = row_ref[...]
        grows = grow_ref[...]
        ga = dot(rws, w_gate)
        up = dot(rws, w_up)
        sig = jax.nn.sigmoid(ga)
        act = ga * sig
        hidden_f = act * up
        hidden = hidden_f.astype(BF)
        dhg = dot(grows, w_down, 1, 1)
        d_gate = jnp.sum(hidden.astype(F32) * dhg, axis=1, keepdims=True)
        dh = dhg * gate
        dga = (dh * up * (sig * (1.0 + ga * (1.0 - sig)))).astype(BF)
        dup = (dh * act).astype(BF)
        if with_out:
            eo = dot(hidden, w_down).astype(BF)
        drow = (dot(dga, w_gate, 1, 1) + dot(dup, w_up, 1, 1)).astype(BF)
        for s in range(n):
            mine = slice(lanes * s, lanes * (s + 1))
            pick = pick_matrix(s_ref[s, pl.ds(at, 1), :], rows)
            dg_ref[s, pl.ds(at, 1), :] = jnp.sum(
                jnp.where(pick, d_gate[mine], 0.0), axis=0, keepdims=True
            )
            todo = [(acc_ref, dx_ref, dot(pick.astype(BF), drow[mine], 0, 0))]
            if with_out:
                gated = jnp.where(pick, g_ref[s, pl.ds(at, 1), :], 0.0).astype(BF)
                todo.append((out_ref, out_ref, dot(gated, eo[mine], 0, 0)))
            for held_ref, final_ref, add in todo:

                @pl.when(e == 0)
                def _():
                    held_ref[s] = add.astype(held_ref.dtype)

                @pl.when((e > 0) & (e < held - 1))
                def _():
                    held_ref[s] = (held_ref[s].astype(F32) + add).astype(held_ref.dtype)

                @pl.when(e == held - 1)
                def _():
                    final_ref[s] = (held_ref[s].astype(F32) + add).astype(BF)

        dslot = (grows.astype(F32) * gate).astype(BF)
        g_gate = dot(rws, dga, 0, 0).astype(BF).reshape(ctx, 1, D // ctx, F)
        g_up = dot(rws, dup, 0, 0).astype(BF).reshape(ctx, 1, D // ctx, F)
        g_down = dot(hidden, dslot, 0, 0).astype(BF).reshape(ctx, 1, F // ctx, D)

        @pl.when(e < half)
        def _():
            o0[...] = g_gate
            o2[...] = g_up
            o4[...] = g_down

        @pl.when(e >= half)
        def _():
            o1[...] = g_gate
            o3[...] = g_up
            o5[...] = g_down

    wide = sds((ctx, half, D // ctx, F), BF)
    tall = sds((ctx, half, F // ctx, D), BF)
    outs = [sds(x.shape, BF), sds(gates.shape, F32), wide, wide, wide, wide, tall, tall]
    out_specs = [full(x.shape), full(gates.shape)] + weight_specs(half, ctx, 1)
    scratch = [
        pltpu.VMEM(x.shape, F32),
        pltpu.VMEM((n * lanes, D), BF),
        pltpu.VMEM((n * lanes, D), BF),
    ]
    if with_out:
        outs.append(sds(x.shape, BF))
        out_specs.append(full(x.shape))
    flops = 2 * held * n * (lanes * D * F * 9 + 3 * lanes * rows * D)
    spec = pl.BlockSpec(memory_space=pltpu.SMEM)
    return call(
        kernel,
        outs,
        [core, x, g, gates, slots] + list(weights),
        flops,
        in_specs=[spec, full(x.shape), full(g.shape), full(gates.shape), full(slots.shape)]
        + weight_specs(half, ctx),
        out_specs=tuple(out_specs),
        grid=(held,),
        scratch=scratch,
    )


def in_chunks(x, most):
    size = max(1, most // x.shape[1])
    return [slice(i, i + size) for i in range(0, x.shape[0], size)]


def experts_forward_all(x, gates, slots, *rest):
    outs = [
        experts_forward(x[c], gates[c], slots[c], *rest) for c in in_chunks(x, 2048)
    ]
    return outs[0] if len(outs) == 1 else jnp.concatenate(outs)


def experts_backward_all(x, g, gates, slots, *rest):
    outs = [
        experts_backward(x[c], g[c], gates[c], slots[c], *rest) for c in in_chunks(x, 2048)
    ]
    if len(outs) == 1:
        return outs[0]
    joined = []
    for k in range(len(outs[0])):
        parts = [o[k] for o in outs]
        if k in (0, 1, 8):
            joined.append(jnp.concatenate(parts))
        else:
            joined.append(sum(p.astype(F32) for p in parts).astype(BF))
    return joined


def per_device(
    grp_size,
    ctx,
    hidden_in,
    grad_out,
    segments,
    routes,
    attn_gain,
    w_query,
    key_weight,
    value_weight,
    w_output,
    ffn_gain,
    w_router,
    w_gate,
    w_up,
    w_down,
):
    micro, tok, _ = hidden_in.shape
    rows = micro * tok
    length = ctx * tok
    hq = QUERY_HEADS // ctx
    dup = ctx // KEY_VALUE_HEADS
    n = grp_size * 2
    held = E // n
    half = held // 2
    every = ("grp", "zq", "zp", "core")
    line = ("zq", "zp", "core")
    core = lax.axis_index("core")
    core_arr = core.astype(jnp.int32).reshape(1)
    ctx_index = (lax.axis_index("zq") * 2 + lax.axis_index("zp")) * 2 + core
    shard = w_query.shape[1]

    def pack(layer):
        wq = w_query[layer].reshape(shard, ctx, HS * hq)
        if hq < 2:
            wq = jnp.pad(wq, ((0, 0), (0, 0), (0, 128 - HS * hq)))
        wk = jnp.repeat(key_weight[layer].reshape(shard, KEY_VALUE_HEADS, HS), dup, axis=1)
        wv = jnp.repeat(value_weight[layer].reshape(shard, KEY_VALUE_HEADS, HS), dup, axis=1)
        qkv = jnp.concatenate([wq, wk, wv], axis=2).reshape(shard, ctx * 256)
        tail = jnp.concatenate(
            [
                w_router[layer],
                attn_gain[layer][:, None],
                ffn_gain[layer][:, None],
                jnp.zeros((shard, 128 - E - 2), BF),
            ],
            axis=1,
        )
        return jnp.concatenate([qkv, w_output[layer], tail], axis=1)

    packed = [
        lax.all_gather(pack(layer), every, axis=0, tiled=True) for layer in range(LAYERS)
    ]

    def to_holders(w):
        quarter = w.reshape(4, half, w.shape[1], w.shape[2])
        return jnp.tile(quarter, (ctx // 4, 1, 1, 1))

    def swap(x):
        return lax.ppermute(x, "core", [(0, 1), (1, 0)])

    def fetch(layer):
        out = []
        for w in (w_gate[layer], w_up[layer], w_down[layer]):
            own = lax.all_to_all(to_holders(w), line, 0, 0, tiled=True)
            out += [own, swap(own)]
        return out

    weights = [fetch(layer) for layer in range(LAYERS)]

    own_segments = lax.dynamic_slice_in_dim(segments, ctx_index * tok, tok, axis=1)
    prompt = jnp.sum((segments == 0).astype(jnp.int32), axis=1, dtype=jnp.int32)
    before = jnp.sum(
        (segments[:, None, :] < own_segments[:, :, None]).astype(jnp.int32),
        axis=2,
        dtype=jnp.int32,
    )
    places = ctx_index * tok + jnp.arange(tok, dtype=jnp.int32)[None, :]
    places = jnp.where(own_segments == 0, places, prompt[:, None] + places - before)
    places = places.reshape(rows).astype(F32)
    lane = jnp.arange(256, dtype=jnp.int32)
    freqs = jnp.exp(
        (lane % (HS // 2)).astype(F32) * (-2.0 * math.log(10000.0) / HS)
    )
    angles = places[:, None] * freqs[None, :]
    turned = (lane < 192)[None, :]
    sign = jnp.where((lane % HS) < HS // 2, -1.0, 1.0)[None, :]
    cos_t = jnp.where(turned, jnp.cos(angles), 1.0)
    sin_t = jnp.where(turned, jnp.sin(angles) * sign, 0.0)
    seg_row = segments[:, None, :]
    seg_col = segments[:, :, None]

    flat = routes.reshape(rows, TOP)
    ids = jnp.arange(E, dtype=jnp.int32)
    chosen = jnp.any(ids[:, None, None] == flat[None, :, :], axis=2)
    marks = chosen.astype(BF).reshape(E, micro, tok)
    earlier = (
        jnp.arange(tok)[:, None] < jnp.arange(tok)[None, :]
    ).astype(BF)
    rank = jnp.einsum("emt,ts->ems", marks, earlier, preferred_element_type=F32)
    slot = rank.astype(jnp.int32) + SLOTS * jnp.arange(micro, dtype=jnp.int32)[None, :, None]
    slot = jnp.where(chosen, slot.reshape(E, rows), -1)
    slot = jnp.pad(
        slot.reshape(n, held, rows), ((0, 0), (0, 8 - held), (0, 0)), constant_values=-1
    )
    chosen_f = chosen.astype(F32)
    last_g = lax.all_gather(grad_out.reshape(rows, D), ("grp", "zp"), axis=0, tiled=False)
    last_g = last_g.reshape(n, rows, D)

    ids_of = iter(range(1, 100))
    saved = []
    parts = (hidden_in.reshape(rows, D),)
    for layer in range(LAYERS):
        got = qkv_forward(parts, packed[layer], cos_t, sin_t, ctx)
        qkv, gains = got[0], got[1]
        stream = parts[0] if layer == 0 else got[2]
        heads = lax.all_to_all(qkv, line, 0, 0, tiled=True)
        out, lse = attention_forward(heads, seg_row, seg_col, ctx, hq, tok)
        mixed = lax.all_to_all(out, line, 0, 0, tiled=True)
        stream1, normed, gates = output_forward(
            mixed, stream, packed[layer], gains, chosen_f, ctx, hq, n, held
        )
        ops = [(normed, "gather"), (gates, "a2a")]
        if layer == 0:
            ops.append((slot, "a2a"))
        moved = exchange(ops, next(ids_of), grp_size)
        if layer == 0:
            slots_here = moved[2]
        saved.append((stream, heads, out, lse, mixed, stream1, normed, gates, gains, moved[0], moved[1]))
        if layer < LAYERS - 1:
            sent = experts_forward_all(
                moved[0], moved[1], slots_here, core_arr, weights[layer], ctx, held
            )
            parts = (stream1, exchange([(sent, "a2a")], next(ids_of), grp_size)[0])

    g = grad_out.reshape(rows, D)
    extra = jnp.zeros((8, D), F32)
    small = [None] * LAYERS
    wide = [None] * LAYERS
    expert = [None] * LAYERS
    for layer in reversed(range(LAYERS)):
        stream, heads, out, lse, mixed, stream1, normed, gates, gains, xs, gates_here = saved[layer]
        last = layer == LAYERS - 1
        if last:
            gs = last_g
        else:
            gs = exchange([(g.astype(BF), "gather")], next(ids_of), grp_size)[0]
        res = experts_backward_all(
            xs, gs, gates_here, slots_here, core_arr, weights[layer], ctx, held, last
        )
        shards = []
        for own, other in ((res[2], res[3]), (res[4], res[5]), (res[6], res[7])):
            total = (own.astype(F32) + swap(other).astype(F32)).astype(BF)
            shards.append(lax.all_to_all(total, line, 0, 0, tiled=True))
        expert[layer] = shards
        if last:
            final_parts = lax.all_to_all(res[8], ("grp", "zp"), 0, 0, tiled=True)
            hidden_out = (
                stream1 + jnp.sum(final_parts.astype(F32), axis=0)
            ).astype(BF).reshape(micro, tok, D)
        d_parts, d_gates = exchange(
            [(res[0], "a2a"), (res[1], "a2a")], next(ids_of), grp_size
        )
        g1, d_mixed, small[layer] = output_backward(
            d_parts, d_gates, gates, g, stream1, normed, mixed, packed[layer], gains, extra,
            ctx, hq, n, held,
        )
        d_out = lax.all_to_all(d_mixed, line, 0, 0, tiled=True)
        dx = attention_backward(heads, d_out, out, lse, seg_row, seg_col, ctx, hq, tok)
        dx = lax.all_to_all(dx, line, 0, 0, tiled=True)
        g, extra, wide[layer] = qkv_backward(
            dx, g1, stream, packed[layer], gains, cos_t, sin_t, ctx
        )
    small = [lax.psum_scatter(s, every, scatter_dimension=0, tiled=True) for s in small]
    wide = [lax.psum_scatter(s, every, scatter_dimension=0, tiled=True) for s in wide]
    first_gain = lax.psum_scatter(extra[0], every, scatter_dimension=0, tiled=True)

    def unpack(layer):
        w = wide[layer].astype(F32).reshape(shard, ctx, 256)
        gq = w[:, :, : HS * hq].reshape(shard, QUERY_HEADS * HS)
        gk = w[:, :, 128:192].reshape(shard, KEY_VALUE_HEADS, dup, HS).sum(axis=2)
        gv = w[:, :, 192:256].reshape(shard, KEY_VALUE_HEADS, dup, HS).sum(axis=2)
        s = small[layer].astype(F32)
        return (
            gq,
            gk.reshape(shard, KEY_VALUE_HEADS * HS),
            gv.reshape(shard, KEY_VALUE_HEADS * HS),
            s[:, :D],
            s[:, D + 33],
            s[:, D : D + E],
        )

    got = [unpack(layer) for layer in range(LAYERS)]

    def stacked(k):
        return jnp.stack([got[layer][k] for layer in range(LAYERS)])

    gain_grad = jnp.stack(
        [first_gain] + [small[layer][:, D + 32].astype(F32) for layer in range(LAYERS - 1)]
    )

    def owned(k):
        out = []
        for layer in range(LAYERS):
            s = expert[layer][k].astype(F32)
            s = s.reshape((ctx // 4, 4 * half) + s.shape[2:]).sum(axis=0)
            out.append(s)
        return jnp.stack(out)

    return (
        hidden_out,
        g.reshape(micro, tok, D),
        gain_grad,
        stacked(0),
        stacked(1),
        stacked(2),
        stacked(3),
        stacked(4),
        stacked(5),
        owned(0),
        owned(1),
        owned(2),
    )


def solution(mesh):
    grp_size = mesh.shape["grp"]
    ctx = mesh.shape["ctx"]
    fine = Mesh(
        mesh.devices.reshape(grp_size, ctx // 4, 2, 2), ("grp", "zq", "zp", "core")
    )
    line = ("zq", "zp", "core")
    every = ("grp",) + line
    row = P("grp", line, None)
    placed = (
        row,
        row,
        P("grp", None),
        row,
        P(None, every),
        P(None, every, None),
        P(None, every, None),
        P(None, every, None),
        P(None, every, None),
        P(None, every),
        P(None, every, None),
        P(None, "grp", line, None),
        P(None, "grp", line, None),
        P(None, "grp", line, None),
    )
    return jax.shard_map(
        functools.partial(per_device, grp_size, ctx),
        mesh=fine,
        in_specs=placed,
        out_specs=(
            row,
            row,
            P(None, every),
            P(None, every, None),
            P(None, every, None),
            P(None, every, None),
            P(None, every, None),
            P(None, every),
            P(None, every, None),
            P(None, "grp", line, None),
            P(None, "grp", line, None),
            P(None, "grp", line, None),
        ),
        check_vma=False,
    )
```

time: 3690 us -> 1910 us (0.52)
  waiting for transfers between devices: 2300 us -> 826 us
  Pallas kernels: 0 us -> 691 us
  matrix products: 582 us -> 0.1 us
  local copies, waits for them, and re-layouts: 366 us -> 37.2 us
  other arithmetic: 148 us -> 63.7 us
    reduce_scatter x7 -> x4, waiting for transfers between devices: 1080 us -> 201 us  [per_device(): lax.psum_scatter(s, every, scatter_dimension=0, tiled=True)]
    all_gather x22 -> x3, waiting for transfers between devices: 698 us -> 0.04 us  [the longest x2 0.02 us: per_device(): lax.all_gather(pack(layer), every, axis=0, tiled=True)]
    pallas_call x0 -> x21, Pallas kernels: none -> 691 us  [the longest x6 427 us: exchange(): pl.pallas_call(kernel, out_shape=tuple(shapes), in_specs=[any_spec] * cou...]
    dot_general x210 -> x1, matrix products: 582 us -> 0.1 us  [per_device(): rank = jnp.einsum('emt,ts->ems', marks, earlier, preferred_element_type=F32)]
    all_to_all x14 -> x17, waiting for transfers between devices: 136 us -> 602 us  [the longest x6 264 us: fetch(): own = lax.all_to_all(to_holders(w), line, 0, 0, tiled=True)]
    unnamed x51 -> x7, waiting for transfers between devices: 383 us -> 2.31 us
    gather x16 -> x0, local copies, waits for them, and re-layouts: 91.1 us -> none  [the longest x4 24.4 us: ffn_forward(): picked_out = returned[local_slot].reshape(row_values, TOP, MODEL_WIDTH)]
    all_gather x2 -> x0, blocking collectives: 80.9 us -> none  [fetch_attn(): lax.all_gather(w_router[layer_index], ('grp', 'ctx'), axis=0, tiled=True)]
  transfers between devices with their start and end apart: 54 -> 36, of which waited for: 40 -> 22; matrix products, arithmetic and copies ran while one was open for 22% -> 4% of each run, Pallas kernels for 0% -> 18%
where the time goes in v1:
time: 1910 us; the launch traced here: 1900 us
  waiting for transfers between devices  826 us (43%)
  Pallas kernels  691 us (36%)
  blocking collectives  180 us (9%)
  starting transfers between devices  84.4 us (4%)
  other arithmetic  63.7 us (3%)
  local copies, waits for them, and re-layouts  37.2 us (2%)
    pallas_call x6, Pallas kernels, exchange(): pl.pallas_call(kernel, out_shape=tuple(shapes), in_specs=[any_spec] * cou...  427 us
    all_to_all x6, waiting for transfers between devices, fetch(): own = lax.all_to_all(to_holders(w), line, 0, 0, tiled=True)  264 us
    pallas_call x15, Pallas kernels, call(): pl.pallas_call(kernel, out_shape=tuple(outs), scratch_shapes=list(scratch...  264 us
    all_to_all x6, waiting for transfers between devices, per_device(): shards.append(lax.all_to_all(total, line, 0, 0, tiled=True))  211 us
    reduce_scatter x4, waiting for transfers between devices, per_device(): lax.psum_scatter(s, every, scatter_dimension=0, tiled=True)  201 us
    unnamed x1, blocking collectives  77.7 us
    all_to_all x1, waiting for transfers between devices, per_device(): final_parts = lax.all_to_all(res[8], ('grp', 'zp'), 0, 0, tiled=True)  49.2 us
  transfers between devices with their start and end apart: 36, of which 22 were waited for; matrix products, arithmetic and copies ran while one was open for 4% of the time, Pallas kernels for 18%

profile of v1, /device:TPU:0, one launch (start us, length us, event | category | flops | bytes accessed | tf_op | source)
XLA Modules:
  0.0 1897.6 jit_solution(16261709994718351539)
XLA Ops:
  16.0 6.3 all-to-all-start.2
  24.1 62.3 %all-to-all-done.2.w0 = bf16[8,2,128,512]{3,2,1,0:T(8,128)(2,1)} async-done(((bf16[8,2,128,512]{3,2,1,0:T(8,128)(2,1)}), bf16[8,2,128,512]{3,2,1,0:T(8,128)(2,1)}, u32[]{:S(2)}, u32[]{:S(2)}) %all-to-all-start.2) | async-done | bytes 2097184 | tf_op jit(solution)/shard_map/all_to_all | solution.py:731
  95.0 53.2 %all-to-all-done.3.w2 = bf16[8,2,128,512]{3,2,1,0:T(8,128)(2,1)} async-done(((bf16[8,2,128,512]{3,2,1,0:T(8,128)(2,1)}), bf16[8,2,128,512]{3,2,1,0:T(8,128)(2,1)}, u32[]{:S(2)}, u32[]{:S(2)}) %all-to-all-start.3) | async-done | bytes 2097184 | tf_op jit(solution)/shard_map/all_to_all | solution.py:731
  156.9 60.8 %all-to-all-done.4.w4 = bf16[8,2,64,1024]{3,2,1,0:T(8,128)(2,1)} async-done(((bf16[8,2,64,1024]{3,2,1,0:T(8,128)(2,1)}), bf16[8,2,64,1024]{3,2,1,0:T(8,128)(2,1)}, u32[]{:S(2)}, u32[]{:S(2)}) %all-to-all-start.4) | async-done | bytes 2097184 | tf_op jit(solution)/shard_map/all_to_all | solution.py:731
  219.2 4.5 all-to-all-start.7
  226.0 5.2 shard_map.229
  231.2 50.5 %all-to-all-done.7.w0 = bf16[8,2,128,512]{3,2,1,0:T(8,128)(2,1)} async-done(((bf16[8,2,128,512]{3,2,1,0:T(8,128)(2,1)}), bf16[8,2,128,512]{3,2,1,0:T(8,128)(2,1)}, u32[]{:S(2)}, u32[]{:S(2)}) %all-to-all-start.7) | async-done | bytes 2097184 | tf_op jit(solution)/shard_map/all_to_all | solution.py:731
  281.8 30.8 %all_to_all.105.x_ref = bf16[8,256,256]{2,1,0:T(8,128)(2,1)} all-to-all(bf16[8,256,256]{2,1,0:T(8,128)(2,1)} %get-tuple-element.65), channel_id=1, replica_groups=mesh['grp'=4,'zq'=2,'zp'=2,'core'=2] {'zq','zp','core'}, dimensions={0} | all-to-all | bytes 2097152 | tf_op jit(solution)/shard_map/all_to_all | solution.py:783
  319.7 9.7 shard_map.230
  329.4 37.3 %all-to-all-done.8.w2 = bf16[8,2,128,512]{3,2,1,0:T(8,128)(2,1)S(1)} async-done(((bf16[8,2,128,512]{3,2,1,0:T(8,128)(2,1)}), bf16[8,2,128,512]{3,2,1,0:T(8,128)(2,1)S(1)}, u32[]{:S(2)}, u32[]{:S(2)}) %all-to-all-start.8) | async-done | bytes 2097184 | tf_op jit(solution)/shard_map/all_to_all | solution.py:731
  372.3 14.6 all-to-all-done.1.m_ref
  388.6 5.0 all-to-all-start.9
  400.1 140.1 %shard_map.232 = (bf16[8,256,1024]{2,1,0:T(8,128)(2,1)}, f32[8,8,256]{2,1,0:T(8,128)}, s32[8,8,256]{2,1,0:T(8,128)}) custom-call(bf16[256,1024]{1,0:T(8,128)(2,1)} %get-tuple-element.69.refs_0_.nm_ref, f32[8,8,256]{2,1,0:T(8,128)} %get-tuple-element.70.refs_1_.gt_ref, s32[8,8,256]{2,1,0:T(8,128)} %pad.4.refs_2_), custom_call_target="tpu_custom_call" | custom-call | bytes 173015040 | tf_op jit(solution)/shard_map/pallas_call | solution.py:116
  541.5 31.7 %shard_map.233.refs_0_ = bf16[8,256,1024]{2,1,0:T(8,128)(2,1)} custom-call(s32[1]{0:T(128)} %bitcast.8.core_ref, bf16[8,256,1024]{2,1,0:T(8,128)(2,1)} %get-tuple-element.71.x_ref, f32[8,8,256]{2,1,0:T(8,128)} %get-tuple-element.72.g_ref, s32[8,8,256]{2,1,0:T(8,128)} %get-tuple-element.73.s_ref, bf16[8,2,128,512]{3,2,1,0:T(8,128)(2,1)} %all-to-all-done.2.w0, ...), custom_call_target="tpu_custom_call" | custom-call | flops 12884901888 | bytes 21102596 | tf_op jit(solution)/shard_map/pallas_call | solution.py:42
  573.2 58.0 %shard_map.234.refs_1_ = bf16[8,256,1024]{2,1,0:T(8,128)(2,1)} custom-call(bf16[8,256,1024]{2,1,0:T(8,128)(2,1)} %shard_map.233.refs_0_), custom_call_target="tpu_custom_call" | custom-call | bytes 167772160 | tf_op jit(solution)/shard_map/pallas_call | solution.py:116
  631.3 7.0 shard_map.235
  638.3 6.3 all-to-all-start.5
  645.6 25.6 %all-to-all-done.5.x_ref = bf16[8,256,256]{2,1,0:T(8,128)(2,1)S(1)} async-done(((bf16[8,256,256]{2,1,0:T(8,128)(2,1)}), bf16[8,256,256]{2,1,0:T(8,128)(2,1)S(1)}, u32[]{:S(2)}, u32[]{:S(2)}) %all-to-all-start.5) | async-done | bytes 1048608 | tf_op jit(solution)/shard_map/all_to_all | solution.py:783
  672.2 9.7 shard_map.236
  681.9 19.5 %all_to_all.106.m_ref = bf16[8,256,128]{2,1,0:T(8,128)(2,1)} all-to-all(bf16[8,256,128]{2,1,0:T(8,128)(2,1)} %get-tuple-element.75.o_ref), channel_id=1, replica_groups=mesh['grp'=4,'zq'=2,'zp'=2,'core'=2] {'zq','zp','core'}, dimensions={0} | all-to-all | bytes 1048576 | tf_op jit(solution)/shard_map/all_to_all | solution.py:785
  705.5 57.8 %shard_map.238 = (bf16[8,256,1024]{2,1,0:T(8,128)(2,1)}, f32[8,8,256]{2,1,0:T(8,128)}) custom-call(bf16[256,1024]{1,0:T(8,128)(2,1)} %get-tuple-element.79.refs_0_.nm_ref, f32[8,8,256]{2,1,0:T(8,128)} %get-tuple-element.80.refs_1_.gt_ref), custom_call_target="tpu_custom_call" | custom-call | bytes 170393600 | tf_op jit(solution)/shard_map/pallas_call | solution.py:116
  763.4 72.8 %shard_map.239 = (bf16[8,256,1024]{2,1,0:T(8,128)(2,1)}, f32[8,8,256]{2,1,0:T(8,128)}, bf16[8,2,128,512]{3,2,1,0:T(8,128)(2,1)}, bf16[8,2,128,512]{3,2,1,0:T(8,1...) custom-call(s32[1]{0:T(128)} %bitcast.8.core_ref, ...), custom_call_target="tpu_custom_call" | custom-call | flops 33822867456 | bytes 42139652 | tf_op jit(solution)/shard_map/pallas_call | solution.py:42
  836.2 57.2 %shard_map.240 = (bf16[8,256,1024]{2,1,0:T(8,128)(2,1)}, f32[8,8,256]{2,1,0:T(8,128)}) custom-call(bf16[8,256,1024]{2,1,0:T(8,128)(2,1)} %get-tuple-element.84.refs_0_, f32[8,8,256]{2,1,0:T(8,128)} %get-tuple-element.85.refs_1_), custom_call_target="tpu_custom_call" | custom-call | bytes 170393600 | tf_op jit(solution)/shard_map/pallas_call | solution.py:116
  894.1 7.5 shard_map.241
  901.6 20.9 %all_to_all.107.d_ref = bf16[8,256,128]{2,1,0:T(8,128)(2,1)} all-to-all(bf16[8,256,128]{2,1,0:T(8,128)(2,1)} %get-tuple-element.88), channel_id=1, replica_groups=mesh['grp'=4,'zq'=2,'zp'=2,'core'=2] {'zq','zp','core'}, dimensions={0} | all-to-all | bytes 1048576 | tf_op jit(solution)/shard_map/all_to_all | solution.py:834
  922.5 13.3 shard_map.242
  935.9 30.8 %all_to_all.108.d_ref = bf16[8,256,256]{2,1,0:T(8,128)(2,1)} all-to-all(bf16[8,256,256]{2,1,0:T(8,128)(2,1)} %shard_map.242), channel_id=1, replica_groups=mesh['grp'=4,'zq'=2,'zp'=2,'core'=2] {'zq','zp','core'}, dimensions={0} | all-to-all | bytes 2097152 | tf_op jit(solution)/shard_map/all_to_all | solution.py:836
  966.7 8.4 shard_map.243
  977.2 56.9 %shard_map.244.gr_ref = bf16[8,256,1024]{2,1,0:T(8,128)(2,1)} custom-call(bf16[256,1024]{1,0:T(8,128)(2,1)} %convert_element_type.130.refs_0_), custom_call_target="tpu_custom_call" | custom-call | bytes 167772160 | tf_op jit(solution)/shard_map/pallas_call | solution.py:116
  1034.2 61.1 %shard_map.245 = (bf16[8,256,1024]{2,1,0:T(8,128)(2,1)}, f32[8,8,256]{2,1,0:T(8,128)}, bf16[8,2,128,512]{3,2,1,0:T(8,128)(2,1)}, bf16[8,2,128,512]{3,2,1,0:T(8,1...) custom-call(s32[1]{0:T(128)} %bitcast.8.core_ref, ...), custom_call_target="tpu_custom_call" | custom-call | flops 33822867456 | bytes 37945348 | tf_op jit(solution)/shard_map/pallas_call | solution.py:42
  1095.3 57.1 %shard_map.246 = (bf16[8,256,1024]{2,1,0:T(8,128)(2,1)}, f32[8,8,256]{2,1,0:T(8,128)}) custom-call(bf16[8,256,1024]{2,1,0:T(8,128)(2,1)} %get-tuple-element.92.refs_0_, f32[8,8,256]{2,1,0:T(8,128)} %get-tuple-element.93.refs_1_), custom_call_target="tpu_custom_call" | custom-call | bytes 170393600 | tf_op jit(solution)/shard_map/pallas_call | solution.py:116
  1152.4 7.7 shard_map.247
  1160.1 5.5 all-to-all-start.13
  1166.1 14.9 all-to-all-done.13.d_ref
  1181.7 13.3 shard_map.248
  1202.4 22.9 %all-to-all-done.14.d_ref = bf16[8,256,256]{2,1,0:T(8,128)(2,1)S(1)} async-done(((bf16[8,256,256]{2,1,0:T(8,128)(2,1)}), bf16[8,256,256]{2,1,0:T(8,128)(2,1)S(1)}, u32[]{:S(2)}, u32[]{:S(2)}) %all-to-all-start.14) | async-done | bytes 1048608 | tf_op jit(solution)/shard_map/all_to_all | solution.py:836
  1238.1 40.8 %all-to-all-done.16 = bf16[8,2,128,512]{3,2,1,0:T(8,128)(2,1)S(1)} async-done(((bf16[8,2,128,512]{3,2,1,0:T(8,128)(2,1)}), bf16[8,2,128,512]{3,2,1,0:T(8,128)(2,1)S(1)}, u32[]{:S(2)}, u32[]{:S(2)}) %all-to-all-start.16) | async-done | bytes 2097184 | tf_op jit(solution)/shard_map/all_to_all | solution.py:820
  1291.9 40.5 %all-to-all-done.18 = bf16[8,2,128,512]{3,2,1,0:T(8,128)(2,1)} async-done(((bf16[8,2,128,512]{3,2,1,0:T(8,128)(2,1)}), bf16[8,2,128,512]{3,2,1,0:T(8,128)(2,1)}, u32[]{:S(2)}, u32[]{:S(2)}) %all-to-all-start.18) | async-done | bytes 2097184 | tf_op jit(solution)/shard_map/all_to_all | solution.py:820
  1337.9 47.9 %all-to-all-done.20 = bf16[8,2,64,1024]{3,2,1,0:T(8,128)(2,1)} async-done(((bf16[8,2,64,1024]{3,2,1,0:T(8,128)(2,1)}), bf16[8,2,64,1024]{3,2,1,0:T(8,128)(2,1)}, u32[]{:S(2)}, u32[]{:S(2)}) %all-to-all-start.20) | async-done | bytes 2097184 | tf_op jit(solution)/shard_map/all_to_all | solution.py:820
  1385.8 5.2 all-to-all-start.10
  1399.7 49.2 %all-to-all-done.10 = bf16[8,256,1024]{2,1,0:T(8,128)(2,1)} async-done(((bf16[8,256,1024]{2,1,0:T(8,128)(2,1)}), bf16[8,256,1024]{2,1,0:T(8,128)(2,1)}, u32[]{:S(2)}, u32[]{:S(2)}) %all-to-all-start.10) | async-done | bytes 4194336 | tf_op jit(solution)/shard_map/all_to_all | solution.py:823
  1448.9 6.5 all-to-all-start.15
  1463.7 42.4 %all-to-all-done.15 = bf16[8,2,128,512]{3,2,1,0:T(8,128)(2,1)} async-done(((bf16[8,2,128,512]{3,2,1,0:T(8,128)(2,1)}), bf16[8,2,128,512]{3,2,1,0:T(8,128)(2,1)}, u32[]{:S(2)}, u32[]{:S(2)}) %all-to-all-start.15) | async-done | bytes 2097184 | tf_op jit(solution)/shard_map/all_to_all | solution.py:820
  1510.5 8.4 shard_map.249
  1527.3 39.2 %all-to-all-done.17 = bf16[8,2,128,512]{3,2,1,0:T(8,128)(2,1)} async-done(((bf16[8,2,128,512]{3,2,1,0:T(8,128)(2,1)}), bf16[8,2,128,512]{3,2,1,0:T(8,128)(2,1)}, u32[]{:S(2)}, u32[]{:S(2)}) %all-to-all-start.17) | async-done | bytes 2097184 | tf_op jit(solution)/shard_map/all_to_all | solution.py:820
  1572.8 77.7 %all-reduce.1 = f32[1024]{0:T(1024)S(1)} all-reduce(f32[1024]{0:T(1024)S(1)} %bitcast.142), channel_id=2, replica_groups=mesh['grp'=4,'zq'=2,'zp'=2,'core'=2] {'grp','zq','zp','core'}, use_global_device_ids=true, to_apply=%region_4.5.clone | all-reduce | flops 1024 | bytes 8192
  1685.4 60.2 %reduce-scatter.9.cloned.1.call-done = bf16[32,2048]{1,0:T(8,128)(2,1)} async-done(((bf16[1024,2048]{1,0:T(8,128)(2,1)}), bf16[32,2048]{1,0:T(8,128)(2,1)}) %reduce-scatter.9.cloned.1.call-update) | async-done | bytes 131088 | tf_op jit(solution)/shard_map/reduce_scatter | solution.py:841
  1746.9 140.4 %reduce-scatter.7.cloned.1.call-done = bf16[32,2048]{1,0:T(8,128)(2,1)} async-done(((bf16[1024,2048]{1,0:T(8,128)(2,1)}), bf16[32,2048]{1,0:T(8,128)(2,1)}) %reduce-scatter.7.cloned.1.call-update) | async-done | bytes 131088 | tf_op jit(solution)/shard_map/reduce_scatter | solution.py:841
  (190 shorter events, 177.6 us)
Async XLA Ops:
  7.2 7.1 copy-start.10
  7.2 218.9 %all-gather.4.cloned.1.call-start = ((), (), s32[]{:S(2)}) async-start(), calls=%async_computation.25 | async-start | bytes 6758400 | tf_op jit(solution)/shard_map/all_gather | solution.py:718
  16.0 70.4 %all-to-all-start.2 = ((bf16[8,2,128,512]{3,2,1,0:T(8,128)(2,1)}), bf16[8,2,128,512]{3,2,1,0:T(8,128)(2,1)}, u32[]{:S(2)}, u32[]{:S(2)}) async-start(bf16[8,2,128,512]{3,2,1,0:T(8,128)(2,1)} %bitcast.11), calls=%async_computation.2 | async-start | bytes 4194304 | tf_op jit(solution)/shard_map/all_to_all | solution.py:731
  87.9 60.4 %all-to-all-start.3 = ((bf16[8,2,128,512]{3,2,1,0:T(8,128)(2,1)}), bf16[8,2,128,512]{3,2,1,0:T(8,128)(2,1)}, u32[]{:S(2)}, u32[]{:S(2)}) async-start(bf16[8,2,128,512]{3,2,1,0:T(8,128)(2,1)} %bitcast.13), calls=%async_computation.3 | async-start | bytes 4194304 | tf_op jit(solution)/shard_map/all_to_all | solution.py:731
  151.1 66.6 %all-to-all-start.4 = ((bf16[8,2,64,1024]{3,2,1,0:T(8,128)(2,1)}), bf16[8,2,64,1024]{3,2,1,0:T(8,128)(2,1)}, u32[]{:S(2)}, u32[]{:S(2)}) async-start(bf16[8,2,64,1024]{3,2,1,0:T(8,128)(2,1)} %bitcast.15), calls=%async_computation.4 | async-start | bytes 4194304 | tf_op jit(solution)/shard_map/all_to_all | solution.py:731
  155.4 475.8 %all-gather.6.cloned.1.call-start = ((), (), s32[]{:S(2)}) async-start(), calls=%async_computation.26 | async-start | bytes 6758400 | tf_op jit(solution)/shard_map/all_gather | solution.py:718
  219.2 4.5 copy-start.13
  219.2 62.6 %all-to-all-start.7 = ((bf16[8,2,128,512]{3,2,1,0:T(8,128)(2,1)}), bf16[8,2,128,512]{3,2,1,0:T(8,128)(2,1)}, u32[]{:S(2)}, u32[]{:S(2)}) async-start(bf16[8,2,128,512]{3,2,1,0:T(8,128)(2,1)} %bitcast.22), calls=%async_computation.7 | async-start | bytes 4194304 | tf_op jit(solution)/shard_map/all_to_all | solution.py:731
  314.1 52.6 %all-to-all-start.8 = ((bf16[8,2,128,512]{3,2,1,0:T(8,128)(2,1)}), bf16[8,2,128,512]{3,2,1,0:T(8,128)(2,1)S(1)}, u32[]{:S(2)}, u32[]{:S(2)}) async-start(bf16[8,2,128,512]{3,2,1,0:T(8,128)(2,1)} %bitcast.24), calls=%async_computation.8 | async-start | bytes 4194304 | tf_op jit(solution)/shard_map/all_to_all | solution.py:731
  366.7 1.3 copy-start.11
  368.1 18.9 all-to-all-start.1
  371.6 391.8 %all-gather.8.cloned.1.call-start = ((), (), s32[]{:S(2)}) async-start(), calls=%async_computation.27 | async-start | bytes 4718592 | tf_op jit(solution)/shard_map/all_gather | solution.py:773
  386.9 1.6 copy-start.5
  388.5 6.0 copy-start.14
  388.6 249.7 %all-to-all-start.9 = ((bf16[8,2,64,1024]{3,2,1,0:T(8,128)(2,1)}), bf16[8,2,64,1024]{3,2,1,0:T(8,128)(2,1)}, u32[]{:S(2)}, u32[]{:S(2)}) async-start(bf16[8,2,64,1024]{3,2,1,0:T(8,128)(2,1)} %bitcast.26), calls=%async_computation.9 | async-start | bytes 4194304 | tf_op jit(solution)/shard_map/all_to_all | solution.py:731
  393.5 146.7 %collective-permute-start = (bf16[8,2,128,512]{3,2,1,0:T(8,128)(2,1)}, bf16[8,2,128,512]{3,2,1,0:T(8,128)(2,1)S(1)}, u32[]{:S(2)}, u32[]{:S(2)}) collective-permute-start(bf16[8,2,128,512]{3,2,1,0:T(8,128)(2,1)} %all-to-all-done.2.w0), channel_id=1, source_target_pairs={{0,1},{1,0},{2,3},{3,2},{4,5},{5,4},{6,7},{7,6},{8,9},{9,8},{10,11... | collective-permute-start | bytes 6291464 | tf_op jit(solution)/shard_map/ppermute | solution.py:726
  394.0 146.2 %collective-permute-start.1 = (bf16[8,2,128,512]{3,2,1,0:T(8,128)(2,1)}, bf16[8,2,128,512]{3,2,1,0:T(8,128)(2,1)}, u32[]{:S(2)}, u32[]{:S(2)}) collective-permute-start(bf16[8,2,128,512]{3,2,1,0:T(8,128)(2,1)} %all-to-all-done.3.w2), channel_id=1, source_target_pairs={{0,1},{1,0},{2,3},{3,2},{4,5},{5,4},{6,7},{7,6},{8,9},{9,8},{10,11... | collective-permute-start | bytes 6291464 | tf_op jit(solution)/shard_map/ppermute | solution.py:726
  394.1 146.1 %collective-permute-start.2 = (bf16[8,2,64,1024]{3,2,1,0:T(8,128)(2,1)}, bf16[8,2,64,1024]{3,2,1,0:T(8,128)(2,1)}, u32[]{:S(2)}, u32[]{:S(2)}) collective-permute-start(bf16[8,2,64,1024]{3,2,1,0:T(8,128)(2,1)} %all-to-all-done.4.w4), channel_id=1, source_target_pairs={{0,1},{1,0},{2,3},{3,2},{4,5},{5,4},{6,7},{7,6},{8,9},{9,8},{10,11... | collective-permute-start | bytes 6291464 | tf_op jit(solution)/shard_map/ppermute | solution.py:726
  638.3 6.8 copy-start.12
  638.3 32.9 %all-to-all-start.5 = ((bf16[8,256,256]{2,1,0:T(8,128)(2,1)}), bf16[8,256,256]{2,1,0:T(8,128)(2,1)S(1)}, u32[]{:S(2)}, u32[]{:S(2)}) async-start(bf16[8,256,256]{2,1,0:T(8,128)(2,1)} %get-tuple-element.74), calls=%async_computation.5 | async-start | bytes 2097152 | tf_op jit(solution)/shard_map/all_to_all | solution.py:783
  644.6 118.7 %collective-permute-start.3 = (bf16[8,2,128,512]{3,2,1,0:T(8,128)(2,1)}, bf16[8,2,128,512]{3,2,1,0:T(8,128)(2,1)}, u32[]{:S(2)}, u32[]{:S(2)}) collective-permute-start(bf16[8,2,128,512]{3,2,1,0:T(8,128)(2,1)} %all-to-all-done.7.w0), channel_id=1, source_target_pairs={{0,1},{1,0},{2,3},{3,2},{4,5},{5,4},{6,7},{7,6},{8,9},{9,8},{10,11... | collective-permute-start | bytes 6291464 | tf_op jit(solution)/shard_map/ppermute | solution.py:726
  645.1 118.2 %collective-permute-start.4 = (bf16[8,2,128,512]{3,2,1,0:T(8,128)(2,1)S(1)}, bf16[8,2,128,512]{3,2,1,0:T(8,128)(2,1)}, u32[]{:S(2)}, u32[]{:S(2)}) collective-permute-start(bf16[8,2,128,512]{3,2,1,0:T(8,128)(2,1)S(1)} %copy-done.12), channel_id=1, source_target_pairs={{0,1},{1,0},{2,3},{3,2},{4,5},{5,4},{6,7},{7,6},{8,9},{9,8},{10,11... | collective-permute-start | bytes 6291464 | tf_op jit(solution)/shard_map/ppermute | solution.py:726
  645.2 118.2 %collective-permute-start.5 = (bf16[8,2,64,1024]{3,2,1,0:T(8,128)(2,1)}, bf16[8,2,64,1024]{3,2,1,0:T(8,128)(2,1)}, u32[]{:S(2)}, u32[]{:S(2)}) collective-permute-start(bf16[8,2,64,1024]{3,2,1,0:T(8,128)(2,1)} %all-to-all-done.9.w4), channel_id=1, source_target_pairs={{0,1},{1,0},{2,3},{3,2},{4,5},{5,4},{6,7},{7,6},{8,9},{9,8},{10,11... | collective-permute-start | bytes 6291464 | tf_op jit(solution)/shard_map/ppermute | solution.py:726
  1160.1 20.8 %all-to-all-start.13 = ((bf16[8,256,128]{2,1,0:T(8,128)(2,1)}), bf16[8,256,128]{2,1,0:T(8,128)(2,1)S(1)}, u32[]{:S(2)}, u32[]{:S(2)}) async-start(bf16[8,256,128]{2,1,0:T(8,128)(2,1)} %get-tuple-element.97), calls=%async_computation.13 | async-start | bytes 1048576 | tf_op jit(solution)/shard_map/all_to_all | solution.py:834
  1165.6 33.2 %collective-permute-start.7 = (bf16[8,2,128,512]{3,2,1,0:T(8,128)(2,1)}, bf16[8,2,128,512]{3,2,1,0:T(8,128)(2,1)}, u32[]{:S(2)}, u32[]{:S(2)}) collective-permute-start(bf16[8,2,128,512]{3,2,1,0:T(8,128)(2,1)} %get-tuple-element.109), channel_id=1, source_target_pairs={{0,1},{1,0},{2,3},{3,2},{4,5},{5,4},{6,7},{7,6},{8,9},{9,8},{10,11... | collective-permute-start | bytes 6291464 | tf_op jit(solution)/shard_map/ppermute | solution.py:726
  1195.1 3.7 copy-start.8
  1195.1 30.2 %all-to-all-start.14 = ((bf16[8,256,256]{2,1,0:T(8,128)(2,1)}), bf16[8,256,256]{2,1,0:T(8,128)(2,1)S(1)}, u32[]{:S(2)}, u32[]{:S(2)}) async-start(bf16[8,256,256]{2,1,0:T(8,128)(2,1)} %shard_map.248), calls=%async_computation.14 | async-start | bytes 2097152 | tf_op jit(solution)/shard_map/all_to_all | solution.py:836
  1226.3 52.6 %all-to-all-start.16 = ((bf16[8,2,128,512]{3,2,1,0:T(8,128)(2,1)}), bf16[8,2,128,512]{3,2,1,0:T(8,128)(2,1)S(1)}, u32[]{:S(2)}, u32[]{:S(2)}) async-start(bf16[8,2,128,512]{3,2,1,0:T(8,128)(2,1)} %add_convert_fusion.4), calls=%async_computation.20 | async-start | bytes 4194304 | tf_op jit(solution)/shard_map/all_to_all | solution.py:820
  1229.9 4.6 collective-permute-start.9
  1278.9 53.4 %all-to-all-start.18 = ((bf16[8,2,128,512]{3,2,1,0:T(8,128)(2,1)}), bf16[8,2,128,512]{3,2,1,0:T(8,128)(2,1)}, u32[]{:S(2)}, u32[]{:S(2)}) async-start(bf16[8,2,128,512]{3,2,1,0:T(8,128)(2,1)} %add_convert_fusion.2), calls=%async_computation.22 | async-start | bytes 4194304 | tf_op jit(solution)/shard_map/all_to_all | solution.py:820
  1283.3 4.6 collective-permute-start.11
  1332.4 53.4 %all-to-all-start.20 = ((bf16[8,2,64,1024]{3,2,1,0:T(8,128)(2,1)}), bf16[8,2,64,1024]{3,2,1,0:T(8,128)(2,1)}, u32[]{:S(2)}, u32[]{:S(2)}) async-start(bf16[8,2,64,1024]{3,2,1,0:T(8,128)(2,1)} %add_convert_fusion), calls=%async_computation.24 | async-start | bytes 4194304 | tf_op jit(solution)/shard_map/all_to_all | solution.py:820
  1336.7 234.2 %reduce-scatter.11.cloned.1.call-start = ((), (), s32[]{:S(2)}) async-start(), calls=%async_computation.31 | async-start | bytes 2433024 | tf_op jit(solution)/shard_map/reduce_scatter | solution.py:840
  1337.3 320.8 %reduce-scatter.5.cloned.1.call-start = ((), (), s32[]{:S(2)}) async-start(), calls=%async_computation.28 | async-start | bytes 2433024 | tf_op jit(solution)/shard_map/reduce_scatter | solution.py:840
  1385.8 63.1 %all-to-all-start.10 = ((bf16[8,256,1024]{2,1,0:T(8,128)(2,1)}), bf16[8,256,1024]{2,1,0:T(8,128)(2,1)}, u32[]{:S(2)}, u32[]{:S(2)}) async-start(bf16[8,256,1024]{2,1,0:T(8,128)(2,1)} %get-tuple-element.83), calls=%async_computation.10 | async-start | bytes 8388608 | tf_op jit(solution)/shard_map/all_to_all | solution.py:823
  1391.0 354.6 %reduce-scatter.9.cloned.1.call-start = ((), (), s32[]{:S(2)}) async-start(), calls=%async_computation.30 | async-start | bytes 4325376 | tf_op jit(solution)/shard_map/reduce_scatter | solution.py:841
  1391.6 4.4 collective-permute-start.6
  1448.9 57.3 %all-to-all-start.15 = ((bf16[8,2,128,512]{3,2,1,0:T(8,128)(2,1)}), bf16[8,2,128,512]{3,2,1,0:T(8,128)(2,1)}, u32[]{:S(2)}, u32[]{:S(2)}) async-start(bf16[8,2,128,512]{3,2,1,0:T(8,128)(2,1)} %add_convert_fusion.5), calls=%async_computation.19 | async-start | bytes 4194304 | tf_op jit(solution)/shard_map/all_to_all | solution.py:820
  1455.4 4.7 collective-permute-start.8
  1506.1 60.4 %all-to-all-start.17 = ((bf16[8,2,128,512]{3,2,1,0:T(8,128)(2,1)}), bf16[8,2,128,512]{3,2,1,0:T(8,128)(2,1)}, u32[]{:S(2)}, u32[]{:S(2)}) async-start(bf16[8,2,128,512]{3,2,1,0:T(8,128)(2,1)} %add_convert_fusion.3), calls=%async_computation.21 | async-start | bytes 4194304 | tf_op jit(solution)/shard_map/all_to_all | solution.py:820
  1510.5 376.8 %reduce-scatter.7.cloned.1.call-start = ((), (), s32[]{:S(2)}) async-start(), calls=%async_computation.29 | async-start | bytes 4325376 | tf_op jit(solution)/shard_map/reduce_scatter | solution.py:841
  1518.9 4.5 collective-permute-start.10
  1566.5 107.3 %all-to-all-start.19 = ((bf16[8,2,64,1024]{3,2,1,0:T(8,128)(2,1)}), bf16[8,2,64,1024]{3,2,1,0:T(8,128)(2,1)}, u32[]{:S(2)}, u32[]{:S(2)}) async-start(bf16[8,2,64,1024]{3,2,1,0:T(8,128)(2,1)} %add_convert_fusion.1), calls=%async_computation.23 | async-start | bytes 4194304 | tf_op jit(solution)/shard_map/all_to_all | solution.py:820
  1662.6 3.2 copy-start.6
  1673.8 2.4 copy-start.2
  1673.8 2.9 copy-start.4
  1676.7 2.8 copy-start.1
  1676.7 3.6 copy-start.3
  (4 other events, 4.2 us)
Sparse Core Ops, SparseCore 0:
  14.4 98.2 all-gather.3
  159.1 88.0 all-gather.5
  373.9 170.8 all-gather.7
  1343.1 132.1 reduce-scatter.10
  1481.9 117.7 reduce-scatter.4
  1601.8 143.7 reduce-scatter.8
  1747.9 139.3 reduce-scatter.6

commit v2 on v1

--- a/solution.py
+++ b/solution.py
@@ -24,7 +24,7 @@
 BF = jnp.bfloat16
 F32 = jnp.float32
 MESH = pl.DeviceIdType.MESH
-VMEM_BYTES = 60 * 1024 * 1024
+VMEM_BYTES = 58 * 1024 * 1024
 
 
 def dot(a, b, ca=1, cb=0):
@@ -60,74 +60,215 @@
     return pl.BlockSpec(tuple(shape), lambda *_: (0,) * n)
 
 
-def exchange(ops, cid, grp_size):
-    n = grp_size * 2
+def size_of(group, sizes):
+    grp_size, ctx, planes = sizes
+    return {"g": grp_size, "tok": planes, "line": ctx, "z": ctx // 2, "sib": 2}[group]
+
+
+def place_in(group, sizes):
+    planes = sizes[2]
+    n = size_of(group, sizes)
+    zp = lax.axis_index("zp")
+    zz = lax.axis_index("zq") * planes + zp
+    core = lax.axis_index("core")
+    if group == "g":
+        return n, lax.axis_index("grp"), lambda p: {"grp": p}
+    if group == "tok":
+        return n, zp, lambda p: {"zp": p}
+    if group == "line":
+        return (
+            n,
+            zz * 2 + core,
+            lambda p: {
+                "zq": p // (2 * planes),
+                "zp": lax.rem(p // 2, planes),
+                "core": lax.rem(p, 2),
+            },
+        )
+    if group == "z":
+        return n, zz, lambda p: {"zq": p // planes, "zp": lax.rem(p, planes)}
+    return n, core, lambda p: {"core": p}
+
+
+def transfer(ops, cid, sizes):
+    grp_size, ctx, _ = sizes
+    groups = []
+    for _, group, what in ops:
+        for name in ("z", "g", "sib") if what == "packed" else (group,):
+            if name not in groups:
+                groups.append(name)
+    shapes = []
+    sems = []
+    total_sems = 0
+    for x, group, what in ops:
+        sems.append(total_sems)
+        if what == "packed":
+            shapes.append(sds((grp_size, ctx) + x.shape, x.dtype))
+            zs = ctx // 2
+            total_sems += zs + zs * grp_size * 2
+            continue
+        n = size_of(group, sizes)
+        total_sems += n
+        rest = {"all": (n,) + x.shape, "own": x.shape, "pick": (n,) + x.shape[1:]}
+        shapes.append(sds(rest[what], x.dtype))
     count = len(ops)
-    modes = [mode for _, mode in ops]
 
     def kernel(*refs):
         ins = refs[:count]
-        outs = refs[count : 2 * count]
-        send, recv, local = refs[2 * count :]
-        me = lax.axis_index("grp") * 2 + lax.axis_index("zp")
+        outs = refs[count : count + len(shapes)]
+        send, recv, local = refs[count + len(shapes) :]
         barrier = pltpu.get_barrier_semaphore()
-
-        def where(k):
-            peer = lax.rem(me + k, n)
-            return peer, {"grp": peer // 2, "zp": lax.rem(peer, 2)}
-
-        for k in range(1, n):
-            _, place = where(k)
-            pl.semaphore_signal(barrier, inc=1, device_id=place, device_id_type=MESH)
-        pl.semaphore_wait(barrier, n - 1)
-        copies = []
-        for k in range(1, n):
-            peer, place = where(k)
-            for i in range(count):
-                src = ins[i] if modes[i] == "gather" else ins[i].at[peer]
-                copy = pltpu.make_async_remote_copy(
-                    src_ref=src,
-                    dst_ref=outs[i].at[me],
-                    send_sem=send.at[i, k],
-                    recv_sem=recv.at[i, k],
-                    device_id=place,
-                    device_id_type=MESH,
+        total = 0
+        for group in groups:
+            n, me, where = place_in(group, sizes)
+            for k in range(1, n):
+                pl.semaphore_signal(
+                    barrier, inc=1, device_id=where(lax.rem(me + k, n)), device_id_type=MESH
                 )
+            total += n - 1
+        pl.semaphore_wait(barrier, total)
+
+        def remote(src, dst, at, place):
+            copy = pltpu.make_async_remote_copy(
+                src_ref=src,
+                dst_ref=dst,
+                send_sem=send.at[at],
+                recv_sem=recv.at[at],
+                device_id=place,
+                device_id_type=MESH,
+            )
+            copy.start()
+            return copy
+
+        sib_place = {"core": 1 - lax.axis_index("core")}
+        sent = []
+        todo = []
+        own_copies = []
+
+        def start(i):
+            _, group, what = ops[i]
+            n, me, where = place_in(group or "g", sizes)
+            out = outs[i]
+            if what == "packed":
+                grp = lax.axis_index("grp")
+                core = lax.axis_index("core")
+                zs, zz, z_place = place_in("z", sizes)
+                copy = pltpu.make_async_copy(ins[i], out.at[grp, zz * 2 + core], local.at[i])
                 copy.start()
-                copies.append(copy)
-        own = []
+                along = []
+                for k in range(1, zs):
+                    along.append(
+                        remote(
+                            ins[i],
+                            out.at[grp, zz * 2 + core],
+                            sems[i] + k,
+                            z_place(lax.rem(zz + k, zs)),
+                        )
+                    )
+                return (i, along, copy)
+            copies = []
+            for k in range(1, n):
+                peer = lax.rem(me + k, n)
+                if what == "all":
+                    src = ins[i]
+                elif what == "own":
+                    src = ins[i].at[peer]
+                else:
+                    src = ins[i].at[lax.rem(peer, ins[i].shape[0])]
+                copies.append(remote(src, out.at[me], sems[i] + k, where(peer)))
+            if what == "all":
+                src = ins[i]
+            elif what == "own":
+                src = ins[i].at[me]
+            else:
+                src = ins[i].at[lax.rem(me, ins[i].shape[0])]
+            copy = pltpu.make_async_copy(src, out.at[me], local.at[i])
+            copy.start()
+            own_copies.append(copy)
+            sent.extend(copies)
+            return None
+
+        def finish_packed(i, along, own):
+            grp = lax.axis_index("grp")
+            core = lax.axis_index("core")
+            zs, zz, _ = place_in("z", sizes)
+            out = outs[i]
+            base = sems[i] + zs
+            over = []
+
+            def spread(j, at):
+                for m in range(1, grp_size):
+                    over.append(
+                        (
+                            remote(
+                                out.at[at[0], at[1]],
+                                out.at[at[0], at[1]],
+                                base + j * grp_size + m,
+                                {"grp": lax.rem(grp + m, grp_size)},
+                            ),
+                            j,
+                            m,
+                        )
+                    )
+
+            def to_core(j, m, at):
+                sent.append(
+                    remote(
+                        out.at[at[0], at[1]],
+                        out.at[at[0], at[1]],
+                        base + zs * grp_size + j * grp_size + m,
+                        sib_place,
+                    )
+                )
+
+            own.wait()
+            for j in range(zs):
+                if j > 0:
+                    along[j - 1].wait_recv()
+                at = (grp, lax.rem(zz - j + zs, zs) * 2 + core)
+                spread(j, at)
+                to_core(j, 0, at)
+            for copy, j, m in over:
+                copy.wait_recv()
+                at = (
+                    lax.rem(grp - m + grp_size, grp_size),
+                    lax.rem(zz - j + zs, zs) * 2 + core,
+                )
+                to_core(j, m, at)
+            for copy in along:
+                copy.wait_send()
+            for copy, _, _ in over:
+                copy.wait_send()
+
+        pending = []
         for i in range(count):
-            src = ins[i] if modes[i] == "gather" else ins[i].at[me]
-            copy = pltpu.make_async_copy(src, outs[i].at[me], local.at[i])
-            copy.start()
-            own.append(copy)
-        for copy in own:
+            got = start(i)
+            if got is not None:
+                pending.append(got)
+        for item in pending:
+            finish_packed(*item)
+        for copy in own_copies:
             copy.wait()
-        for copy in copies:
+        for copy in sent:
             copy.wait()
 
-    shapes = []
-    total = 0
-    for x, mode in ops:
-        shape = (n,) + x.shape if mode == "gather" else x.shape
-        shapes.append(sds(shape, x.dtype))
-        total += math.prod(shape) * x.dtype.itemsize
+    total = sum(math.prod(o.shape) * jnp.dtype(o.dtype).itemsize for o in shapes)
     any_spec = pl.BlockSpec(memory_space=pl.ANY)
     return pl.pallas_call(
         kernel,
         out_shape=tuple(shapes),
         in_specs=[any_spec] * count,
-        out_specs=tuple([any_spec] * count),
+        out_specs=tuple([any_spec] * len(shapes)),
         scratch_shapes=[
-            pltpu.SemaphoreType.DMA((count, n)),
-            pltpu.SemaphoreType.DMA((count, n)),
+            pltpu.SemaphoreType.DMA((total_sems,)),
+            pltpu.SemaphoreType.DMA((total_sems,)),
             pltpu.SemaphoreType.DMA((count,)),
         ],
         compiler_params=pltpu.CompilerParams(collective_id=cid, has_side_effects=True),
         cost_estimate=pl.CostEstimate(
             flops=0, bytes_accessed=40 * int(total), transcendentals=0
         ),
-    )(*[x for x, _ in ops])
+    )(*[x for x, _, _ in ops])
 
 
 def swap_halves(x):
@@ -328,11 +469,10 @@
         top = jnp.max(logits, axis=0, keepdims=True)
         p = jnp.where(named, jnp.exp(logits - top), 0.0)
         gates = p / jnp.sum(p, axis=0, keepdims=True)
-        gate_ref[...] = jnp.zeros(gate_ref.shape, F32)
         for j in range(n):
-            gate_ref[j, 0:held, :] = gates[held * j : held * (j + 1)]
-
-    outs = [sds((rows, D), F32), sds((rows, D), BF), sds((n, 8, rows), F32)]
+            gate_ref[j] = gates[held * j : held * (j + 1)]
+
+    outs = [sds((rows, D), F32), sds((rows, D), BF), sds((n, held, rows), F32)]
     return call(
         kernel,
         outs,
@@ -365,8 +505,8 @@
     tail = (256 * ctx + D) // 128
 
     def kernel(p_ref, dg_ref, gt_ref, g_ref, x_ref, nm_ref, m_ref, w_ref, t_ref, gain_ref, ex_ref, g1_ref, dm_ref, gw_ref):
-        gates_v = jnp.concatenate([gt_ref[j, 0:held, :] for j in range(n)], axis=0)
-        dgate_v = jnp.concatenate([dg_ref[j, 0:held, :] for j in range(n)], axis=0)
+        gates_v = jnp.concatenate([gt_ref[j] for j in range(n)], axis=0)
+        dgate_v = jnp.concatenate([dg_ref[j] for j in range(n)], axis=0)
         mean = jnp.sum(gates_v * dgate_v, axis=0, keepdims=True)
         d_logits = (gates_v * (dgate_v - mean)).astype(BF)
         d_logits = jnp.concatenate([d_logits, jnp.zeros((128 - E, rows), BF)], axis=0)
@@ -449,40 +589,23 @@
     return at == slot_row
 
 
-def weight_specs(half, ctx, buffers=2):
-    def own(e):
-        return (0, jnp.minimum(e, half - 1), 0, 0)
-
-    def other(e):
-        return (0, jnp.maximum(e - half, 0), 0, 0)
-
-    wide = (ctx, 1, D // ctx, F)
-    tall = (ctx, 1, F // ctx, D)
-    kinds = [(wide, own), (wide, other)] * 2 + [(tall, own), (tall, other)]
+def weight_specs(buffers):
     return [
-        pl.BlockSpec(shape, index, pipeline_mode=pl.Buffered(buffers))
-        for shape, index in kinds
+        pl.BlockSpec((1,) + shape, lambda e: (e, 0, 0), pipeline_mode=pl.Buffered(buffers))
+        for shape in ((D, F), (D, F), (F, D))
     ]
 
 
-def pick_weights(e, half, refs, shape):
-    own, other = refs
-    return jnp.where(e < half, own[...], other[...]).reshape(shape)
-
-
-def experts_forward(x, gates, slots, core, weights, ctx, held):
+def experts_forward(x, gates, slots, weights, held):
     n, rows, _ = x.shape
-    half = held // 2
     lanes = 2 * SLOTS
 
-    def kernel(core_ref, x_ref, g_ref, s_ref, w0, w1, w2, w3, w4, w5, out_ref, acc_ref, row_ref, eo_ref):
+
+    def kernel(x_ref, g_ref, s_ref, w0, w1, w2, out_ref, acc_ref, row_ref, eo_ref):
         e = pl.program_id(0)
-        at = lax.rem(e + core_ref[0] * half, held)
-        w_gate = pick_weights(e, half, (w0, w1), (D, F))
-        w_up = pick_weights(e, half, (w2, w3), (D, F))
-        w_down = pick_weights(e, half, (w4, w5), (F, D))
+        w_gate, w_up, w_down = w0[0], w1[0], w2[0]
         for s in range(n):
-            pick = pick_matrix(s_ref[s, pl.ds(at, 1), :], rows).astype(BF)
+            pick = pick_matrix(s_ref[s, pl.ds(e, 1), :], rows).astype(BF)
             row_ref[lanes * s : lanes * (s + 1), :] = dot(pick, x_ref[s]).astype(BF)
         rws = row_ref[...]
         ga = dot(rws, w_gate)
@@ -490,8 +613,8 @@
         hidden = (ga * jax.nn.sigmoid(ga) * up).astype(BF)
         eo_ref[...] = dot(hidden, w_down).astype(BF)
         for s in range(n):
-            pick = pick_matrix(s_ref[s, pl.ds(at, 1), :], rows)
-            gated = jnp.where(pick, g_ref[s, pl.ds(at, 1), :], 0.0).astype(BF)
+            pick = pick_matrix(s_ref[s, pl.ds(e, 1), :], rows)
+            gated = jnp.where(pick, g_ref[s, pl.ds(e, 1), :], 0.0).astype(BF)
             add = dot(gated, eo_ref[lanes * s : lanes * (s + 1), :], 0, 0)
 
             @pl.when(e == 0)
@@ -507,14 +630,12 @@
                 out_ref[s] = (acc_ref[s].astype(F32) + add).astype(BF)
 
     flops = 2 * held * n * (lanes * D * F * 3 + 2 * lanes * rows * D)
-    spec = pl.BlockSpec(memory_space=pltpu.SMEM)
     return call(
         kernel,
         [sds(x.shape, BF)],
-        [core, x, gates, slots] + list(weights),
+        [x, gates, slots] + list(weights),
         flops,
-        in_specs=[spec, full(x.shape), full(gates.shape), full(slots.shape)]
-        + weight_specs(half, ctx),
+        in_specs=[full(x.shape), full(gates.shape), full(slots.shape)] + weight_specs(2),
         out_specs=(full(x.shape),),
         grid=(held,),
         scratch=[
@@ -525,30 +646,28 @@
     )[0]
 
 
-def experts_backward(x, g, gates, slots, core, weights, ctx, held, with_out):
+def experts_backward(x, g, gates, slots, weights, held, with_out):
     n, rows, _ = x.shape
-    half = held // 2
     lanes = 2 * SLOTS
 
-    def kernel(core_ref, x_ref, gr_ref, g_ref, s_ref, w0, w1, w2, w3, w4, w5, *rest):
-        dx_ref, dg_ref, o0, o1, o2, o3, o4, o5 = rest[:8]
+
+    def kernel(x_ref, gr_ref, g_ref, s_ref, w0, w1, w2, *rest):
+        dx_ref, dg_ref = rest[:2]
+        grad_refs, rest = rest[2:5], rest[5:]
         if with_out:
-            out_ref, acc_ref, row_ref, grow_ref = rest[8:]
+            out_ref, acc_ref, row_ref, grow_ref = rest
         else:
-            acc_ref, row_ref, grow_ref = rest[8:]
+            acc_ref, row_ref, grow_ref = rest
         e = pl.program_id(0)
-        at = lax.rem(e + core_ref[0] * half, held)
-        w_gate = pick_weights(e, half, (w0, w1), (D, F))
-        w_up = pick_weights(e, half, (w2, w3), (D, F))
-        w_down = pick_weights(e, half, (w4, w5), (F, D))
+        w_gate, w_up, w_down = w0[0], w1[0], w2[0]
         slot_gates = []
         for s in range(n):
             mine = slice(lanes * s, lanes * (s + 1))
-            pick = pick_matrix(s_ref[s, pl.ds(at, 1), :], rows)
+            pick = pick_matrix(s_ref[s, pl.ds(e, 1), :], rows)
             low = pick.astype(BF)
             row_ref[mine, :] = dot(low, x_ref[s]).astype(BF)
             grow_ref[mine, :] = dot(low, gr_ref[s]).astype(BF)
-            gated = jnp.where(pick, g_ref[s, pl.ds(at, 1), :], 0.0)
+            gated = jnp.where(pick, g_ref[s, pl.ds(e, 1), :], 0.0)
             slot_gates.append(jnp.sum(gated, axis=1, keepdims=True))
         gate = jnp.concatenate(slot_gates, axis=0)
         rws = row_ref[...]
@@ -569,13 +688,13 @@
         drow = (dot(dga, w_gate, 1, 1) + dot(dup, w_up, 1, 1)).astype(BF)
         for s in range(n):
             mine = slice(lanes * s, lanes * (s + 1))
-            pick = pick_matrix(s_ref[s, pl.ds(at, 1), :], rows)
-            dg_ref[s, pl.ds(at, 1), :] = jnp.sum(
+            pick = pick_matrix(s_ref[s, pl.ds(e, 1), :], rows)
+            dg_ref[s, pl.ds(e, 1), :] = jnp.sum(
                 jnp.where(pick, d_gate[mine], 0.0), axis=0, keepdims=True
             )
             todo = [(acc_ref, dx_ref, dot(pick.astype(BF), drow[mine], 0, 0))]
             if with_out:
-                gated = jnp.where(pick, g_ref[s, pl.ds(at, 1), :], 0.0).astype(BF)
+                gated = jnp.where(pick, g_ref[s, pl.ds(e, 1), :], 0.0).astype(BF)
                 todo.append((out_ref, out_ref, dot(gated, eo[mine], 0, 0)))
             for held_ref, final_ref, add in todo:
 
@@ -592,26 +711,12 @@
                     final_ref[s] = (held_ref[s].astype(F32) + add).astype(BF)
 
         dslot = (grows.astype(F32) * gate).astype(BF)
-        g_gate = dot(rws, dga, 0, 0).astype(BF).reshape(ctx, 1, D // ctx, F)
-        g_up = dot(rws, dup, 0, 0).astype(BF).reshape(ctx, 1, D // ctx, F)
-        g_down = dot(hidden, dslot, 0, 0).astype(BF).reshape(ctx, 1, F // ctx, D)
-
-        @pl.when(e < half)
-        def _():
-            o0[...] = g_gate
-            o2[...] = g_up
-            o4[...] = g_down
-
-        @pl.when(e >= half)
-        def _():
-            o1[...] = g_gate
-            o3[...] = g_up
-            o5[...] = g_down
-
-    wide = sds((ctx, half, D // ctx, F), BF)
-    tall = sds((ctx, half, F // ctx, D), BF)
-    outs = [sds(x.shape, BF), sds(gates.shape, F32), wide, wide, wide, wide, tall, tall]
-    out_specs = [full(x.shape), full(gates.shape)] + weight_specs(half, ctx, 1)
+        grads = [dot(rws, dga, 0, 0), dot(rws, dup, 0, 0), dot(hidden, dslot, 0, 0)]
+        for ref, value in zip(grad_refs, grads):
+            ref[0] = value.astype(BF)
+
+    outs = [sds(x.shape, BF), sds(gates.shape, F32)] + [sds(w.shape, BF) for w in weights]
+    out_specs = [full(x.shape), full(gates.shape)] + weight_specs(2)
     scratch = [
         pltpu.VMEM(x.shape, F32),
         pltpu.VMEM((n * lanes, D), BF),
@@ -621,51 +726,21 @@
         outs.append(sds(x.shape, BF))
         out_specs.append(full(x.shape))
     flops = 2 * held * n * (lanes * D * F * 9 + 3 * lanes * rows * D)
-    spec = pl.BlockSpec(memory_space=pltpu.SMEM)
     return call(
         kernel,
         outs,
-        [core, x, g, gates, slots] + list(weights),
+        [x, g, gates, slots] + list(weights),
         flops,
-        in_specs=[spec, full(x.shape), full(g.shape), full(gates.shape), full(slots.shape)]
-        + weight_specs(half, ctx),
+        in_specs=[full(x.shape), full(g.shape), full(gates.shape), full(slots.shape)]
+        + weight_specs(2),
         out_specs=tuple(out_specs),
         grid=(held,),
         scratch=scratch,
     )
 
 
-def in_chunks(x, most):
-    size = max(1, most // x.shape[1])
-    return [slice(i, i + size) for i in range(0, x.shape[0], size)]
-
-
-def experts_forward_all(x, gates, slots, *rest):
-    outs = [
-        experts_forward(x[c], gates[c], slots[c], *rest) for c in in_chunks(x, 2048)
-    ]
-    return outs[0] if len(outs) == 1 else jnp.concatenate(outs)
-
-
-def experts_backward_all(x, g, gates, slots, *rest):
-    outs = [
-        experts_backward(x[c], g[c], gates[c], slots[c], *rest) for c in in_chunks(x, 2048)
-    ]
-    if len(outs) == 1:
-        return outs[0]
-    joined = []
-    for k in range(len(outs[0])):
-        parts = [o[k] for o in outs]
-        if k in (0, 1, 8):
-            joined.append(jnp.concatenate(parts))
-        else:
-            joined.append(sum(p.astype(F32) for p in parts).astype(BF))
-    return joined
-
-
 def per_device(
-    grp_size,
-    ctx,
+    sizes,
     hidden_in,
     grad_out,
     segments,
@@ -683,18 +758,21 @@
 ):
     micro, tok, _ = hidden_in.shape
     rows = micro * tok
-    length = ctx * tok
+    grp_size, ctx, planes = sizes
     hq = QUERY_HEADS // ctx
     dup = ctx // KEY_VALUE_HEADS
-    n = grp_size * 2
-    held = E // n
-    half = held // 2
+    held = 2 * grp_size
     every = ("grp", "zq", "zp", "core")
     line = ("zq", "zp", "core")
     core = lax.axis_index("core")
-    core_arr = core.astype(jnp.int32).reshape(1)
-    ctx_index = (lax.axis_index("zq") * 2 + lax.axis_index("zp")) * 2 + core
+    ctx_index = (lax.axis_index("zq") * planes + lax.axis_index("zp")) * 2 + core
     shard = w_query.shape[1]
+
+    def by_plane(x, axis, back=False):
+        dims = (planes, grp_size, 2) if back else (grp_size, planes, 2)
+        head, tail = x.shape[:axis], x.shape[axis + 1 :]
+        y = jnp.swapaxes(x.reshape(head + dims + tail), axis, axis + 1)
+        return y.reshape(x.shape)
 
     def pack(layer):
         wq = w_query[layer].reshape(shard, ctx, HS * hq)
@@ -705,7 +783,7 @@
         qkv = jnp.concatenate([wq, wk, wv], axis=2).reshape(shard, ctx * 256)
         tail = jnp.concatenate(
             [
-                w_router[layer],
+                by_plane(w_router[layer], 1),
                 attn_gain[layer][:, None],
                 ffn_gain[layer][:, None],
                 jnp.zeros((shard, 128 - E - 2), BF),
@@ -714,25 +792,26 @@
         )
         return jnp.concatenate([qkv, w_output[layer], tail], axis=1)
 
-    packed = [
-        lax.all_gather(pack(layer), every, axis=0, tiled=True) for layer in range(LAYERS)
-    ]
-
-    def to_holders(w):
-        quarter = w.reshape(4, half, w.shape[1], w.shape[2])
-        return jnp.tile(quarter, (ctx // 4, 1, 1, 1))
+    ids_of = iter(range(1, 100))
+
+    def move(*ops):
+        return transfer(ops, next(ids_of), sizes)
 
     def swap(x):
         return lax.ppermute(x, "core", [(0, 1), (1, 0)])
 
-    def fetch(layer):
-        out = []
-        for w in (w_gate[layer], w_up[layer], w_down[layer]):
-            own = lax.all_to_all(to_holders(w), line, 0, 0, tiled=True)
-            out += [own, swap(own)]
-        return out
-
-    weights = [fetch(layer) for layer in range(LAYERS)]
+    def picks(layer, members):
+        ws = (w_gate[layer], w_up[layer], w_down[layer])
+        return [(ws[k], "line", "pick") for k in members]
+
+    def plane_gather(w):
+        w = w.reshape(1, w.shape[0] * w.shape[1], w.shape[2])
+        return lax.all_gather(w, ("grp", "core"), axis=0, tiled=True)
+
+    grad_rows = grad_out.reshape(rows, D)
+    first, *ready = move((pack(0), None, "packed"), *picks(0, (0, 1, 2)))
+    packed = [first.reshape(D, -1), None]
+    weights = [[plane_gather(w) for w in ready], []]
 
     own_segments = lax.dynamic_slice_in_dim(segments, ctx_index * tok, tok, axis=1)
     prompt = jnp.sum((segments == 0).astype(jnp.int32), axis=1, dtype=jnp.int32)
@@ -757,7 +836,7 @@
     seg_col = segments[:, :, None]
 
     flat = routes.reshape(rows, TOP)
-    ids = jnp.arange(E, dtype=jnp.int32)
+    ids = by_plane(jnp.arange(E, dtype=jnp.int32), 0)
     chosen = jnp.any(ids[:, None, None] == flat[None, :, :], axis=2)
     marks = chosen.astype(BF).reshape(E, micro, tok)
     earlier = (
@@ -766,14 +845,12 @@
     rank = jnp.einsum("emt,ts->ems", marks, earlier, preferred_element_type=F32)
     slot = rank.astype(jnp.int32) + SLOTS * jnp.arange(micro, dtype=jnp.int32)[None, :, None]
     slot = jnp.where(chosen, slot.reshape(E, rows), -1)
-    slot = jnp.pad(
-        slot.reshape(n, held, rows), ((0, 0), (0, 8 - held), (0, 0)), constant_values=-1
-    )
+
+    slot = slot.reshape(planes, held, rows)
     chosen_f = chosen.astype(F32)
-    last_g = lax.all_gather(grad_out.reshape(rows, D), ("grp", "zp"), axis=0, tiled=False)
-    last_g = last_g.reshape(n, rows, D)
-
-    ids_of = iter(range(1, 100))
+
+    last_g = lax.all_gather(grad_rows, "zp", axis=0, tiled=False)
+
     saved = []
     parts = (hidden_in.reshape(rows, D),)
     for layer in range(LAYERS):
@@ -784,22 +861,33 @@
         out, lse = attention_forward(heads, seg_row, seg_col, ctx, hq, tok)
         mixed = lax.all_to_all(out, line, 0, 0, tiled=True)
         stream1, normed, gates = output_forward(
-            mixed, stream, packed[layer], gains, chosen_f, ctx, hq, n, held
+            mixed, stream, packed[layer], gains, chosen_f, ctx, hq, planes, held
         )
-        ops = [(normed, "gather"), (gates, "a2a")]
+        ops = [(normed, "tok", "all"), (gates, "tok", "own")]
         if layer == 0:
-            ops.append((slot, "a2a"))
-        moved = exchange(ops, next(ids_of), grp_size)
+            xs, gates_here, slots_here, second, *ready = move(
+                *ops, (slot, "tok", "own"), (pack(1), None, "packed"), *picks(1, (0,))
+            )
+            packed[1] = second.reshape(D, -1)
+            weights[1] += [plane_gather(w) for w in ready]
+        else:
+            xs, gates_here = move(*ops)
+        saved.append((stream, heads, out, lse, mixed, stream1, normed, gates, gains, xs, gates_here))
         if layer == 0:
-            slots_here = moved[2]
-        saved.append((stream, heads, out, lse, mixed, stream1, normed, gates, gains, moved[0], moved[1]))
-        if layer < LAYERS - 1:
-            sent = experts_forward_all(
-                moved[0], moved[1], slots_here, core_arr, weights[layer], ctx, held
-            )
-            parts = (stream1, exchange([(sent, "a2a")], next(ids_of), grp_size)[0])
-
-    g = grad_out.reshape(rows, D)
+            sent = experts_forward(xs, gates_here, slots_here, weights[0], held)
+            came, *ready = move((sent, "tok", "own"), *picks(1, (1, 2)))
+            weights[1] += [plane_gather(w) for w in ready]
+            parts = (stream1, came)
+
+    def plane_scatter(r):
+        r = lax.psum_scatter(r, ("grp", "core"), scatter_dimension=0, tiled=True)
+        return r.reshape(ctx, r.shape[1] // ctx, r.shape[2])
+
+    def owned_rows(r):
+        r = r.astype(F32).reshape((ctx // (2 * planes), 2 * planes) + r.shape[1:])
+        return jnp.sum(r, axis=0)
+
+    g = grad_rows
     extra = jnp.zeros((8, D), F32)
     small = [None] * LAYERS
     wide = [None] * LAYERS
@@ -810,26 +898,26 @@
         if last:
             gs = last_g
         else:
-            gs = exchange([(g.astype(BF), "gather")], next(ids_of), grp_size)[0]
-        res = experts_backward_all(
-            xs, gs, gates_here, slots_here, core_arr, weights[layer], ctx, held, last
-        )
-        shards = []
-        for own, other in ((res[2], res[3]), (res[4], res[5]), (res[6], res[7])):
-            total = (own.astype(F32) + swap(other).astype(F32)).astype(BF)
-            shards.append(lax.all_to_all(total, line, 0, 0, tiled=True))
-        expert[layer] = shards
+            gs, last_gate, last_up = move(
+                (g.astype(BF), "tok", "all"),
+                (expert[1][0], "line", "own"),
+                (expert[1][1], "line", "own"),
+            )
+        res = experts_backward(xs, gs, gates_here, slots_here, weights[layer], held, last)
+        expert[layer] = [plane_scatter(r) for r in res[2:5]]
+        back = [(res[0], "tok", "own"), (res[1], "tok", "own")]
         if last:
-            final_parts = lax.all_to_all(res[8], ("grp", "zp"), 0, 0, tiled=True)
+            d_parts, d_gates, final_parts = move(*back, (res[5], "tok", "own"))
             hidden_out = (
-                stream1 + jnp.sum(final_parts.astype(F32), axis=0)
-            ).astype(BF).reshape(micro, tok, D)
-        d_parts, d_gates = exchange(
-            [(res[0], "a2a"), (res[1], "a2a")], next(ids_of), grp_size
-        )
+                (stream1 + jnp.sum(final_parts.astype(F32), axis=0))
+                .astype(BF)
+                .reshape(micro, tok, D)
+            )
+        else:
+            d_parts, d_gates, last_down = move(*back, (expert[1][2], "line", "own"))
         g1, d_mixed, small[layer] = output_backward(
             d_parts, d_gates, gates, g, stream1, normed, mixed, packed[layer], gains, extra,
-            ctx, hq, n, held,
+            ctx, hq, planes, held,
         )
         d_out = lax.all_to_all(d_mixed, line, 0, 0, tiled=True)
         dx = attention_backward(heads, d_out, out, lse, seg_row, seg_col, ctx, hq, tok)
@@ -837,23 +925,38 @@
         g, extra, wide[layer] = qkv_backward(
             dx, g1, stream, packed[layer], gains, cos_t, sin_t, ctx
         )
-    small = [lax.psum_scatter(s, every, scatter_dimension=0, tiled=True) for s in small]
-    wide = [lax.psum_scatter(s, every, scatter_dimension=0, tiled=True) for s in wide]
-    first_gain = lax.psum_scatter(extra[0], every, scatter_dimension=0, tiled=True)
+    at_34 = jnp.arange(D + 128) == D + 34
+    small[0] = jnp.where(at_34[None, :], extra[0][:, None].astype(BF), small[0])
+    joined = [jnp.concatenate([wide[k], small[k]], axis=1) for k in range(LAYERS)]
+    last_owned = lax.psum_scatter(joined[1], every, scatter_dimension=0, tiled=True)
+    halves = joined[0].reshape(grp_size, ctx // 2, 2, shard, -1)
+    theirs = lax.dynamic_index_in_dim(halves, 1 - core, 2, keepdims=False)
+    ours = lax.dynamic_index_in_dim(halves, core, 2, keepdims=False)
+    chip = (ours.astype(F32) + swap(theirs).astype(F32)).astype(BF)
+    plane, first_gate, first_up = move(
+        (chip, "g", "own"), (expert[0][0], "line", "own"), (expert[0][1], "line", "own")
+    )
+    plane = jnp.sum(plane.astype(F32), axis=0).astype(BF)
+    column, first_down = move((plane, "z", "own"), (expert[0][2], "line", "own"))
+    owned_attn = [jnp.sum(column.astype(F32), axis=0), last_owned.astype(F32)]
+    owned_experts = [
+        [owned_rows(r) for r in (first_gate, first_up, first_down)],
+        [owned_rows(r) for r in (last_gate, last_up, last_down)],
+    ]
 
     def unpack(layer):
-        w = wide[layer].astype(F32).reshape(shard, ctx, 256)
+        w = owned_attn[layer][:, : 256 * ctx].reshape(shard, ctx, 256)
         gq = w[:, :, : HS * hq].reshape(shard, QUERY_HEADS * HS)
         gk = w[:, :, 128:192].reshape(shard, KEY_VALUE_HEADS, dup, HS).sum(axis=2)
         gv = w[:, :, 192:256].reshape(shard, KEY_VALUE_HEADS, dup, HS).sum(axis=2)
-        s = small[layer].astype(F32)
+        s = owned_attn[layer][:, 256 * ctx :]
         return (
             gq,
             gk.reshape(shard, KEY_VALUE_HEADS * HS),
             gv.reshape(shard, KEY_VALUE_HEADS * HS),
             s[:, :D],
             s[:, D + 33],
-            s[:, D : D + E],
+            by_plane(s[:, D : D + E], 1, back=True),
         )
 
     got = [unpack(layer) for layer in range(LAYERS)]
@@ -862,16 +965,12 @@
         return jnp.stack([got[layer][k] for layer in range(LAYERS)])
 
     gain_grad = jnp.stack(
-        [first_gain] + [small[layer][:, D + 32].astype(F32) for layer in range(LAYERS - 1)]
+        [owned_attn[0][:, 256 * ctx + D + 34]]
+        + [owned_attn[k][:, 256 * ctx + D + 32] for k in range(LAYERS - 1)]
     )
 
     def owned(k):
-        out = []
-        for layer in range(LAYERS):
-            s = expert[layer][k].astype(F32)
-            s = s.reshape((ctx // 4, 4 * half) + s.shape[2:]).sum(axis=0)
-            out.append(s)
-        return jnp.stack(out)
+        return jnp.stack([owned_experts[layer][k] for layer in range(LAYERS)])
 
     return (
         hidden_out,
@@ -892,8 +991,10 @@
 def solution(mesh):
     grp_size = mesh.shape["grp"]
     ctx = mesh.shape["ctx"]
+    planes = E // grp_size // 2
     fine = Mesh(
-        mesh.devices.reshape(grp_size, ctx // 4, 2, 2), ("grp", "zq", "zp", "core")
+        mesh.devices.reshape(grp_size, ctx // (2 * planes), planes, 2),
+        ("grp", "zq", "zp", "core"),
     )
     line = ("zq", "zp", "core")
     every = ("grp",) + line
@@ -915,7 +1016,7 @@
         P(None, "grp", line, None),
     )
     return jax.shard_map(
-        functools.partial(per_device, grp_size, ctx),
+        functools.partial(per_device, (grp_size, ctx, planes)),
         mesh=fine,
         in_specs=placed,
         out_specs=(

time: 1910 us -> 1350 us (0.71)
  waiting for transfers between devices: 826 us -> 123 us
  Pallas kernels: 691 us -> 963 us
  starting transfers between devices: 84.4 us -> 18.5 us
  blocking collectives: 180 us -> 145 us
  other arithmetic: 63.7 us -> 41.4 us
    all_to_all x14 -> x0, waiting for transfers between devices: 539 us -> none  [the longest x6 264 us: fetch(): own = lax.all_to_all(to_holders(w), line, 0, 0, tiled=True)]
    pallas_call x6 -> x9, Pallas kernels: 427 us -> 712 us  [transfer(): pl.pallas_call(kernel, out_shape=tuple(shapes), in_specs=[any_spec] * cou...]
    reduce_scatter x4 -> x7, waiting for transfers between devices: 201 us -> 43.1 us  [the longest x6 43.1 us: plane_scatter(): r = lax.psum_scatter(r, ('grp', 'core'), scatter_dimension=0, tiled=True)]
    unnamed x1 -> x0, blocking collectives: 77.7 us -> none
    all_to_all x14 -> x0, starting transfers between devices: 66.3 us -> none  [the longest x6 28.1 us: fetch(): own = lax.all_to_all(to_holders(w), line, 0, 0, tiled=True)]
    all_to_all x1 -> x2, blocking collectives: 20.9 us -> 57.3 us  [per_device(): d_out = lax.all_to_all(d_mixed, line, 0, 0, tiled=True)]
    ppermute x12 -> x1, waiting for transfers between devices: 21.1 us -> 0.01 us  [swap(): return lax.ppermute(x, 'core', [(0, 1), (1, 0)])]
    convert_element_type x10 -> x3, other arithmetic: 27 us -> 7.32 us  [the longest x1 5.49 us: per_device(): chip = (ours.astype(F32) + swap(theirs).astype(F32)).astype(BF)]
  transfers between devices with their start and end apart: 36 -> 18, of which waited for: 22 -> 6; matrix products, arithmetic and copies ran while one was open for 4% -> 3% of each run, Pallas kernels for 18% -> 58%
where the time goes in v2:
time: 1350 us; the launch traced here: 1330 us
  Pallas kernels  963 us (71%)
  blocking collectives  145 us (11%)
  waiting for transfers between devices  123 us (9%)
  other arithmetic  41.4 us (3%)
  local copies, waits for them, and re-layouts  28.8 us (2%)
  starting transfers between devices  18.5 us (1%)
  between operations  15 us (1%)
    pallas_call x9, Pallas kernels, transfer(): pl.pallas_call(kernel, out_shape=tuple(shapes), in_specs=[any_spec] * cou...  712 us
    pallas_call x15, Pallas kernels, call(): pl.pallas_call(kernel, out_shape=tuple(outs), scratch_shapes=list(scratch...  251 us
    all_to_all x2, blocking collectives, per_device(): d_out = lax.all_to_all(d_mixed, line, 0, 0, tiled=True)  57.3 us
    reduce_scatter x6, waiting for transfers between devices, plane_scatter(): r = lax.psum_scatter(r, ('grp', 'core'), scatter_dimension=0, tiled=True)  43.1 us
    all_to_all x1, blocking collectives, per_device(): heads = lax.all_to_all(qkv, line, 0, 0, tiled=True)  36.7 us
    all_to_all x1, blocking collectives, per_device(): dx = lax.all_to_all(dx, line, 0, 0, tiled=True)  30.8 us
  transfers between devices with their start and end apart: 18, of which 6 were waited for; matrix products, arithmetic and copies ran while one was open for 3% of the time, Pallas kernels for 58%

profile of v2, /device:TPU:0, one launch (start us, length us, event | category | flops | bytes accessed | tf_op | source)
XLA Modules:
  0.0 1334.4 jit_solution(9438563401844707567)
XLA Ops:
  13.7 3.3 slice_bitcast_fusion
  16.9 2.1 slice_bitcast_fusion.1
  19.8 86.2 %shard_map.229 = (bf16[4,8,32,3200]{3,2,1,0:T(8,128)(2,1)}, bf16[8,128,512]{2,1,0:T(8,128)(2,1)}, bf16[8,128,512]{2,1,0:T(8,128)(2,1)}, bf16[8,64,1024]{2,1,0:T(8,128)(2,1)}) custom-call(bf16[32,3200]{1,0:T(8,128)(2,1)} %concatenate.19.refs_0_, bf16[8,128,512]{2,1,0:T(8,128)(2,1)} %get-tuple-element.209.refs_1_, ...), custom_call_target="tpu_custom_call" | custom-call | bytes 387973120 | tf_op jit(solution)/shard_map/pallas_call | solution.py:257
  110.5 5.2 shard_map.230
  115.7 10.2 all-to-all-start
  127.9 24.6 %all-to-all-done.x_ref = bf16[8,256,256]{2,1,0:T(8,128)(2,1)S(1)} async-done(((bf16[8,256,256]{2,1,0:T(8,128)(2,1)}), bf16[8,256,256]{2,1,0:T(8,128)(2,1)S(1)}, u32[]{:S(2)}, u32[]{:S(2)}) %all-to-all-start) | async-done | bytes 1048608 | tf_op jit(solution)/shard_map/all_to_all | solution.py:860
  153.4 9.7 shard_map.231
  163.2 3.5 all-to-all-start.1
  170.0 11.9 all-to-all-done.1.m_ref
  182.8 4.0 shard_map.232
  186.7 107.5 %shard_map.233 = (bf16[4,256,1024]{2,1,0:T(8,128)(2,1)}, f32[4,8,256]{2,1,0:T(8,128)}, s32[4,8,256]{2,1,0:T(8,128)}, bf16[4,8,32,3200]{3,2,1,0:T(8,128)(2,1)}, bf16[8,128,512]{2,1,0:T(8,128)(2,1)}) custom-call(bf16[256,1024]{1,0:T(8,128)(2,1)} %get-tuple-element.83.refs_0_.nm_ref, f32[4,8,256]{2,1,0:T(8,128)} %get-tuple-element.84.refs_1_.gt_ref, ...), custom_call_target="tpu_custom_call" | custom-call | bytes 390594560 | tf_op jit(solution)/shard_map/pallas_call | solution.py:257
  294.6 11.7 all-gather.12.cloned.1.call-done.w2
  306.2 30.1 %shard_map.234.refs_0_ = bf16[4,256,1024]{2,1,0:T(8,128)(2,1)} custom-call(bf16[4,256,1024]{2,1,0:T(8,128)(2,1)} %get-tuple-element.85.x_ref, f32[4,8,256]{2,1,0:T(8,128)} %get-tuple-element.86.g_ref, s32[4,8,256]{2,1,0:T(8,128)} %get-tuple-element.87.s_ref, bf16[8,1024,512]{2,1,0:T(8,128)(2,1)} %all-gather.8.cloned.1.call-done.w0, ...), custom_call_target="tpu_custom_call" | custom-call | flops 12884901888 | bytes 29425664 | tf_op jit(solution)/shard_map/pallas_call | solution.py:42
  336.3 105.7 %shard_map.235 = (bf16[4,256,1024]{2,1,0:T(8,128)(2,1)}, bf16[8,128,512]{2,1,0:T(8,128)(2,1)}, bf16[8,64,1024]{2,1,0:T(8,128)(2,1)}) custom-call(bf16[4,256,1024]{2,1,0:T(8,128)(2,1)} %shard_map.234.refs_0_, bf16[8,128,512]{2,1,0:T(8,128)(2,1)} %get-tuple-element.185.refs_1_, bf16[8,64,1024]{2,1,0:T(8,128)(2,1)} %get-tuple-element.183.refs_2_), custom_call_target="tpu_custom_call" | custom-call | bytes 167772160 | tf_op jit(solution)/shard_map/pallas_call | solution.py:257
  442.9 6.2 shard_map.236
  449.1 36.7 %all_to_all.40.x_ref = bf16[8,256,256]{2,1,0:T(8,128)(2,1)} all-to-all(bf16[8,256,256]{2,1,0:T(8,128)(2,1)} %get-tuple-element.93), channel_id=1, replica_groups=mesh['grp'=4,'zq'=1,'zp'=4,'core'=2] {'zq','zp','core'}, dimensions={0} | all-to-all | bytes 2097152 | tf_op jit(solution)/shard_map/all_to_all | solution.py:860
  485.8 9.7 shard_map.237
  495.5 19.9 %all_to_all.41.m_ref = bf16[8,256,128]{2,1,0:T(8,128)(2,1)} all-to-all(bf16[8,256,128]{2,1,0:T(8,128)(2,1)} %get-tuple-element.94.o_ref), channel_id=1, replica_groups=mesh['grp'=4,'zq'=1,'zp'=4,'core'=2] {'zq','zp','core'}, dimensions={0} | all-to-all | bytes 1048576 | tf_op jit(solution)/shard_map/all_to_all | solution.py:862
  515.4 4.1 shard_map.238
  519.5 49.1 %shard_map.239 = (bf16[4,256,1024]{2,1,0:T(8,128)(2,1)}, f32[4,8,256]{2,1,0:T(8,128)}) custom-call(bf16[256,1024]{1,0:T(8,128)(2,1)} %get-tuple-element.98.refs_0_.nm_ref, f32[4,8,256]{2,1,0:T(8,128)} %get-tuple-element.99.refs_1_.gt_ref), custom_call_target="tpu_custom_call" | custom-call | bytes 85196800 | tf_op jit(solution)/shard_map/pallas_call | solution.py:257
  568.7 67.1 %shard_map.240 = (bf16[4,256,1024]{2,1,0:T(8,128)(2,1)}, f32[4,8,256]{2,1,0:T(8,128)}, bf16[8,1024,512]{2,1,0:T(8,128)(2,1)}, bf16[8,1024,512]{2,1,0:T(8,128)(2,...) custom-call(bf16[4,256,1024]{2,1,0:T(8,128)(2,1)} %get-tuple-element.100.x_ref, ...), custom_call_target="tpu_custom_call" | custom-call | flops 33822867456 | bytes 58818560 | tf_op jit(solution)/shard_map/pallas_call | solution.py:42
  637.2 83.3 %shard_map.241 = (bf16[4,256,1024]{2,1,0:T(8,128)(2,1)}, f32[4,8,256]{2,1,0:T(8,128)}, bf16[4,256,1024]{2,1,0:T(8,128)(2,1)}) custom-call(bf16[4,256,1024]{2,1,0:T(8,128)(2,1)} %get-tuple-element.105.refs_0_, f32[4,8,256]{2,1,0:T(8,128)} %get-tuple-element.106.refs_1_, bf16[4,256,1024]{2,1,0:T(8,128)(2,1)} %get-tuple-element.107.refs_2_), custom_call_target="tpu_custom_call" | custom-call | bytes 169082880 | tf_op jit(solution)/shard_map/pallas_call | solution.py:257
  721.1 8.0 shard_map.242
  729.1 28.4 %all_to_all.42.d_ref = bf16[8,256,128]{2,1,0:T(8,128)(2,1)} all-to-all(bf16[8,256,128]{2,1,0:T(8,128)(2,1)} %get-tuple-element.111), channel_id=1, replica_groups=mesh['grp'=4,'zq'=1,'zp'=4,'core'=2] {'zq','zp','core'}, dimensions={0} | all-to-all | bytes 1048576 | tf_op jit(solution)/shard_map/all_to_all | solution.py:922
  757.6 13.3 %shard_map.243 = bf16[8,256,256]{2,1,0:T(8,128)(2,1)} custom-call(bf16[8,256,256]{2,1,0:T(8,128)(2,1)} %all_to_all.40.x_ref, bf16[8,256,128]{2,1,0:T(8,128)(2,1)} %all_to_all.42.d_ref, bf16[8,256,128]{2,1,0:T(8,128)(2,1)} %get-tuple-element.94.o_ref, f32[2,1024,128]{2,1,0:T(8,128)} %get-tuple-element.112.l_ref, s32[2,1,1024]{2,1,0:T(1,128)} %broadcast_in_dim.83.sr_ref, ...), custom_call_target="tpu_custom_call" | custom-call | flops 1342177280 | bytes 4210688 | tf_op jit(solution)/shard_map/pallas_call | solution.py:42
  770.9 30.8 %all_to_all.43.d_ref = bf16[8,256,256]{2,1,0:T(8,128)(2,1)} all-to-all(bf16[8,256,256]{2,1,0:T(8,128)(2,1)} %shard_map.243), channel_id=1, replica_groups=mesh['grp'=4,'zq'=1,'zp'=4,'core'=2] {'zq','zp','core'}, dimensions={0} | all-to-all | bytes 2097152 | tf_op jit(solution)/shard_map/all_to_all | solution.py:924
  801.7 8.6 shard_map.244
  810.4 5.8 pad_maximum_fusion.1
  818.3 106.5 %shard_map.245 = (bf16[4,256,1024]{2,1,0:T(8,128)(2,1)}, bf16[8,128,512]{2,1,0:T(8,128)(2,1)}, bf16[8,128,512]{2,1,0:T(8,128)(2,1)}) custom-call(bf16[256,1024]{1,0:T(8,128)(2,1)} %convert_element_type.84.refs_0_, bf16[8,128,512]{2,1,0:T(8,128)(2,1)} %bitcast.143, bf16[8,128,512]{2,1,0:T(8,128)(2,1)} %bitcast.145), custom_call_target="tpu_custom_call" | custom-call | bytes 167772160 | tf_op jit(solution)/shard_map/pallas_call | solution.py:257
  924.8 56.0 %shard_map.246 = (bf16[4,256,1024]{2,1,0:T(8,128)(2,1)}, f32[4,8,256]{2,1,0:T(8,128)}, bf16[8,1024,512]{2,1,0:T(8,128)(2,1)}, bf16[8,1024,512]{2,1,0:T(8,128)(2,1)}, bf16[8,512,1024]{2,1,0:T(8,128)(2,1)}) custom-call(bf16[4,256,1024]{2,1,0:T(8,128)(2,1)} %get-tuple-element.85.x_ref, bf16[4,256,1024]{2,1,0:T(8,128)(2,1)} %get-tuple-element.117.gr_ref, ...), custom_call_target="tpu_custom_call" | custom-call | flops 33822867456 | bytes 56721408 | tf_op jit(solution)/shard_map/pallas_call | solution.py:42
  982.1 84.0 %shard_map.247 = (bf16[4,256,1024]{2,1,0:T(8,128)(2,1)}, f32[4,8,256]{2,1,0:T(8,128)}, bf16[8,64,1024]{2,1,0:T(8,128)(2,1)}) custom-call(bf16[4,256,1024]{2,1,0:T(8,128)(2,1)} %get-tuple-element.118.refs_0_, f32[4,8,256]{2,1,0:T(8,128)} %get-tuple-element.119.refs_1_, bf16[8,64,1024]{2,1,0:T(8,128)(2,1)} %bitcast.138), custom_call_target="tpu_custom_call" | custom-call | bytes 127139840 | tf_op jit(solution)/shard_map/pallas_call | solution.py:257
  1066.2 6.9 shard_map.248
  1073.0 28.9 %all_to_all.44.d_ref = bf16[8,256,128]{2,1,0:T(8,128)(2,1)} all-to-all(bf16[8,256,128]{2,1,0:T(8,128)(2,1)} %get-tuple-element.124), channel_id=1, replica_groups=mesh['grp'=4,'zq'=1,'zp'=4,'core'=2] {'zq','zp','core'}, dimensions={0} | all-to-all | bytes 1048576 | tf_op jit(solution)/shard_map/all_to_all | solution.py:922
  1101.9 13.3 shard_map.249
  1115.3 3.9 all-to-all-start.7
  1119.1 26.5 %all-to-all-done.7.d_ref = bf16[8,256,256]{2,1,0:T(8,128)(2,1)S(1)} async-done(((bf16[8,256,256]{2,1,0:T(8,128)(2,1)}), bf16[8,256,256]{2,1,0:T(8,128)(2,1)S(1)}, u32[]{:S(2)}, u32[]{:S(2)}) %all-to-all-start.7) | async-done | bytes 1048608 | tf_op jit(solution)/shard_map/all_to_all | solution.py:924
  1146.6 8.9 shard_map.250
  1158.1 3.7 pad_maximum_fusion
  1165.5 2.1 convert_reduce_fusion
  1171.9 5.5 fusion.refs_0_
  1177.4 16.2 %reduce-scatter.16.cloned.1.call-done = bf16[1,1024,512]{2,1,0:T(8,128)(2,1)} async-done(((bf16[8,1024,512]{2,1,0:T(8,128)(2,1)}), bf16[1,1024,512]{2,1,0:T(8,128)(2,1)}) %reduce-scatter.16.cloned.1.call-update) | async-done | bytes 1048592 | tf_op jit(solution)/shard_map/reduce_scatter | solution.py:883
  1193.6 52.2 %shard_map.251 = (bf16[4,4,32,3200]{3,2,1,0:T(8,128)(2,1)}, bf16[8,128,512]{2,1,0:T(8,128)(2,1)}, bf16[8,128,512]{2,1,0:T(8,128)(2,1)}) custom-call(bf16[4,4,32,3200]{3,2,1,0:T(8,128)(2,1)} %fusion.refs_0_, bf16[8,128,512]{2,1,0:T(8,128)(2,1)} %bitcast.153, bf16[8,128,512]{2,1,0:T(8,128)(2,1)} %bitcast.154), custom_call_target="tpu_custom_call" | custom-call | bytes 214958080 | tf_op jit(solution)/shard_map/pallas_call | solution.py:257
  1245.7 3.7 reduce_sum.55.refs_0_
  1249.4 26.9 %reduce-scatter.18.cloned.1.call-done = bf16[1,512,1024]{2,1,0:T(8,128)(2,1)} async-done(((bf16[8,512,1024]{2,1,0:T(8,128)(2,1)}), bf16[1,512,1024]{2,1,0:T(8,128)(2,1)}) %reduce-scatter.18.cloned.1.call-update) | async-done | bytes 1048592 | tf_op jit(solution)/shard_map/reduce_scatter | solution.py:883
  1276.3 37.2 %shard_map.252 = (bf16[4,32,3200]{2,1,0:T(8,128)(2,1)}, bf16[8,64,1024]{2,1,0:T(8,128)(2,1)}) custom-call(bf16[4,32,3200]{2,1,0:T(8,128)(2,1)} %reduce_sum.55.refs_0_, bf16[8,64,1024]{2,1,0:T(8,128)(2,1)} %bitcast.139), custom_call_target="tpu_custom_call" | custom-call | bytes 74711040 | tf_op jit(solution)/shard_map/pallas_call | solution.py:257
  1320.4 2.3 maximum_convert_fusion
  1322.7 2.3 maximum_convert_fusion.1
  1325.0 2.3 maximum_convert_fusion.2
  (167 shorter events, 43.5 us)
Async XLA Ops:
  7.2 9.8 copy-start.8
  7.2 287.4 %all-gather.8.cloned.1.call-start = ((), (), s32[]{:S(2)}) async-start(), calls=%async_computation.15 | async-start | bytes 9437184 | tf_op jit(solution)/shard_map/all_gather | solution.py:809
  13.7 3.3 copy-start.9
  19.8 88.4 %copy-start.16 = (s32[2,1024]{1,0:T(2,128)S(1)}, s32[2,1024]{1,0:T(2,128)}, u32[]{:S(2)}) copy-start(s32[2,1024]{1,0:T(2,128)} %param.16) | copy-start | bytes 24580
  106.1 188.5 %all-gather.10.cloned.1.call-start = ((), (), s32[]{:S(2)}) async-start(), calls=%async_computation.16 | async-start | bytes 9437184 | tf_op jit(solution)/shard_map/all_gather | solution.py:809
  106.8 199.4 %all-gather.12.cloned.1.call-start = ((), (), s32[]{:S(2)}) async-start(), calls=%async_computation.17 | async-start | bytes 9437184 | tf_op jit(solution)/shard_map/all_gather | solution.py:809
  107.6 461.1 %all-gather.14.cloned.1.call-start = ((), (), s32[]{:S(2)}) async-start(), calls=%async_computation.18 | async-start | bytes 2621440 | tf_op jit(solution)/shard_map/all_gather | solution.py:852
  115.7 51.2 %copy-start.17 = (s32[2,128,8]{1,2,0:T(8,128)S(1)}, s32[2,128,8]{1,2,0:T(8,128)}, u32[]{:S(2)}) copy-start(s32[2,128,8]{1,2,0:T(8,128)} %param.17) | copy-start | bytes 24580
  115.7 36.8 %all-to-all-start = ((bf16[8,256,256]{2,1,0:T(8,128)(2,1)}), bf16[8,256,256]{2,1,0:T(8,128)(2,1)S(1)}, u32[]{:S(2)}, u32[]{:S(2)}) async-start(bf16[8,256,256]{2,1,0:T(8,128)(2,1)} %get-tuple-element.79), calls=%async_computation | async-start | bytes 2097152 | tf_op jit(solution)/shard_map/all_to_all | solution.py:860
  152.4 1.0 copy-start.1
  163.2 18.8 %all-to-all-start.1 = ((bf16[8,256,128]{2,1,0:T(8,128)(2,1)}), bf16[8,256,128]{2,1,0:T(8,128)(2,1)S(1)}, u32[]{:S(2)}, u32[]{:S(2)}) async-start(bf16[8,256,128]{2,1,0:T(8,128)(2,1)} %get-tuple-element.80.o_ref), calls=%async_computation.1 | async-start | bytes 1048576 | tf_op jit(solution)/shard_map/all_to_all | solution.py:862
  166.7 402.0 %all-gather.16.cloned.1.call-start = ((), (), s32[]{:S(2)}) async-start(), calls=%async_computation.19 | async-start | bytes 9437184 | tf_op jit(solution)/shard_map/all_gather | solution.py:809
  182.0 0.8 copy-start.2
  294.3 274.4 %all-gather.18.cloned.1.call-start = ((), (), s32[]{:S(2)}) async-start(), calls=%async_computation.20 | async-start | bytes 9437184 | tf_op jit(solution)/shard_map/all_gather | solution.py:809
  442.1 126.6 %all-gather.20.cloned.1.call-start = ((), (), s32[]{:S(2)}) async-start(), calls=%async_computation.21 | async-start | bytes 9437184 | tf_op jit(solution)/shard_map/all_gather | solution.py:809
  442.9 375.4 %reduce-scatter.8.cloned.1.call-start = ((), (), s32[]{:S(2)}) async-start(), calls=%async_computation.22 | async-start | bytes 9437184 | tf_op jit(solution)/shard_map/reduce_scatter | solution.py:883
  635.8 182.4 %reduce-scatter.10.cloned.1.call-start = ((), (), s32[]{:S(2)}) async-start(), calls=%async_computation.23 | async-start | bytes 9437184 | tf_op jit(solution)/shard_map/reduce_scatter | solution.py:883
  636.6 345.5 %reduce-scatter.12.cloned.1.call-start = ((), (), s32[]{:S(2)}) async-start(), calls=%async_computation.24 | async-start | bytes 9437184 | tf_op jit(solution)/shard_map/reduce_scatter | solution.py:883
  637.2 531.4 %reduce-scatter.20.cloned.1.call-start = ((), (), s32[]{:S(2)}) async-start(), calls=%async_computation.28 | async-start | bytes 6758400 | tf_op jit(solution)/shard_map/reduce_scatter | solution.py:931
  801.7 8.6 copy-start.6
  816.1 1.3 copy-start.4
  816.2 361.2 %reduce-scatter.14.cloned.1.call-start = ((), (), s32[]{:S(2)}) async-start(), calls=%async_computation.25 | async-start | bytes 9437184 | tf_op jit(solution)/shard_map/reduce_scatter | solution.py:883
  980.8 212.8 %reduce-scatter.16.cloned.1.call-start = ((), (), s32[]{:S(2)}) async-start(), calls=%async_computation.26 | async-start | bytes 9437184 | tf_op jit(solution)/shard_map/reduce_scatter | solution.py:883
  981.5 294.8 %reduce-scatter.18.cloned.1.call-start = ((), (), s32[]{:S(2)}) async-start(), calls=%async_computation.27 | async-start | bytes 9437184 | tf_op jit(solution)/shard_map/reduce_scatter | solution.py:883
  1115.3 30.4 %all-to-all-start.7 = ((bf16[8,256,256]{2,1,0:T(8,128)(2,1)}), bf16[8,256,256]{2,1,0:T(8,128)(2,1)S(1)}, u32[]{:S(2)}, u32[]{:S(2)}) async-start(bf16[8,256,256]{2,1,0:T(8,128)(2,1)} %shard_map.249), calls=%async_computation.10 | async-start | bytes 2097152 | tf_op jit(solution)/shard_map/all_to_all | solution.py:924
  1145.6 1.0 copy-start.5
  1146.6 9.7 copy-start.7
  1161.8 3.7 copy-start
  1161.8 5.8 copy-start.3
  1165.5 6.4 collective-permute-start
  1313.5 6.9 copy-start.11
  1313.5 6.9 copy-start.14
  1319.8 2.9 copy-start.10
  1319.8 2.9 copy-start.13
  1322.7 2.3 copy-start.12
  1322.7 2.4 copy-start.15
Sparse Core Ops, SparseCore 0:
  106.2 60.8 all-gather.7
  168.9 63.1 all-gather.9
  234.0 72.1 all-gather.11
  307.7 81.5 all-gather.13
  391.0 52.8 all-gather.15
  445.7 57.3 all-gather.17
  504.9 54.4 all-gather.19
  636.0 71.1 reduce-scatter.7
  711.0 71.2 reduce-scatter.9
  785.6 71.2 reduce-scatter.11
  859.3 165.7 reduce-scatter.19
  1028.8 89.9 reduce-scatter.13
  1122.3 71.2 reduce-scatter.15
  1197.3 78.9 reduce-scatter.17

commit v3 on v2

--- a/solution.py
+++ b/solution.py
@@ -24,7 +24,9 @@
 BF = jnp.bfloat16
 F32 = jnp.float32
 MESH = pl.DeviceIdType.MESH
+PIECES = 8
 VMEM_BYTES = 58 * 1024 * 1024
+TAIL = 3 * D // 128
 
 
 def dot(a, b, ca=1, cb=0):
@@ -108,9 +110,11 @@
             total_sems += zs + zs * grp_size * 2
             continue
         n = size_of(group, sizes)
-        total_sems += n
-        rest = {"all": (n,) + x.shape, "own": x.shape, "pick": (n,) + x.shape[1:]}
-        shapes.append(sds(rest[what], x.dtype))
+        total_sems += PIECES if group == "sib" else n
+        rest = x.shape[1:] if group == "sib" else x.shape
+        if what != "own":
+            rest = (n,) + (x.shape if what == "all" else x.shape[1:])
+        shapes.append(sds(rest, x.dtype))
     count = len(ops)
 
     def kernel(*refs):
@@ -142,7 +146,6 @@
 
         sib_place = {"core": 1 - lax.axis_index("core")}
         sent = []
-        todo = []
         own_copies = []
 
         def start(i):
@@ -166,6 +169,14 @@
                         )
                     )
                 return (i, along, copy)
+            if group == "sib":
+                size = ins[i].shape[1] // PIECES
+                for j in range(PIECES):
+                    part = pl.ds(j * size, size)
+                    sent.append(
+                        remote(ins[i].at[1 - me, part], out.at[part], sems[i] + j, where(1 - me))
+                    )
+                return None
             copies = []
             for k in range(1, n):
                 peer = lax.rem(me + k, n)
@@ -283,11 +294,14 @@
     return lax.rsqrt(jnp.mean(x * x, axis=-1, keepdims=True) + EPSILON)
 
 
-def qkv_forward(stream_parts, packed, cos_t, sin_t, ctx):
+def in_order(parts):
+    return parts[0] if len(parts) == 1 else jnp.concatenate(parts, axis=1)
+
+
+def qkv_forward(stream_parts, packed, cos_t, sin_t, ctx, hq):
     first = len(stream_parts) == 1
     rows = stream_parts[0].shape[0]
-    width = 256 * ctx
-    tail = (width + D) // 128
+    dup = ctx // KEY_VALUE_HEADS
 
     def kernel(*refs):
         if first:
@@ -304,14 +318,26 @@
         normed = (x * inv_rms_of(x) * gains[0:1]).astype(BF)
         cos_v = c_ref[...]
         sin_v = s_ref[...]
+        parts = []
+        for i in range(8):
+            y = dot(normed, w_ref[:, 256 * i : 256 * (i + 1)])
+            if i < 6:
+                y = y * cos_v + swap_halves(y) * sin_v
+            parts.append(y.astype(BF))
+        queries, keys, values = in_order(parts[:4]), in_order(parts[4:6]), in_order(parts[6:])
         for i in range(ctx):
-            y = dot(normed, w_ref[:, 256 * i : 256 * (i + 1)])
-            out_ref[i] = (y * cos_v + swap_halves(y) * sin_v).astype(BF)
+            mine = [queries[:, HS * hq * i : HS * hq * (i + 1)]]
+            if hq < 2:
+                mine.append(jnp.zeros((rows, 128 - HS * hq), BF))
+            kv = i // dup
+            mine.append(keys[:, HS * kv : HS * (kv + 1)])
+            mine.append(values[:, HS * kv : HS * (kv + 1)])
+            out_ref[i] = in_order(mine)
 
     args = list(stream_parts) + [packed, packed, cos_t, sin_t]
     in_specs = [full(a.shape) for a in stream_parts] + [
-        pl.BlockSpec((D, width), lambda i: (0, 0)),
-        pl.BlockSpec((D, 128), lambda i: (0, tail)),
+        pl.BlockSpec((D, 2 * D), lambda i: (0, 0)),
+        pl.BlockSpec((D, 128), lambda i: (0, TAIL)),
         full(cos_t.shape),
         full(sin_t.shape),
     ]
@@ -322,7 +348,7 @@
         kernel,
         outs,
         args,
-        2 * rows * D * width,
+        4 * rows * D * D,
         in_specs=in_specs,
         out_specs=tuple(full(o.shape) for o in outs),
         grid=(1,),
@@ -455,8 +481,6 @@
 
 def output_forward(mixed, stream, packed, gains, chosen, ctx, hq, n, held):
     rows = stream.shape[0]
-    at = 256 * ctx // D
-    tail = (256 * ctx + D) // 128
 
     def kernel(m_ref, x_ref, w_ref, t_ref, g_ref, c_ref, s_ref, n_ref, gate_ref):
         x = x_ref[...].astype(F32) + dot(side_by_side(m_ref, ctx, hq), w_ref[...])
@@ -481,14 +505,19 @@
         in_specs=[
             full(mixed.shape),
             full(stream.shape),
-            pl.BlockSpec((D, D), lambda i: (0, at)),
-            pl.BlockSpec((D, 128), lambda i: (0, tail)),
+            pl.BlockSpec((D, D), lambda i: (0, 2)),
+            pl.BlockSpec((D, 128), lambda i: (0, TAIL)),
             full(gains.shape),
             full(chosen.shape),
         ],
         out_specs=tuple(full(o.shape) for o in outs),
         grid=(1,),
     )
+
+
+def by_core(x, shard):
+    y = x.astype(BF).reshape(x.shape[0] // (2 * shard), 2, shard, x.shape[1])
+    return [y[:, c].reshape(x.shape[0] // 2, x.shape[1]) for c in range(2)]
 
 
 def norm_back(x, gain, d_normed):
@@ -499,12 +528,10 @@
     return dx, grad_gain
 
 
-def output_backward(parts, d_gates, gates, g, stream, normed, mixed, packed, gains, extra, ctx, hq, n, held):
+def output_backward(parts, d_gates, gates, g, stream, normed, mixed, packed, gains, ctx, hq, n, shard):
     rows = stream.shape[0]
-    at = 256 * ctx // D
-    tail = (256 * ctx + D) // 128
-
-    def kernel(p_ref, dg_ref, gt_ref, g_ref, x_ref, nm_ref, m_ref, w_ref, t_ref, gain_ref, ex_ref, g1_ref, dm_ref, gw_ref):
+
+    def kernel(p_ref, dg_ref, gt_ref, g_ref, x_ref, nm_ref, m_ref, w_ref, t_ref, gain_ref, g1_ref, dm_ref, gw_ref):
         gates_v = jnp.concatenate([gt_ref[j] for j in range(n)], axis=0)
         dgate_v = jnp.concatenate([dg_ref[j] for j in range(n)], axis=0)
         mean = jnp.sum(gates_v * dgate_v, axis=0, keepdims=True)
@@ -525,18 +552,20 @@
             if hq < 2:
                 part = jnp.concatenate([part, jnp.zeros((rows, 128 - HS * hq), BF)], axis=1)
             dm_ref[i] = part
-        gw_ref[:, 0:D] = dot(side_by_side(m_ref, ctx, hq), low, 0, 0).astype(BF)
+        grad_out = dot(side_by_side(m_ref, ctx, hq), low, 0, 0)
+        for c, value in enumerate(by_core(grad_out, shard)):
+            gw_ref[c, :, 0:D] = value
         grad_router = dot(nm_ref[...], d_logits, 0, 1)
         row = lax.broadcasted_iota(jnp.int32, (128, D), 0)
         cols = jnp.where(row == 33, jnp.broadcast_to(grad_gain, (128, D)), 0.0)
-        cols = jnp.where(row == 32, jnp.broadcast_to(ex_ref[0:1, :], (128, D)), cols)
-        gw_ref[:, D : D + 128] = (grad_router + jnp.transpose(cols)).astype(BF)
-
-    outs = [sds((rows, D), F32), sds((ctx, rows, 128), BF), sds((D, D + 128), BF)]
-    args = [parts, d_gates, gates, g, stream, normed, mixed, packed, packed, gains, extra]
+        for c, value in enumerate(by_core(grad_router + jnp.transpose(cols), shard)):
+            gw_ref[c, :, D : D + 128] = value
+
+    outs = [sds((rows, D), F32), sds((ctx, rows, 128), BF), sds((2, D // 2, D + 128), BF)]
+    args = [parts, d_gates, gates, g, stream, normed, mixed, packed, packed, gains]
     in_specs = [full(a.shape) for a in args]
-    in_specs[7] = pl.BlockSpec((D, D), lambda i: (0, at))
-    in_specs[8] = pl.BlockSpec((D, 128), lambda i: (0, tail))
+    in_specs[7] = pl.BlockSpec((D, D), lambda i: (0, 2))
+    in_specs[8] = pl.BlockSpec((D, 128), lambda i: (0, TAIL))
     return call(
         kernel,
         outs,
@@ -548,36 +577,59 @@
     )
 
 
-def qkv_backward(dx, g1, stream, packed, gains, cos_t, sin_t, ctx):
+def qkv_backward(dx, g1, stream, packed, gains, cos_t, sin_t, ctx, hq, shard):
     rows = g1.shape[0]
-    width = 256 * ctx
-
-    def kernel(d_ref, g_ref, x_ref, w_ref, gain_ref, c_ref, s_ref, out_ref, gain_out, gw_ref):
+    dup = ctx // KEY_VALUE_HEADS
+
+    def kernel(d_ref, g_ref, x_ref, w_ref, gain_ref, c_ref, s_ref, out_ref, gw_ref):
         x = x_ref[...].astype(F32)
         gain = gain_ref[0:1]
         normed = (x * inv_rms_of(x) * gain).astype(BF)
         cos_v = c_ref[...]
         sin_v = s_ref[...]
+        queries = in_order([d_ref[i][:, : HS * hq] for i in range(ctx)])
+        both = []
+        for head in range(KEY_VALUE_HEADS):
+            total = d_ref[head * dup][:, 128:256]
+            if dup > 1:
+                total = total.astype(F32)
+                for r in range(1, dup):
+                    total = total + d_ref[head * dup + r][:, 128:256].astype(F32)
+            both.append(total)
+        keys = in_order([t[:, :HS] for t in both])
+        values = in_order([t[:, HS:] for t in both])
         d_normed = jnp.zeros((rows, D), F32)
-        for i in range(ctx):
-            y = d_ref[i].astype(F32)
-            lin = (y * cos_v - swap_halves(y) * sin_v).astype(BF)
+        for i in range(8):
+            if i < 4:
+                y = queries[:, 256 * i : 256 * (i + 1)]
+            elif i < 6:
+                y = keys[:, 256 * (i - 4) : 256 * (i - 3)]
+            else:
+                y = values[:, 256 * (i - 6) : 256 * (i - 5)]
+            if i < 6:
+                y = y.astype(F32)
+                y = y * cos_v - swap_halves(y) * sin_v
+            lin = y.astype(BF)
             cols = slice(256 * i, 256 * (i + 1))
             d_normed = d_normed + dot(lin, w_ref[:, cols], 1, 1)
-            gw_ref[:, cols] = dot(normed, lin, 0, 0).astype(BF)
+            for c, value in enumerate(by_core(dot(normed, lin, 0, 0), shard)):
+                gw_ref[c, :, cols] = value
         back, grad_gain = norm_back(x, gain, d_normed)
         out_ref[...] = g_ref[...] + back
-        gain_out[...] = jnp.broadcast_to(grad_gain, (8, D))
-
-    outs = [sds((rows, D), F32), sds((8, D), F32), sds((D, width), BF)]
+        row = lax.broadcasted_iota(jnp.int32, (128, D), 0)
+        cols = jnp.where(row == 0, jnp.broadcast_to(grad_gain, (128, D)), 0.0)
+        for c, value in enumerate(by_core(jnp.transpose(cols), shard)):
+            gw_ref[c, :, 2 * D : 2 * D + 128] = value
+
+    outs = [sds((rows, D), F32), sds((2, D // 2, 2 * D + 128), BF)]
     args = [dx, g1, stream, packed, gains, cos_t, sin_t]
     in_specs = [full(a.shape) for a in args]
-    in_specs[3] = pl.BlockSpec((D, width), lambda i: (0, 0))
+    in_specs[3] = pl.BlockSpec((D, 2 * D), lambda i: (0, 0))
     return call(
         kernel,
         outs,
         args,
-        4 * rows * D * width,
+        8 * rows * D * D,
         in_specs=in_specs,
         out_specs=tuple(full(o.shape) for o in outs),
         grid=(1,),
@@ -589,11 +641,22 @@
     return at == slot_row
 
 
-def weight_specs(buffers):
+def weight_specs(weights):
     return [
-        pl.BlockSpec((1,) + shape, lambda e: (e, 0, 0), pipeline_mode=pl.Buffered(buffers))
-        for shape in ((D, F), (D, F), (F, D))
+        pl.BlockSpec((1,) + w.shape[1:], lambda e: (e, 0, 0, 0)) for w in weights
     ]
+
+
+def matrices(first_ref, second_ref):
+    ctx, depth, _ = first_ref.shape[1:]
+    half = F // ctx
+    second = second_ref[0]
+    return (
+        first_ref[0].reshape(D, F),
+        second[:, :depth].reshape(D, F),
+        second[:, depth : depth + half].reshape(F, D // 2),
+        second[:, depth + half :].reshape(F, D // 2),
+    )
 
 
 def experts_forward(x, gates, slots, weights, held):
@@ -601,9 +664,9 @@
     lanes = 2 * SLOTS
 
 
-    def kernel(x_ref, g_ref, s_ref, w0, w1, w2, out_ref, acc_ref, row_ref, eo_ref):
+    def kernel(x_ref, g_ref, s_ref, w0, w1, out_ref, acc_ref, row_ref, eo_ref):
         e = pl.program_id(0)
-        w_gate, w_up, w_down = w0[0], w1[0], w2[0]
+        w_gate, w_up, down_l, down_r = matrices(w0, w1)
         for s in range(n):
             pick = pick_matrix(s_ref[s, pl.ds(e, 1), :], rows).astype(BF)
             row_ref[lanes * s : lanes * (s + 1), :] = dot(pick, x_ref[s]).astype(BF)
@@ -611,7 +674,8 @@
         ga = dot(rws, w_gate)
         up = dot(rws, w_up)
         hidden = (ga * jax.nn.sigmoid(ga) * up).astype(BF)
-        eo_ref[...] = dot(hidden, w_down).astype(BF)
+        eo_ref[:, : D // 2] = dot(hidden, down_l).astype(BF)
+        eo_ref[:, D // 2 :] = dot(hidden, down_r).astype(BF)
         for s in range(n):
             pick = pick_matrix(s_ref[s, pl.ds(e, 1), :], rows)
             gated = jnp.where(pick, g_ref[s, pl.ds(e, 1), :], 0.0).astype(BF)
@@ -635,7 +699,7 @@
         [sds(x.shape, BF)],
         [x, gates, slots] + list(weights),
         flops,
-        in_specs=[full(x.shape), full(gates.shape), full(slots.shape)] + weight_specs(2),
+        in_specs=[full(x.shape), full(gates.shape), full(slots.shape)] + weight_specs(weights),
         out_specs=(full(x.shape),),
         grid=(held,),
         scratch=[
@@ -651,15 +715,15 @@
     lanes = 2 * SLOTS
 
 
-    def kernel(x_ref, gr_ref, g_ref, s_ref, w0, w1, w2, *rest):
+    def kernel(x_ref, gr_ref, g_ref, s_ref, w0, w1, *rest):
         dx_ref, dg_ref = rest[:2]
-        grad_refs, rest = rest[2:5], rest[5:]
+        first_grad, second_grad, *rest = rest[2:]
         if with_out:
             out_ref, acc_ref, row_ref, grow_ref = rest
         else:
             acc_ref, row_ref, grow_ref = rest
         e = pl.program_id(0)
-        w_gate, w_up, w_down = w0[0], w1[0], w2[0]
+        w_gate, w_up, down_l, down_r = matrices(w0, w1)
         slot_gates = []
         for s in range(n):
             mine = slice(lanes * s, lanes * (s + 1))
@@ -678,13 +742,13 @@
         act = ga * sig
         hidden_f = act * up
         hidden = hidden_f.astype(BF)
-        dhg = dot(grows, w_down, 1, 1)
+        dhg = dot(grows[:, : D // 2], down_l, 1, 1) + dot(grows[:, D // 2 :], down_r, 1, 1)
         d_gate = jnp.sum(hidden.astype(F32) * dhg, axis=1, keepdims=True)
         dh = dhg * gate
         dga = (dh * up * (sig * (1.0 + ga * (1.0 - sig)))).astype(BF)
         dup = (dh * act).astype(BF)
         if with_out:
-            eo = dot(hidden, w_down).astype(BF)
+            eo = jnp.concatenate([dot(hidden, down_l), dot(hidden, down_r)], axis=1).astype(BF)
         drow = (dot(dga, w_gate, 1, 1) + dot(dup, w_up, 1, 1)).astype(BF)
         for s in range(n):
             mine = slice(lanes * s, lanes * (s + 1))
@@ -711,12 +775,19 @@
                     final_ref[s] = (held_ref[s].astype(F32) + add).astype(BF)
 
         dslot = (grows.astype(F32) * gate).astype(BF)
-        grads = [dot(rws, dga, 0, 0), dot(rws, dup, 0, 0), dot(hidden, dslot, 0, 0)]
-        for ref, value in zip(grad_refs, grads):
-            ref[0] = value.astype(BF)
+        ctx, depth, _ = first_grad.shape[1:]
+        part = F // ctx
+        first_grad[0] = dot(rws, dga, 0, 0).astype(BF).reshape(ctx, depth, F)
+        second_grad[0, :, :depth, :] = dot(rws, dup, 0, 0).astype(BF).reshape(ctx, depth, F)
+        for k in range(2):
+            cols = dslot[:, D // 2 * k : D // 2 * (k + 1)]
+            at_row = depth + part * k
+            second_grad[0, :, at_row : at_row + part, :] = (
+                dot(hidden, cols, 0, 0).astype(BF).reshape(ctx, part, D // 2)
+            )
 
     outs = [sds(x.shape, BF), sds(gates.shape, F32)] + [sds(w.shape, BF) for w in weights]
-    out_specs = [full(x.shape), full(gates.shape)] + weight_specs(2)
+    out_specs = [full(x.shape), full(gates.shape)] + weight_specs(weights)
     scratch = [
         pltpu.VMEM(x.shape, F32),
         pltpu.VMEM((n * lanes, D), BF),
@@ -732,7 +803,7 @@
         [x, g, gates, slots] + list(weights),
         flops,
         in_specs=[full(x.shape), full(g.shape), full(gates.shape), full(slots.shape)]
-        + weight_specs(2),
+        + weight_specs(weights),
         out_specs=tuple(out_specs),
         grid=(held,),
         scratch=scratch,
@@ -760,7 +831,6 @@
     rows = micro * tok
     grp_size, ctx, planes = sizes
     hq = QUERY_HEADS // ctx
-    dup = ctx // KEY_VALUE_HEADS
     held = 2 * grp_size
     every = ("grp", "zq", "zp", "core")
     line = ("zq", "zp", "core")
@@ -775,14 +845,12 @@
         return y.reshape(x.shape)
 
     def pack(layer):
-        wq = w_query[layer].reshape(shard, ctx, HS * hq)
-        if hq < 2:
-            wq = jnp.pad(wq, ((0, 0), (0, 0), (0, 128 - HS * hq)))
-        wk = jnp.repeat(key_weight[layer].reshape(shard, KEY_VALUE_HEADS, HS), dup, axis=1)
-        wv = jnp.repeat(value_weight[layer].reshape(shard, KEY_VALUE_HEADS, HS), dup, axis=1)
-        qkv = jnp.concatenate([wq, wk, wv], axis=2).reshape(shard, ctx * 256)
-        tail = jnp.concatenate(
+        return jnp.concatenate(
             [
+                w_query[layer],
+                key_weight[layer],
+                value_weight[layer],
+                w_output[layer],
                 by_plane(w_router[layer], 1),
                 attn_gain[layer][:, None],
                 ffn_gain[layer][:, None],
@@ -790,7 +858,6 @@
             ],
             axis=1,
         )
-        return jnp.concatenate([qkv, w_output[layer], tail], axis=1)
 
     ids_of = iter(range(1, 100))
 
@@ -800,18 +867,21 @@
     def swap(x):
         return lax.ppermute(x, "core", [(0, 1), (1, 0)])
 
-    def picks(layer, members):
-        ws = (w_gate[layer], w_up[layer], w_down[layer])
-        return [(ws[k], "line", "pick") for k in members]
+    def second_shard(layer):
+        down = w_down[layer]
+        return jnp.concatenate([w_up[layer], down[:, :, : D // 2], down[:, :, D // 2 :]], axis=1)
 
     def plane_gather(w):
-        w = w.reshape(1, w.shape[0] * w.shape[1], w.shape[2])
-        return lax.all_gather(w, ("grp", "core"), axis=0, tiled=True)
+        return lax.all_gather(w[None], ("grp", "core"), axis=0, tiled=True)
 
     grad_rows = grad_out.reshape(rows, D)
-    first, *ready = move((pack(0), None, "packed"), *picks(0, (0, 1, 2)))
+    (gate_parts,) = move((w_gate[0], "line", "pick"))
+    gate_parts, own_pack, own_second = lax.optimization_barrier(
+        (gate_parts, pack(0), second_shard(0))
+    )
+    first, second_parts = move((own_pack, None, "packed"), (own_second, "line", "pick"))
     packed = [first.reshape(D, -1), None]
-    weights = [[plane_gather(w) for w in ready], []]
+    weights = [[plane_gather(gate_parts), plane_gather(second_parts)], None]
 
     own_segments = lax.dynamic_slice_in_dim(segments, ctx_index * tok, tok, axis=1)
     prompt = jnp.sum((segments == 0).astype(jnp.int32), axis=1, dtype=jnp.int32)
@@ -828,10 +898,9 @@
         (lane % (HS // 2)).astype(F32) * (-2.0 * math.log(10000.0) / HS)
     )
     angles = places[:, None] * freqs[None, :]
-    turned = (lane < 192)[None, :]
     sign = jnp.where((lane % HS) < HS // 2, -1.0, 1.0)[None, :]
-    cos_t = jnp.where(turned, jnp.cos(angles), 1.0)
-    sin_t = jnp.where(turned, jnp.sin(angles) * sign, 0.0)
+    cos_t = jnp.cos(angles)
+    sin_t = jnp.sin(angles) * sign
     seg_row = segments[:, None, :]
     seg_col = segments[:, :, None]
 
@@ -849,111 +918,135 @@
     slot = slot.reshape(planes, held, rows)
     chosen_f = chosen.astype(F32)
 
-    last_g = lax.all_gather(grad_rows, "zp", axis=0, tiled=False)
-
     saved = []
     parts = (hidden_in.reshape(rows, D),)
     for layer in range(LAYERS):
-        got = qkv_forward(parts, packed[layer], cos_t, sin_t, ctx)
+        got = qkv_forward(parts, packed[layer], cos_t, sin_t, ctx, hq)
         qkv, gains = got[0], got[1]
         stream = parts[0] if layer == 0 else got[2]
-        heads = lax.all_to_all(qkv, line, 0, 0, tiled=True)
+        (heads,) = move((qkv, "line", "own"))
         out, lse = attention_forward(heads, seg_row, seg_col, ctx, hq, tok)
-        mixed = lax.all_to_all(out, line, 0, 0, tiled=True)
+        (mixed,) = move((out, "line", "own"))
         stream1, normed, gates = output_forward(
             mixed, stream, packed[layer], gains, chosen_f, ctx, hq, planes, held
         )
         ops = [(normed, "tok", "all"), (gates, "tok", "own")]
         if layer == 0:
-            xs, gates_here, slots_here, second, *ready = move(
-                *ops, (slot, "tok", "own"), (pack(1), None, "packed"), *picks(1, (0,))
+            xs, gates_here, slots_here, late_gate = move(
+                *ops, (slot, "tok", "own"), (w_gate[1], "line", "pick")
             )
-            packed[1] = second.reshape(D, -1)
-            weights[1] += [plane_gather(w) for w in ready]
+            late_g, late_second, _ = lax.optimization_barrier(
+                (grad_rows, second_shard(1), xs)
+            )
+            last_g = lax.all_gather(late_g, "zp", axis=0, tiled=False)
+            late_gate = plane_gather(late_gate)
         else:
             xs, gates_here = move(*ops)
         saved.append((stream, heads, out, lse, mixed, stream1, normed, gates, gains, xs, gates_here))
         if layer == 0:
             sent = experts_forward(xs, gates_here, slots_here, weights[0], held)
-            came, *ready = move((sent, "tok", "own"), *picks(1, (1, 2)))
-            weights[1] += [plane_gather(w) for w in ready]
+            came, after, late_second = move(
+                (sent, "tok", "own"), (pack(1), None, "packed"), (late_second, "line", "pick")
+            )
+            packed[1] = after.reshape(D, -1)
+            weights[1] = [late_gate, plane_gather(late_second)]
             parts = (stream1, came)
 
     def plane_scatter(r):
-        r = lax.psum_scatter(r, ("grp", "core"), scatter_dimension=0, tiled=True)
-        return r.reshape(ctx, r.shape[1] // ctx, r.shape[2])
+        return lax.psum_scatter(r, ("grp", "core"), scatter_dimension=0, tiled=True)[0]
 
     def owned_rows(r):
         r = r.astype(F32).reshape((ctx // (2 * planes), 2 * planes) + r.shape[1:])
         return jnp.sum(r, axis=0)
 
+    def between_cores(x):
+        theirs = lax.dynamic_index_in_dim(x, 1 - core, 0, keepdims=False)
+        return with_other(x, swap(theirs))
+
+    def with_other(x, came):
+        ours = lax.dynamic_index_in_dim(x, core, 0, keepdims=False)
+        return by_owner((ours.astype(F32) + came.astype(F32)).astype(BF))
+
+    def by_owner(x):
+        return x.reshape(grp_size, ctx // 2, shard, x.shape[1])
+
+    def over_grp(x):
+        return jnp.sum(x.astype(F32), axis=0).astype(BF)
+
     g = grad_rows
-    extra = jnp.zeros((8, D), F32)
-    small = [None] * LAYERS
-    wide = [None] * LAYERS
-    expert = [None] * LAYERS
     for layer in reversed(range(LAYERS)):
         stream, heads, out, lse, mixed, stream1, normed, gates, gains, xs, gates_here = saved[layer]
         last = layer == LAYERS - 1
         if last:
             gs = last_g
         else:
-            gs, last_gate, last_up = move(
-                (g.astype(BF), "tok", "all"),
-                (expert[1][0], "line", "own"),
-                (expert[1][1], "line", "own"),
+            gs, last_small, came = move(
+                (g.astype(BF), "tok", "all"), (over_grp(small), "z", "own"), (wide, "sib", "own")
+            )
+            wide = with_other(wide, came)
+            gs, *last_experts = lax.optimization_barrier((gs, *last_experts))
+            last_experts = [lax.all_to_all(r, line, 0, 0, tiled=True) for r in last_experts]
+            final_parts, _ = lax.optimization_barrier((final_parts, gs))
+            final_sum = lax.psum_scatter(final_parts, "zp", scatter_dimension=0, tiled=True)
+            hidden_out = (
+                (saved[1][5] + final_sum[0].astype(F32)).astype(BF).reshape(micro, tok, D)
             )
         res = experts_backward(xs, gs, gates_here, slots_here, weights[layer], held, last)
-        expert[layer] = [plane_scatter(r) for r in res[2:5]]
+        if not last:
+            *res, last_second = lax.optimization_barrier((*res, last_experts[1]))
+            last_experts[1] = last_second
+        experts = [plane_scatter(r) for r in res[2:4]]
         back = [(res[0], "tok", "own"), (res[1], "tok", "own")]
         if last:
-            d_parts, d_gates, final_parts = move(*back, (res[5], "tok", "own"))
-            hidden_out = (
-                (stream1 + jnp.sum(final_parts.astype(F32), axis=0))
-                .astype(BF)
-                .reshape(micro, tok, D)
-            )
+            last_experts = experts
+            final_parts = res[4]
+            d_parts, d_gates = move(*back)
         else:
-            d_parts, d_gates, last_down = move(*back, (expert[1][2], "line", "own"))
-        g1, d_mixed, small[layer] = output_backward(
-            d_parts, d_gates, gates, g, stream1, normed, mixed, packed[layer], gains, extra,
-            ctx, hq, planes, held,
+            d_parts, d_gates, last_wide = move(*back, (wide, "g", "own"))
+        g1, d_mixed, small = output_backward(
+            d_parts, d_gates, gates, g, stream1, normed, mixed, packed[layer], gains,
+            ctx, hq, planes, shard,
         )
-        d_out = lax.all_to_all(d_mixed, line, 0, 0, tiled=True)
+        ops = [(d_mixed, "line", "own"), (small, "sib", "own")]
+        if last:
+            d_out, came = move(*ops)
+        else:
+            d_out, came, last_wide = move(*ops, (over_grp(last_wide), "z", "own"))
+        small = with_other(small, came)
         dx = attention_backward(heads, d_out, out, lse, seg_row, seg_col, ctx, hq, tok)
-        dx = lax.all_to_all(dx, line, 0, 0, tiled=True)
-        g, extra, wide[layer] = qkv_backward(
-            dx, g1, stream, packed[layer], gains, cos_t, sin_t, ctx
+        dx, small = move((dx, "line", "own"), (small, "g", "own"))
+        g, wide = qkv_backward(
+            dx, g1, stream, packed[layer], gains, cos_t, sin_t, ctx, hq, shard
         )
-    at_34 = jnp.arange(D + 128) == D + 34
-    small[0] = jnp.where(at_34[None, :], extra[0][:, None].astype(BF), small[0])
-    joined = [jnp.concatenate([wide[k], small[k]], axis=1) for k in range(LAYERS)]
-    last_owned = lax.psum_scatter(joined[1], every, scatter_dimension=0, tiled=True)
-    halves = joined[0].reshape(grp_size, ctx // 2, 2, shard, -1)
-    theirs = lax.dynamic_index_in_dim(halves, 1 - core, 2, keepdims=False)
-    ours = lax.dynamic_index_in_dim(halves, core, 2, keepdims=False)
-    chip = (ours.astype(F32) + swap(theirs).astype(F32)).astype(BF)
-    plane, first_gate, first_up = move(
-        (chip, "g", "own"), (expert[0][0], "line", "own"), (expert[0][1], "line", "own")
-    )
-    plane = jnp.sum(plane.astype(F32), axis=0).astype(BF)
-    column, first_down = move((plane, "z", "own"), (expert[0][2], "line", "own"))
-    owned_attn = [jnp.sum(column.astype(F32), axis=0), last_owned.astype(F32)]
-    owned_experts = [
-        [owned_rows(r) for r in (first_gate, first_up, first_down)],
-        [owned_rows(r) for r in (last_gate, last_up, last_down)],
-    ]
+    first_wide, first_gate, first_small = move(
+        (between_cores(wide), "g", "own"),
+        (experts[0], "line", "own"),
+        (over_grp(small), "z", "own"),
+    )
+    first_wide, first_second = move(
+        (over_grp(first_wide), "z", "own"), (experts[1], "line", "own")
+    )
+
+    def along_z(x):
+        return jnp.sum(x.astype(F32), axis=0)
+
+    wides = [along_z(first_wide), along_z(last_wide)]
+    smalls = [along_z(first_small), along_z(last_small)]
+    def matrices_of(first, second):
+        first, second = owned_rows(first), owned_rows(second)
+        depth, part = D // ctx, F // ctx
+        down = [second[:, depth + part * k : depth + part * (k + 1)] for k in range(2)]
+        return first, second[:, :depth], jnp.concatenate(down, axis=2)
+
+    owned_experts = [matrices_of(first_gate, first_second), matrices_of(*last_experts)]
 
     def unpack(layer):
-        w = owned_attn[layer][:, : 256 * ctx].reshape(shard, ctx, 256)
-        gq = w[:, :, : HS * hq].reshape(shard, QUERY_HEADS * HS)
-        gk = w[:, :, 128:192].reshape(shard, KEY_VALUE_HEADS, dup, HS).sum(axis=2)
-        gv = w[:, :, 192:256].reshape(shard, KEY_VALUE_HEADS, dup, HS).sum(axis=2)
-        s = owned_attn[layer][:, 256 * ctx :]
+        w, s = wides[layer], smalls[layer]
+        kv = KEY_VALUE_HEADS * HS
         return (
-            gq,
-            gk.reshape(shard, KEY_VALUE_HEADS * HS),
-            gv.reshape(shard, KEY_VALUE_HEADS * HS),
+            w[:, :D],
+            w[:, D : D + kv],
+            w[:, D + kv : 2 * D],
             s[:, :D],
             s[:, D + 33],
             by_plane(s[:, D : D + E], 1, back=True),
@@ -964,10 +1057,7 @@
     def stacked(k):
         return jnp.stack([got[layer][k] for layer in range(LAYERS)])
 
-    gain_grad = jnp.stack(
-        [owned_attn[0][:, 256 * ctx + D + 34]]
-        + [owned_attn[k][:, 256 * ctx + D + 32] for k in range(LAYERS - 1)]
-    )
+    gain_grad = jnp.stack([w[:, 2 * D] for w in wides])
 
     def owned(k):
         return jnp.stack([owned_experts[layer][k] for layer in range(LAYERS)])

time: 1350 us -> 1190 us (0.88)
  blocking collectives: 145 us -> 0 us
  waiting for transfers between devices: 123 us -> 41.1 us
  Pallas kernels: 963 us -> 1020 us
    all_to_all x5 -> x0, blocking collectives: 145 us -> none  [the longest x2 57.3 us: per_device(): d_out = lax.all_to_all(d_mixed, line, 0, 0, tiled=True)]
    pallas_call x9 -> x18, Pallas kernels: 712 us -> 774 us  [transfer(): pl.pallas_call(kernel, out_shape=tuple(shapes), in_specs=[any_spec] * cou...]
    all_to_all x3 -> x2, waiting for transfers between devices: 63 us -> 26.7 us  [per_device(): lax.all_to_all(r, line, 0, 0, tiled=True)]
    reduce_scatter x7 -> x5, waiting for transfers between devices: 43.1 us -> 12.4 us  [the longest x4 12.4 us: plane_scatter(): lax.psum_scatter(r, ('grp', 'core'), scatter_dimension=0, tiled=True)[0]]
  transfers between devices with their start and end apart: 18 -> 13, of which waited for: 6 -> 2; matrix products, arithmetic and copies ran while one was open for 3% -> 5% of each run, Pallas kernels for 58% -> 76%
where the time goes in v3:
time: 1190 us; the launch traced here: 1170 us
  Pallas kernels  1020 us (86%)
  other arithmetic  50 us (4%)
  waiting for transfers between devices  41.1 us (3%)
  local copies, waits for them, and re-layouts  24.2 us (2%)
  between operations  15.3 us (1%)
    pallas_call x18, Pallas kernels, transfer(): pl.pallas_call(kernel, out_shape=tuple(shapes), in_specs=[any_spec] * cou...  774 us
    pallas_call x15, Pallas kernels, call(): pl.pallas_call(kernel, out_shape=tuple(outs), scratch_shapes=list(scratch...  250 us
    all_to_all x2, waiting for transfers between devices, per_device(): lax.all_to_all(r, line, 0, 0, tiled=True)  26.7 us
  transfers between devices with their start and end apart: 13, of which 2 were waited for; matrix products, arithmetic and copies ran while one was open for 5% of the time, Pallas kernels for 76%

profile of v3, /device:TPU:0, one launch (start us, length us, event | category | flops | bytes accessed | tf_op | source)
XLA Modules:
  0.0 1165.4 jit_solution(2315187083436254014)
XLA Ops:
  7.3 3.2 slice_bitcast_fusion.4
  10.5 23.0 %shard_map.229 = bf16[8,128,512]{2,1,0:T(8,128)(2,1)} custom-call(bf16[8,128,512]{2,1,0:T(8,128)(2,1)} %get-tuple-element.219.refs_0_), custom_call_target="tpu_custom_call" | custom-call | bytes 41943040 | tf_op jit(solution)/shard_map/pallas_call | solution.py:268
  39.1 70.1 %shard_map.230 = (bf16[4,8,32,3200]{3,2,1,0:T(8,128)(2,1)}, bf16[8,256,512]{2,1,0:T(8,128)(2,1)}) custom-call(bf16[32,3200]{1,0:T(8,128)(2,1)} %concatenate.18.refs_0_, bf16[8,256,512]{2,1,0:T(8,128)(2,1)} %pad_maximum_fusion.2.refs_1_), custom_call_target="tpu_custom_call" | custom-call | bytes 346030080 | tf_op jit(solution)/shard_map/pallas_call | solution.py:268
  112.2 5.1 shard_map.231
  117.3 23.5 %shard_map.232.x_ref = bf16[8,256,256]{2,1,0:T(8,128)(2,1)} custom-call(bf16[8,256,256]{2,1,0:T(8,128)(2,1)} %get-tuple-element.96.refs_0_), custom_call_target="tpu_custom_call" | custom-call | bytes 41943040 | tf_op jit(solution)/shard_map/pallas_call | solution.py:268
  142.1 9.7 shard_map.233
  151.8 17.9 %shard_map.234.m_ref = bf16[8,256,128]{2,1,0:T(8,128)(2,1)} custom-call(bf16[8,256,128]{2,1,0:T(8,128)(2,1)} %get-tuple-element.97.refs_0_.o_ref), custom_call_target="tpu_custom_call" | custom-call | bytes 20971520 | tf_op jit(solution)/shard_map/pallas_call | solution.py:268
  170.8 4.0 shard_map.235
  175.4 68.7 %shard_map.236 = (bf16[4,256,1024]{2,1,0:T(8,128)(2,1)}, f32[4,8,256]{2,1,0:T(8,128)}, s32[4,8,256]{2,1,0:T(8,128)}, bf16[8,128,512]{2,1,0:T(8,128)(2,1)}) custom-call(bf16[256,1024]{1,0:T(8,128)(2,1)} %get-tuple-element.100.refs_0_.nm_ref, f32[4,8,256]{2,1,0:T(8,128)} %get-tuple-element.101.refs_1_.gt_ref, s32[4,8,256]{2,1,0:T(8,128)} %bitcast_select_fusion.refs_2_, ...), custom_call_target="tpu_custom_call" | custom-call | bytes 128450560 | tf_op jit(solution)/shard_map/pallas_call | solution.py:268
  247.7 29.9 %shard_map.237.refs_0_ = bf16[4,256,1024]{2,1,0:T(8,128)(2,1)} custom-call(bf16[4,256,1024]{2,1,0:T(8,128)(2,1)} %get-tuple-element.102.x_ref, f32[4,8,256]{2,1,0:T(8,128)} %get-tuple-element.103.g_ref, s32[4,8,256]{2,1,0:T(8,128)} %get-tuple-element.104.s_ref, bf16[8,8,128,512]{3,2,1,0:T(8,128)(2,1)} %bitcast.180, bf16[8,8,256,512]{3,2,1,0:T(8,128)(2,1)} %bitcast.177), custom_call_target="tpu_custom_call" | custom-call | flops 12884901888 | bytes 29425664 | tf_op jit(solution)/shard_map/pallas_call | solution.py:44
  277.6 135.9 %shard_map.238 = (bf16[4,256,1024]{2,1,0:T(8,128)(2,1)}, bf16[4,8,32,3200]{3,2,1,0:T(8,128)(2,1)}, bf16[8,256,512]{2,1,0:T(8,128)(2,1)}) custom-call(bf16[4,256,1024]{2,1,0:T(8,128)(2,1)} %shard_map.237.refs_0_, bf16[32,3200]{1,0:T(8,128)(2,1)} %concatenate.20.refs_1_, bf16[8,256,512]{2,1,0:T(8,128)(2,1)} %pad_maximum_fusion.3.refs_2_), custom_call_target="tpu_custom_call" | custom-call | bytes 429916160 | tf_op jit(solution)/shard_map/pallas_call | solution.py:268
  413.6 6.0 shard_map.239
  419.6 21.4 %shard_map.240.x_ref = bf16[8,256,256]{2,1,0:T(8,128)(2,1)} custom-call(bf16[8,256,256]{2,1,0:T(8,128)(2,1)} %get-tuple-element.110.refs_0_), custom_call_target="tpu_custom_call" | custom-call | bytes 41943040 | tf_op jit(solution)/shard_map/pallas_call | solution.py:268
  441.1 9.7 shard_map.241
  450.8 17.9 %shard_map.242.m_ref = bf16[8,256,128]{2,1,0:T(8,128)(2,1)} custom-call(bf16[8,256,128]{2,1,0:T(8,128)(2,1)} %get-tuple-element.111.refs_0_.o_ref), custom_call_target="tpu_custom_call" | custom-call | bytes 20971520 | tf_op jit(solution)/shard_map/pallas_call | solution.py:268
  468.7 4.1 shard_map.243
  472.8 53.3 %shard_map.244 = (bf16[4,256,1024]{2,1,0:T(8,128)(2,1)}, f32[4,8,256]{2,1,0:T(8,128)}) custom-call(bf16[256,1024]{1,0:T(8,128)(2,1)} %get-tuple-element.115.refs_0_.nm_ref, f32[4,8,256]{2,1,0:T(8,128)} %get-tuple-element.116.refs_1_.gt_ref), custom_call_target="tpu_custom_call" | custom-call | bytes 85196800 | tf_op jit(solution)/shard_map/pallas_call | solution.py:268
  526.1 67.0 %shard_map.245 = (bf16[4,256,1024]{2,1,0:T(8,128)(2,1)}, f32[4,8,256]{2,1,0:T(8,128)}, bf16[8,8,128,512]{3,2,1,0:T(8,128)(2,1)}, bf16[8,8,256,512]{3,2,1,0:T(8,128)(2,1)}, bf16[4,256,1024]{2,1,0:T(8,128)(2,1)}) custom-call(bf16[4,256,1024]{2,1,0:T(8,128)(2,1)} %get-tuple-element.117.x_ref, bf16[4,256,1024]{2,1,0:T(8,128)(2,1)} %bitcast.183, ...), custom_call_target="tpu_custom_call" | custom-call | flops 33822867456 | bytes 58818560 | tf_op jit(solution)/shard_map/pallas_call | solution.py:44
  594.0 49.5 %shard_map.246 = (bf16[4,256,1024]{2,1,0:T(8,128)(2,1)}, f32[4,8,256]{2,1,0:T(8,128)}) custom-call(bf16[4,256,1024]{2,1,0:T(8,128)(2,1)} %get-tuple-element.123.refs_0_, f32[4,8,256]{2,1,0:T(8,128)} %get-tuple-element.124.refs_1_), custom_call_target="tpu_custom_call" | custom-call | bytes 85196800 | tf_op jit(solution)/shard_map/pallas_call | solution.py:268
  643.5 6.7 shard_map.247
  650.2 12.1 %shard_map.248 = (bf16[8,256,128]{2,1,0:T(8,128)(2,1)}, bf16[512,1152]{1,0:T(8,128)(2,1)}) custom-call(bf16[8,256,128]{2,1,0:T(8,128)(2,1)} %get-tuple-element.127.refs_0_, bf16[2,512,1152]{2,1,0:T(8,128)(2,1)} %get-tuple-element.128.refs_1_), custom_call_target="tpu_custom_call" | custom-call | bytes 68157440 | tf_op jit(solution)/shard_map/pallas_call | solution.py:268
  662.4 13.7 %shard_map.249.refs_0_ = bf16[8,256,256]{2,1,0:T(8,128)(2,1)} custom-call(bf16[8,256,256]{2,1,0:T(8,128)(2,1)} %shard_map.240.x_ref, bf16[8,256,128]{2,1,0:T(8,128)(2,1)} %get-tuple-element.129.d_ref, bf16[8,256,128]{2,1,0:T(8,128)(2,1)} %get-tuple-element.111.refs_0_.o_ref, f32[2,1024,128]{2,1,0:T(8,128)} %get-tuple-element.130.l_ref, ...), custom_call_target="tpu_custom_call" | custom-call | flops 1342177280 | bytes 4210688 | tf_op jit(solution)/shard_map/pallas_call | solution.py:44
  677.4 28.8 %shard_map.250 = (bf16[8,256,256]{2,1,0:T(8,128)(2,1)}, bf16[4,4,32,1152]{3,2,1,0:T(8,128)(2,1)}) custom-call(bf16[8,256,256]{2,1,0:T(8,128)(2,1)} %shard_map.249.refs_0_, bf16[4,4,32,1152]{3,2,1,0:T(8,128)(2,1)} %bitcast.153), custom_call_target="tpu_custom_call" | custom-call | bytes 89128960 | tf_op jit(solution)/shard_map/pallas_call | solution.py:268
  706.2 8.5 shard_map.251
  714.7 2.2 convert_element_type.130.refs_0_
  717.9 60.9 %shard_map.252 = (bf16[4,256,1024]{2,1,0:T(8,128)(2,1)}, bf16[4,32,1152]{2,1,0:T(8,128)(2,1)}, bf16[512,2176]{1,0:T(8,128)(2,1)}) custom-call(bf16[256,1024]{1,0:T(8,128)(2,1)} %convert_element_type.130.refs_0_, bf16[4,32,1152]{2,1,0:T(8,128)(2,1)} %reduce_sum.120.refs_1_, bf16[2,512,2176]{2,1,0:T(8,128)(2,1)} %get-tuple-element.136.refs_2_), custom_call_target="tpu_custom_call" | custom-call | bytes 184811520 | tf_op jit(solution)/shard_map/pallas_call | solution.py:268
  778.8 12.4 %reduce-scatter.8.cloned.1.call-done = bf16[1,8,256,512]{3,2,1,0:T(8,128)(2,1)} async-done(((bf16[8,8,256,512]{3,2,1,0:T(8,128)(2,1)}), bf16[1,8,256,512]{3,2,1,0:T(8,128)(2,1)}) %reduce-scatter.8.cloned.1.call-update) | async-done | bytes 2097168 | tf_op jit(solution)/shard_map/reduce_scatter | solution.py:956
  791.3 4.6 all-to-all-start
  795.9 56.0 %shard_map.253 = (bf16[4,256,1024]{2,1,0:T(8,128)(2,1)}, f32[4,8,256]{2,1,0:T(8,128)}, bf16[8,8,128,512]{3,2,1,0:T(8,128)(2,1)}, bf16[8,8,256,512]{3,2,1,0:T(8,128)(2,1)}) custom-call(bf16[4,256,1024]{2,1,0:T(8,128)(2,1)} %get-tuple-element.102.x_ref, bf16[4,256,1024]{2,1,0:T(8,128)(2,1)} %get-tuple-element.140.gr_ref, ...), custom_call_target="tpu_custom_call" | custom-call | flops 33822867456 | bytes 56721408 | tf_op jit(solution)/shard_map/pallas_call | solution.py:44
  851.9 26.7 %all-to-all-done = bf16[8,256,512]{2,1,0:T(8,128)(2,1)S(1)} async-done(((bf16[8,256,512]{2,1,0:T(8,128)(2,1)}), bf16[8,256,512]{2,1,0:T(8,128)(2,1)S(1)}, u32[]{:S(2)}, u32[]{:S(2)}) %all-to-all-start) | async-done | bytes 2097184 | tf_op jit(solution)/shard_map/all_to_all | solution.py:988
  879.2 4.2 fusion.1
  883.4 49.3 %shard_map.254 = (bf16[4,256,1024]{2,1,0:T(8,128)(2,1)}, f32[4,8,256]{2,1,0:T(8,128)}, bf16[4,4,32,2176]{3,2,1,0:T(8,128)(2,1)}) custom-call(bf16[4,256,1024]{2,1,0:T(8,128)(2,1)} %get-tuple-element.147.refs_0_, f32[4,8,256]{2,1,0:T(8,128)} %get-tuple-element.148.refs_1_, bf16[4,4,32,2176]{3,2,1,0:T(8,128)(2,1)} %bitcast.149), custom_call_target="tpu_custom_call" | custom-call | bytes 174325760 | tf_op jit(solution)/shard_map/pallas_call | solution.py:268
  932.7 2.9 reduce_sum.121.refs_2_
  935.6 6.8 shard_map.255
  942.4 25.4 %shard_map.256 = (bf16[8,256,128]{2,1,0:T(8,128)(2,1)}, bf16[512,1152]{1,0:T(8,128)(2,1)}, bf16[4,32,2176]{2,1,0:T(8,128)(2,1)}) custom-call(bf16[8,256,128]{2,1,0:T(8,128)(2,1)} %get-tuple-element.152.refs_0_, bf16[2,512,1152]{2,1,0:T(8,128)(2,1)} %get-tuple-element.153.refs_1_, bf16[4,32,2176]{2,1,0:T(8,128)(2,1)} %reduce_sum.121.refs_2_), custom_call_target="tpu_custom_call" | custom-call | bytes 90439680 | tf_op jit(solution)/shard_map/pallas_call | solution.py:268
  967.9 14.5 %shard_map.257.refs_0_ = bf16[8,256,256]{2,1,0:T(8,128)(2,1)} custom-call(bf16[8,256,256]{2,1,0:T(8,128)(2,1)} %shard_map.232.x_ref, bf16[8,256,128]{2,1,0:T(8,128)(2,1)} %get-tuple-element.155.d_ref, bf16[8,256,128]{2,1,0:T(8,128)(2,1)} %get-tuple-element.97.refs_0_.o_ref, f32[2,1024,128]{2,1,0:T(8,128)} %get-tuple-element.156.l_ref, ...), custom_call_target="tpu_custom_call" | custom-call | flops 1342177280 | bytes 4210688 | tf_op jit(solution)/shard_map/pallas_call | solution.py:44
  983.7 27.2 %shard_map.258 = (bf16[8,256,256]{2,1,0:T(8,128)(2,1)}, bf16[4,4,32,1152]{3,2,1,0:T(8,128)(2,1)}) custom-call(bf16[8,256,256]{2,1,0:T(8,128)(2,1)} %shard_map.257.refs_0_, bf16[4,4,32,1152]{3,2,1,0:T(8,128)(2,1)} %bitcast.154), custom_call_target="tpu_custom_call" | custom-call | bytes 89128960 | tf_op jit(solution)/shard_map/pallas_call | solution.py:268
  1010.9 8.6 shard_map.259
  1019.6 3.2 dynamic-slice_bitcast_fusion
  1024.3 5.2 all-to-all-start.1
  1036.8 4.4 fusion
  1041.3 42.8 %shard_map.260 = (bf16[4,4,32,2176]{3,2,1,0:T(8,128)(2,1)}, bf16[8,128,512]{2,1,0:T(8,128)(2,1)}, bf16[4,32,1152]{2,1,0:T(8,128)(2,1)}) custom-call(bf16[4,4,32,2176]{3,2,1,0:T(8,128)(2,1)} %bitcast.148, bf16[8,128,512]{2,1,0:T(8,128)(2,1)} %bitcast.159, bf16[4,32,1152]{2,1,0:T(8,128)(2,1)} %reduce_sum.122.refs_2_), custom_call_target="tpu_custom_call" | custom-call | bytes 142868480 | tf_op jit(solution)/shard_map/pallas_call | solution.py:268
  1084.1 3.1 reduce_sum.123.refs_0_
  1095.9 3.5 maximum_convert_fusion
  1099.4 46.2 %shard_map.261 = (bf16[4,32,2176]{2,1,0:T(8,128)(2,1)}, bf16[8,256,512]{2,1,0:T(8,128)(2,1)}) custom-call(bf16[4,32,2176]{2,1,0:T(8,128)(2,1)} %reduce_sum.123.refs_0_, bf16[8,256,512]{2,1,0:T(8,128)(2,1)} %bitcast.157), custom_call_target="tpu_custom_call" | custom-call | bytes 106168320 | tf_op jit(solution)/shard_map/pallas_call | solution.py:268
  1146.9 2.3 convert_element_type.150
  1152.8 2.7 pad_maximum_fusion
  1155.7 2.3 pad_maximum_fusion.1
  (165 shorter events, 42.8 us)
Async XLA Ops:
  7.2 26.2 %copy-start.21 = (bf16[2,32,32]{2,1,0:T(8,128)(2,1)S(1)}, bf16[2,32,32]{2,1,0:T(8,128)(2,1)}, u32[]{:S(2)}) copy-start(bf16[2,32,32]{2,1,0:T(8,128)(2,1)} %param.24) | copy-start | bytes 12292
  7.2 26.4 %copy-start.23 = (bf16[2,32]{1,0:T(2,128)(2,1)S(1)}, bf16[2,32]{1,0:T(2,128)(2,1)}, u32[]{:S(2)}) copy-start(bf16[2,32]{1,0:T(2,128)(2,1)} %param.18) | copy-start | bytes 388
  7.2 26.5 %copy-start.24 = (bf16[2,32]{1,0:T(2,128)(2,1)S(1)}, bf16[2,32]{1,0:T(2,128)(2,1)}, u32[]{:S(2)}) copy-start(bf16[2,32]{1,0:T(2,128)(2,1)} %param.23) | copy-start | bytes 388
  7.2 26.7 %copy-start.5 = (bf16[2,8,64,1024]{3,2,1,0:T(8,128)(2,1)S(1)}, bf16[2,8,64,1024]{3,2,1,0:T(8,128)(2,1)}, u32[]{:S(2)}) copy-start(bf16[2,8,64,1024]{3,2,1,0:T(8,128)(2,1)} %param.27) | copy-start | bytes 6291460
  7.2 240.5 %all-gather.11.cloned.1.call-start = ((), (), s32[]{:S(2)}) async-start(), calls=%async_computation.12 | async-start | bytes 9437184 | tf_op jit(solution)/shard_map/all_gather | solution.py:875
  33.9 1.6 copy-start.6
  35.5 0.9 copy-start.17
  35.5 1.0 copy-start.18
  35.5 1.0 copy-start.19
  35.5 1.0 copy-start.20
  39.0 70.3 %copy-start.16 = (s32[2,1024]{1,0:T(2,128)S(1)}, s32[2,1024]{1,0:T(2,128)}, u32[]{:S(2)}) copy-start(s32[2,1024]{1,0:T(2,128)} %param.16) | copy-start | bytes 24580
  39.0 208.7 %all-gather.13.cloned.1.call-start = ((), (), s32[]{:S(2)}) async-start(), calls=%async_computation.13 | async-start | bytes 18874368 | tf_op jit(solution)/shard_map/all_gather | solution.py:875
  109.3 416.8 %all-gather.15.cloned.1.call-start = ((), (), s32[]{:S(2)}) async-start(), calls=%async_computation.14 | async-start | bytes 2621440 | tf_op jit(solution)/shard_map/all_gather | solution.py:941
  140.7 29.1 %copy-start.22 = (s32[2,128,8]{1,2,0:T(8,128)S(1)}, s32[2,128,8]{1,2,0:T(8,128)}, u32[]{:S(2)}) copy-start(s32[2,128,8]{1,2,0:T(8,128)} %param.17) | copy-start | bytes 24580
  245.7 280.4 %all-gather.17.cloned.1.call-start = ((), (), s32[]{:S(2)}) async-start(), calls=%async_computation.15 | async-start | bytes 9437184 | tf_op jit(solution)/shard_map/all_gather | solution.py:875
  246.3 279.8 %all-gather.19.cloned.1.call-start = ((), (), s32[]{:S(2)}) async-start(), calls=%async_computation.16 | async-start | bytes 18874368 | tf_op jit(solution)/shard_map/all_gather | solution.py:875
  413.5 365.3 %reduce-scatter.6.cloned.1.call-start = ((), (), s32[]{:S(2)}) async-start(), calls=%async_computation.7 | async-start | bytes 9437184 | tf_op jit(solution)/shard_map/reduce_scatter | solution.py:956
  593.2 198.0 %reduce-scatter.8.cloned.1.call-start = ((), (), s32[]{:S(2)}) async-start(), calls=%async_computation.8 | async-start | bytes 18874368 | tf_op jit(solution)/shard_map/reduce_scatter | solution.py:956
  593.9 440.8 %reduce-scatter.10.cloned.1.call-start = ((), (), s32[]{:S(2)}) async-start(), calls=%async_computation.9 | async-start | bytes 2621440 | tf_op jit(solution)/shard_map/reduce_scatter | solution.py:990
  662.4 13.8 %copy-start.2 = (bf16[2,512,1152]{2,1,0:T(8,128)(2,1)S(1)}, bf16[2,512,1152]{2,1,0:T(8,128)(2,1)}, u32[]{:S(2)}) copy-start(bf16[2,512,1152]{2,1,0:T(8,128)(2,1)} %get-tuple-element.128.refs_1_) | copy-start | bytes 7077892
  662.4 13.8 %copy-start.10 = (bf16[512,1152]{1,0:T(8,128)(2,1)S(1)}, bf16[512,1152]{1,0:T(8,128)(2,1)}, u32[]{:S(2)}) copy-start(bf16[512,1152]{1,0:T(8,128)(2,1)} %get-tuple-element.131) | copy-start | bytes 3538948
  714.7 2.2 copy-start.8
  791.3 87.4 %all-to-all-start = ((bf16[8,256,512]{2,1,0:T(8,128)(2,1)}), bf16[8,256,512]{2,1,0:T(8,128)(2,1)S(1)}, u32[]{:S(2)}, u32[]{:S(2)}) async-start(bf16[8,256,512]{2,1,0:T(8,128)(2,1)} %bitcast.158), calls=%async_computation.3 | async-start | bytes 4194304 | tf_op jit(solution)/shard_map/all_to_all | solution.py:988
  795.9 245.4 %reduce-scatter.12.cloned.1.call-start = ((), (), s32[]{:S(2)}) async-start(), calls=%async_computation.10 | async-start | bytes 9437184 | tf_op jit(solution)/shard_map/reduce_scatter | solution.py:956
  878.6 220.7 %reduce-scatter.14.cloned.1.call-start = ((), (), s32[]{:S(2)}) async-start(), calls=%async_computation.11 | async-start | bytes 18874368 | tf_op jit(solution)/shard_map/reduce_scatter | solution.py:956
  967.8 14.6 %copy-start.3 = (bf16[2,512,1152]{2,1,0:T(8,128)(2,1)S(1)}, bf16[2,512,1152]{2,1,0:T(8,128)(2,1)}, u32[]{:S(2)}) copy-start(bf16[2,512,1152]{2,1,0:T(8,128)(2,1)} %get-tuple-element.153.refs_1_) | copy-start | bytes 7077892
  967.8 14.5 %copy-start.9 = (bf16[512,1152]{1,0:T(8,128)(2,1)S(1)}, bf16[512,1152]{1,0:T(8,128)(2,1)}, u32[]{:S(2)}) copy-start(bf16[512,1152]{1,0:T(8,128)(2,1)} %get-tuple-element.157) | copy-start | bytes 3538948
  1019.6 3.2 copy-start.13
  1022.7 6.7 copy-start.7
  1022.7 14.1 %collective-permute-start = (bf16[512,2176]{1,0:T(8,128)(2,1)}, bf16[512,2176]{1,0:T(8,128)(2,1)}, u32[]{:S(2)}, u32[]{:S(2)}) collective-permute-start(bf16[512,2176]{1,0:T(8,128)(2,1)} %dynamic-slice_bitcast_fusion), channel_id=1, source_target_pairs={{0,1},{1,0},{2,3},{3,2},{4,5},{5,4},{6,7},{7,6},{8,9},{9,8},{10,11... | collective-permute-start | bytes 6684680 | tf_op jit(solution)/shard_map/ppermute | solution.py:868
  1024.3 71.6 %all-to-all-start.1 = ((bf16[8,128,512]{2,1,0:T(8,128)(2,1)}), bf16[8,128,512]{2,1,0:T(8,128)(2,1)}, u32[]{:S(2)}, u32[]{:S(2)}) async-start(bf16[8,128,512]{2,1,0:T(8,128)(2,1)} %bitcast.160), calls=%async_computation.6 | async-start | bytes 2097152 | tf_op jit(solution)/shard_map/all_to_all | solution.py:988
  1030.4 1.1 copy-start.12
  1033.2 1.5 copy-start.4
  1084.1 11.8 %copy-start.11 = (bf16[8,128,512]{2,1,0:T(8,128)(2,1)S(1)}, bf16[8,128,512]{2,1,0:T(8,128)(2,1)}, u32[]{:S(2)}) copy-start(bf16[8,128,512]{2,1,0:T(8,128)(2,1)} %get-tuple-element.170) | copy-start | bytes 3145732
  1146.9 2.3 copy-start
  1149.5 0.7 copy-start.25
  1149.5 1.9 copy-start.15
  1149.5 2.6 copy-start.14
  1149.5 3.3 copy-start.1
Sparse Core Ops, SparseCore 0:
  39.2 87.9 all-gather.10
  129.0 89.0 all-gather.12
  245.8 81.4 all-gather.14
  329.0 84.0 all-gather.16
  414.8 96.5 all-gather.18
  593.3 77.9 reduce-scatter.5
  675.3 115.9 reduce-scatter.7
  794.2 73.7 reduce-scatter.9
  878.8 74.9 reduce-scatter.11
  957.6 138.1 reduce-scatter.13

commit v4 on v3

--- a/solution.py
+++ b/solution.py
@@ -110,7 +110,7 @@
             total_sems += zs + zs * grp_size * 2
             continue
         n = size_of(group, sizes)
-        total_sems += PIECES if group == "sib" else n
+        total_sems += PIECES if group == "sib" else 2 * n if what == "all" else n
         rest = x.shape[1:] if group == "sib" else x.shape
         if what != "own":
             rest = (n,) + (x.shape if what == "all" else x.shape[1:])
@@ -152,6 +152,20 @@
             _, group, what = ops[i]
             n, me, where = place_in(group or "g", sizes)
             out = outs[i]
+            if what == "all":
+                copy = pltpu.make_async_copy(ins[i], out.at[me], local.at[i])
+                copy.start()
+                own_copies.append(copy)
+
+                @pl.when(me < n - 1)
+                def _():
+                    hop(i, n, ins[i], me, 1).start()
+
+                @pl.when(me > 0)
+                def _():
+                    hop(i, n, ins[i], me, -1).start()
+
+                return None
             if what == "packed":
                 grp = lax.axis_index("grp")
                 core = lax.axis_index("core")
@@ -180,16 +194,12 @@
             copies = []
             for k in range(1, n):
                 peer = lax.rem(me + k, n)
-                if what == "all":
-                    src = ins[i]
-                elif what == "own":
+                if what == "own":
                     src = ins[i].at[peer]
                 else:
                     src = ins[i].at[lax.rem(peer, ins[i].shape[0])]
                 copies.append(remote(src, out.at[me], sems[i] + k, where(peer)))
-            if what == "all":
-                src = ins[i]
-            elif what == "own":
+            if what == "own":
                 src = ins[i].at[me]
             else:
                 src = ins[i].at[lax.rem(me, ins[i].shape[0])]
@@ -198,6 +208,50 @@
             own_copies.append(copy)
             sent.extend(copies)
             return None
+
+        def hop(i, n, src, block, way):
+            _, me, where = place_in(ops[i][1], sizes)
+            return pltpu.make_async_remote_copy(
+                src_ref=src,
+                dst_ref=outs[i].at[block],
+                send_sem=send.at[sems[i] + block + (0 if way > 0 else n)],
+                recv_sem=recv.at[sems[i] + block],
+                device_id=where(me + way),
+                device_id_type=MESH,
+            )
+
+        def finish_all(i):
+            n, me, _ = place_in(ops[i][1], sizes)
+            out = outs[i]
+            for far in range(1, n):
+                low, high = me - far, me + far
+
+                @pl.when(low >= 0)
+                def _():
+                    hop(i, n, out.at[low], low, 1).wait_recv()
+
+                    @pl.when(me < n - 1)
+                    def _():
+                        hop(i, n, out.at[low], low, 1).start()
+
+                @pl.when(high <= n - 1)
+                def _():
+                    hop(i, n, out.at[high], high, -1).wait_recv()
+
+                    @pl.when(me > 0)
+                    def _():
+                        hop(i, n, out.at[high], high, -1).start()
+
+            for far in range(n):
+                low, high = me - far, me + far
+
+                @pl.when((low >= 0) & (me < n - 1))
+                def _():
+                    hop(i, n, ins[i] if far == 0 else out.at[low], low, 1).wait_send()
+
+                @pl.when((high <= n - 1) & (me > 0))
+                def _():
+                    hop(i, n, ins[i] if far == 0 else out.at[high], high, -1).wait_send()
 
         def finish_packed(i, along, own):
             grp = lax.axis_index("grp")
@@ -258,6 +312,9 @@
                 pending.append(got)
         for item in pending:
             finish_packed(*item)
+        for i in range(count):
+            if ops[i][2] == "all":
+                finish_all(i)
         for copy in own_copies:
             copy.wait()
         for copy in sent:
@@ -710,18 +767,14 @@
     )[0]
 
 
-def experts_backward(x, g, gates, slots, weights, held, with_out):
+def experts_backward(x, g, gates, slots, weights, held):
     n, rows, _ = x.shape
     lanes = 2 * SLOTS
 
 
     def kernel(x_ref, gr_ref, g_ref, s_ref, w0, w1, *rest):
         dx_ref, dg_ref = rest[:2]
-        first_grad, second_grad, *rest = rest[2:]
-        if with_out:
-            out_ref, acc_ref, row_ref, grow_ref = rest
-        else:
-            acc_ref, row_ref, grow_ref = rest
+        first_grad, second_grad, acc_ref, row_ref, grow_ref = rest[2:]
         e = pl.program_id(0)
         w_gate, w_up, down_l, down_r = matrices(w0, w1)
         slot_gates = []
@@ -747,8 +800,6 @@
         dh = dhg * gate
         dga = (dh * up * (sig * (1.0 + ga * (1.0 - sig)))).astype(BF)
         dup = (dh * act).astype(BF)
-        if with_out:
-            eo = jnp.concatenate([dot(hidden, down_l), dot(hidden, down_r)], axis=1).astype(BF)
         drow = (dot(dga, w_gate, 1, 1) + dot(dup, w_up, 1, 1)).astype(BF)
         for s in range(n):
             mine = slice(lanes * s, lanes * (s + 1))
@@ -756,23 +807,19 @@
             dg_ref[s, pl.ds(e, 1), :] = jnp.sum(
                 jnp.where(pick, d_gate[mine], 0.0), axis=0, keepdims=True
             )
-            todo = [(acc_ref, dx_ref, dot(pick.astype(BF), drow[mine], 0, 0))]
-            if with_out:
-                gated = jnp.where(pick, g_ref[s, pl.ds(e, 1), :], 0.0).astype(BF)
-                todo.append((out_ref, out_ref, dot(gated, eo[mine], 0, 0)))
-            for held_ref, final_ref, add in todo:
-
-                @pl.when(e == 0)
-                def _():
-                    held_ref[s] = add.astype(held_ref.dtype)
-
-                @pl.when((e > 0) & (e < held - 1))
-                def _():
-                    held_ref[s] = (held_ref[s].astype(F32) + add).astype(held_ref.dtype)
-
-                @pl.when(e == held - 1)
-                def _():
-                    final_ref[s] = (held_ref[s].astype(F32) + add).astype(BF)
+            add = dot(pick.astype(BF), drow[mine], 0, 0)
+
+            @pl.when(e == 0)
+            def _():
+                acc_ref[s] = add
+
+            @pl.when((e > 0) & (e < held - 1))
+            def _():
+                acc_ref[s] += add
+
+            @pl.when(e == held - 1)
+            def _():
+                dx_ref[s] = (acc_ref[s] + add).astype(BF)
 
         dslot = (grows.astype(F32) * gate).astype(BF)
         ctx, depth, _ = first_grad.shape[1:]
@@ -793,9 +840,6 @@
         pltpu.VMEM((n * lanes, D), BF),
         pltpu.VMEM((n * lanes, D), BF),
     ]
-    if with_out:
-        outs.append(sds(x.shape, BF))
-        out_specs.append(full(x.shape))
     flops = 2 * held * n * (lanes * D * F * 9 + 3 * lanes * rows * D)
     return call(
         kernel,
@@ -807,6 +851,78 @@
         out_specs=tuple(out_specs),
         grid=(held,),
         scratch=scratch,
+    )
+
+
+def attention_gradients(*parts):
+    shard = parts[0].shape[1]
+    kv = KEY_VALUE_HEADS * HS
+    widths = (D, kv, kv, D, 128, 128)
+
+    def kernel(w0, w1, s0, s1, *outs):
+        for layer, (w_ref, s_ref) in enumerate(((w0, s0), (w1, s1))):
+            w = w_ref[0].astype(F32)
+            s = s_ref[0].astype(F32)
+            for j in range(1, w_ref.shape[0]):
+                w = w + w_ref[j].astype(F32)
+                s = s + s_ref[j].astype(F32)
+            outs[0][layer] = w[:, :D]
+            outs[1][layer] = w[:, D : D + kv]
+            outs[2][layer] = w[:, D + kv : 2 * D]
+            outs[3][layer] = s[:, :D]
+            outs[4][layer] = w[:, 2 * D :]
+            outs[5][layer] = s[:, D:]
+
+    outs = [sds((LAYERS, shard, w), F32) for w in widths]
+    return call(
+        kernel,
+        outs,
+        list(parts),
+        0,
+        in_specs=[full(x.shape) for x in parts],
+        out_specs=tuple(full(o.shape) for o in outs),
+        grid=(1,),
+    )
+
+
+def expert_gradients(layers, members):
+    pairs = [x for pair in layers for x in pair]
+    depth = pairs[0].shape[1]
+    part = (pairs[1].shape[1] - depth) // 2
+    holders = pairs[0].shape[0] // members
+
+    def kernel(*refs):
+        ins, (gate_ref, up_ref, down_ref) = refs[:4], refs[4:]
+        for layer in range(LAYERS):
+            first, second = [
+                functools.reduce(
+                    lambda x, y: x + y, [r[j, 0].astype(F32) for j in range(holders)]
+                )
+                for r in ins[2 * layer : 2 * layer + 2]
+            ]
+            gate_ref[layer, 0] = first
+            up_ref[layer, 0] = second[:depth]
+            down_ref[layer, 0, :, : D // 2] = second[depth : depth + part]
+            down_ref[layer, 0, :, D // 2 :] = second[depth + part :]
+
+    args = [x.reshape((holders, members) + x.shape[1:]) for x in pairs]
+    outs = [
+        sds((LAYERS, members, depth, F), F32),
+        sds((LAYERS, members, depth, F), F32),
+        sds((LAYERS, members, part, D), F32),
+    ]
+    return call(
+        kernel,
+        outs,
+        args,
+        0,
+        in_specs=[
+            pl.BlockSpec((holders, 1) + x.shape[2:], lambda e: (0, e, 0, 0)) for x in args
+        ],
+        out_specs=tuple(
+            pl.BlockSpec((LAYERS, 1) + o.shape[2:], lambda e: (0, e, 0, 0)) for o in outs
+        ),
+        grid=(members,),
     )
 
 
@@ -871,6 +987,11 @@
         down = w_down[layer]
         return jnp.concatenate([w_up[layer], down[:, :, : D // 2], down[:, :, D // 2 :]], axis=1)
 
+    def along_line(w):
+        copies = ctx // w.shape[0]
+        w = jnp.tile(w, (copies, 1, 1)) if copies > 1 else w
+        return lax.all_to_all(w, line, 0, 0, tiled=True)
+
     def plane_gather(w):
         return lax.all_gather(w[None], ("grp", "core"), axis=0, tiled=True)
 
@@ -880,7 +1001,8 @@
         (gate_parts, pack(0), second_shard(0))
     )
     first, second_parts = move((own_pack, None, "packed"), (own_second, "line", "pick"))
-    packed = [first.reshape(D, -1), None]
+    first, late_pack = lax.optimization_barrier((first, pack(1)))
+    packed = [first.reshape(D, -1), lax.all_gather(late_pack, every, axis=0, tiled=True)]
     weights = [[plane_gather(gate_parts), plane_gather(second_parts)], None]
 
     own_segments = lax.dynamic_slice_in_dim(segments, ctx_index * tok, tok, axis=1)
@@ -935,29 +1057,25 @@
             xs, gates_here, slots_here, late_gate = move(
                 *ops, (slot, "tok", "own"), (w_gate[1], "line", "pick")
             )
-            late_g, late_second, _ = lax.optimization_barrier(
-                (grad_rows, second_shard(1), xs)
-            )
-            last_g = lax.all_gather(late_g, "zp", axis=0, tiled=False)
+            late_second, xs = lax.optimization_barrier((second_shard(1), xs))
+            late_second = along_line(late_second)
             late_gate = plane_gather(late_gate)
         else:
-            xs, gates_here = move(*ops)
+            xs, gates_here, last_g = move(*ops, (grad_rows, "tok", "all"))
         saved.append((stream, heads, out, lse, mixed, stream1, normed, gates, gains, xs, gates_here))
+        sent = experts_forward(xs, gates_here, slots_here, weights[layer], held)
         if layer == 0:
-            sent = experts_forward(xs, gates_here, slots_here, weights[0], held)
-            came, after, late_second = move(
-                (sent, "tok", "own"), (pack(1), None, "packed"), (late_second, "line", "pick")
-            )
-            packed[1] = after.reshape(D, -1)
+            sent, late_second = lax.optimization_barrier((sent, late_second))
+            (came,) = move((sent, "tok", "own"))
             weights[1] = [late_gate, plane_gather(late_second)]
             parts = (stream1, came)
 
+    sent, last_g = lax.optimization_barrier((sent, last_g))
+    final_sum = lax.psum_scatter(sent, "zp", scatter_dimension=0, tiled=True)[0]
+    last_stream = stream1
+
     def plane_scatter(r):
         return lax.psum_scatter(r, ("grp", "core"), scatter_dimension=0, tiled=True)[0]
-
-    def owned_rows(r):
-        r = r.astype(F32).reshape((ctx // (2 * planes), 2 * planes) + r.shape[1:])
-        return jnp.sum(r, axis=0)
 
     def between_cores(x):
         theirs = lax.dynamic_index_in_dim(x, 1 - core, 0, keepdims=False)
@@ -984,24 +1102,21 @@
                 (g.astype(BF), "tok", "all"), (over_grp(small), "z", "own"), (wide, "sib", "own")
             )
             wide = with_other(wide, came)
-            gs, *last_experts = lax.optimization_barrier((gs, *last_experts))
-            last_experts = [lax.all_to_all(r, line, 0, 0, tiled=True) for r in last_experts]
-            final_parts, _ = lax.optimization_barrier((final_parts, gs))
-            final_sum = lax.psum_scatter(final_parts, "zp", scatter_dimension=0, tiled=True)
-            hidden_out = (
-                (saved[1][5] + final_sum[0].astype(F32)).astype(BF).reshape(micro, tok, D)
-            )
-        res = experts_backward(xs, gs, gates_here, slots_here, weights[layer], held, last)
+            gs, last_second = lax.optimization_barrier((gs, last_experts[1]))
+            last_second = lax.all_to_all(last_second, line, 0, 0, tiled=True)
+        res = experts_backward(xs, gs, gates_here, slots_here, weights[layer], held)
         if not last:
-            *res, last_second = lax.optimization_barrier((*res, last_experts[1]))
-            last_experts[1] = last_second
-        experts = [plane_scatter(r) for r in res[2:4]]
+            *res, last_second = lax.optimization_barrier((*res, last_second))
+        if last:
+            *res, final_sum = lax.optimization_barrier((*res, final_sum))
+        second_grads = plane_scatter(res[3])
         back = [(res[0], "tok", "own"), (res[1], "tok", "own")]
         if last:
-            last_experts = experts
-            final_parts = res[4]
             d_parts, d_gates = move(*back)
+            gate_grads, d_parts = lax.optimization_barrier((res[2], d_parts))
+            last_experts = [plane_scatter(gate_grads), second_grads]
         else:
+            experts = [plane_scatter(res[2]), second_grads]
             d_parts, d_gates, last_wide = move(*back, (wide, "g", "own"))
         g1, d_mixed, small = output_backward(
             d_parts, d_gates, gates, g, stream1, normed, mixed, packed[layer], gains,
@@ -1014,67 +1129,40 @@
             d_out, came, last_wide = move(*ops, (over_grp(last_wide), "z", "own"))
         small = with_other(small, came)
         dx = attention_backward(heads, d_out, out, lse, seg_row, seg_col, ctx, hq, tok)
-        dx, small = move((dx, "line", "own"), (small, "g", "own"))
+        ops = [(dx, "line", "own"), (small, "g", "own")]
+        if last:
+            dx, small = move(*ops)
+        else:
+            dx, small, last_gate = move(*ops, (last_experts[0], "line", "own"))
         g, wide = qkv_backward(
             dx, g1, stream, packed[layer], gains, cos_t, sin_t, ctx, hq, shard
         )
-    first_wide, first_gate, first_small = move(
+    hidden_out = (last_stream + final_sum.astype(F32)).astype(BF).reshape(micro, tok, D)
+    first_wide, first_second, first_small = move(
         (between_cores(wide), "g", "own"),
-        (experts[0], "line", "own"),
+        (experts[1], "line", "own"),
         (over_grp(small), "z", "own"),
     )
-    first_wide, first_second = move(
-        (over_grp(first_wide), "z", "own"), (experts[1], "line", "own")
-    )
-
-    def along_z(x):
-        return jnp.sum(x.astype(F32), axis=0)
-
-    wides = [along_z(first_wide), along_z(last_wide)]
-    smalls = [along_z(first_small), along_z(last_small)]
-    def matrices_of(first, second):
-        first, second = owned_rows(first), owned_rows(second)
-        depth, part = D // ctx, F // ctx
-        down = [second[:, depth + part * k : depth + part * (k + 1)] for k in range(2)]
-        return first, second[:, :depth], jnp.concatenate(down, axis=2)
-
-    owned_experts = [matrices_of(first_gate, first_second), matrices_of(*last_experts)]
-
-    def unpack(layer):
-        w, s = wides[layer], smalls[layer]
-        kv = KEY_VALUE_HEADS * HS
-        return (
-            w[:, :D],
-            w[:, D : D + kv],
-            w[:, D + kv : 2 * D],
-            s[:, :D],
-            s[:, D + 33],
-            by_plane(s[:, D : D + E], 1, back=True),
-        )
-
-    got = [unpack(layer) for layer in range(LAYERS)]
-
-    def stacked(k):
-        return jnp.stack([got[layer][k] for layer in range(LAYERS)])
-
-    gain_grad = jnp.stack([w[:, 2 * D] for w in wides])
-
-    def owned(k):
-        return jnp.stack([owned_experts[layer][k] for layer in range(LAYERS)])
-
+    first_wide, first_gate = move(
+        (over_grp(first_wide), "z", "own"), (experts[0], "line", "own")
+    )
+
+    grads = attention_gradients(first_wide, last_wide, first_small, last_small)
+    gq, gk, gv, go, gain_tail, tail = grads
+    tops = expert_gradients(
+        [(first_gate, first_second), (last_gate, last_second)], 2 * planes
+    )
     return (
         hidden_out,
         g.reshape(micro, tok, D),
-        gain_grad,
-        stacked(0),
-        stacked(1),
-        stacked(2),
-        stacked(3),
-        stacked(4),
-        stacked(5),
-        owned(0),
-        owned(1),
-        owned(2),
+        gain_tail[:, :, 0],
+        gq,
+        gk,
+        gv,
+        go,
+        tail[:, :, 33],
+        by_plane(tail[:, :, :E], 2, back=True),
+        *tops,
     )
 
 

time: 1190 us -> 1140 us (0.958)
  other arithmetic: 50 us -> 28 us
  Pallas kernels: 1020 us -> 1000 us
    pallas_call x18, Pallas kernels: 774 us -> 721 us  [transfer(): pl.pallas_call(kernel, out_shape=tuple(shapes), in_specs=[any_spec] * cou...]
    pallas_call x15 -> x18, Pallas kernels: 250 us -> 280 us  [call(): pl.pallas_call(kernel, out_shape=tuple(outs), scratch_shapes=list(scratch...]
    another operation x12 -> x0, other arithmetic: 14.8 us -> none  [the longest x5 8.87 us: owned(): return jnp.stack([owned_experts[layer][k] for layer in range(LAYERS)])]
    all_to_all x2, waiting for transfers between devices: 26.7 us -> 40.7 us  [the longest x1 40.7 us: along_line(): return lax.all_to_all(w, line, 0, 0, tiled=True)]
    reduce_scatter x4, waiting for transfers between devices: 12.4 us -> 0.03 us  [plane_scatter(): lax.psum_scatter(r, ('grp', 'core'), scatter_dimension=0, tiled=True)[0]]
  transfers between devices with their start and end apart: 13 -> 13, of which waited for: 2 -> 2; matrix products, arithmetic and copies ran while one was open for 5% -> 3% of each run, Pallas kernels for 76% -> 81%
where the time goes in v4:
time: 1140 us; the launch traced here: 1120 us
  Pallas kernels  1000 us (88%)
  waiting for transfers between devices  43.7 us (4%)
  other arithmetic  28 us (2%)
  local copies, waits for them, and re-layouts  20.7 us (2%)
  between operations  15.2 us (1%)
    pallas_call x18, Pallas kernels, transfer(): pl.pallas_call(kernel, out_shape=tuple(shapes), in_specs=[any_spec] * cou...  721 us
    pallas_call x18, Pallas kernels, call(): pl.pallas_call(kernel, out_shape=tuple(outs), scratch_shapes=list(scratch...  280 us
    all_to_all x1, waiting for transfers between devices, along_line(): return lax.all_to_all(w, line, 0, 0, tiled=True)  40.7 us
  transfers between devices with their start and end apart: 13, of which 2 were waited for; matrix products, arithmetic and copies ran while one was open for 3% of the time, Pallas kernels for 81%

profile of v4, /device:TPU:0, one launch (start us, length us, event | category | flops | bytes accessed | tf_op | source)
XLA Modules:
  0.0 1120.3 jit_solution(7278466206476909986)
XLA Ops:
  7.3 3.2 slice_bitcast_fusion
  10.5 23.0 %shard_map.229 = bf16[8,128,512]{2,1,0:T(8,128)(2,1)} custom-call(bf16[8,128,512]{2,1,0:T(8,128)(2,1)} %get-tuple-element.247.refs_0_), custom_call_target="tpu_custom_call" | custom-call | bytes 41943040 | tf_op jit(solution)/shard_map/pallas_call | solution.py:325
  39.1 70.1 %shard_map.230 = (bf16[4,8,32,3200]{3,2,1,0:T(8,128)(2,1)}, bf16[8,256,512]{2,1,0:T(8,128)(2,1)}) custom-call(bf16[32,3200]{1,0:T(8,128)(2,1)} %concatenate.12.refs_0_, bf16[8,256,512]{2,1,0:T(8,128)(2,1)} %pad_maximum_fusion.refs_1_), custom_call_target="tpu_custom_call" | custom-call | bytes 346030080 | tf_op jit(solution)/shard_map/pallas_call | solution.py:325
  113.5 5.2 shard_map.231
  118.7 23.3 %shard_map.232.x_ref = bf16[8,256,256]{2,1,0:T(8,128)(2,1)} custom-call(bf16[8,256,256]{2,1,0:T(8,128)(2,1)} %get-tuple-element.115.refs_0_), custom_call_target="tpu_custom_call" | custom-call | bytes 41943040 | tf_op jit(solution)/shard_map/pallas_call | solution.py:325
  143.3 9.7 shard_map.233
  153.0 17.9 %shard_map.234.m_ref = bf16[8,256,128]{2,1,0:T(8,128)(2,1)} custom-call(bf16[8,256,128]{2,1,0:T(8,128)(2,1)} %get-tuple-element.116.refs_0_.o_ref), custom_call_target="tpu_custom_call" | custom-call | bytes 20971520 | tf_op jit(solution)/shard_map/pallas_call | solution.py:325
  172.0 4.0 shard_map.235
  176.6 71.3 %shard_map.236 = (bf16[4,256,1024]{2,1,0:T(8,128)(2,1)}, f32[4,8,256]{2,1,0:T(8,128)}, s32[4,8,256]{2,1,0:T(8,128)}, bf16[8,128,512]{2,1,0:T(8,128)(2,1)}) custom-call(bf16[256,1024]{1,0:T(8,128)(2,1)} %get-tuple-element.119.refs_0_.nm_ref, f32[4,8,256]{2,1,0:T(8,128)} %get-tuple-element.120.refs_1_.gt_ref, s32[4,8,256]{2,1,0:T(8,128)} %bitcast_select_fusion.refs_2_, ...), custom_call_target="tpu_custom_call" | custom-call | bytes 128450560 | tf_op jit(solution)/shard_map/pallas_call | solution.py:325
  249.5 3.6 all-to-all-start
  253.5 29.9 %shard_map.237.refs_0_ = bf16[4,256,1024]{2,1,0:T(8,128)(2,1)} custom-call(bf16[4,256,1024]{2,1,0:T(8,128)(2,1)} %get-tuple-element.122.x_ref, f32[4,8,256]{2,1,0:T(8,128)} %get-tuple-element.123.g_ref, s32[4,8,256]{2,1,0:T(8,128)} %get-tuple-element.124.s_ref, bf16[8,8,128,512]{3,2,1,0:T(8,128)(2,1)} %bitcast.140, bf16[8,8,256,512]{3,2,1,0:T(8,128)(2,1)} %bitcast.136), custom_call_target="tpu_custom_call" | custom-call | flops 12884901888 | bytes 29425664 | tf_op jit(solution)/shard_map/pallas_call | solution.py:44
  283.4 40.7 %all-to-all-done = bf16[8,256,512]{2,1,0:T(8,128)(2,1)S(1)} async-done(((bf16[8,256,512]{2,1,0:T(8,128)(2,1)}), bf16[8,256,512]{2,1,0:T(8,128)(2,1)S(1)}, u32[]{:S(2)}, u32[]{:S(2)}) %all-to-all-start) | async-done | bytes 2097184 | tf_op jit(solution)/shard_map/all_to_all | solution.py:993
  325.4 38.6 %shard_map.238.refs_1_ = bf16[4,256,1024]{2,1,0:T(8,128)(2,1)} custom-call(bf16[4,256,1024]{2,1,0:T(8,128)(2,1)} %shard_map.237.refs_0_), custom_call_target="tpu_custom_call" | custom-call | bytes 83886080 | tf_op jit(solution)/shard_map/pallas_call | solution.py:325
  364.1 6.1 shard_map.239
  370.1 29.7 %shard_map.240.x_ref = bf16[8,256,256]{2,1,0:T(8,128)(2,1)} custom-call(bf16[8,256,256]{2,1,0:T(8,128)(2,1)} %get-tuple-element.130.refs_0_), custom_call_target="tpu_custom_call" | custom-call | bytes 41943040 | tf_op jit(solution)/shard_map/pallas_call | solution.py:325
  399.8 9.8 shard_map.241
  409.6 17.9 %shard_map.242.m_ref = bf16[8,256,128]{2,1,0:T(8,128)(2,1)} custom-call(bf16[8,256,128]{2,1,0:T(8,128)(2,1)} %get-tuple-element.131.refs_0_.o_ref), custom_call_target="tpu_custom_call" | custom-call | bytes 20971520 | tf_op jit(solution)/shard_map/pallas_call | solution.py:325
  427.5 4.1 shard_map.243
  431.6 79.0 %shard_map.244 = (bf16[4,256,1024]{2,1,0:T(8,128)(2,1)}, f32[4,8,256]{2,1,0:T(8,128)}, bf16[4,256,1024]{2,1,0:T(8,128)(2,1)}) custom-call(bf16[256,1024]{1,0:T(8,128)(2,1)} %get-tuple-element.135.refs_0_.nm_ref, f32[4,8,256]{2,1,0:T(8,128)} %get-tuple-element.136.refs_1_.gt_ref, bf16[256,1024]{1,0:T(8,128)(2,1)} %bitcast.117), custom_call_target="tpu_custom_call" | custom-call | bytes 169082880 | tf_op jit(solution)/shard_map/pallas_call | solution.py:325
  510.6 29.9 %shard_map.245 = bf16[4,256,1024]{2,1,0:T(8,128)(2,1)} custom-call(bf16[4,256,1024]{2,1,0:T(8,128)(2,1)} %get-tuple-element.137.x_ref, f32[4,8,256]{2,1,0:T(8,128)} %get-tuple-element.138.g_ref, s32[4,8,256]{2,1,0:T(8,128)} %get-tuple-element.124.s_ref, bf16[8,8,128,512]{3,2,1,0:T(8,128)(2,1)} %bitcast.142, bf16[8,8,256,512]{3,2,1,0:T(8,128)(2,1)} %bitcast.138), custom_call_target="tpu_custom_call" | custom-call | flops 12884901888 | bytes 29425664 | tf_op jit(solution)/shard_map/pallas_call | solution.py:44
  541.0 55.8 %shard_map.246 = (bf16[4,256,1024]{2,1,0:T(8,128)(2,1)}, f32[4,8,256]{2,1,0:T(8,128)}, bf16[8,8,128,512]{3,2,1,0:T(8,128)(2,1)}, bf16[8,8,256,512]{3,2,1,0:T(8,128)(2,1)}) custom-call(bf16[4,256,1024]{2,1,0:T(8,128)(2,1)} %get-tuple-element.137.x_ref, bf16[4,256,1024]{2,1,0:T(8,128)(2,1)} %get-tuple-element.142.gr_ref, ...), custom_call_target="tpu_custom_call" | custom-call | flops 33822867456 | bytes 56721408 | tf_op jit(solution)/shard_map/pallas_call | solution.py:44
  596.8 47.7 %shard_map.247 = (bf16[4,256,1024]{2,1,0:T(8,128)(2,1)}, f32[4,8,256]{2,1,0:T(8,128)}) custom-call(bf16[4,256,1024]{2,1,0:T(8,128)(2,1)} %get-tuple-element.150.refs_0_, f32[4,8,256]{2,1,0:T(8,128)} %get-tuple-element.151.refs_1_), custom_call_target="tpu_custom_call" | custom-call | bytes 85196800 | tf_op jit(solution)/shard_map/pallas_call | solution.py:325
  644.6 6.9 shard_map.248
  651.4 12.1 %shard_map.249 = (bf16[8,256,128]{2,1,0:T(8,128)(2,1)}, bf16[512,1152]{1,0:T(8,128)(2,1)}) custom-call(bf16[8,256,128]{2,1,0:T(8,128)(2,1)} %get-tuple-element.155.refs_0_, bf16[2,512,1152]{2,1,0:T(8,128)(2,1)} %get-tuple-element.156.refs_1_), custom_call_target="tpu_custom_call" | custom-call | bytes 68157440 | tf_op jit(solution)/shard_map/pallas_call | solution.py:325
  663.6 13.8 %shard_map.250.refs_0_ = bf16[8,256,256]{2,1,0:T(8,128)(2,1)} custom-call(bf16[8,256,256]{2,1,0:T(8,128)(2,1)} %shard_map.240.x_ref, bf16[8,256,128]{2,1,0:T(8,128)(2,1)} %get-tuple-element.157.d_ref, bf16[8,256,128]{2,1,0:T(8,128)(2,1)} %get-tuple-element.131.refs_0_.o_ref, f32[2,1024,128]{2,1,0:T(8,128)} %get-tuple-element.158.l_ref, ...), custom_call_target="tpu_custom_call" | custom-call | flops 1342177280 | bytes 4210688 | tf_op jit(solution)/shard_map/pallas_call | solution.py:44
  678.7 30.5 %shard_map.251 = (bf16[8,256,256]{2,1,0:T(8,128)(2,1)}, bf16[4,4,32,1152]{3,2,1,0:T(8,128)(2,1)}) custom-call(bf16[8,256,256]{2,1,0:T(8,128)(2,1)} %shard_map.250.refs_0_, bf16[4,4,32,1152]{3,2,1,0:T(8,128)(2,1)} %bitcast.115), custom_call_target="tpu_custom_call" | custom-call | bytes 89128960 | tf_op jit(solution)/shard_map/pallas_call | solution.py:325
  709.2 8.8 shard_map.252
  718.0 2.2 convert_element_type.109.refs_0_
  721.2 47.8 %shard_map.253 = (bf16[4,256,1024]{2,1,0:T(8,128)(2,1)}, bf16[4,32,1152]{2,1,0:T(8,128)(2,1)}, bf16[512,2176]{1,0:T(8,128)(2,1)}) custom-call(bf16[256,1024]{1,0:T(8,128)(2,1)} %convert_element_type.109.refs_0_, bf16[4,32,1152]{2,1,0:T(8,128)(2,1)} %reduce_sum.68.refs_1_, bf16[2,512,2176]{2,1,0:T(8,128)(2,1)} %get-tuple-element.164.refs_2_), custom_call_target="tpu_custom_call" | custom-call | bytes 184811520 | tf_op jit(solution)/shard_map/pallas_call | solution.py:325
  769.0 3.6 all-to-all-start.1
  772.7 56.1 %shard_map.254 = (bf16[4,256,1024]{2,1,0:T(8,128)(2,1)}, f32[4,8,256]{2,1,0:T(8,128)}, bf16[8,8,128,512]{3,2,1,0:T(8,128)(2,1)}, bf16[8,8,256,512]{3,2,1,0:T(8,128)(2,1)}) custom-call(bf16[4,256,1024]{2,1,0:T(8,128)(2,1)} %get-tuple-element.122.x_ref, bf16[4,256,1024]{2,1,0:T(8,128)(2,1)} %get-tuple-element.167.gr_ref, ...), custom_call_target="tpu_custom_call" | custom-call | flops 33822867456 | bytes 56721408 | tf_op jit(solution)/shard_map/pallas_call | solution.py:44
  831.8 3.5 fusion.1
  835.3 51.1 %shard_map.255 = (bf16[4,256,1024]{2,1,0:T(8,128)(2,1)}, f32[4,8,256]{2,1,0:T(8,128)}, bf16[4,4,32,2176]{3,2,1,0:T(8,128)(2,1)}) custom-call(bf16[4,256,1024]{2,1,0:T(8,128)(2,1)} %get-tuple-element.173.refs_0_, f32[4,8,256]{2,1,0:T(8,128)} %get-tuple-element.174.refs_1_, bf16[4,4,32,2176]{3,2,1,0:T(8,128)(2,1)} %bitcast.109), custom_call_target="tpu_custom_call" | custom-call | bytes 174325760 | tf_op jit(solution)/shard_map/pallas_call | solution.py:325
  886.4 3.0 reduce_sum.69.refs_2_
  889.4 7.0 shard_map.256
  896.4 25.4 %shard_map.257 = (bf16[8,256,128]{2,1,0:T(8,128)(2,1)}, bf16[512,1152]{1,0:T(8,128)(2,1)}, bf16[4,32,2176]{2,1,0:T(8,128)(2,1)}) custom-call(bf16[8,256,128]{2,1,0:T(8,128)(2,1)} %get-tuple-element.178.refs_0_, bf16[2,512,1152]{2,1,0:T(8,128)(2,1)} %get-tuple-element.179.refs_1_, bf16[4,32,2176]{2,1,0:T(8,128)(2,1)} %reduce_sum.69.refs_2_), custom_call_target="tpu_custom_call" | custom-call | bytes 90439680 | tf_op jit(solution)/shard_map/pallas_call | solution.py:325
  921.9 14.1 %shard_map.258.refs_0_ = bf16[8,256,256]{2,1,0:T(8,128)(2,1)} custom-call(bf16[8,256,256]{2,1,0:T(8,128)(2,1)} %shard_map.232.x_ref, bf16[8,256,128]{2,1,0:T(8,128)(2,1)} %get-tuple-element.181.d_ref, bf16[8,256,128]{2,1,0:T(8,128)(2,1)} %get-tuple-element.116.refs_0_.o_ref, f32[2,1024,128]{2,1,0:T(8,128)} %get-tuple-element.182.l_ref, ...), custom_call_target="tpu_custom_call" | custom-call | flops 1342177280 | bytes 4210688 | tf_op jit(solution)/shard_map/pallas_call | solution.py:44
  937.2 44.0 %shard_map.259 = (bf16[8,256,256]{2,1,0:T(8,128)(2,1)}, bf16[4,4,32,1152]{3,2,1,0:T(8,128)(2,1)}, bf16[8,128,512]{2,1,0:T(8,128)(2,1)}) custom-call(bf16[8,256,256]{2,1,0:T(8,128)(2,1)} %shard_map.258.refs_0_, bf16[4,4,32,1152]{3,2,1,0:T(8,128)(2,1)} %bitcast.114, bf16[8,128,512]{2,1,0:T(8,128)(2,1)} %bitcast.121), custom_call_target="tpu_custom_call" | custom-call | bytes 131072000 | tf_op jit(solution)/shard_map/pallas_call | solution.py:325
  981.2 8.3 shard_map.260
  989.6 1.9 dynamic-slice_bitcast_fusion
  991.5 3.0 collective-permute-start
  996.4 2.2 collective-permute-done
  998.6 4.3 fusion
  1002.9 59.9 %shard_map.261 = (bf16[4,4,32,2176]{3,2,1,0:T(8,128)(2,1)}, bf16[8,256,512]{2,1,0:T(8,128)(2,1)}, bf16[4,32,1152]{2,1,0:T(8,128)(2,1)}) custom-call(bf16[4,4,32,2176]{3,2,1,0:T(8,128)(2,1)} %bitcast.108, bf16[8,256,512]{2,1,0:T(8,128)(2,1)} %bitcast.119, bf16[4,32,1152]{2,1,0:T(8,128)(2,1)} %reduce_sum.70.refs_2_), custom_call_target="tpu_custom_call" | custom-call | bytes 184811520 | tf_op jit(solution)/shard_map/pallas_call | solution.py:325
  1062.8 2.9 reduce_sum.71.refs_0_
  1065.7 31.8 %shard_map.262 = (bf16[4,32,2176]{2,1,0:T(8,128)(2,1)}, bf16[8,128,512]{2,1,0:T(8,128)(2,1)}) custom-call(bf16[4,32,2176]{2,1,0:T(8,128)(2,1)} %reduce_sum.71.refs_0_, bf16[8,128,512]{2,1,0:T(8,128)(2,1)} %bitcast.122), custom_call_target="tpu_custom_call" | custom-call | bytes 64225280 | tf_op jit(solution)/shard_map/pallas_call | solution.py:325
  1097.5 2.3 shard_map.263
  1104.3 8.7 shard_map.264
  (126 shorter events, 29.6 us)
Async XLA Ops:
  7.2 26.2 %copy-start.18 = (bf16[2,32,32]{2,1,0:T(8,128)(2,1)S(1)}, bf16[2,32,32]{2,1,0:T(8,128)(2,1)}, u32[]{:S(2)}) copy-start(bf16[2,32,32]{2,1,0:T(8,128)(2,1)} %param.24) | copy-start | bytes 12292
  7.2 26.4 %copy-start.20 = (bf16[2,32]{1,0:T(2,128)(2,1)S(1)}, bf16[2,32]{1,0:T(2,128)(2,1)}, u32[]{:S(2)}) copy-start(bf16[2,32]{1,0:T(2,128)(2,1)} %param.18) | copy-start | bytes 388
  7.2 26.5 %copy-start.21 = (bf16[2,32]{1,0:T(2,128)(2,1)S(1)}, bf16[2,32]{1,0:T(2,128)(2,1)}, u32[]{:S(2)}) copy-start(bf16[2,32]{1,0:T(2,128)(2,1)} %param.23) | copy-start | bytes 388
  7.2 26.6 %copy-start.6 = (bf16[2,8,64,1024]{3,2,1,0:T(8,128)(2,1)S(1)}, bf16[2,8,64,1024]{3,2,1,0:T(8,128)(2,1)}, u32[]{:S(2)}) copy-start(bf16[2,8,64,1024]{3,2,1,0:T(8,128)(2,1)} %param.27) | copy-start | bytes 6291460
  7.2 246.2 %all-gather.12.cloned.1.call-start = ((), (), s32[]{:S(2)}) async-start(), calls=%async_computation.13 | async-start | bytes 9437184 | tf_op jit(solution)/shard_map/all_gather | solution.py:996
  33.9 1.6 copy-start.7
  35.5 0.9 copy-start.14
  35.5 1.0 copy-start.15
  35.5 1.0 copy-start.16
  35.5 1.0 copy-start.17
  39.0 71.6 %copy-start.13 = (s32[2,1024]{1,0:T(2,128)S(1)}, s32[2,1024]{1,0:T(2,128)}, u32[]{:S(2)}) copy-start(s32[2,1024]{1,0:T(2,128)} %param.16) | copy-start | bytes 24580
  39.0 214.4 %all-gather.14.cloned.1.call-start = ((), (), s32[]{:S(2)}) async-start(), calls=%async_computation.14 | async-start | bytes 18874368 | tf_op jit(solution)/shard_map/all_gather | solution.py:996
  109.3 254.8 %all-gather.10.cloned.1.call-start = ((), (), s32[]{:S(2)}) async-start(), calls=%async_computation.7 | async-start | bytes 6758400 | tf_op jit(solution)/shard_map/all_gather | solution.py:1005
  110.5 400.1 %all-gather.16.cloned.1.call-start = ((), (), s32[]{:S(2)}) async-start(), calls=%async_computation.15 | async-start | bytes 9437184 | tf_op jit(solution)/shard_map/all_gather | solution.py:996
  142.0 29.0 %copy-start.19 = (s32[2,128,8]{1,2,0:T(8,128)S(1)}, s32[2,128,8]{1,2,0:T(8,128)}, u32[]{:S(2)}) copy-start(s32[2,128,8]{1,2,0:T(8,128)} %param.17) | copy-start | bytes 24580
  249.5 74.5 %all-to-all-start = ((bf16[8,256,512]{2,1,0:T(8,128)(2,1)}), bf16[8,256,512]{2,1,0:T(8,128)(2,1)S(1)}, u32[]{:S(2)}, u32[]{:S(2)}) async-start(bf16[8,256,512]{2,1,0:T(8,128)(2,1)} %pad_maximum_fusion.1), calls=%async_computation | async-start | bytes 4194304 | tf_op jit(solution)/shard_map/all_to_all | solution.py:993
  253.2 257.5 %all-gather.18.cloned.1.call-start = ((), (), s32[]{:S(2)}) async-start(), calls=%async_computation.16 | async-start | bytes 18874368 | tf_op jit(solution)/shard_map/all_gather | solution.py:996
  324.1 1.3 copy-start.1
  325.4 271.4 %reduce-scatter.6.cloned.1.call-start = ((), (), s32[]{:S(2)}) async-start(), calls=%async_computation.8 | async-start | bytes 2621440 | tf_op jit(solution)/shard_map/reduce_scatter | solution.py:1074
  540.5 228.5 %reduce-scatter.8.cloned.1.call-start = ((), (), s32[]{:S(2)}) async-start(), calls=%async_computation.9 | async-start | bytes 18874368 | tf_op jit(solution)/shard_map/reduce_scatter | solution.py:1078
  596.8 340.5 %reduce-scatter.10.cloned.1.call-start = ((), (), s32[]{:S(2)}) async-start(), calls=%async_computation.10 | async-start | bytes 9437184 | tf_op jit(solution)/shard_map/reduce_scatter | solution.py:1078
  663.6 13.8 %copy-start.2 = (bf16[2,512,1152]{2,1,0:T(8,128)(2,1)S(1)}, bf16[2,512,1152]{2,1,0:T(8,128)(2,1)}, u32[]{:S(2)}) copy-start(bf16[2,512,1152]{2,1,0:T(8,128)(2,1)} %get-tuple-element.156.refs_1_) | copy-start | bytes 7077892
  663.6 13.8 %copy-start.11 = (bf16[512,1152]{1,0:T(8,128)(2,1)S(1)}, bf16[512,1152]{1,0:T(8,128)(2,1)}, u32[]{:S(2)}) copy-start(bf16[512,1152]{1,0:T(8,128)(2,1)} %get-tuple-element.159) | copy-start | bytes 3538948
  718.0 2.2 copy-start.9
  769.0 59.8 %all-to-all-start.1 = ((bf16[8,256,512]{2,1,0:T(8,128)(2,1)}), bf16[8,256,512]{2,1,0:T(8,128)(2,1)S(1)}, u32[]{:S(2)}, u32[]{:S(2)}) async-start(bf16[8,256,512]{2,1,0:T(8,128)(2,1)} %bitcast.120), calls=%async_computation.3 | async-start | bytes 4194304 | tf_op jit(solution)/shard_map/all_to_all | solution.py:1106
  772.6 230.2 %reduce-scatter.12.cloned.1.call-start = ((), (), s32[]{:S(2)}) async-start(), calls=%async_computation.11 | async-start | bytes 18874368 | tf_op jit(solution)/shard_map/reduce_scatter | solution.py:1078
  828.8 1.4 copy-start
  830.1 235.5 %reduce-scatter.14.cloned.1.call-start = ((), (), s32[]{:S(2)}) async-start(), calls=%async_computation.12 | async-start | bytes 9437184 | tf_op jit(solution)/shard_map/reduce_scatter | solution.py:1078
  830.2 1.6 copy-start.5
  921.8 14.1 %copy-start.3 = (bf16[2,512,1152]{2,1,0:T(8,128)(2,1)S(1)}, bf16[2,512,1152]{2,1,0:T(8,128)(2,1)}, u32[]{:S(2)}) copy-start(bf16[2,512,1152]{2,1,0:T(8,128)(2,1)} %get-tuple-element.179.refs_1_) | copy-start | bytes 7077892
  921.9 14.1 %copy-start.10 = (bf16[512,1152]{1,0:T(8,128)(2,1)S(1)}, bf16[512,1152]{1,0:T(8,128)(2,1)}, u32[]{:S(2)}) copy-start(bf16[512,1152]{1,0:T(8,128)(2,1)} %get-tuple-element.183) | copy-start | bytes 3538948
  989.6 4.9 copy-start.4
  989.6 4.9 copy-start.12
  989.6 5.9 copy-start.8
  991.5 7.1 collective-permute-start
Sparse Core Ops, SparseCore 0:
  39.2 87.9 all-gather.11
  129.0 89.0 all-gather.13
  221.0 100.3 all-gather.9
  323.1 52.4 all-gather.15
  377.9 89.8 all-gather.17
  540.7 42.8 reduce-scatter.5
  596.9 126.1 reduce-scatter.7
  726.9 70.4 reduce-scatter.9
  828.9 115.4 reduce-scatter.11
  947.7 100.1 reduce-scatter.13

commit v5 on v4

--- a/solution.py
+++ b/solution.py
@@ -33,23 +33,21 @@
     return lax.dot_general(a, b, (((ca,), (cb,)), ((), ())), preferred_element_type=F32)
 
 
-def call(kernel, outs, args, flops, in_specs=None, out_specs=None, grid=None, scratch=()):
+def call(kernel, outs, args, flops, in_specs, out_specs, grid, scratch=(), cid=None):
     nbytes = sum(a.size * a.dtype.itemsize for a in args)
     nbytes += sum(math.prod(o.shape) * jnp.dtype(o.dtype).itemsize for o in outs)
-    kw = {} if grid is None else {"grid": grid}
-    if in_specs is not None:
-        kw["in_specs"] = in_specs
-    if out_specs is not None:
-        kw["out_specs"] = out_specs
+    extra = {} if cid is None else {"collective_id": cid, "has_side_effects": True}
     return pl.pallas_call(
         kernel,
         out_shape=tuple(outs),
         scratch_shapes=list(scratch),
-        compiler_params=pltpu.CompilerParams(vmem_limit_bytes=VMEM_BYTES),
+        in_specs=in_specs,
+        out_specs=out_specs,
+        grid=grid,
+        compiler_params=pltpu.CompilerParams(vmem_limit_bytes=VMEM_BYTES, **extra),
         cost_estimate=pl.CostEstimate(
             flops=int(flops), bytes_accessed=int(nbytes), transcendentals=0
         ),
-        **kw,
     )(*args)
 
 
@@ -113,7 +111,7 @@
         total_sems += PIECES if group == "sib" else 2 * n if what == "all" else n
         rest = x.shape[1:] if group == "sib" else x.shape
         if what != "own":
-            rest = (n,) + (x.shape if what == "all" else x.shape[1:])
+            rest = (n,) + (x.shape if what == "all" else x.shape[2:])
         shapes.append(sds(rest, x.dtype))
     count = len(ops)
 
@@ -197,12 +195,12 @@
                 if what == "own":
                     src = ins[i].at[peer]
                 else:
-                    src = ins[i].at[lax.rem(peer, ins[i].shape[0])]
+                    src = ins[i].at[what, lax.rem(peer, ins[i].shape[1])]
                 copies.append(remote(src, out.at[me], sems[i] + k, where(peer)))
             if what == "own":
                 src = ins[i].at[me]
             else:
-                src = ins[i].at[lax.rem(me, ins[i].shape[0])]
+                src = ins[i].at[what, lax.rem(me, ins[i].shape[1])]
             copy = pltpu.make_async_copy(src, out.at[me], local.at[i])
             copy.start()
             own_copies.append(copy)
@@ -337,6 +335,101 @@
             flops=0, bytes_accessed=40 * int(total), transcendentals=0
         ),
     )(*[x for x, _, _ in ops])
+
+
+ANY_SPEC = pl.BlockSpec(memory_space=pl.ANY)
+
+
+class Carried:
+    def __init__(self, ops, sizes):
+        self.sizes = sizes
+        self.ops = ops
+        self.shapes = []
+        self.first = []
+        self.total = 0
+        for x, group, what in ops:
+            n = size_of(group, sizes)
+            shape = x.shape if what == "own" else (n,) + x.shape[2:]
+            self.shapes.append(sds(shape, x.dtype))
+            self.first.append(self.total)
+            self.total += n
+
+    def scratch(self):
+        if not self.ops:
+            return []
+        return [
+            pltpu.SemaphoreType.DMA((self.total,)),
+            pltpu.SemaphoreType.DMA((self.total,)),
+            pltpu.SemaphoreType.DMA((len(self.ops),)),
+        ]
+
+    def enter(self, groups):
+        barrier = pltpu.get_barrier_semaphore()
+        total = 0
+        for group in groups:
+            n, me, where = place_in(group, self.sizes)
+            for k in range(1, n):
+                pl.semaphore_signal(
+                    barrier, inc=1, device_id=where(lax.rem(me + k, n)), device_id_type=MESH
+                )
+            total += n - 1
+        pl.semaphore_wait(barrier, total)
+
+    def copies(self, ins, outs, sems):
+        made = []
+        for i, (_, group, what) in enumerate(self.ops):
+            send, recv, local = sems
+            n, me, where = place_in(group, self.sizes)
+
+            def part(j, i=i, what=what):
+                if what == "own":
+                    return ins[i].at[j]
+                return ins[i].at[what, lax.rem(j, ins[i].shape[1])]
+
+            for k in range(1, n):
+                peer = lax.rem(me + k, n)
+                made.append(
+                    pltpu.make_async_remote_copy(
+                        src_ref=part(peer),
+                        dst_ref=outs[i].at[me],
+                        send_sem=send.at[self.first[i] + k],
+                        recv_sem=recv.at[self.first[i] + k],
+                        device_id=where(peer),
+                        device_id_type=MESH,
+                    )
+                )
+            made.append(pltpu.make_async_copy(part(me), outs[i].at[me], local.at[i]))
+        return made
+
+
+def head_copies(buf, out, sems, m, ctx, tok, sizes):
+    send, recv, local = sems
+    n, me, where = place_in("line", sizes)
+    rows = pl.ds(m * tok, tok)
+    made = []
+    for k in range(1, n):
+        peer = lax.rem(me + k, n)
+        made.append(
+            pltpu.make_async_remote_copy(
+                src_ref=buf.at[m, peer],
+                dst_ref=out.at[me, rows],
+                send_sem=send.at[m * n + k],
+                recv_sem=recv.at[m * n + k],
+                device_id=where(peer),
+                device_id_type=MESH,
+            )
+        )
+    made.append(pltpu.make_async_copy(buf.at[m, me], out.at[me, rows], local.at[m]))
+    return made
+
+
+def head_scratch(micro, ctx, tok, width):
+    return [
+        pltpu.VMEM((micro, ctx, tok, width), BF),
+        pltpu.SemaphoreType.DMA((micro * ctx,)),
+        pltpu.SemaphoreType.DMA((micro * ctx,)),
+        pltpu.SemaphoreType.DMA((micro,)),
+    ]
 
 
 def swap_halves(x):
@@ -420,12 +513,15 @@
     return (ki <= qi) & ((sr == 0) | (sr == seg_col))
 
 
-def attention_forward(x, seg_row, seg_col, ctx, hq, tok):
+def attention_forward(x, seg_row, seg_col, ctx, hq, tok, sizes, cid):
     micro = x.shape[1] // tok
     length = ctx * tok
     per = QB // tok
 
-    def kernel(x_ref, sr_ref, sc_ref, o_ref, l_ref):
+    meet = Carried([], sizes)
+
+    def kernel(x_ref, sr_ref, sc_ref, o_ref, l_ref, mixed_ref, buf, *sems):
+        m = pl.program_id(0)
         xs = x_ref[...].reshape(length, 256)
         ks = xs[:, 128:192]
         vs = xs[:, 192:256]
@@ -447,14 +543,31 @@
             for _ in range(hq, 2):
                 outs.append(jnp.zeros((QB, HS), F32))
                 lses.append(jnp.zeros((QB, HS), F32))
-            o_ref[qb * per : (qb + 1) * per] = (
-                jnp.concatenate(outs, axis=1).astype(BF).reshape(per, tok, 128)
-            )
+            done = jnp.concatenate(outs, axis=1).astype(BF).reshape(per, tok, 128)
+            o_ref[qb * per : (qb + 1) * per] = done
+            buf[m, qb * per : (qb + 1) * per] = done
             l_ref[0, rows, :] = jnp.concatenate(lses, axis=1)
+
+        @pl.when(m == 0)
+        def _():
+            meet.enter(["line"])
+
+        for copy in head_copies(buf, mixed_ref, sems, m, ctx, tok, sizes):
+            copy.start()
+
+        @pl.when(m == micro - 1)
+        def _():
+            for j in range(micro):
+                for copy in head_copies(buf, mixed_ref, sems, j, ctx, tok, sizes):
+                    copy.wait()
 
     return call(
         kernel,
-        [sds((ctx, micro * tok, 128), BF), sds((micro, length, 128), F32)],
+        [
+            sds((ctx, micro * tok, 128), BF),
+            sds((micro, length, 128), F32),
+            sds((ctx, micro * tok, 128), BF),
+        ],
         [x, seg_row, seg_col],
         2 * micro * hq * length * length * HS,
         in_specs=[
@@ -465,17 +578,35 @@
         out_specs=(
             pl.BlockSpec((ctx, tok, 128), lambda m: (0, m, 0)),
             pl.BlockSpec((1, length, 128), lambda m: (m, 0, 0)),
+            ANY_SPEC,
         ),
         grid=(micro,),
-    )
-
-
-def attention_backward(x, d_out, out, lse, seg_row, seg_col, ctx, hq, tok):
+        scratch=head_scratch(micro, ctx, tok, 128),
+        cid=cid,
+    )
+
+
+def attention_backward(x, d_out, out, lse, seg_row, seg_col, ctx, hq, tok, ops, sizes, cid):
     micro = x.shape[1] // tok
     length = ctx * tok
     per = QB // tok
 
-    def kernel(x_ref, d_ref, o_ref, l_ref, sr_ref, sc_ref, dx_ref, dk_ref, dv_ref):
+    carry = Carried(ops, sizes)
+    count = len(ops)
+
+    def kernel(x_ref, d_ref, o_ref, l_ref, sr_ref, sc_ref, *rest):
+        ins, out_ref, outs = rest[:count], rest[count], rest[count + 1 : 2 * count + 1]
+        dk_ref, dv_ref, buf, *sems = rest[2 * count + 1 :]
+        sems, carry_sems = sems[:3], sems[3:]
+        m = pl.program_id(0)
+        dx_ref = buf.at[m]
+
+        @pl.when(m == 0)
+        def _():
+            carry.enter(["line"] + [group for _, group, _ in ops if group != "line"])
+            for copy in carry.copies(ins, outs, carry_sems):
+                copy.start()
+
         xs = x_ref[...].reshape(length, 256)
         ks = xs[:, 128:192]
         vs = xs[:, 192:256]
@@ -512,11 +643,21 @@
             .astype(BF)
             .reshape(ctx, tok, 128)
         )
+        for copy in head_copies(buf, out_ref, sems, m, ctx, tok, sizes):
+            copy.start()
+
+        @pl.when(m == micro - 1)
+        def _():
+            for j in range(micro):
+                for copy in head_copies(buf, out_ref, sems, j, ctx, tok, sizes):
+                    copy.wait()
+            for copy in carry.copies(ins, outs, carry_sems):
+                copy.wait()
 
     return call(
         kernel,
-        [sds((ctx, micro * tok, 256), BF)],
-        [x, d_out, out, lse, seg_row, seg_col],
+        [sds((ctx, micro * tok, 256), BF)] + carry.shapes,
+        [x, d_out, out, lse, seg_row, seg_col] + [o[0] for o in ops],
         5 * micro * hq * length * length * HS,
         in_specs=[
             pl.BlockSpec((ctx, tok, 256), lambda m: (0, m, 0)),
@@ -525,11 +666,15 @@
             pl.BlockSpec((1, length, 128), lambda m: (m, 0, 0)),
             pl.BlockSpec((1, 1, length), lambda m: (m, 0, 0)),
             pl.BlockSpec((1, length, 1), lambda m: (m, 0, 0)),
-        ],
-        out_specs=(pl.BlockSpec((ctx, tok, 256), lambda m: (0, m, 0)),),
+        ]
+        + [ANY_SPEC] * count,
+        out_specs=tuple([ANY_SPEC] * (count + 1)),
         grid=(micro,),
-        scratch=[pltpu.VMEM((length, HS), F32), pltpu.VMEM((length, HS), F32)],
-    )[0]
+        scratch=[pltpu.VMEM((length, HS), F32), pltpu.VMEM((length, HS), F32)]
+        + head_scratch(micro, ctx, tok, 256)
+        + carry.scratch(),
+        cid=cid,
+    )
 
 
 def side_by_side(m_ref, ctx, hq):
@@ -716,13 +861,26 @@
     )
 
 
-def experts_forward(x, gates, slots, weights, held):
+def experts_forward(x, gates, slots, weights, held, ops=(), sizes=None, cid=None):
     n, rows, _ = x.shape
     lanes = 2 * SLOTS
 
 
-    def kernel(x_ref, g_ref, s_ref, w0, w1, out_ref, acc_ref, row_ref, eo_ref):
+    carry = Carried(ops, sizes)
+    count = len(ops)
+
+    def kernel(x_ref, g_ref, s_ref, w0, w1, *rest):
+        ins, out_ref, outs = rest[:count], rest[count], rest[count + 1 : 2 * count + 1]
+        acc_ref, row_ref, eo_ref, *sems = rest[2 * count + 1 :]
         e = pl.program_id(0)
+        if count:
+
+            @pl.when(e == 0)
+            def _():
+                carry.enter(sorted(set(group for _, group, _ in ops)))
+                for copy in carry.copies(ins, outs, sems):
+                    copy.start()
+
         w_gate, w_up, down_l, down_r = matrices(w0, w1)
         for s in range(n):
             pick = pick_matrix(s_ref[s, pl.ds(e, 1), :], rows).astype(BF)
@@ -750,21 +908,32 @@
             def _():
                 out_ref[s] = (acc_ref[s].astype(F32) + add).astype(BF)
 
+        if count:
+
+            @pl.when(e == held - 1)
+            def _():
+                for copy in carry.copies(ins, outs, sems):
+                    copy.wait()
+
     flops = 2 * held * n * (lanes * D * F * 3 + 2 * lanes * rows * D)
     return call(
         kernel,
-        [sds(x.shape, BF)],
-        [x, gates, slots] + list(weights),
+        [sds(x.shape, BF)] + carry.shapes,
+        [x, gates, slots] + list(weights) + [o[0] for o in ops],
         flops,
-        in_specs=[full(x.shape), full(gates.shape), full(slots.shape)] + weight_specs(weights),
-        out_specs=(full(x.shape),),
+        in_specs=[full(x.shape), full(gates.shape), full(slots.shape)]
+        + weight_specs(weights)
+        + [ANY_SPEC] * count,
+        out_specs=tuple([full(x.shape)] + [ANY_SPEC] * count),
         grid=(held,),
         scratch=[
             pltpu.VMEM(x.shape, F32),
             pltpu.VMEM((n * lanes, D), BF),
             pltpu.VMEM((n * lanes, D), BF),
-        ],
-    )[0]
+        ]
+        + carry.scratch(),
+        cid=cid,
+    )
 
 
 def experts_backward(x, g, gates, slots, weights, held):
@@ -824,14 +993,15 @@
         dslot = (grows.astype(F32) * gate).astype(BF)
         ctx, depth, _ = first_grad.shape[1:]
         part = F // ctx
-        first_grad[0] = dot(rws, dga, 0, 0).astype(BF).reshape(ctx, depth, F)
-        second_grad[0, :, :depth, :] = dot(rws, dup, 0, 0).astype(BF).reshape(ctx, depth, F)
+        both = dot(rws, jnp.concatenate([dga, dup], axis=1), 0, 0).astype(BF)
+        first_grad[0] = both[:, :F].reshape(ctx, depth, F)
+        second_grad[0, :, :depth, :] = both[:, F:].reshape(ctx, depth, F)
+        down = dot(hidden, dslot, 0, 0).astype(BF)
         for k in range(2):
-            cols = dslot[:, D // 2 * k : D // 2 * (k + 1)]
             at_row = depth + part * k
-            second_grad[0, :, at_row : at_row + part, :] = (
-                dot(hidden, cols, 0, 0).astype(BF).reshape(ctx, part, D // 2)
-            )
+            second_grad[0, :, at_row : at_row + part, :] = down[
+                :, D // 2 * k : D // 2 * (k + 1)
+            ].reshape(ctx, part, D // 2)
 
     outs = [sds(x.shape, BF), sds(gates.shape, F32)] + [sds(w.shape, BF) for w in weights]
     out_specs = [full(x.shape), full(gates.shape)] + weight_specs(weights)
@@ -996,11 +1166,11 @@
         return lax.all_gather(w[None], ("grp", "core"), axis=0, tiled=True)
 
     grad_rows = grad_out.reshape(rows, D)
-    (gate_parts,) = move((w_gate[0], "line", "pick"))
+    (gate_parts,) = move((w_gate, "line", 0))
     gate_parts, own_pack, own_second = lax.optimization_barrier(
         (gate_parts, pack(0), second_shard(0))
     )
-    first, second_parts = move((own_pack, None, "packed"), (own_second, "line", "pick"))
+    first, second_parts = move((own_pack, None, "packed"), (own_second[None], "line", 0))
     first, late_pack = lax.optimization_barrier((first, pack(1)))
     packed = [first.reshape(D, -1), lax.all_gather(late_pack, every, axis=0, tiled=True)]
     weights = [[plane_gather(gate_parts), plane_gather(second_parts)], None]
@@ -1047,28 +1217,31 @@
         qkv, gains = got[0], got[1]
         stream = parts[0] if layer == 0 else got[2]
         (heads,) = move((qkv, "line", "own"))
-        out, lse = attention_forward(heads, seg_row, seg_col, ctx, hq, tok)
-        (mixed,) = move((out, "line", "own"))
+        out, lse, mixed = attention_forward(
+            heads, seg_row, seg_col, ctx, hq, tok, sizes, next(ids_of)
+        )
         stream1, normed, gates = output_forward(
             mixed, stream, packed[layer], gains, chosen_f, ctx, hq, planes, held
         )
         ops = [(normed, "tok", "all"), (gates, "tok", "own")]
         if layer == 0:
             xs, gates_here, slots_here, late_gate = move(
-                *ops, (slot, "tok", "own"), (w_gate[1], "line", "pick")
+                *ops, (slot, "tok", "own"), (w_gate, "line", 1)
             )
-            late_second, xs = lax.optimization_barrier((second_shard(1), xs))
-            late_second = along_line(late_second)
             late_gate = plane_gather(late_gate)
         else:
             xs, gates_here, last_g = move(*ops, (grad_rows, "tok", "all"))
         saved.append((stream, heads, out, lse, mixed, stream1, normed, gates, gains, xs, gates_here))
-        sent = experts_forward(xs, gates_here, slots_here, weights[layer], held)
         if layer == 0:
-            sent, late_second = lax.optimization_barrier((sent, late_second))
+            sent, late_second = experts_forward(
+                xs, gates_here, slots_here, weights[0], held,
+                [(second_shard(1)[None], "line", 0)], sizes, next(ids_of),
+            )
             (came,) = move((sent, "tok", "own"))
             weights[1] = [late_gate, plane_gather(late_second)]
             parts = (stream1, came)
+        else:
+            (sent,) = experts_forward(xs, gates_here, slots_here, weights[1], held)
 
     sent, last_g = lax.optimization_barrier((sent, last_g))
     final_sum = lax.psum_scatter(sent, "zp", scatter_dimension=0, tiled=True)[0]
@@ -1128,12 +1301,14 @@
         else:
             d_out, came, last_wide = move(*ops, (over_grp(last_wide), "z", "own"))
         small = with_other(small, came)
-        dx = attention_backward(heads, d_out, out, lse, seg_row, seg_col, ctx, hq, tok)
-        ops = [(dx, "line", "own"), (small, "g", "own")]
-        if last:
-            dx, small = move(*ops)
-        else:
-            dx, small, last_gate = move(*ops, (last_experts[0], "line", "own"))
+        ops = [(small, "g", "own")]
+        if not last:
+            ops.append((last_experts[0], "line", "own"))
+        dx, small, *came = attention_backward(
+            heads, d_out, out, lse, seg_row, seg_col, ctx, hq, tok, ops, sizes, next(ids_of)
+        )
+        if not last:
+            last_gate = came[0]
         g, wide = qkv_backward(
             dx, g1, stream, packed[layer], gains, cos_t, sin_t, ctx, hq, shard
         )

time: 1140 us -> 1110 us (0.974)
  waiting for transfers between devices: 43.7 us -> 3.01 us
  Pallas kernels: 1000 us -> 1020 us
    pallas_call x18, Pallas kernels: 280 us -> 388 us  [call(): pl.pallas_call(kernel, out_shape=tuple(outs), scratch_shapes=list(scratch...]
    pallas_call x18 -> x14, Pallas kernels: 721 us -> 633 us  [transfer(): pl.pallas_call(kernel, out_shape=tuple(shapes), in_specs=[any_spec] * cou...]
    all_to_all x1 -> x0, waiting for transfers between devices: 40.7 us -> none  [along_line(): return lax.all_to_all(w, line, 0, 0, tiled=True)]
  transfers between devices with their start and end apart: 13 -> 12, of which waited for: 2 -> 1; matrix products, arithmetic and copies ran while one was open for 3% -> 3% of each run, Pallas kernels for 81% -> 85%
where the time goes in v5:
time: 1110 us; the launch traced here: 1090 us
  Pallas kernels  1020 us (92%)
  other arithmetic  30.7 us (3%)
  local copies, waits for them, and re-layouts  16.1 us (1%)
  between operations  15.1 us (1%)
    pallas_call x14, Pallas kernels, transfer(): pl.pallas_call(kernel, out_shape=tuple(shapes), in_specs=[any_spec] * cou...  633 us
    pallas_call x18, Pallas kernels, call(): pl.pallas_call(kernel, out_shape=tuple(outs), scratch_shapes=list(scratch...  388 us
  transfers between devices with their start and end apart: 12, of which 1 were waited for; matrix products, arithmetic and copies ran while one was open for 3% of the time, Pallas kernels for 85%

profile of v5, /device:TPU:0, one launch (start us, length us, event | category | flops | bytes accessed | tf_op | source)
XLA Modules:
  0.0 1092.0 jit_solution(918538047286092772)
XLA Ops:
  7.3 23.0 %shard_map.229 = bf16[8,128,512]{2,1,0:T(8,128)(2,1)} custom-call(bf16[2,8,128,512]{3,2,1,0:T(8,128)(2,1)} %refs_3_.1), custom_call_target="tpu_custom_call" | custom-call | bytes 41943040 | tf_op jit(solution)/shard_map/pallas_call | solution.py:323
  30.9 1.4 copy-done.6
  33.7 1.5 pad_maximum_fusion
  36.0 70.2 %shard_map.230 = (bf16[4,8,32,3200]{3,2,1,0:T(8,128)(2,1)}, bf16[8,256,512]{2,1,0:T(8,128)(2,1)}) custom-call(bf16[32,3200]{1,0:T(8,128)(2,1)} %concatenate.12.refs_0_, bf16[1,8,256,512]{3,2,1,0:T(8,128)(2,1)} %bitcast.110), custom_call_target="tpu_custom_call" | custom-call | bytes 346030080 | tf_op jit(solution)/shard_map/pallas_call | solution.py:323
  108.6 1.8 fusion.5
  110.4 5.2 shard_map.231
  115.6 23.3 %shard_map.232.x_ref = bf16[8,256,256]{2,1,0:T(8,128)(2,1)} custom-call(bf16[8,256,256]{2,1,0:T(8,128)(2,1)} %get-tuple-element.115.refs_0_), custom_call_target="tpu_custom_call" | custom-call | bytes 41943040 | tf_op jit(solution)/shard_map/pallas_call | solution.py:323
  141.4 25.9 %shard_map.233 = (bf16[8,256,128]{2,1,0:T(8,128)(2,1)}, f32[2,1024,128]{2,1,0:T(8,128)}, bf16[8,256,128]{2,1,0:T(8,128)(2,1)}) custom-call(bf16[8,256,256]{2,1,0:T(8,128)(2,1)} %shard_map.232.x_ref, s32[2,1,1024]{2,1,0:T(1,128)} %broadcast_in_dim.58.sr_ref, s32[2,1024,1]{2,1,0:T(8,128)} %copy.85.sc_ref), custom_call_target="tpu_custom_call" | custom-call | flops 536870912 | bytes 3162112 | tf_op jit(solution)/shard_map/pallas_call | solution.py:40
  167.3 4.4 shard_map.234
  172.2 69.4 %shard_map.235 = (bf16[4,256,1024]{2,1,0:T(8,128)(2,1)}, f32[4,8,256]{2,1,0:T(8,128)}, s32[4,8,256]{2,1,0:T(8,128)}, bf16[8,128,512]{2,1,0:T(8,128)(2,1)}) custom-call(bf16[256,1024]{1,0:T(8,128)(2,1)} %get-tuple-element.119.refs_0_.nm_ref, f32[4,8,256]{2,1,0:T(8,128)} %get-tuple-element.120.refs_1_.gt_ref, s32[4,8,256]{2,1,0:T(8,128)} %bitcast_select_fusion.refs_2_, ...), custom_call_target="tpu_custom_call" | custom-call | bytes 128450560 | tf_op jit(solution)/shard_map/pallas_call | solution.py:323
  242.0 1.6 maximum_bitcast_fusion.rest_0_
  243.5 48.3 %shard_map.236 = (bf16[4,256,1024]{2,1,0:T(8,128)(2,1)}, bf16[8,256,512]{2,1,0:T(8,128)(2,1)}) custom-call(bf16[4,256,1024]{2,1,0:T(8,128)(2,1)} %get-tuple-element.121.x_ref, f32[4,8,256]{2,1,0:T(8,128)} %get-tuple-element.122.g_ref, s32[4,8,256]{2,1,0:T(8,128)} %get-tuple-element.123.s_ref, bf16[8,8,128,512]{3,2,1,0:T(8,128)(2,1)} %bitcast.140, ...), custom_call_target="tpu_custom_call" | custom-call | flops 12884901888 | bytes 33619968 | tf_op jit(solution)/shard_map/pallas_call | solution.py:40
  291.9 64.2 %shard_map.237.refs_1_ = bf16[4,256,1024]{2,1,0:T(8,128)(2,1)} custom-call(bf16[4,256,1024]{2,1,0:T(8,128)(2,1)} %get-tuple-element.126.refs_0_), custom_call_target="tpu_custom_call" | custom-call | bytes 83886080 | tf_op jit(solution)/shard_map/pallas_call | solution.py:323
  356.1 6.1 shard_map.238
  362.3 31.9 %shard_map.239.x_ref = bf16[8,256,256]{2,1,0:T(8,128)(2,1)} custom-call(bf16[8,256,256]{2,1,0:T(8,128)(2,1)} %get-tuple-element.128.refs_0_), custom_call_target="tpu_custom_call" | custom-call | bytes 41943040 | tf_op jit(solution)/shard_map/pallas_call | solution.py:323
  394.2 25.9 %shard_map.240 = (bf16[8,256,128]{2,1,0:T(8,128)(2,1)}, f32[2,1024,128]{2,1,0:T(8,128)}, bf16[8,256,128]{2,1,0:T(8,128)(2,1)}) custom-call(bf16[8,256,256]{2,1,0:T(8,128)(2,1)} %shard_map.239.x_ref, s32[2,1,1024]{2,1,0:T(1,128)} %broadcast_in_dim.58.sr_ref, s32[2,1024,1]{2,1,0:T(8,128)} %copy.85.sc_ref), custom_call_target="tpu_custom_call" | custom-call | flops 536870912 | bytes 3162112 | tf_op jit(solution)/shard_map/pallas_call | solution.py:40
  420.1 4.1 shard_map.241
  424.2 74.9 %shard_map.242 = (bf16[4,256,1024]{2,1,0:T(8,128)(2,1)}, f32[4,8,256]{2,1,0:T(8,128)}, bf16[4,256,1024]{2,1,0:T(8,128)(2,1)}) custom-call(bf16[256,1024]{1,0:T(8,128)(2,1)} %get-tuple-element.133.refs_0_.nm_ref, f32[4,8,256]{2,1,0:T(8,128)} %get-tuple-element.134.refs_1_.gt_ref, bf16[256,1024]{1,0:T(8,128)(2,1)} %bitcast.117), custom_call_target="tpu_custom_call" | custom-call | bytes 169082880 | tf_op jit(solution)/shard_map/pallas_call | solution.py:323
  499.2 29.9 %shard_map.243 = bf16[4,256,1024]{2,1,0:T(8,128)(2,1)} custom-call(bf16[4,256,1024]{2,1,0:T(8,128)(2,1)} %get-tuple-element.135.x_ref, f32[4,8,256]{2,1,0:T(8,128)} %get-tuple-element.136.g_ref, s32[4,8,256]{2,1,0:T(8,128)} %get-tuple-element.123.s_ref, bf16[8,8,128,512]{3,2,1,0:T(8,128)(2,1)} %bitcast.142, bf16[8,8,256,512]{3,2,1,0:T(8,128)(2,1)} %bitcast.138), custom_call_target="tpu_custom_call" | custom-call | flops 12884901888 | bytes 29425664 | tf_op jit(solution)/shard_map/pallas_call | solution.py:40
  529.6 55.8 %shard_map.244 = (bf16[4,256,1024]{2,1,0:T(8,128)(2,1)}, f32[4,8,256]{2,1,0:T(8,128)}, bf16[8,8,128,512]{3,2,1,0:T(8,128)(2,1)}, bf16[8,8,256,512]{3,2,1,0:T(8,128)(2,1)}) custom-call(bf16[4,256,1024]{2,1,0:T(8,128)(2,1)} %get-tuple-element.135.x_ref, bf16[4,256,1024]{2,1,0:T(8,128)(2,1)} %get-tuple-element.140.gr_ref, ...), custom_call_target="tpu_custom_call" | custom-call | flops 33822867456 | bytes 56721408 | tf_op jit(solution)/shard_map/pallas_call | solution.py:40
  585.4 47.8 %shard_map.245 = (bf16[4,256,1024]{2,1,0:T(8,128)(2,1)}, f32[4,8,256]{2,1,0:T(8,128)}) custom-call(bf16[4,256,1024]{2,1,0:T(8,128)(2,1)} %get-tuple-element.148.refs_0_, f32[4,8,256]{2,1,0:T(8,128)} %get-tuple-element.149.refs_1_), custom_call_target="tpu_custom_call" | custom-call | bytes 85196800 | tf_op jit(solution)/shard_map/pallas_call | solution.py:323
  633.3 6.7 shard_map.246
  640.0 12.3 %shard_map.247 = (bf16[8,256,128]{2,1,0:T(8,128)(2,1)}, bf16[512,1152]{1,0:T(8,128)(2,1)}) custom-call(bf16[8,256,128]{2,1,0:T(8,128)(2,1)} %get-tuple-element.153.refs_0_, bf16[2,512,1152]{2,1,0:T(8,128)(2,1)} %get-tuple-element.154.refs_1_), custom_call_target="tpu_custom_call" | custom-call | bytes 68157440 | tf_op jit(solution)/shard_map/pallas_call | solution.py:323
  652.4 2.7 fusion.3
  655.0 33.8 %shard_map.248 = (bf16[8,256,256]{2,1,0:T(8,128)(2,1)}, bf16[4,4,32,1152]{3,2,1,0:T(8,128)(2,1)}) custom-call(bf16[8,256,256]{2,1,0:T(8,128)(2,1)} %shard_map.239.x_ref, bf16[8,256,128]{2,1,0:T(8,128)(2,1)} %get-tuple-element.155.d_ref, bf16[8,256,128]{2,1,0:T(8,128)(2,1)} %get-tuple-element.156.o_ref, f32[2,1024,128]{2,1,0:T(8,128)} %get-tuple-element.157.l_ref, ...), custom_call_target="tpu_custom_call" | custom-call | flops 1342177280 | bytes 6569984 | tf_op jit(solution)/shard_map/pallas_call | solution.py:40
  688.8 8.5 shard_map.249
  697.4 2.3 convert_element_type.109.refs_0_
  700.6 50.0 %shard_map.250 = (bf16[4,256,1024]{2,1,0:T(8,128)(2,1)}, bf16[4,32,1152]{2,1,0:T(8,128)(2,1)}, bf16[512,2176]{1,0:T(8,128)(2,1)}) custom-call(bf16[256,1024]{1,0:T(8,128)(2,1)} %convert_element_type.109.refs_0_, bf16[4,32,1152]{2,1,0:T(8,128)(2,1)} %reduce_sum.68.refs_1_, bf16[2,512,2176]{2,1,0:T(8,128)(2,1)} %get-tuple-element.163.refs_2_), custom_call_target="tpu_custom_call" | custom-call | bytes 184811520 | tf_op jit(solution)/shard_map/pallas_call | solution.py:323
  750.6 3.6 all-to-all-start
  754.3 56.3 %shard_map.251 = (bf16[4,256,1024]{2,1,0:T(8,128)(2,1)}, f32[4,8,256]{2,1,0:T(8,128)}, bf16[8,8,128,512]{3,2,1,0:T(8,128)(2,1)}, bf16[8,8,256,512]{3,2,1,0:T(8,128)(2,1)}) custom-call(bf16[4,256,1024]{2,1,0:T(8,128)(2,1)} %get-tuple-element.121.x_ref, bf16[4,256,1024]{2,1,0:T(8,128)(2,1)} %get-tuple-element.166.gr_ref, ...), custom_call_target="tpu_custom_call" | custom-call | flops 33822867456 | bytes 56721408 | tf_op jit(solution)/shard_map/pallas_call | solution.py:40
  813.6 3.5 fusion.1
  817.1 51.2 %shard_map.252 = (bf16[4,256,1024]{2,1,0:T(8,128)(2,1)}, f32[4,8,256]{2,1,0:T(8,128)}, bf16[4,4,32,2176]{3,2,1,0:T(8,128)(2,1)}) custom-call(bf16[4,256,1024]{2,1,0:T(8,128)(2,1)} %get-tuple-element.172.refs_0_, f32[4,8,256]{2,1,0:T(8,128)} %get-tuple-element.173.refs_1_, bf16[4,4,32,2176]{3,2,1,0:T(8,128)(2,1)} %bitcast.108), custom_call_target="tpu_custom_call" | custom-call | bytes 174325760 | tf_op jit(solution)/shard_map/pallas_call | solution.py:323
  868.3 2.9 reduce_sum.69.refs_2_
  871.2 7.0 shard_map.253
  878.3 25.5 %shard_map.254 = (bf16[8,256,128]{2,1,0:T(8,128)(2,1)}, bf16[512,1152]{1,0:T(8,128)(2,1)}, bf16[4,32,2176]{2,1,0:T(8,128)(2,1)}) custom-call(bf16[8,256,128]{2,1,0:T(8,128)(2,1)} %get-tuple-element.177.refs_0_, bf16[2,512,1152]{2,1,0:T(8,128)(2,1)} %get-tuple-element.178.refs_1_, bf16[4,32,2176]{2,1,0:T(8,128)(2,1)} %reduce_sum.69.refs_2_), custom_call_target="tpu_custom_call" | custom-call | bytes 90439680 | tf_op jit(solution)/shard_map/pallas_call | solution.py:323
  903.8 2.6 fusion.2
  906.4 49.9 %shard_map.255 = (bf16[8,256,256]{2,1,0:T(8,128)(2,1)}, bf16[4,4,32,1152]{3,2,1,0:T(8,128)(2,1)}, bf16[8,128,512]{2,1,0:T(8,128)(2,1)}) custom-call(bf16[8,256,256]{2,1,0:T(8,128)(2,1)} %shard_map.232.x_ref, bf16[8,256,128]{2,1,0:T(8,128)(2,1)} %get-tuple-element.180.d_ref, bf16[8,256,128]{2,1,0:T(8,128)(2,1)} %get-tuple-element.181.o_ref, ...), custom_call_target="tpu_custom_call" | custom-call | flops 1342177280 | bytes 8667136 | tf_op jit(solution)/shard_map/pallas_call | solution.py:40
  956.3 9.1 shard_map.256
  965.5 1.9 dynamic-slice_bitcast_fusion
  970.4 2.2 collective-permute-done
  972.6 4.2 fusion
  976.8 57.8 %shard_map.257 = (bf16[4,4,32,2176]{3,2,1,0:T(8,128)(2,1)}, bf16[8,256,512]{2,1,0:T(8,128)(2,1)}, bf16[4,32,1152]{2,1,0:T(8,128)(2,1)}) custom-call(bf16[4,4,32,2176]{3,2,1,0:T(8,128)(2,1)} %bitcast.107, bf16[8,256,512]{2,1,0:T(8,128)(2,1)} %bitcast.119, bf16[4,32,1152]{2,1,0:T(8,128)(2,1)} %reduce_sum.70.refs_2_), custom_call_target="tpu_custom_call" | custom-call | bytes 184811520 | tf_op jit(solution)/shard_map/pallas_call | solution.py:323
  1034.6 3.0 reduce_sum.71.refs_0_
  1037.6 31.7 %shard_map.258 = (bf16[4,32,2176]{2,1,0:T(8,128)(2,1)}, bf16[8,128,512]{2,1,0:T(8,128)(2,1)}) custom-call(bf16[4,32,2176]{2,1,0:T(8,128)(2,1)} %reduce_sum.71.refs_0_, bf16[8,128,512]{2,1,0:T(8,128)(2,1)} %bitcast.122), custom_call_target="tpu_custom_call" | custom-call | bytes 64225280 | tf_op jit(solution)/shard_map/pallas_call | solution.py:323
  1069.3 2.3 shard_map.259
  1071.6 1.4 slice_reduce_fusion.1
  1073.0 1.5 slice_reduce_fusion
  1076.0 8.7 shard_map.260
  (113 shorter events, 17.5 us)
Async XLA Ops:
  7.2 23.1 %copy-start.15 = (bf16[2,32,32]{2,1,0:T(8,128)(2,1)S(1)}, bf16[2,32,32]{2,1,0:T(8,128)(2,1)}, u32[]{:S(2)}) copy-start(bf16[2,32,32]{2,1,0:T(8,128)(2,1)} %param.24) | copy-start | bytes 12292
  7.2 23.3 %copy-start.17 = (bf16[2,32]{1,0:T(2,128)(2,1)S(1)}, bf16[2,32]{1,0:T(2,128)(2,1)}, u32[]{:S(2)}) copy-start(bf16[2,32]{1,0:T(2,128)(2,1)} %param.18) | copy-start | bytes 388
  7.2 23.4 %copy-start.18 = (bf16[2,32]{1,0:T(2,128)(2,1)S(1)}, bf16[2,32]{1,0:T(2,128)(2,1)}, u32[]{:S(2)}) copy-start(bf16[2,32]{1,0:T(2,128)(2,1)} %param.23) | copy-start | bytes 388
  7.2 23.5 %copy-start.5 = (bf16[2,8,64,1024]{3,2,1,0:T(8,128)(2,1)S(1)}, bf16[2,8,64,1024]{3,2,1,0:T(8,128)(2,1)}, u32[]{:S(2)}) copy-start(bf16[2,8,64,1024]{3,2,1,0:T(8,128)(2,1)} %param.27) | copy-start | bytes 6291460
  7.2 236.3 %all-gather.12.cloned.1.call-start = ((), (), s32[]{:S(2)}) async-start(), calls=%async_computation.12 | async-start | bytes 9437184 | tf_op jit(solution)/shard_map/all_gather | solution.py:1166
  30.7 1.6 copy-start.6
  32.3 0.9 copy-start.11
  32.3 1.0 copy-start.12
  32.4 1.0 copy-start.13
  32.4 1.0 copy-start.14
  35.9 207.6 %all-gather.14.cloned.1.call-start = ((), (), s32[]{:S(2)}) async-start(), calls=%async_computation.13 | async-start | bytes 18874368 | tf_op jit(solution)/shard_map/all_gather | solution.py:1166
  36.0 71.5 %copy-start.10 = (s32[2,1024]{1,0:T(2,128)S(1)}, s32[2,1024]{1,0:T(2,128)}, u32[]{:S(2)}) copy-start(s32[2,1024]{1,0:T(2,128)} %param.16) | copy-start | bytes 24580
  106.2 249.9 %all-gather.10.cloned.1.call-start = ((), (), s32[]{:S(2)}) async-start(), calls=%async_computation.6 | async-start | bytes 6758400 | tf_op jit(solution)/shard_map/all_gather | solution.py:1175
  107.4 391.7 %all-gather.16.cloned.1.call-start = ((), (), s32[]{:S(2)}) async-start(), calls=%async_computation.14 | async-start | bytes 9437184 | tf_op jit(solution)/shard_map/all_gather | solution.py:1166
  115.6 24.8 %copy-start.16 = (s32[2,128,8]{1,2,0:T(8,128)S(1)}, s32[2,128,8]{1,2,0:T(8,128)}, u32[]{:S(2)}) copy-start(s32[2,128,8]{1,2,0:T(8,128)} %param.17) | copy-start | bytes 24580
  241.7 257.5 %all-gather.18.cloned.1.call-start = ((), (), s32[]{:S(2)}) async-start(), calls=%async_computation.15 | async-start | bytes 18874368 | tf_op jit(solution)/shard_map/all_gather | solution.py:1166
  291.9 293.5 %reduce-scatter.6.cloned.1.call-start = ((), (), s32[]{:S(2)}) async-start(), calls=%async_computation.7 | async-start | bytes 2621440 | tf_op jit(solution)/shard_map/reduce_scatter | solution.py:1247
  529.1 221.5 %reduce-scatter.8.cloned.1.call-start = ((), (), s32[]{:S(2)}) async-start(), calls=%async_computation.8 | async-start | bytes 18874368 | tf_op jit(solution)/shard_map/reduce_scatter | solution.py:1251
  585.4 321.0 %reduce-scatter.10.cloned.1.call-start = ((), (), s32[]{:S(2)}) async-start(), calls=%async_computation.9 | async-start | bytes 9437184 | tf_op jit(solution)/shard_map/reduce_scatter | solution.py:1251
  640.0 12.3 %copy-start.1 = (bf16[2,512,1152]{2,1,0:T(8,128)(2,1)S(1)}, bf16[2,512,1152]{2,1,0:T(8,128)(2,1)}, u32[]{:S(2)}) copy-start(bf16[2,512,1152]{2,1,0:T(8,128)(2,1)} %get-tuple-element.154.refs_1_) | copy-start | bytes 7077892
  697.4 2.3 copy-start.8
  750.6 60.0 %all-to-all-start = ((bf16[8,256,512]{2,1,0:T(8,128)(2,1)}), bf16[8,256,512]{2,1,0:T(8,128)(2,1)S(1)}, u32[]{:S(2)}, u32[]{:S(2)}) async-start(bf16[8,256,512]{2,1,0:T(8,128)(2,1)} %bitcast.120), calls=%async_computation.2 | async-start | bytes 4194304 | tf_op jit(solution)/shard_map/all_to_all | solution.py:1279
  754.3 222.5 %reduce-scatter.12.cloned.1.call-start = ((), (), s32[]{:S(2)}) async-start(), calls=%async_computation.10 | async-start | bytes 18874368 | tf_op jit(solution)/shard_map/reduce_scatter | solution.py:1251
  810.6 1.4 copy-start
  812.0 225.6 %reduce-scatter.14.cloned.1.call-start = ((), (), s32[]{:S(2)}) async-start(), calls=%async_computation.11 | async-start | bytes 9437184 | tf_op jit(solution)/shard_map/reduce_scatter | solution.py:1251
  812.0 1.6 copy-start.4
  878.3 25.5 %copy-start.2 = (bf16[2,512,1152]{2,1,0:T(8,128)(2,1)S(1)}, bf16[2,512,1152]{2,1,0:T(8,128)(2,1)}, u32[]{:S(2)}) copy-start(bf16[2,512,1152]{2,1,0:T(8,128)(2,1)} %get-tuple-element.178.refs_1_) | copy-start | bytes 7077892
  965.5 3.0 copy-start.3
  965.5 3.0 copy-start.9
  965.5 3.9 copy-start.7
  967.4 5.1 collective-permute-start
Sparse Core Ops, SparseCore 0:
  36.0 87.9 all-gather.11
  125.9 89.0 all-gather.13
  218.5 99.8 all-gather.9
  320.2 54.7 all-gather.15
  376.7 89.9 all-gather.17
  529.2 43.7 reduce-scatter.5
  585.5 126.7 reduce-scatter.7
  716.1 71.2 reduce-scatter.9
  810.8 128.9 reduce-scatter.11
  943.0 92.2 reduce-scatter.13

commit v6 on v5

--- a/solution.py
+++ b/solution.py
@@ -350,6 +350,10 @@
         for x, group, what in ops:
             n = size_of(group, sizes)
             shape = x.shape if what == "own" else (n,) + x.shape[2:]
+            if what == "all":
+                shape = (n,) + x.shape
+            elif group == "sib":
+                shape = x.shape[1:]
             self.shapes.append(sds(shape, x.dtype))
             self.first.append(self.total)
             self.total += n
@@ -382,6 +386,8 @@
             n, me, where = place_in(group, self.sizes)
 
             def part(j, i=i, what=what):
+                if what == "all":
+                    return ins[i]
                 if what == "own":
                     return ins[i].at[j]
                 return ins[i].at[what, lax.rem(j, ins[i].shape[1])]
@@ -391,14 +397,15 @@
                 made.append(
                     pltpu.make_async_remote_copy(
                         src_ref=part(peer),
-                        dst_ref=outs[i].at[me],
+                        dst_ref=outs[i] if group == "sib" else outs[i].at[me],
                         send_sem=send.at[self.first[i] + k],
                         recv_sem=recv.at[self.first[i] + k],
                         device_id=where(peer),
                         device_id_type=MESH,
                     )
                 )
-            made.append(pltpu.make_async_copy(part(me), outs[i].at[me], local.at[i]))
+            if group != "sib":
+                made.append(pltpu.make_async_copy(part(me), outs[i].at[me], local.at[i]))
         return made
 
 
@@ -448,12 +455,16 @@
     return parts[0] if len(parts) == 1 else jnp.concatenate(parts, axis=1)
 
 
-def qkv_forward(stream_parts, packed, cos_t, sin_t, ctx, hq):
+def qkv_forward(stream_parts, packed, cos_t, sin_t, ctx, hq, sizes, cid):
     first = len(stream_parts) == 1
     rows = stream_parts[0].shape[0]
     dup = ctx // KEY_VALUE_HEADS
 
+    meet = Carried([], sizes)
+
     def kernel(*refs):
+        refs, (buf, *sems) = refs[:-4], refs[-4:]
+        meet.enter(["line"])
         if first:
             h_ref, w_ref, t_ref, c_ref, s_ref, out_ref, gains_ref = refs
             x = h_ref[...].astype(F32)
@@ -482,7 +493,12 @@
             kv = i // dup
             mine.append(keys[:, HS * kv : HS * (kv + 1)])
             mine.append(values[:, HS * kv : HS * (kv + 1)])
-            out_ref[i] = in_order(mine)
+            buf[0, i] = in_order(mine)
+        copies = head_copies(buf, out_ref, sems, 0, ctx, rows, sizes)
+        for copy in copies:
+            copy.start()
+        for copy in copies:
+            copy.wait()
 
     args = list(stream_parts) + [packed, packed, cos_t, sin_t]
     in_specs = [full(a.shape) for a in stream_parts] + [
@@ -500,8 +516,10 @@
         args,
         4 * rows * D * D,
         in_specs=in_specs,
-        out_specs=tuple(full(o.shape) for o in outs),
+        out_specs=(ANY_SPEC,) + tuple(full(o.shape) for o in outs[1:]),
         grid=(1,),
+        scratch=head_scratch(1, ctx, rows, 256),
+        cid=cid,
     )
 
 
@@ -730,10 +748,20 @@
     return dx, grad_gain
 
 
-def output_backward(parts, d_gates, gates, g, stream, normed, mixed, packed, gains, ctx, hq, n, shard):
+def output_backward(parts, d_gates, gates, g, stream, normed, mixed, packed, gains, ctx, hq, n, shard, ops, sizes, cid):
     rows = stream.shape[0]
 
-    def kernel(p_ref, dg_ref, gt_ref, g_ref, x_ref, nm_ref, m_ref, w_ref, t_ref, gain_ref, g1_ref, dm_ref, gw_ref):
+    carry = Carried(ops, sizes)
+    count = len(ops)
+
+    def kernel(p_ref, dg_ref, gt_ref, g_ref, x_ref, nm_ref, m_ref, w_ref, t_ref, gain_ref, *rest):
+        ins, (g1_ref, gw_ref, dm_ref) = rest[:count], rest[count : count + 3]
+        carried, rest = rest[count + 3 : 2 * count + 3], rest[2 * count + 3 :]
+        buf, sems, carry_sems = rest[0], rest[1:4], rest[4:]
+        carry.enter(["line"] + [group for _, group, _ in ops])
+        others = carry.copies(ins, carried, carry_sems)
+        for copy in others:
+            copy.start()
         gates_v = jnp.concatenate([gt_ref[j] for j in range(n)], axis=0)
         dgate_v = jnp.concatenate([dg_ref[j] for j in range(n)], axis=0)
         mean = jnp.sum(gates_v * dgate_v, axis=0, keepdims=True)
@@ -753,7 +781,10 @@
             part = dm[:, HS * hq * i : HS * hq * (i + 1)]
             if hq < 2:
                 part = jnp.concatenate([part, jnp.zeros((rows, 128 - HS * hq), BF)], axis=1)
-            dm_ref[i] = part
+            buf[0, i] = part
+        copies = head_copies(buf, dm_ref, sems, 0, ctx, rows, sizes)
+        for copy in copies:
+            copy.start()
         grad_out = dot(side_by_side(m_ref, ctx, hq), low, 0, 0)
         for c, value in enumerate(by_core(grad_out, shard)):
             gw_ref[c, :, 0:D] = value
@@ -762,20 +793,24 @@
         cols = jnp.where(row == 33, jnp.broadcast_to(grad_gain, (128, D)), 0.0)
         for c, value in enumerate(by_core(grad_router + jnp.transpose(cols), shard)):
             gw_ref[c, :, D : D + 128] = value
-
-    outs = [sds((rows, D), F32), sds((ctx, rows, 128), BF), sds((2, D // 2, D + 128), BF)]
+        for copy in copies + others:
+            copy.wait()
+
+    outs = [sds((rows, D), F32), sds((2, D // 2, D + 128), BF), sds((ctx, rows, 128), BF)]
     args = [parts, d_gates, gates, g, stream, normed, mixed, packed, packed, gains]
     in_specs = [full(a.shape) for a in args]
     in_specs[7] = pl.BlockSpec((D, D), lambda i: (0, 2))
     in_specs[8] = pl.BlockSpec((D, 128), lambda i: (0, TAIL))
     return call(
         kernel,
-        outs,
-        args,
+        outs + carry.shapes,
+        args + [o[0] for o in ops],
         4 * rows * D * D,
-        in_specs=in_specs,
-        out_specs=tuple(full(o.shape) for o in outs),
+        in_specs=in_specs + [ANY_SPEC] * count,
+        out_specs=tuple([full(o.shape) for o in outs[:2]] + [ANY_SPEC] * (count + 1)),
         grid=(1,),
+        scratch=head_scratch(1, ctx, rows, 128) + carry.scratch(),
+        cid=cid,
     )
 
 
@@ -932,19 +967,32 @@
             pltpu.VMEM((n * lanes, D), BF),
         ]
         + carry.scratch(),
-        cid=cid,
-    )
-
-
-def experts_backward(x, g, gates, slots, weights, held):
+        cid=cid if count else None,
+    )
+
+
+def experts_backward(x, g, gates, slots, weights, held, ops=(), sizes=None, cid=None):
     n, rows, _ = x.shape
     lanes = 2 * SLOTS
 
 
+    carry = Carried(ops, sizes)
+    count = len(ops)
+
     def kernel(x_ref, gr_ref, g_ref, s_ref, w0, w1, *rest):
-        dx_ref, dg_ref = rest[:2]
-        first_grad, second_grad, acc_ref, row_ref, grow_ref = rest[2:]
+        ins, rest = rest[:count], rest[count:]
+        dx_ref, dg_ref, first_grad, second_grad, *rest = rest
+        carried, rest = rest[:count], rest[count:]
+        acc_ref, row_ref, grow_ref, *sems = rest
         e = pl.program_id(0)
+        if count:
+
+            @pl.when(e == 0)
+            def _():
+                carry.enter(sorted(set(group for _, group, _ in ops)))
+                for copy in carry.copies(ins, carried, sems):
+                    copy.start()
+
         w_gate, w_up, down_l, down_r = matrices(w0, w1)
         slot_gates = []
         for s in range(n):
@@ -1002,6 +1050,12 @@
             second_grad[0, :, at_row : at_row + part, :] = down[
                 :, D // 2 * k : D // 2 * (k + 1)
             ].reshape(ctx, part, D // 2)
+        if count:
+
+            @pl.when(e == held - 1)
+            def _():
+                for copy in carry.copies(ins, carried, sems):
+                    copy.wait()
 
     outs = [sds(x.shape, BF), sds(gates.shape, F32)] + [sds(w.shape, BF) for w in weights]
     out_specs = [full(x.shape), full(gates.shape)] + weight_specs(weights)
@@ -1013,14 +1067,16 @@
     flops = 2 * held * n * (lanes * D * F * 9 + 3 * lanes * rows * D)
     return call(
         kernel,
-        outs,
-        [x, g, gates, slots] + list(weights),
+        outs + carry.shapes,
+        [x, g, gates, slots] + list(weights) + [o[0] for o in ops],
         flops,
         in_specs=[full(x.shape), full(g.shape), full(gates.shape), full(slots.shape)]
-        + weight_specs(weights),
-        out_specs=tuple(out_specs),
+        + weight_specs(weights)
+        + [ANY_SPEC] * count,
+        out_specs=tuple(out_specs + [ANY_SPEC] * count),
         grid=(held,),
-        scratch=scratch,
+        scratch=scratch + carry.scratch(),
+        cid=cid if count else None,
     )
 
 
@@ -1213,10 +1269,11 @@
     saved = []
     parts = (hidden_in.reshape(rows, D),)
     for layer in range(LAYERS):
-        got = qkv_forward(parts, packed[layer], cos_t, sin_t, ctx, hq)
-        qkv, gains = got[0], got[1]
+        got = qkv_forward(
+            parts, packed[layer], cos_t, sin_t, ctx, hq, sizes, next(ids_of)
+        )
+        heads, gains = got[0], got[1]
         stream = parts[0] if layer == 0 else got[2]
-        (heads,) = move((qkv, "line", "own"))
         out, lse, mixed = attention_forward(
             heads, seg_row, seg_col, ctx, hq, tok, sizes, next(ids_of)
         )
@@ -1230,7 +1287,7 @@
             )
             late_gate = plane_gather(late_gate)
         else:
-            xs, gates_here, last_g = move(*ops, (grad_rows, "tok", "all"))
+            xs, gates_here = move(*ops)
         saved.append((stream, heads, out, lse, mixed, stream1, normed, gates, gains, xs, gates_here))
         if layer == 0:
             sent, late_second = experts_forward(
@@ -1241,7 +1298,10 @@
             weights[1] = [late_gate, plane_gather(late_second)]
             parts = (stream1, came)
         else:
-            (sent,) = experts_forward(xs, gates_here, slots_here, weights[1], held)
+            sent, last_g = experts_forward(
+                xs, gates_here, slots_here, weights[1], held,
+                [(grad_rows, "tok", "all")], sizes, next(ids_of),
+            )
 
     sent, last_g = lax.optimization_barrier((sent, last_g))
     final_sum = lax.psum_scatter(sent, "zp", scatter_dimension=0, tiled=True)[0]
@@ -1272,16 +1332,17 @@
             gs = last_g
         else:
             gs, last_small, came = move(
-                (g.astype(BF), "tok", "all"), (over_grp(small), "z", "own"), (wide, "sib", "own")
+                (g.astype(BF), "tok", "all"), (small, "g", "own"), (wide, "sib", "own")
             )
             wide = with_other(wide, came)
-            gs, last_second = lax.optimization_barrier((gs, last_experts[1]))
-            last_second = lax.all_to_all(last_second, line, 0, 0, tiled=True)
-        res = experts_backward(xs, gs, gates_here, slots_here, weights[layer], held)
-        if not last:
-            *res, last_second = lax.optimization_barrier((*res, last_second))
+        ops = [] if last else [(last_experts[1], "line", "own")]
+        res = experts_backward(
+            xs, gs, gates_here, slots_here, weights[layer], held, ops, sizes, next(ids_of)
+        )
         if last:
             *res, final_sum = lax.optimization_barrier((*res, final_sum))
+        else:
+            last_second = res[4]
         second_grads = plane_scatter(res[3])
         back = [(res[0], "tok", "own"), (res[1], "tok", "own")]
         if last:
@@ -1290,25 +1351,24 @@
             last_experts = [plane_scatter(gate_grads), second_grads]
         else:
             experts = [plane_scatter(res[2]), second_grads]
-            d_parts, d_gates, last_wide = move(*back, (wide, "g", "own"))
-        g1, d_mixed, small = output_backward(
+            d_parts, d_gates, last_wide, last_small = move(
+                *back, (wide, "g", "own"), (over_grp(last_small), "z", "own")
+            )
+        ops = [] if last else [(over_grp(last_wide), "z", "own")]
+        g1, small, d_out, *came = output_backward(
             d_parts, d_gates, gates, g, stream1, normed, mixed, packed[layer], gains,
-            ctx, hq, planes, shard,
+            ctx, hq, planes, shard, ops, sizes, next(ids_of),
         )
-        ops = [(d_mixed, "line", "own"), (small, "sib", "own")]
-        if last:
-            d_out, came = move(*ops)
-        else:
-            d_out, came, last_wide = move(*ops, (over_grp(last_wide), "z", "own"))
-        small = with_other(small, came)
-        ops = [(small, "g", "own")]
+        ops = [(small, "sib", "own")]
         if not last:
+            last_wide = came[0]
             ops.append((last_experts[0], "line", "own"))
-        dx, small, *came = attention_backward(
+        dx, came, *more = attention_backward(
             heads, d_out, out, lse, seg_row, seg_col, ctx, hq, tok, ops, sizes, next(ids_of)
         )
+        small = with_other(small, came)
         if not last:
-            last_gate = came[0]
+            last_gate = more[0]
         g, wide = qkv_backward(
             dx, g1, stream, packed[layer], gains, cos_t, sin_t, ctx, hq, shard
         )
@@ -1316,10 +1376,12 @@
     first_wide, first_second, first_small = move(
         (between_cores(wide), "g", "own"),
         (experts[1], "line", "own"),
-        (over_grp(small), "z", "own"),
-    )
-    first_wide, first_gate = move(
-        (over_grp(first_wide), "z", "own"), (experts[0], "line", "own")
+        (small, "g", "own"),
+    )
+    first_wide, first_gate, first_small = move(
+        (over_grp(first_wide), "z", "own"),
+        (experts[0], "line", "own"),
+        (over_grp(first_small), "z", "own"),
     )
 
     grads = attention_gradients(first_wide, last_wide, first_small, last_small)

time: 1110 us -> 1090 us (0.982); the launches traced: 1090 us -> 1080 us
    pallas_call x18, Pallas kernels: 388 us -> 494 us  [call(): pl.pallas_call(kernel, out_shape=tuple(outs), scratch_shapes=list(scratch...]
    pallas_call x14 -> x10, Pallas kernels: 633 us -> 529 us  [transfer(): pl.pallas_call(kernel, out_shape=tuple(shapes), in_specs=[any_spec] * cou...]
  transfers between devices with their start and end apart: 12 -> 11, of which waited for: 1 -> 2; matrix products, arithmetic and copies ran while one was open for 3% -> 3% of each run, Pallas kernels for 85% -> 83%
where the time goes in v6:
time: 1090 us; the launch traced here: 1080 us
  Pallas kernels  1020 us (94%)
  other arithmetic  25.9 us (2%)
  between operations  15.2 us (1%)
  local copies, waits for them, and re-layouts  14.6 us (1%)
    pallas_call x10, Pallas kernels, transfer(): pl.pallas_call(kernel, out_shape=tuple(shapes), in_specs=[any_spec] * cou...  529 us
    pallas_call x18, Pallas kernels, call(): pl.pallas_call(kernel, out_shape=tuple(outs), scratch_shapes=list(scratch...  494 us
  transfers between devices with their start and end apart: 11, of which 2 were waited for; matrix products, arithmetic and copies ran while one was open for 3% of the time, Pallas kernels for 83%

profile of v6, /device:TPU:0, one launch (start us, length us, event | category | flops | bytes accessed | tf_op | source)
XLA Modules:
  0.0 1084.9 jit_solution(9369623984098545610)
XLA Ops:
  7.3 23.0 %shard_map.229 = bf16[8,128,512]{2,1,0:T(8,128)(2,1)} custom-call(bf16[2,8,128,512]{3,2,1,0:T(8,128)(2,1)} %refs_3_.1), custom_call_target="tpu_custom_call" | custom-call | bytes 41943040 | tf_op jit(solution)/shard_map/pallas_call | solution.py:323
  30.9 1.4 copy-done.6
  33.7 1.5 pad_maximum_fusion
  36.0 70.2 %shard_map.230 = (bf16[4,8,32,3200]{3,2,1,0:T(8,128)(2,1)}, bf16[8,256,512]{2,1,0:T(8,128)(2,1)}) custom-call(bf16[32,3200]{1,0:T(8,128)(2,1)} %concatenate.12.refs_0_, bf16[1,8,256,512]{3,2,1,0:T(8,128)(2,1)} %bitcast.109), custom_call_target="tpu_custom_call" | custom-call | bytes 346030080 | tf_op jit(solution)/shard_map/pallas_call | solution.py:323
  108.1 1.3 copy.85.sc_ref
  111.1 1.8 fusion.5
  112.9 27.9 %shard_map.231 = (bf16[8,256,256]{2,1,0:T(8,128)(2,1)}, f32[8,1024]{1,0:T(8,128)}) custom-call(bf16[256,1024]{1,0:T(8,128)(2,1)} %bitcast.110, bf16[1024,3200]{1,0:T(8,128)(2,1)} %bitcast.100, bf16[1024,3200]{1,0:T(8,128)(2,1)} %bitcast.101, f32[256,256]{1,0:T(8,128)} %get-tuple-element.247.refs_3_.refs_4_.c_ref, ...), custom_call_target="tpu_custom_call" | custom-call | flops 1073741824 | bytes 15237120 | tf_op jit(solution)/shard_map/pallas_call | solution.py:40
  140.8 26.0 %shard_map.232 = (bf16[8,256,128]{2,1,0:T(8,128)(2,1)}, f32[2,1024,128]{2,1,0:T(8,128)}, bf16[8,256,128]{2,1,0:T(8,128)(2,1)}) custom-call(bf16[8,256,256]{2,1,0:T(8,128)(2,1)} %get-tuple-element.106.x_ref, s32[2,1,1024]{2,1,0:T(1,128)} %broadcast_in_dim.58.sr_ref, s32[2,1024,1]{2,1,0:T(8,128)} %copy.85.sc_ref), custom_call_target="tpu_custom_call" | custom-call | flops 536870912 | bytes 3162112 | tf_op jit(solution)/shard_map/pallas_call | solution.py:40
  166.8 4.8 shard_map.233
  172.2 69.4 %shard_map.234 = (bf16[4,256,1024]{2,1,0:T(8,128)(2,1)}, f32[4,8,256]{2,1,0:T(8,128)}, s32[4,8,256]{2,1,0:T(8,128)}, bf16[8,128,512]{2,1,0:T(8,128)(2,1)}) custom-call(bf16[256,1024]{1,0:T(8,128)(2,1)} %get-tuple-element.110.refs_0_.nm_ref, f32[4,8,256]{2,1,0:T(8,128)} %get-tuple-element.111.refs_1_.gt_ref, s32[4,8,256]{2,1,0:T(8,128)} %bitcast_select_fusion.refs_2_, ...), custom_call_target="tpu_custom_call" | custom-call | bytes 128450560 | tf_op jit(solution)/shard_map/pallas_call | solution.py:323
  242.0 1.6 maximum_bitcast_fusion.rest_0_
  243.5 48.3 %shard_map.235 = (bf16[4,256,1024]{2,1,0:T(8,128)(2,1)}, bf16[8,256,512]{2,1,0:T(8,128)(2,1)}) custom-call(bf16[4,256,1024]{2,1,0:T(8,128)(2,1)} %get-tuple-element.112.x_ref, f32[4,8,256]{2,1,0:T(8,128)} %get-tuple-element.113.g_ref, s32[4,8,256]{2,1,0:T(8,128)} %get-tuple-element.114.s_ref, bf16[8,8,128,512]{3,2,1,0:T(8,128)(2,1)} %bitcast.139, ...), custom_call_target="tpu_custom_call" | custom-call | flops 12884901888 | bytes 33619968 | tf_op jit(solution)/shard_map/pallas_call | solution.py:40
  291.9 64.2 %shard_map.236.refs_1_ = bf16[4,256,1024]{2,1,0:T(8,128)(2,1)} custom-call(bf16[4,256,1024]{2,1,0:T(8,128)(2,1)} %get-tuple-element.117.refs_0_), custom_call_target="tpu_custom_call" | custom-call | bytes 83886080 | tf_op jit(solution)/shard_map/pallas_call | solution.py:323
  356.1 37.8 %shard_map.237 = (bf16[8,256,256]{2,1,0:T(8,128)(2,1)}, f32[8,1024]{1,0:T(8,128)}, f32[256,1024]{1,0:T(8,128)}) custom-call(f32[256,1024]{1,0:T(8,128)} %get-tuple-element.109.refs_0_.x_ref, bf16[4,256,1024]{2,1,0:T(8,128)(2,1)} %shard_map.236.refs_1_, bf16[1024,3200]{1,0:T(8,128)(2,1)} %all-gather.10.cloned.1.call-done.refs_2_.refs_3_.w_ref.t_ref, ...), custom_call_target="tpu_custom_call" | custom-call | flops 1073741824 | bytes 18907136 | tf_op jit(solution)/shard_map/pallas_call | solution.py:40
  393.9 26.0 %shard_map.238 = (bf16[8,256,128]{2,1,0:T(8,128)(2,1)}, f32[2,1024,128]{2,1,0:T(8,128)}, bf16[8,256,128]{2,1,0:T(8,128)(2,1)}) custom-call(bf16[8,256,256]{2,1,0:T(8,128)(2,1)} %get-tuple-element.119.x_ref, s32[2,1,1024]{2,1,0:T(1,128)} %broadcast_in_dim.58.sr_ref, s32[2,1024,1]{2,1,0:T(8,128)} %copy.85.sc_ref), custom_call_target="tpu_custom_call" | custom-call | flops 536870912 | bytes 3162112 | tf_op jit(solution)/shard_map/pallas_call | solution.py:40
  419.9 4.1 shard_map.239
  424.1 41.5 %shard_map.240 = (bf16[4,256,1024]{2,1,0:T(8,128)(2,1)}, f32[4,8,256]{2,1,0:T(8,128)}) custom-call(bf16[256,1024]{1,0:T(8,128)(2,1)} %get-tuple-element.124.refs_0_.nm_ref, f32[4,8,256]{2,1,0:T(8,128)} %get-tuple-element.125.refs_1_.gt_ref), custom_call_target="tpu_custom_call" | custom-call | bytes 85196800 | tf_op jit(solution)/shard_map/pallas_call | solution.py:323
  465.5 1.3 all-gather.18.cloned.1.call-done
  466.8 42.8 %shard_map.241 = (bf16[4,256,1024]{2,1,0:T(8,128)(2,1)}, bf16[4,256,1024]{2,1,0:T(8,128)(2,1)}) custom-call(bf16[4,256,1024]{2,1,0:T(8,128)(2,1)} %get-tuple-element.126.x_ref, f32[4,8,256]{2,1,0:T(8,128)} %get-tuple-element.127.g_ref, s32[4,8,256]{2,1,0:T(8,128)} %get-tuple-element.114.s_ref, bf16[8,8,128,512]{3,2,1,0:T(8,128)(2,1)} %bitcast.141, ...), custom_call_target="tpu_custom_call" | custom-call | flops 12884901888 | bytes 32047104 | tf_op jit(solution)/shard_map/pallas_call | solution.py:40
  510.1 55.8 %shard_map.242 = (bf16[4,256,1024]{2,1,0:T(8,128)(2,1)}, f32[4,8,256]{2,1,0:T(8,128)}, bf16[8,8,128,512]{3,2,1,0:T(8,128)(2,1)}, bf16[8,8,256,512]{3,2,1,0:T(8,128)(2,1)}) custom-call(bf16[4,256,1024]{2,1,0:T(8,128)(2,1)} %get-tuple-element.126.x_ref, bf16[4,256,1024]{2,1,0:T(8,128)(2,1)} %get-tuple-element.130.gr_ref, ...), custom_call_target="tpu_custom_call" | custom-call | flops 33822867456 | bytes 56721408 | tf_op jit(solution)/shard_map/pallas_call | solution.py:40
  565.9 60.3 %shard_map.243 = (bf16[4,256,1024]{2,1,0:T(8,128)(2,1)}, f32[4,8,256]{2,1,0:T(8,128)}) custom-call(bf16[4,256,1024]{2,1,0:T(8,128)(2,1)} %get-tuple-element.138.refs_0_, f32[4,8,256]{2,1,0:T(8,128)} %get-tuple-element.139.refs_1_), custom_call_target="tpu_custom_call" | custom-call | bytes 85196800 | tf_op jit(solution)/shard_map/pallas_call | solution.py:323
  626.3 18.3 %shard_map.244 = (f32[256,1024]{1,0:T(8,128)}, bf16[2,512,1152]{2,1,0:T(8,128)(2,1)}, bf16[8,256,128]{2,1,0:T(8,128)(2,1)}) custom-call(bf16[4,256,1024]{2,1,0:T(8,128)(2,1)} %get-tuple-element.141.p_ref, f32[4,8,256]{2,1,0:T(8,128)} %get-tuple-element.142.dg_ref, f32[4,8,256]{2,1,0:T(8,128)} %get-tuple-element.125.refs_1_.gt_ref, ...), custom_call_target="tpu_custom_call" | custom-call | flops 1073741824 | bytes 21856256 | tf_op jit(solution)/shard_map/pallas_call | solution.py:40
  644.6 33.4 %shard_map.245 = (bf16[8,256,256]{2,1,0:T(8,128)(2,1)}, bf16[512,1152]{1,0:T(8,128)(2,1)}) custom-call(bf16[8,256,256]{2,1,0:T(8,128)(2,1)} %get-tuple-element.119.x_ref, bf16[8,256,128]{2,1,0:T(8,128)(2,1)} %get-tuple-element.143.d_ref, bf16[8,256,128]{2,1,0:T(8,128)(2,1)} %get-tuple-element.144.o_ref, f32[2,1024,128]{2,1,0:T(8,128)} %get-tuple-element.145.l_ref, ...), custom_call_target="tpu_custom_call" | custom-call | flops 1342177280 | bytes 7749632 | tf_op jit(solution)/shard_map/pallas_call | solution.py:40
  678.0 8.9 shard_map.246
  686.9 2.2 convert_element_type.105.refs_0_
  689.1 1.3 fusion.3
  690.4 44.8 %shard_map.247 = (bf16[4,256,1024]{2,1,0:T(8,128)(2,1)}, bf16[4,4,32,1152]{3,2,1,0:T(8,128)(2,1)}, bf16[512,2176]{1,0:T(8,128)(2,1)}) custom-call(bf16[256,1024]{1,0:T(8,128)(2,1)} %convert_element_type.105.refs_0_, bf16[4,4,32,1152]{3,2,1,0:T(8,128)(2,1)} %bitcast.114, bf16[2,512,2176]{2,1,0:T(8,128)(2,1)} %get-tuple-element.151.refs_2_), custom_call_target="tpu_custom_call" | custom-call | bytes 220200960 | tf_op jit(solution)/shard_map/pallas_call | solution.py:323
  735.3 60.0 %shard_map.248 = (bf16[4,256,1024]{2,1,0:T(8,128)(2,1)}, f32[4,8,256]{2,1,0:T(8,128)}, bf16[8,8,128,512]{3,2,1,0:T(8,128)(2,1)}, bf16[8,8,256,512]{3,2,1,0:T(8,128)(2,1)}, bf16[8,256,512]{2,1,0:T(8,128)(2,1)}) custom-call(bf16[4,256,1024]{2,1,0:T(8,128)(2,1)} %get-tuple-element.112.x_ref, bf16[4,256,1024]{2,1,0:T(8,128)(2,1)} %get-tuple-element.152.gr_ref, ...), custom_call_target="tpu_custom_call" | custom-call | flops 33822867456 | bytes 60915712 | tf_op jit(solution)/shard_map/pallas_call | solution.py:40
  796.6 1.0 reduce_sum.68.refs_3_
  797.5 3.8 fusion.1
  801.3 55.4 %shard_map.249 = (bf16[4,256,1024]{2,1,0:T(8,128)(2,1)}, f32[4,8,256]{2,1,0:T(8,128)}, bf16[4,4,32,2176]{3,2,1,0:T(8,128)(2,1)}, bf16[4,32,1152]{2,1,0:T(8,128)(2,1)}) custom-call(bf16[4,256,1024]{2,1,0:T(8,128)(2,1)} %get-tuple-element.154.refs_0_, f32[4,8,256]{2,1,0:T(8,128)} %get-tuple-element.155.refs_1_, bf16[4,4,32,2176]{3,2,1,0:T(8,128)(2,1)} %bitcast.108, ...), custom_call_target="tpu_custom_call" | custom-call | bytes 186122240 | tf_op jit(solution)/shard_map/pallas_call | solution.py:323
  856.8 2.9 reduce_sum.69.rest_0_
  859.7 29.3 %shard_map.250 = (f32[256,1024]{1,0:T(8,128)}, bf16[2,512,1152]{2,1,0:T(8,128)(2,1)}, bf16[8,256,128]{2,1,0:T(8,128)(2,1)}, bf16[4,32,2176]{2,1,0:T(8,128)(2,1)}) custom-call(bf16[4,256,1024]{2,1,0:T(8,128)(2,1)} %get-tuple-element.158.p_ref, f32[4,8,256]{2,1,0:T(8,128)} %get-tuple-element.159.dg_ref, f32[4,8,256]{2,1,0:T(8,128)} %get-tuple-element.111.refs_1_.gt_ref, ...), custom_call_target="tpu_custom_call" | custom-call | flops 1073741824 | bytes 23494656 | tf_op jit(solution)/shard_map/pallas_call | solution.py:40
  889.0 51.2 %shard_map.251 = (bf16[8,256,256]{2,1,0:T(8,128)(2,1)}, bf16[512,1152]{1,0:T(8,128)(2,1)}, bf16[8,128,512]{2,1,0:T(8,128)(2,1)}) custom-call(bf16[8,256,256]{2,1,0:T(8,128)(2,1)} %get-tuple-element.106.x_ref, bf16[8,256,128]{2,1,0:T(8,128)(2,1)} %get-tuple-element.161.d_ref, bf16[8,256,128]{2,1,0:T(8,128)(2,1)} %get-tuple-element.162.o_ref, ...), custom_call_target="tpu_custom_call" | custom-call | flops 1342177280 | bytes 9846784 | tf_op jit(solution)/shard_map/pallas_call | solution.py:40
  940.2 8.4 shard_map.252
  948.6 2.0 dynamic-slice_bitcast_fusion
  950.6 1.4 collective-permute-start
  952.0 1.0 add_convert_fusion
  953.0 1.3 fusion.2
  954.3 1.7 collective-permute-done
  956.0 1.9 fusion
  957.9 55.9 %shard_map.253 = (bf16[4,4,32,2176]{3,2,1,0:T(8,128)(2,1)}, bf16[8,256,512]{2,1,0:T(8,128)(2,1)}, bf16[4,4,32,1152]{3,2,1,0:T(8,128)(2,1)}) custom-call(bf16[4,4,32,2176]{3,2,1,0:T(8,128)(2,1)} %bitcast.107, bf16[8,256,512]{2,1,0:T(8,128)(2,1)} %bitcast.117, bf16[4,4,32,1152]{3,2,1,0:T(8,128)(2,1)} %bitcast.113), custom_call_target="tpu_custom_call" | custom-call | bytes 220200960 | tf_op jit(solution)/shard_map/pallas_call | solution.py:323
  1013.8 3.0 reduce_sum.70.refs_0_
  1017.8 44.3 %shard_map.254 = (bf16[4,32,2176]{2,1,0:T(8,128)(2,1)}, bf16[8,128,512]{2,1,0:T(8,128)(2,1)}, bf16[4,32,1152]{2,1,0:T(8,128)(2,1)}) custom-call(bf16[4,32,2176]{2,1,0:T(8,128)(2,1)} %reduce_sum.70.refs_0_, bf16[8,128,512]{2,1,0:T(8,128)(2,1)} %bitcast.118, bf16[4,32,1152]{2,1,0:T(8,128)(2,1)} %reduce_sum.71.refs_2_), custom_call_target="tpu_custom_call" | custom-call | bytes 76021760 | tf_op jit(solution)/shard_map/pallas_call | solution.py:323
  1062.1 2.3 shard_map.255
  1064.4 1.4 slice_reduce_fusion.1
  1065.8 1.5 slice_reduce_fusion
  1068.9 8.7 shard_map.256
  (111 shorter events, 11.6 us)
Async XLA Ops:
  7.2 23.1 %copy-start.17 = (bf16[2,32,32]{2,1,0:T(8,128)(2,1)S(1)}, bf16[2,32,32]{2,1,0:T(8,128)(2,1)}, u32[]{:S(2)}) copy-start(bf16[2,32,32]{2,1,0:T(8,128)(2,1)} %param.24) | copy-start | bytes 12292
  7.2 23.3 %copy-start.19 = (bf16[2,32]{1,0:T(2,128)(2,1)S(1)}, bf16[2,32]{1,0:T(2,128)(2,1)}, u32[]{:S(2)}) copy-start(bf16[2,32]{1,0:T(2,128)(2,1)} %param.18) | copy-start | bytes 388
  7.2 23.4 %copy-start.20 = (bf16[2,32]{1,0:T(2,128)(2,1)S(1)}, bf16[2,32]{1,0:T(2,128)(2,1)}, u32[]{:S(2)}) copy-start(bf16[2,32]{1,0:T(2,128)(2,1)} %param.23) | copy-start | bytes 388
  7.2 23.5 %copy-start.5 = (bf16[2,8,64,1024]{3,2,1,0:T(8,128)(2,1)S(1)}, bf16[2,8,64,1024]{3,2,1,0:T(8,128)(2,1)}, u32[]{:S(2)}) copy-start(bf16[2,8,64,1024]{3,2,1,0:T(8,128)(2,1)} %param.27) | copy-start | bytes 6291460
  7.2 236.3 %all-gather.12.cloned.1.call-start = ((), (), s32[]{:S(2)}) async-start(), calls=%async_computation.11 | async-start | bytes 9437184 | tf_op jit(solution)/shard_map/all_gather | solution.py:1222
  30.7 1.6 copy-start.6
  32.3 0.9 copy-start.13
  32.3 1.0 copy-start.14
  32.4 1.0 copy-start.15
  32.4 1.0 copy-start.16
  35.9 207.6 %all-gather.14.cloned.1.call-start = ((), (), s32[]{:S(2)}) async-start(), calls=%async_computation.12 | async-start | bytes 18874368 | tf_op jit(solution)/shard_map/all_gather | solution.py:1222
  36.0 71.5 %copy-start.12 = (s32[2,1024]{1,0:T(2,128)S(1)}, s32[2,1024]{1,0:T(2,128)}, u32[]{:S(2)}) copy-start(s32[2,1024]{1,0:T(2,128)} %param.16) | copy-start | bytes 24580
  106.2 3.4 copy-start.18
  106.2 249.9 %all-gather.10.cloned.1.call-start = ((), (), s32[]{:S(2)}) async-start(), calls=%async_computation.5 | async-start | bytes 6758400 | tf_op jit(solution)/shard_map/all_gather | solution.py:1231
  107.5 358.1 %all-gather.16.cloned.1.call-start = ((), (), s32[]{:S(2)}) async-start(), calls=%async_computation.13 | async-start | bytes 9437184 | tf_op jit(solution)/shard_map/all_gather | solution.py:1222
  241.7 225.1 %all-gather.18.cloned.1.call-start = ((), (), s32[]{:S(2)}) async-start(), calls=%async_computation.14 | async-start | bytes 18874368 | tf_op jit(solution)/shard_map/all_gather | solution.py:1222
  291.9 274.0 %reduce-scatter.6.cloned.1.call-start = ((), (), s32[]{:S(2)}) async-start(), calls=%async_computation.6 | async-start | bytes 2621440 | tf_op jit(solution)/shard_map/reduce_scatter | solution.py:1307
  509.6 225.7 %reduce-scatter.8.cloned.1.call-start = ((), (), s32[]{:S(2)}) async-start(), calls=%async_computation.7 | async-start | bytes 18874368 | tf_op jit(solution)/shard_map/reduce_scatter | solution.py:1311
  565.9 323.1 %reduce-scatter.10.cloned.1.call-start = ((), (), s32[]{:S(2)}) async-start(), calls=%async_computation.8 | async-start | bytes 9437184 | tf_op jit(solution)/shard_map/reduce_scatter | solution.py:1311
  626.2 331.6 %reduce-scatter.12.cloned.1.call-start = ((), (), s32[]{:S(2)}) async-start(), calls=%async_computation.9 | async-start | bytes 18874368 | tf_op jit(solution)/shard_map/reduce_scatter | solution.py:1311
  678.0 11.1 %copy-start = (bf16[2,512,1152]{2,1,0:T(8,128)(2,1)S(1)}, bf16[2,512,1152]{2,1,0:T(8,128)(2,1)}, u32[]{:S(2)}) copy-start(bf16[2,512,1152]{2,1,0:T(8,128)(2,1)} %get-tuple-element.146.rest_0_) | copy-start | bytes 7077892
  686.9 2.2 copy-start.10
  795.3 222.5 %reduce-scatter.14.cloned.1.call-start = ((), (), s32[]{:S(2)}) async-start(), calls=%async_computation.10 | async-start | bytes 9437184 | tf_op jit(solution)/shard_map/reduce_scatter | solution.py:1311
  795.3 1.3 copy-start.7
  795.3 2.2 copy-start.4
  940.2 11.9 %copy-start.11 = (bf16[1,256,1024]{2,1,0:T(8,128)(2,1)S(1)}, bf16[1,256,1024]{2,1,0:T(8,128)(2,1)}, u32[]{:S(2)}) copy-start(bf16[1,256,1024]{2,1,0:T(8,128)(2,1)} %reduce-scatter.6.cloned.1.call-done) | copy-start | bytes 1572868
  948.6 3.4 copy-start.3
  948.6 4.4 copy-start.1
  948.6 4.4 copy-start.9
  950.6 5.4 collective-permute-start
  952.0 4.0 copy-start.2
  1013.8 3.0 copy-start.8
Sparse Core Ops, SparseCore 0:
  36.0 88.1 all-gather.11
  126.1 88.9 all-gather.13
  218.5 99.8 all-gather.9
  320.2 54.7 all-gather.15
  376.7 90.0 all-gather.17
  509.7 54.0 reduce-scatter.5
  567.8 124.3 reduce-scatter.7
  696.0 71.2 reduce-scatter.9
  795.4 114.0 reduce-scatter.11
  912.8 88.5 reduce-scatter.13

commit v7 on v6

--- a/solution.py
+++ b/solution.py
@@ -368,6 +368,12 @@
         ]
 
     def enter(self, groups):
+        self.wait(self.greet(groups))
+
+    def wait(self, total):
+        pl.semaphore_wait(pltpu.get_barrier_semaphore(), total)
+
+    def greet(self, groups):
         barrier = pltpu.get_barrier_semaphore()
         total = 0
         for group in groups:
@@ -377,7 +383,7 @@
                     barrier, inc=1, device_id=where(lax.rem(me + k, n)), device_id_type=MESH
                 )
             total += n - 1
-        pl.semaphore_wait(barrier, total)
+        return total
 
     def copies(self, ins, outs, sems):
         made = []
@@ -464,7 +470,7 @@
 
     def kernel(*refs):
         refs, (buf, *sems) = refs[:-4], refs[-4:]
-        meet.enter(["line"])
+        greeted = meet.greet(["line"])
         if first:
             h_ref, w_ref, t_ref, c_ref, s_ref, out_ref, gains_ref = refs
             x = h_ref[...].astype(F32)
@@ -494,6 +500,7 @@
             mine.append(keys[:, HS * kv : HS * (kv + 1)])
             mine.append(values[:, HS * kv : HS * (kv + 1)])
             buf[0, i] = in_order(mine)
+        meet.wait(greeted)
         copies = head_copies(buf, out_ref, sems, 0, ctx, rows, sizes)
         for copy in copies:
             copy.start()
@@ -818,7 +825,7 @@
     rows = g1.shape[0]
     dup = ctx // KEY_VALUE_HEADS
 
-    def kernel(d_ref, g_ref, x_ref, w_ref, gain_ref, c_ref, s_ref, out_ref, gw_ref):
+    def kernel(d_ref, g_ref, x_ref, w_ref, gain_ref, c_ref, s_ref, out_ref, gw_ref, low_ref):
         x = x_ref[...].astype(F32)
         gain = gain_ref[0:1]
         normed = (x * inv_rms_of(x) * gain).astype(BF)
@@ -852,13 +859,15 @@
             for c, value in enumerate(by_core(dot(normed, lin, 0, 0), shard)):
                 gw_ref[c, :, cols] = value
         back, grad_gain = norm_back(x, gain, d_normed)
-        out_ref[...] = g_ref[...] + back
+        total = g_ref[...] + back
+        out_ref[...] = total
+        low_ref[...] = total.astype(BF)
         row = lax.broadcasted_iota(jnp.int32, (128, D), 0)
         cols = jnp.where(row == 0, jnp.broadcast_to(grad_gain, (128, D)), 0.0)
         for c, value in enumerate(by_core(jnp.transpose(cols), shard)):
             gw_ref[c, :, 2 * D : 2 * D + 128] = value
 
-    outs = [sds((rows, D), F32), sds((2, D // 2, 2 * D + 128), BF)]
+    outs = [sds((rows, D), F32), sds((2, D // 2, 2 * D + 128), BF), sds((rows, D), BF)]
     args = [dx, g1, stream, packed, gains, cos_t, sin_t]
     in_specs = [full(a.shape) for a in args]
     in_specs[3] = pl.BlockSpec((D, 2 * D), lambda i: (0, 0))
@@ -1332,7 +1341,7 @@
             gs = last_g
         else:
             gs, last_small, came = move(
-                (g.astype(BF), "tok", "all"), (small, "g", "own"), (wide, "sib", "own")
+                (low_g, "tok", "all"), (small, "g", "own"), (wide, "sib", "own")
             )
             wide = with_other(wide, came)
         ops = [] if last else [(last_experts[1], "line", "own")]
@@ -1369,7 +1378,7 @@
         small = with_other(small, came)
         if not last:
             last_gate = more[0]
-        g, wide = qkv_backward(
+        g, wide, low_g = qkv_backward(
             dx, g1, stream, packed[layer], gains, cos_t, sin_t, ctx, hq, shard
         )
     hidden_out = (last_stream + final_sum.astype(F32)).astype(BF).reshape(micro, tok, D)

time: 1090 us -> 1090 us (level)
  no operation moved by 1% of the time
where the time goes in v7:
time: 1090 us; the launch traced here: 1080 us
  Pallas kernels  1020 us (94%)
  other arithmetic  23.6 us (2%)
  between operations  15.2 us (1%)
  local copies, waits for them, and re-layouts  14.6 us (1%)
    pallas_call x10, Pallas kernels, transfer(): pl.pallas_call(kernel, out_shape=tuple(shapes), in_specs=[any_spec] * cou...  532 us
    pallas_call x18, Pallas kernels, call(): pl.pallas_call(kernel, out_shape=tuple(outs), scratch_shapes=list(scratch...  491 us
  transfers between devices with their start and end apart: 11, of which 2 were waited for; matrix products, arithmetic and copies ran while one was open for 3% of the time, Pallas kernels for 83%

profile of v7, /device:TPU:0, one launch (start us, length us, event | category | flops | bytes accessed | tf_op | source)
XLA Modules:
  0.0 1083.3 jit_solution(14384970061345743894)
XLA Ops:
  7.3 23.0 %shard_map.229 = bf16[8,128,512]{2,1,0:T(8,128)(2,1)} custom-call(bf16[2,8,128,512]{3,2,1,0:T(8,128)(2,1)} %refs_3_.1), custom_call_target="tpu_custom_call" | custom-call | bytes 41943040 | tf_op jit(solution)/shard_map/pallas_call | solution.py:323
  30.9 1.4 copy-done.6
  33.7 1.5 pad_maximum_fusion
  36.0 70.2 %shard_map.230 = (bf16[4,8,32,3200]{3,2,1,0:T(8,128)(2,1)}, bf16[8,256,512]{2,1,0:T(8,128)(2,1)}) custom-call(bf16[32,3200]{1,0:T(8,128)(2,1)} %concatenate.12.refs_0_, bf16[1,8,256,512]{3,2,1,0:T(8,128)(2,1)} %bitcast.109), custom_call_target="tpu_custom_call" | custom-call | bytes 346030080 | tf_op jit(solution)/shard_map/pallas_call | solution.py:323
  108.1 1.3 copy.85.sc_ref
  111.1 1.8 fusion.5
  112.9 26.4 %shard_map.231 = (bf16[8,256,256]{2,1,0:T(8,128)(2,1)}, f32[8,1024]{1,0:T(8,128)}) custom-call(bf16[256,1024]{1,0:T(8,128)(2,1)} %bitcast.110, bf16[1024,3200]{1,0:T(8,128)(2,1)} %bitcast.100, bf16[1024,3200]{1,0:T(8,128)(2,1)} %bitcast.101, f32[256,256]{1,0:T(8,128)} %get-tuple-element.249.refs_3_.refs_4_.c_ref, ...), custom_call_target="tpu_custom_call" | custom-call | flops 1073741824 | bytes 15237120 | tf_op jit(solution)/shard_map/pallas_call | solution.py:40
  139.3 26.0 %shard_map.232 = (bf16[8,256,128]{2,1,0:T(8,128)(2,1)}, f32[2,1024,128]{2,1,0:T(8,128)}, bf16[8,256,128]{2,1,0:T(8,128)(2,1)}) custom-call(bf16[8,256,256]{2,1,0:T(8,128)(2,1)} %get-tuple-element.107.x_ref, s32[2,1,1024]{2,1,0:T(1,128)} %broadcast_in_dim.58.sr_ref, s32[2,1024,1]{2,1,0:T(8,128)} %copy.85.sc_ref), custom_call_target="tpu_custom_call" | custom-call | flops 536870912 | bytes 3162112 | tf_op jit(solution)/shard_map/pallas_call | solution.py:40
  165.3 5.0 shard_map.233
  170.9 69.4 %shard_map.234 = (bf16[4,256,1024]{2,1,0:T(8,128)(2,1)}, f32[4,8,256]{2,1,0:T(8,128)}, s32[4,8,256]{2,1,0:T(8,128)}, bf16[8,128,512]{2,1,0:T(8,128)(2,1)}) custom-call(bf16[256,1024]{1,0:T(8,128)(2,1)} %get-tuple-element.111.refs_0_.nm_ref, f32[4,8,256]{2,1,0:T(8,128)} %get-tuple-element.112.refs_1_.gt_ref, s32[4,8,256]{2,1,0:T(8,128)} %bitcast_select_fusion.refs_2_, ...), custom_call_target="tpu_custom_call" | custom-call | bytes 128450560 | tf_op jit(solution)/shard_map/pallas_call | solution.py:323
  240.6 1.6 maximum_bitcast_fusion.rest_0_
  242.1 47.0 %shard_map.235 = (bf16[4,256,1024]{2,1,0:T(8,128)(2,1)}, bf16[8,256,512]{2,1,0:T(8,128)(2,1)}) custom-call(bf16[4,256,1024]{2,1,0:T(8,128)(2,1)} %get-tuple-element.113.x_ref, f32[4,8,256]{2,1,0:T(8,128)} %get-tuple-element.114.g_ref, s32[4,8,256]{2,1,0:T(8,128)} %get-tuple-element.115.s_ref, bf16[8,8,128,512]{3,2,1,0:T(8,128)(2,1)} %bitcast.139, ...), custom_call_target="tpu_custom_call" | custom-call | flops 12884901888 | bytes 33619968 | tf_op jit(solution)/shard_map/pallas_call | solution.py:40
  289.2 66.6 %shard_map.236.refs_1_ = bf16[4,256,1024]{2,1,0:T(8,128)(2,1)} custom-call(bf16[4,256,1024]{2,1,0:T(8,128)(2,1)} %get-tuple-element.118.refs_0_), custom_call_target="tpu_custom_call" | custom-call | bytes 83886080 | tf_op jit(solution)/shard_map/pallas_call | solution.py:323
  355.9 36.2 %shard_map.237 = (bf16[8,256,256]{2,1,0:T(8,128)(2,1)}, f32[8,1024]{1,0:T(8,128)}, f32[256,1024]{1,0:T(8,128)}) custom-call(f32[256,1024]{1,0:T(8,128)} %get-tuple-element.110.refs_0_.x_ref, bf16[4,256,1024]{2,1,0:T(8,128)(2,1)} %shard_map.236.refs_1_, bf16[1024,3200]{1,0:T(8,128)(2,1)} %all-gather.10.cloned.1.call-done.refs_2_.refs_3_.w_ref.t_ref, ...), custom_call_target="tpu_custom_call" | custom-call | flops 1073741824 | bytes 18907136 | tf_op jit(solution)/shard_map/pallas_call | solution.py:40
  392.1 26.0 %shard_map.238 = (bf16[8,256,128]{2,1,0:T(8,128)(2,1)}, f32[2,1024,128]{2,1,0:T(8,128)}, bf16[8,256,128]{2,1,0:T(8,128)(2,1)}) custom-call(bf16[8,256,256]{2,1,0:T(8,128)(2,1)} %get-tuple-element.120.x_ref, s32[2,1,1024]{2,1,0:T(1,128)} %broadcast_in_dim.58.sr_ref, s32[2,1024,1]{2,1,0:T(8,128)} %copy.85.sc_ref), custom_call_target="tpu_custom_call" | custom-call | flops 536870912 | bytes 3162112 | tf_op jit(solution)/shard_map/pallas_call | solution.py:40
  418.1 5.3 shard_map.239
  423.4 41.5 %shard_map.240 = (bf16[4,256,1024]{2,1,0:T(8,128)(2,1)}, f32[4,8,256]{2,1,0:T(8,128)}) custom-call(bf16[256,1024]{1,0:T(8,128)(2,1)} %get-tuple-element.125.refs_0_.nm_ref, f32[4,8,256]{2,1,0:T(8,128)} %get-tuple-element.126.refs_1_.gt_ref), custom_call_target="tpu_custom_call" | custom-call | bytes 85196800 | tf_op jit(solution)/shard_map/pallas_call | solution.py:323
  464.9 2.2 all-gather.18.cloned.1.call-done
  467.1 42.8 %shard_map.241 = (bf16[4,256,1024]{2,1,0:T(8,128)(2,1)}, bf16[4,256,1024]{2,1,0:T(8,128)(2,1)}) custom-call(bf16[4,256,1024]{2,1,0:T(8,128)(2,1)} %get-tuple-element.127.x_ref, f32[4,8,256]{2,1,0:T(8,128)} %get-tuple-element.128.g_ref, s32[4,8,256]{2,1,0:T(8,128)} %get-tuple-element.115.s_ref, bf16[8,8,128,512]{3,2,1,0:T(8,128)(2,1)} %bitcast.141, ...), custom_call_target="tpu_custom_call" | custom-call | flops 12884901888 | bytes 32047104 | tf_op jit(solution)/shard_map/pallas_call | solution.py:40
  510.4 55.8 %shard_map.242 = (bf16[4,256,1024]{2,1,0:T(8,128)(2,1)}, f32[4,8,256]{2,1,0:T(8,128)}, bf16[8,8,128,512]{3,2,1,0:T(8,128)(2,1)}, bf16[8,8,256,512]{3,2,1,0:T(8,128)(2,1)}) custom-call(bf16[4,256,1024]{2,1,0:T(8,128)(2,1)} %get-tuple-element.127.x_ref, bf16[4,256,1024]{2,1,0:T(8,128)(2,1)} %get-tuple-element.131.gr_ref, ...), custom_call_target="tpu_custom_call" | custom-call | flops 33822867456 | bytes 56721408 | tf_op jit(solution)/shard_map/pallas_call | solution.py:40
  566.3 60.3 %shard_map.243 = (bf16[4,256,1024]{2,1,0:T(8,128)(2,1)}, f32[4,8,256]{2,1,0:T(8,128)}) custom-call(bf16[4,256,1024]{2,1,0:T(8,128)(2,1)} %get-tuple-element.139.refs_0_, f32[4,8,256]{2,1,0:T(8,128)} %get-tuple-element.140.refs_1_), custom_call_target="tpu_custom_call" | custom-call | bytes 85196800 | tf_op jit(solution)/shard_map/pallas_call | solution.py:323
  626.6 18.3 %shard_map.244 = (f32[256,1024]{1,0:T(8,128)}, bf16[2,512,1152]{2,1,0:T(8,128)(2,1)}, bf16[8,256,128]{2,1,0:T(8,128)(2,1)}) custom-call(bf16[4,256,1024]{2,1,0:T(8,128)(2,1)} %get-tuple-element.142.p_ref, f32[4,8,256]{2,1,0:T(8,128)} %get-tuple-element.143.dg_ref, f32[4,8,256]{2,1,0:T(8,128)} %get-tuple-element.126.refs_1_.gt_ref, ...), custom_call_target="tpu_custom_call" | custom-call | flops 1073741824 | bytes 21856256 | tf_op jit(solution)/shard_map/pallas_call | solution.py:40
  644.9 33.5 %shard_map.245 = (bf16[8,256,256]{2,1,0:T(8,128)(2,1)}, bf16[512,1152]{1,0:T(8,128)(2,1)}) custom-call(bf16[8,256,256]{2,1,0:T(8,128)(2,1)} %get-tuple-element.120.x_ref, bf16[8,256,128]{2,1,0:T(8,128)(2,1)} %get-tuple-element.144.d_ref, bf16[8,256,128]{2,1,0:T(8,128)(2,1)} %get-tuple-element.145.o_ref, f32[2,1024,128]{2,1,0:T(8,128)} %get-tuple-element.146.l_ref, ...), custom_call_target="tpu_custom_call" | custom-call | flops 1342177280 | bytes 7749632 | tf_op jit(solution)/shard_map/pallas_call | solution.py:40
  678.4 9.1 shard_map.246
  687.5 1.3 fusion.3
  688.8 44.8 %shard_map.247 = (bf16[4,256,1024]{2,1,0:T(8,128)(2,1)}, bf16[4,4,32,1152]{3,2,1,0:T(8,128)(2,1)}, bf16[512,2176]{1,0:T(8,128)(2,1)}) custom-call(bf16[256,1024]{1,0:T(8,128)(2,1)} %get-tuple-element.150.refs_0_, bf16[4,4,32,1152]{3,2,1,0:T(8,128)(2,1)} %bitcast.114, bf16[2,512,2176]{2,1,0:T(8,128)(2,1)} %get-tuple-element.152.refs_2_), custom_call_target="tpu_custom_call" | custom-call | bytes 220200960 | tf_op jit(solution)/shard_map/pallas_call | solution.py:323
  733.6 59.9 %shard_map.248 = (bf16[4,256,1024]{2,1,0:T(8,128)(2,1)}, f32[4,8,256]{2,1,0:T(8,128)}, bf16[8,8,128,512]{3,2,1,0:T(8,128)(2,1)}, bf16[8,8,256,512]{3,2,1,0:T(8,128)(2,1)}, bf16[8,256,512]{2,1,0:T(8,128)(2,1)}) custom-call(bf16[4,256,1024]{2,1,0:T(8,128)(2,1)} %get-tuple-element.113.x_ref, bf16[4,256,1024]{2,1,0:T(8,128)(2,1)} %get-tuple-element.153.gr_ref, ...), custom_call_target="tpu_custom_call" | custom-call | flops 33822867456 | bytes 60915712 | tf_op jit(solution)/shard_map/pallas_call | solution.py:40
  794.9 1.0 reduce_sum.68.refs_3_
  795.9 3.7 fusion.1
  799.6 55.4 %shard_map.249 = (bf16[4,256,1024]{2,1,0:T(8,128)(2,1)}, f32[4,8,256]{2,1,0:T(8,128)}, bf16[4,4,32,2176]{3,2,1,0:T(8,128)(2,1)}, bf16[4,32,1152]{2,1,0:T(8,128)(2,1)}) custom-call(bf16[4,256,1024]{2,1,0:T(8,128)(2,1)} %get-tuple-element.155.refs_0_, f32[4,8,256]{2,1,0:T(8,128)} %get-tuple-element.156.refs_1_, bf16[4,4,32,2176]{3,2,1,0:T(8,128)(2,1)} %bitcast.108, ...), custom_call_target="tpu_custom_call" | custom-call | bytes 186122240 | tf_op jit(solution)/shard_map/pallas_call | solution.py:323
  855.0 2.9 reduce_sum.69.rest_0_
  857.9 29.3 %shard_map.250 = (f32[256,1024]{1,0:T(8,128)}, bf16[2,512,1152]{2,1,0:T(8,128)(2,1)}, bf16[8,256,128]{2,1,0:T(8,128)(2,1)}, bf16[4,32,2176]{2,1,0:T(8,128)(2,1)}) custom-call(bf16[4,256,1024]{2,1,0:T(8,128)(2,1)} %get-tuple-element.159.p_ref, f32[4,8,256]{2,1,0:T(8,128)} %get-tuple-element.160.dg_ref, f32[4,8,256]{2,1,0:T(8,128)} %get-tuple-element.112.refs_1_.gt_ref, ...), custom_call_target="tpu_custom_call" | custom-call | flops 1073741824 | bytes 23494656 | tf_op jit(solution)/shard_map/pallas_call | solution.py:40
  887.2 51.2 %shard_map.251 = (bf16[8,256,256]{2,1,0:T(8,128)(2,1)}, bf16[512,1152]{1,0:T(8,128)(2,1)}, bf16[8,128,512]{2,1,0:T(8,128)(2,1)}) custom-call(bf16[8,256,256]{2,1,0:T(8,128)(2,1)} %get-tuple-element.107.x_ref, bf16[8,256,128]{2,1,0:T(8,128)(2,1)} %get-tuple-element.163.d_ref, bf16[8,256,128]{2,1,0:T(8,128)(2,1)} %get-tuple-element.164.o_ref, ...), custom_call_target="tpu_custom_call" | custom-call | flops 1342177280 | bytes 9846784 | tf_op jit(solution)/shard_map/pallas_call | solution.py:40
  938.4 8.6 shard_map.252
  947.0 2.0 dynamic-slice_bitcast_fusion
  949.1 1.3 collective-permute-start
  950.4 1.0 add_convert_fusion
  951.4 1.3 fusion.2
  952.6 1.7 collective-permute-done
  954.4 1.9 fusion
  956.2 56.0 %shard_map.253 = (bf16[4,4,32,2176]{3,2,1,0:T(8,128)(2,1)}, bf16[8,256,512]{2,1,0:T(8,128)(2,1)}, bf16[4,4,32,1152]{3,2,1,0:T(8,128)(2,1)}) custom-call(bf16[4,4,32,2176]{3,2,1,0:T(8,128)(2,1)} %bitcast.107, bf16[8,256,512]{2,1,0:T(8,128)(2,1)} %bitcast.117, bf16[4,4,32,1152]{3,2,1,0:T(8,128)(2,1)} %bitcast.113), custom_call_target="tpu_custom_call" | custom-call | bytes 220200960 | tf_op jit(solution)/shard_map/pallas_call | solution.py:323
  1012.3 3.0 reduce_sum.70.refs_0_
  1015.3 0.9 reduce_sum.71.refs_2_
  1016.2 44.3 %shard_map.254 = (bf16[4,32,2176]{2,1,0:T(8,128)(2,1)}, bf16[8,128,512]{2,1,0:T(8,128)(2,1)}, bf16[4,32,1152]{2,1,0:T(8,128)(2,1)}) custom-call(bf16[4,32,2176]{2,1,0:T(8,128)(2,1)} %reduce_sum.70.refs_0_, bf16[8,128,512]{2,1,0:T(8,128)(2,1)} %bitcast.118, bf16[4,32,1152]{2,1,0:T(8,128)(2,1)} %reduce_sum.71.refs_2_), custom_call_target="tpu_custom_call" | custom-call | bytes 76021760 | tf_op jit(solution)/shard_map/pallas_call | solution.py:323
  1060.5 2.3 shard_map.255
  1062.9 1.4 slice_reduce_fusion.1
  1064.3 1.5 slice_reduce_fusion
  1067.3 8.7 shard_map.256
  (110 shorter events, 10.7 us)
Async XLA Ops:
  7.2 23.1 %copy-start.17 = (bf16[2,32,32]{2,1,0:T(8,128)(2,1)S(1)}, bf16[2,32,32]{2,1,0:T(8,128)(2,1)}, u32[]{:S(2)}) copy-start(bf16[2,32,32]{2,1,0:T(8,128)(2,1)} %param.24) | copy-start | bytes 12292
  7.2 23.3 %copy-start.19 = (bf16[2,32]{1,0:T(2,128)(2,1)S(1)}, bf16[2,32]{1,0:T(2,128)(2,1)}, u32[]{:S(2)}) copy-start(bf16[2,32]{1,0:T(2,128)(2,1)} %param.18) | copy-start | bytes 388
  7.2 23.4 %copy-start.20 = (bf16[2,32]{1,0:T(2,128)(2,1)S(1)}, bf16[2,32]{1,0:T(2,128)(2,1)}, u32[]{:S(2)}) copy-start(bf16[2,32]{1,0:T(2,128)(2,1)} %param.23) | copy-start | bytes 388
  7.2 23.5 %copy-start.5 = (bf16[2,8,64,1024]{3,2,1,0:T(8,128)(2,1)S(1)}, bf16[2,8,64,1024]{3,2,1,0:T(8,128)(2,1)}, u32[]{:S(2)}) copy-start(bf16[2,8,64,1024]{3,2,1,0:T(8,128)(2,1)} %param.27) | copy-start | bytes 6291460
  7.2 234.9 %all-gather.12.cloned.1.call-start = ((), (), s32[]{:S(2)}) async-start(), calls=%async_computation.11 | async-start | bytes 9437184 | tf_op jit(solution)/shard_map/all_gather | solution.py:1231
  30.7 1.6 copy-start.6
  32.3 0.9 copy-start.13
  32.3 1.0 copy-start.14
  32.4 1.0 copy-start.15
  32.4 1.0 copy-start.16
  35.9 206.2 %all-gather.14.cloned.1.call-start = ((), (), s32[]{:S(2)}) async-start(), calls=%async_computation.12 | async-start | bytes 18874368 | tf_op jit(solution)/shard_map/all_gather | solution.py:1231
  36.0 71.5 %copy-start.12 = (s32[2,1024]{1,0:T(2,128)S(1)}, s32[2,1024]{1,0:T(2,128)}, u32[]{:S(2)}) copy-start(s32[2,1024]{1,0:T(2,128)} %param.16) | copy-start | bytes 24580
  106.2 3.4 copy-start.18
  106.2 249.7 %all-gather.10.cloned.1.call-start = ((), (), s32[]{:S(2)}) async-start(), calls=%async_computation.5 | async-start | bytes 6758400 | tf_op jit(solution)/shard_map/all_gather | solution.py:1240
  107.5 357.5 %all-gather.16.cloned.1.call-start = ((), (), s32[]{:S(2)}) async-start(), calls=%async_computation.13 | async-start | bytes 9437184 | tf_op jit(solution)/shard_map/all_gather | solution.py:1231
  240.3 226.8 %all-gather.18.cloned.1.call-start = ((), (), s32[]{:S(2)}) async-start(), calls=%async_computation.14 | async-start | bytes 18874368 | tf_op jit(solution)/shard_map/all_gather | solution.py:1231
  289.1 277.1 %reduce-scatter.6.cloned.1.call-start = ((), (), s32[]{:S(2)}) async-start(), calls=%async_computation.6 | async-start | bytes 2621440 | tf_op jit(solution)/shard_map/reduce_scatter | solution.py:1316
  510.0 223.6 %reduce-scatter.8.cloned.1.call-start = ((), (), s32[]{:S(2)}) async-start(), calls=%async_computation.7 | async-start | bytes 18874368 | tf_op jit(solution)/shard_map/reduce_scatter | solution.py:1320
  566.2 321.0 %reduce-scatter.10.cloned.1.call-start = ((), (), s32[]{:S(2)}) async-start(), calls=%async_computation.8 | async-start | bytes 9437184 | tf_op jit(solution)/shard_map/reduce_scatter | solution.py:1320
  626.6 329.7 %reduce-scatter.12.cloned.1.call-start = ((), (), s32[]{:S(2)}) async-start(), calls=%async_computation.9 | async-start | bytes 18874368 | tf_op jit(solution)/shard_map/reduce_scatter | solution.py:1320
  678.4 9.1 copy-start
  678.4 9.1 copy-start.10
  793.6 222.6 %reduce-scatter.14.cloned.1.call-start = ((), (), s32[]{:S(2)}) async-start(), calls=%async_computation.10 | async-start | bytes 9437184 | tf_op jit(solution)/shard_map/reduce_scatter | solution.py:1320
  793.6 1.3 copy-start.7
  793.6 2.2 copy-start.4
  938.4 12.0 %copy-start.11 = (bf16[1,256,1024]{2,1,0:T(8,128)(2,1)S(1)}, bf16[1,256,1024]{2,1,0:T(8,128)(2,1)}, u32[]{:S(2)}) copy-start(bf16[1,256,1024]{2,1,0:T(8,128)(2,1)} %reduce-scatter.6.cloned.1.call-done) | copy-start | bytes 1572868
  947.0 3.4 copy-start.3
  947.0 4.3 copy-start.1
  947.0 4.3 copy-start.9
  949.1 5.3 collective-permute-start
  950.4 4.0 copy-start.2
  1012.3 3.0 copy-start.8
Sparse Core Ops, SparseCore 0:
  36.0 87.9 all-gather.11
  125.9 89.0 all-gather.13
  218.5 101.7 all-gather.9
  322.0 53.4 all-gather.15
  377.2 89.8 all-gather.17
  510.1 54.0 reduce-scatter.5
  568.1 124.3 reduce-scatter.7
  696.4 71.2 reduce-scatter.9
  793.7 114.1 reduce-scatter.11
  911.2 88.6 reduce-scatter.13
